TPU v7x, 32 devices: a whole 2x2x4 slice. The times are simulated.
32 devices in a mesh: dp: 16 (over z, y, x), rep: 2 (over core).
Axes of the slice: x: 2, y: 2, z: 4, core: 2. Of those that a mesh axis runs over, the one named last changes fastest.
Arguments:
- table: float32 [131072, 400], P(('dp', 'rep')), may hold values from -6 to 6
- batch_index: int32 [32768], P(('dp', 'rep')), may hold values from 0 to 4095
- labels: int32 [32768], P(('dp', 'rep')), may hold values from 0 to 46
- w_branch: float32 [4, 100, 512], P(None, None, 'dp'), may hold values from -0.625 to 0.625
- w_merge: float32 [2048, 512], P('dp'), may hold values from -0.125 to 0.125
- w_class: float32 [512, 47], P('dp'), may hold values from -0.5 to 0.5
- small_params: float32 [20, 512], P(None, 'dp'), as said below
- first_branch: float32 [4, 100, 512], P(None, None, 'dp'), may hold values from -0.0014648438 to 0.0014648438
- first_merge: float32 [2048, 512], P('dp'), may hold values from -0.0014648438 to 0.0014648438
- first_class: float32 [512, 47], P('dp'), may hold values from -0.0014648438 to 0.0014648438
- first_small: float32 [20, 512], P(None, 'dp'), may hold values from -0.00390625 to 0.00390625
- second_branch: float32 [4, 100, 512], P(None, None, 'dp'), may hold values from 7.7659046e-10 to 3.1063618e-09
- second_merge: float32 [2048, 512], P('dp'), may hold values from 7.7659046e-10 to 3.1063618e-09
- second_class: float32 [512, 47], P('dp'), may hold values from 7.7659046e-10 to 3.1063618e-09
- second_small: float32 [20, 512], P(None, 'dp'), may hold values from 6.989314e-09 to 2.7957256e-08
Outputs:
- new_branch: float32 [4, 100, 512], P(None, None, 'dp')
- new_merge: float32 [2048, 512], P('dp')
- new_class: float32 [512, 47], P('dp')
- new_small: float32 [20, 512], P(None, 'dp')
- moment_branch: float32 [4, 100, 512], P(None, None, 'dp')
- moment_merge: float32 [2048, 512], P('dp')
- moment_class: float32 [512, 47], P('dp')
- moment_small: float32 [20, 512], P(None, 'dp')
- square_branch: float32 [4, 100, 512], P(None, None, 'dp')
- square_merge: float32 [2048, 512], P('dp')
- square_class: float32 [512, 47], P('dp')
- square_small: float32 [20, 512], P(None, 'dp')
- copy_branch: bfloat16 [4, 100, 512], P(None, None, 'dp')
- copy_merge: bfloat16 [2048, 512], P('dp')
- copy_class: bfloat16 [512, 47], P('dp')
- copy_small: bfloat16 [20, 512], P(None, 'dp')
- grad_norm: float32 [], replicated
- row_grads: float32 [32768, 400], P(('dp', 'rep'))
Inputs may be any that keep to these rules, and one draw needn't show every extreme that they name: `batch_index`: each entry indexes a row of the block of 4096 table rows that lies on the same device as the entry. `small_params`: gains lie in 0.3 to 2.0, slopes in 0.05 to 0.45.
All inputs are finite; a program needn't handle non-finite values.
Results may differ from a plain program's by a relative error of at most 0.011.
Values may be sent and summed in bfloat16 or wider, within the bound.
No kernel may reach another device: no remote copies, remote signals or barrier semaphores. Data moves between devices by JAX's collectives and lax.ppermute only.
A program may use at most 128 MiB of HBM per device.

v0:
```python
import jax
import jax.numpy as jnp
from jax import lax
from jax.sharding import PartitionSpec as P

HOPS = 4
STEP = 7


EPS_NORM = 1e-05


def leaky(value, slope):
    return slope * value + (1.0 - slope) * value * jax.nn.sigmoid(value)


def leaky_back(upstream, value, slope):
    sig = jax.nn.sigmoid(value)
    slope_term = jnp.sum(upstream * value * (1.0 - sig), axis=0)
    derivative = slope + (1.0 - slope) * (sig + value * sig * (1.0 - sig))
    return (upstream * derivative, slope_term)


def cross_dot(left, right):
    return lax.dot_general(
        left, right, (((0,), (0,)), ((), ())), preferred_element_type=jnp.float32
    )


def back_dot(left, right):
    return lax.dot_general(
        left, right, (((1,), (1,)), ((), ())), preferred_element_type=jnp.float32
    )


def adamw(weight, grad, moment, square, scale, rate):
    clipped = grad * scale
    moment_new = 0.9 * moment + 0.1 * clipped
    square_new = 0.999 * square + 0.001 * clipped * clipped
    fix_one = 1.0 - 0.9**STEP
    fix_two = 1.0 - 0.999**STEP
    update = moment_new / fix_one / (jnp.sqrt(square_new / fix_two) + 1e-08) + 0.01 * weight
    weight_new = weight - rate * update
    return (weight_new, moment_new, square_new)


def on_device(
    table,
    batch_index,
    labels,
    w_branch,
    w_merge,
    w_class,
    small_params,
    first_branch,
    first_merge,
    first_class,
    first_small,
    second_branch,
    second_merge,
    second_class,
    second_small,
):
    batch = batch_index.shape[0]
    row_count = batch * lax.axis_size("dp") * lax.axis_size("rep")
    d_in = w_branch.shape[1]
    hidden = w_merge.shape[1]
    hidden_width = HOPS * hidden
    classes = w_class.shape[1]
    rows = jnp.take(table, batch_index, axis=0)
    input_features = rows.astype(jnp.bfloat16).reshape(batch, HOPS, d_in)
    branch_full, merge_full, class_full, small_full = (
        lax.all_gather(w_branch.astype(jnp.bfloat16), "dp", axis=2, tiled=True),
        lax.all_gather(w_merge.astype(jnp.bfloat16), "dp", axis=0, tiled=True),
        lax.all_gather(w_class.astype(jnp.bfloat16), "dp", axis=0, tiled=True),
        lax.all_gather(small_params.astype(jnp.bfloat16), "dp", axis=1, tiled=True),
    )
    params = small_full.astype(jnp.float32)
    gain1 = params[0:HOPS].reshape(hidden_width)
    shift1 = params[HOPS : 2 * HOPS].reshape(hidden_width)
    slope1 = params[2 * HOPS : 3 * HOPS].reshape(hidden_width)
    slope_join = params[3 * HOPS : 4 * HOPS].reshape(hidden_width)
    gain2 = params[4 * HOPS]
    shift2 = params[4 * HOPS + 1]
    slope2 = params[4 * HOPS + 2]
    bias3 = params[4 * HOPS + 3, :classes]
    first_pre = jnp.einsum(
        "fsq,sqv->fsv", input_features, branch_full, preferred_element_type=jnp.float32
    ).reshape(batch, hidden_width)
    sums_one = lax.psum(
        (jnp.sum(first_pre, axis=0), jnp.sum(first_pre * first_pre, axis=0)), ("dp", "rep")
    )
    mean1 = sums_one[0] / row_count
    inv1 = lax.rsqrt(sums_one[1] / row_count - mean1 * mean1 + EPS_NORM)
    norm1 = (first_pre - mean1) * inv1
    lin1 = gain1 * norm1 + shift1
    act1 = leaky(lin1, slope1)
    joined_low = leaky(act1, slope_join).astype(jnp.bfloat16)
    pre2 = jnp.dot(joined_low, merge_full, preferred_element_type=jnp.float32)
    sums_two = lax.psum((jnp.sum(pre2, axis=0), jnp.sum(pre2 * pre2, axis=0)), ("dp", "rep"))
    mean2 = sums_two[0] / row_count
    inv2 = lax.rsqrt(sums_two[1] / row_count - mean2 * mean2 + EPS_NORM)
    norm2 = (pre2 - mean2) * inv2
    lin2 = gain2 * norm2 + shift2
    act2_low = leaky(lin2, slope2).astype(jnp.bfloat16)
    logits = jnp.dot(act2_low, class_full, preferred_element_type=jnp.float32) + bias3
    probs = jax.nn.softmax(logits, axis=1)
    onehot = (labels[:, None] == jnp.arange(classes, dtype=jnp.int32)[None, :]).astype(jnp.float32)
    dlogits = (probs - onehot).astype(jnp.bfloat16)
    branch_back, merge_back, class_back = (
        lax.all_gather(w_branch.astype(jnp.bfloat16), "dp", axis=2, tiled=True),
        lax.all_gather(w_merge.astype(jnp.bfloat16), "dp", axis=0, tiled=True),
        lax.all_gather(w_class.astype(jnp.bfloat16), "dp", axis=0, tiled=True),
    )
    grad_class = cross_dot(act2_low, dlogits)
    grad_bias3 = jnp.sum(dlogits.astype(jnp.float32), axis=0)
    dact2 = back_dot(dlogits, class_back)
    dy2, grad_slope2 = leaky_back(dact2, lin2, slope2)
    gain2_part = jnp.sum(dy2 * norm2, axis=0)
    shift2_part = jnp.sum(dy2, axis=0)
    totals_two = lax.psum((shift2_part, gain2_part), ("dp", "rep"))
    dpre2 = (
        inv2
        * (
            gain2 * dy2
            - gain2 * totals_two[0] / row_count
            - norm2 * gain2 * totals_two[1] / row_count
        )
    ).astype(jnp.bfloat16)
    grad_merge = cross_dot(joined_low, dpre2)
    djoined = back_dot(dpre2, merge_back)
    dact1, grad_slope_join = leaky_back(djoined, act1, slope_join)
    dy1, grad_slope1 = leaky_back(dact1, lin1, slope1)
    gain1_part = jnp.sum(dy1 * norm1, axis=0)
    shift1_part = jnp.sum(dy1, axis=0)
    totals_one = lax.psum((shift1_part, gain1_part), ("dp", "rep"))
    first_grad = (
        inv1
        * (
            gain1 * dy1
            - gain1 * totals_one[0] / row_count
            - norm1 * gain1 * totals_one[1] / row_count
        )
    ).astype(jnp.bfloat16)
    first_grad = first_grad.reshape(batch, HOPS, hidden)
    branch_gradient = jnp.einsum(
        "pze,pzv->zev", input_features, first_grad, preferred_element_type=jnp.float32
    )
    row_grads = jnp.einsum(
        "fsz,sez->fse", first_grad, branch_back, preferred_element_type=jnp.float32
    ).reshape(batch, HOPS * d_in)
    bias_row = jnp.zeros((hidden,), jnp.float32).at[:classes].set(grad_bias3)
    grad_small = jnp.concatenate(
        [
            gain1_part.reshape(HOPS, hidden),
            shift1_part.reshape(HOPS, hidden),
            grad_slope1.reshape(HOPS, hidden),
            grad_slope_join.reshape(HOPS, hidden),
            gain2_part[None],
            shift2_part[None],
            grad_slope2[None],
            bias_row[None],
        ],
        axis=0,
    )
    paired = (
        lax.psum(branch_gradient.astype(jnp.bfloat16), "rep").astype(jnp.float32),
        lax.psum(grad_merge.astype(jnp.bfloat16), "rep").astype(jnp.float32),
        lax.psum(grad_class.astype(jnp.bfloat16), "rep").astype(jnp.float32),
        lax.psum(grad_small.astype(jnp.bfloat16), "rep").astype(jnp.float32),
    )
    shares = (
        lax.psum_scatter(paired[0], "dp", scatter_dimension=2, tiled=True),
        lax.psum_scatter(paired[1], "dp", scatter_dimension=0, tiled=True),
        lax.psum_scatter(paired[2], "dp", scatter_dimension=0, tiled=True),
        lax.psum_scatter(paired[3], "dp", scatter_dimension=1, tiled=True),
    )
    local_squares = jnp.float32(0.0)
    for share in shares:
        local_squares = local_squares + jnp.sum(share * share)
    grad_norm = jnp.sqrt(lax.psum(local_squares, "dp"))
    scale = 1.0 / jnp.maximum(grad_norm, 1.0)
    weights = (w_branch, w_merge, w_class, small_params)
    firsts = (first_branch, first_merge, first_class, first_small)
    seconds = (second_branch, second_merge, second_class, second_small)
    rates = (0.05, 0.05, 0.05, 0.3)
    results = [
        adamw(w, g, m, v, scale, r)
        for w, g, m, v, r in zip(weights, shares, firsts, seconds, rates)
    ]
    news = tuple((r[0] for r in results))
    moments = tuple((r[1] for r in results))
    squares = tuple((r[2] for r in results))
    copies = tuple((r.astype(jnp.bfloat16) for r in news))
    return (
        news[0],
        news[1],
        news[2],
        news[3],
        moments[0],
        moments[1],
        moments[2],
        moments[3],
        squares[0],
        squares[1],
        squares[2],
        squares[3],
        copies[0],
        copies[1],
        copies[2],
        copies[3],
        grad_norm,
        row_grads,
    )


def solution(mesh):
    placed = (
        P(("dp", "rep"), None),
        P(("dp", "rep")),
        P(("dp", "rep")),
        P(None, None, "dp"),
        P("dp", None),
        P("dp", None),
        P(None, "dp"),
        P(None, None, "dp"),
        P("dp", None),
        P("dp", None),
        P(None, "dp"),
        P(None, None, "dp"),
        P("dp", None),
        P("dp", None),
        P(None, "dp"),
    )
    return jax.shard_map(
        on_device,
        mesh=mesh,
        in_specs=placed,
        out_specs=(
            P(None, None, "dp"),
            P("dp", None),
            P("dp", None),
            P(None, "dp"),
            P(None, None, "dp"),
            P("dp", None),
            P("dp", None),
            P(None, "dp"),
            P(None, None, "dp"),
            P("dp", None),
            P("dp", None),
            P(None, "dp"),
            P(None, None, "dp"),
            P("dp", None),
            P("dp", None),
            P(None, "dp"),
            P(),
            P(("dp", "rep"), None),
        ),
        check_vma=False,
    )
```

profile of v0, /device:TPU:0, one launch (start us, length us, event | category | flops | bytes accessed | tf_op | source)
XLA Modules:
  0.0 804.2 jit_solution(16714491165405822003)
XLA Ops:
  7.2 1.6 convert_element_type.82
  11.8 0.8 convert_element_type.78
  12.6 43.0 %all-gather = bf16[16,32,20]{1,2,0:T(8,128)(2,1)S(1)} all-gather(bf16[1,32,20]{1,2,0:T(8,128)(2,1)S(1)} %convert_bitcast_fusion), channel_id=1, replica_groups=mesh['dp'=16,'rep'=2] {'dp'}, dimensions={0}, use_global_device_ids=true | all-gather | bytes 21760 | tf_op jit(solution)/shard_map/all_gather | solution.py:76
  55.8 40.4 %all_gather.15 = bf16[4,100,512]{1,2,0:T(8,128)(2,1)S(1)} all-gather(bf16[4,100,32]{1,2,0:T(8,128)(2,1)S(1)} %convert_element_type.78), channel_id=1, replica_groups=mesh['dp'=16,'rep'=2] {'dp'}, dimensions={2}, use_global_device_ids=true | all-gather | bytes 435200 | tf_op jit(solution)/shard_map/all_gather | solution.py:73
  96.2 6.9 copy.50
  103.1 6.7 gather_fusion
  110.5 4.5 fusion
  115.0 9.2 %copy.53 = f32[1024,2048]{1,0:T(8,128)} copy(f32[1024,2048]{0,1:T(8,128)} %bitcast.71) | data formatting | bytes 16777216 | tf_op jit(solution)/shard_map/reshape | solution.py:89
  124.2 37.0 %all-reduce.4 = (f32[2048]{0:T(1024)S(1)}, f32[2048]{0:T(1024)S(1)}) all-reduce(f32[2048]{0:T(1024)S(1)} %bitcast.97, f32[2048]{0:T(1024)S(1)} %bitcast.96), channel_id=1, replica_groups=mesh['dp'=16,'rep'=2] {'dp','rep'}, use_global_device_ids=true, to_apply=%region_3.4 | all-reduce | flops 4096 | bytes 32768 | tf_op jit(solution)/shard_map/psum | solution.py:90
  161.1 43.3 %all_gather.18 = bf16[512,47]{1,0:T(8,128)(2,1)} all-gather(bf16[32,47]{1,0:T(8,128)(2,1)S(1)} %convert_element_type.84), channel_id=1, replica_groups=mesh['dp'=16,'rep'=2] {'dp'}, dimensions={0}, use_global_device_ids=true | all-gather | bytes 51136 | tf_op jit(solution)/shard_map/all_gather | solution.py:75
  205.5 9.1 %add_convert_fusion = bf16[1024,2048]{1,0:T(8,128)(2,1)} fusion(f32[2048]{0:T(1024)S(1)} %get-tuple-element.89, f32[2048]{0:T(1024)S(1)} %bitcast.86, f32[2048]{0:T(1024)S(1)} %broadcast_subtract_fusion.1, f32[2048]{0:T(1024)S(1)} %bitcast.92, f32[2048]{0:T(1024)S(1)} %get-tuple-element.82, f32[1024,2048]{1,0:T(8,128)} %copy.53, ...), kind=kLoop, calls=%fused_computation.10 | loop fusion | flops 39845888 | bytes 12648448 | tf_op jit(solution)/shard_map/convert_element_type | solution.py:98
  214.7 5.2 multiply_reduce_fusion.5
  219.9 37.1 %all-reduce.3 = (f32[512]{0:T(512)}, f32[512]{0:T(512)}) all-reduce(f32[512]{0:T(512)S(1)} %get-tuple-element.40, f32[512]{0:T(512)S(1)} %get-tuple-element.39), channel_id=1, replica_groups=mesh['dp'=16,'rep'=2] {'dp','rep'}, use_global_device_ids=true, to_apply=%region_7.8 | all-reduce | flops 1024 | bytes 8192 | tf_op jit(solution)/shard_map/psum | solution.py:100
  257.7 1.6 add_convert_fusion.1
  259.2 1.3 fusion.32
  260.7 1.4 fusion.30
  262.0 1.1 convolution_convert_fusion.1
  263.2 4.2 multiply_reduce_fusion.3
  268.6 41.4 %all-reduce.2 = (f32[512]{0:T(512)}, f32[512]{0:T(512)}) all-reduce(f32[512]{0:T(512)} %copy-done.14, f32[512]{0:T(512)} %copy-done.15), channel_id=1, replica_groups=mesh['dp'=16,'rep'=2] {'dp','rep'}, use_global_device_ids=true, to_apply=%region_13.14 | all-reduce | flops 1024 | bytes 8192 | tf_op jit(solution)/shard_map/psum | solution.py:121
  310.0 0.8 multiply_multiply_fusion.5
  310.9 2.7 multiply_convert_fusion.1
  313.6 3.8 convolution_convert_fusion
  317.4 13.9 %multiply_reduce_fusion = (bf16[2048]{0:T(1024)(128)(2,1)S(1)}, bf16[2048]{0:T(1024)(128)(2,1)S(1)}, f32[2048]{0:T(1024)S(1)}, f32[2048]{0:T(1024)S(1)}, f32[1024,2048]{1,0:T(8,128)}) fusion(f32[2048]{0:T(1024)S(1)} %broadcast_subtract_fusion.1, f32[2048]{0:T(1024)S(1)} %bitcast.93, f32[2048]{0:T(1024)S(1)} %get-tuple-element.82, ...), kind=kOutput, calls=%fused_computation.4 | convolution fusion | flops 2225070080 | bytes 20013056 | tf_op jit(solution)/shard_map/dot_general | solution.py:31
  331.3 40.2 %all-reduce.1 = (f32[2048]{0:T(1024)S(1)}, f32[2048]{0:T(1024)S(1)}) all-reduce(f32[2048]{0:T(1024)S(1)} %get-tuple-element.32, f32[2048]{0:T(1024)S(1)} %get-tuple-element.33), channel_id=1, replica_groups=mesh['dp'=16,'rep'=2] {'dp','rep'}, use_global_device_ids=true, to_apply=%region_17.18 | all-reduce | flops 4096 | bytes 32768 | tf_op jit(solution)/shard_map/psum | solution.py:136
  371.7 1.9 concatenate.6
  373.8 7.3 multiply_convert_fusion
  381.1 1.9 copy-done
  383.0 2.5 fusion.10
  385.6 5.8 all-reduce.10.cloned.1.call-done
  391.4 1.6 copy.56
  393.1 1.6 convert_element_type.94
  394.8 23.1 %all-reduce.12.cloned.1.call-done = (bf16[4,100,512]{1,2,0:T(8,128)(2,1)}, bf16[2048,512]{1,0:T(8,128)(2,1)}) async-done(((bf16[4,100,512]{1,2,0:T(8,128)(2,1)}, bf16[2048,512]{1,0:T(8,128)(2,1)}), (bf16[4,100,512]{1,2,0:T(8,128)(2,1)}, bf16[2048,512]{1,0:T(8,128)(2,1)})) %all-reduce.12.cloned.1.call-update) | async-done | bytes 2506768 | tf_op jit(solution)/shard_map/psum | solution.py:167
  417.9 2.1 convert_element_type.90
  420.1 4.2 convert_element_type.92
  424.4 3.7 fusion.7
  428.1 69.9 %reduce-scatter.13.cloned.1.call-done = f32[32,20]{1,0:T(8,128)} async-done(((f32[512,20]{1,0:T(8,128)}), f32[32,20]{1,0:T(8,128)}) %reduce-scatter.13.cloned.1.call-update) | async-done | bytes 2576
  499.4 73.8 %reduce-scatter.11.cloned.1.call-done = f32[32,47]{1,0:T(8,128)} async-done(((f32[512,47]{1,0:T(8,128)}), f32[32,47]{1,0:T(8,128)}) %reduce-scatter.11.cloned.1.call-update) | async-done | bytes 6032 | tf_op jit(solution)/shard_map/reduce_scatter | solution.py:175
  573.1 1.3 multiply_reduce_fusion.8
  574.5 75.5 %reduce-scatter.7.cloned.1.call-done = f32[4,100,32]{1,2,0:T(8,128)} async-done(((f32[4,100,512]{1,2,0:T(8,128)}), f32[4,100,32]{1,2,0:T(8,128)}) %reduce-scatter.7.cloned.1.call-update) | async-done | bytes 51216 | tf_op jit(solution)/shard_map/reduce_scatter | solution.py:173
  650.0 1.5 multiply_reduce_fusion.7
  651.5 92.4 %reduce-scatter.9.cloned.1.call-done = f32[128,512]{1,0:T(8,128)} async-done(((f32[2048,512]{1,0:T(8,128)}), f32[128,512]{1,0:T(8,128)}) %reduce-scatter.9.cloned.1.call-update) | async-done | bytes 262160 | tf_op jit(solution)/shard_map/reduce_scatter | solution.py:174
  743.9 1.7 multiply_reduce_fusion.6
  748.2 1.3 reshape.135
  749.5 40.5 %psum.103 = f32[]{:T(128)} all-reduce(f32[]{:T(128)S(6)} %add.234), channel_id=1, replica_groups=mesh['dp'=16,'rep'=2] {'dp'}, use_global_device_ids=true, to_apply=%region_34.35 | all-reduce | flops 1 | bytes 8 | tf_op jit(solution)/shard_map/psum | solution.py:181
  790.8 1.4 fusion.22
  792.2 1.4 fusion.24
  793.5 1.6 fusion.28
  795.1 1.1 fusion.26
  (99 shorter events, 8.9 us)
Async XLA Ops:
  7.2 207.5 %all-gather.3.cloned.1.call-start = ((), (), s32[]{:S(2)}) async-start(), calls=%async_computation.4 | async-start | bytes 2228224 | tf_op jit(solution)/shard_map/all_gather | solution.py:74
  8.9 382.5 %all-reduce.10.cloned.1.call-start = ((), (), s32[]{:S(2)}) async-start(), calls=%async_computation.9 | async-start | bytes 311296 | tf_op jit(solution)/shard_map/psum | solution.py:169
  9.6 100.9 %copy-start.16 = (pred[1024]{0:T(1024)(128)(4,1)}, pred[1024]{0:T(1024)(128)(4,1)S(1)}, u32[]{:S(2)}) copy-start(pred[1024]{0:T(1024)(128)(4,1)S(1)} %compare_and_fusion) | copy-start | bytes 3076
  256.9 6.2 copy-start.4
  267.4 0.6 copy-start.14
  267.4 1.1 copy-start.15
  310.0 3.5 copy-start.1
  310.8 6.5 slice-start
  313.5 3.8 slice-start.1
  313.6 3.8 copy-start.21
  317.4 54.2 %copy-start.20 = (bf16[512]{0:T(512)(128)(2,1)S(1)}, bf16[512]{0:T(512)(128)(2,1)}, u32[]{:S(2)}) copy-start(bf16[512]{0:T(512)(128)(2,1)} %get-tuple-element.36) | copy-start | bytes 3076
  317.4 54.2 %copy-start.18 = (bf16[512]{0:T(512)(128)(2,1)S(1)}, bf16[512]{0:T(512)(128)(2,1)}, u32[]{:S(2)}) copy-start(bf16[512]{0:T(512)(128)(2,1)} %convert.38) | copy-start | bytes 3076
  317.4 54.2 %copy-start.19 = (bf16[47]{0:T(256)(128)(2,1)S(1)}, bf16[47]{0:T(256)(128)(2,1)}, u32[]{:S(2)}) copy-start(bf16[47]{0:T(256)(128)(2,1)} %get-tuple-element.69) | copy-start | bytes 286
  373.5 44.4 %all-reduce.12.cloned.1.call-start = ((), (), s32[]{:S(2)}) async-start(), calls=%async_computation.10 | async-start | bytes 5242880 | tf_op jit(solution)/shard_map/psum | solution.py:167
  373.8 9.2 %copy-start.17 = (pred[1024]{0:T(1024)(128)(4,1)S(1)}, pred[1024]{0:T(1024)(128)(4,1)}, u32[]{:S(2)}) copy-start(pred[1024]{0:T(1024)(128)(4,1)} %copy-done.16) | copy-start | bytes 3076
  381.1 1.9 copy-start
  385.5 112.5 %reduce-scatter.13.cloned.1.call-start = ((), (), s32[]{:S(2)}) async-start(), calls=%async_computation.8 | async-start | bytes 278528
  393.0 180.1 %reduce-scatter.11.cloned.1.call-start = ((), (), s32[]{:S(2)}) async-start(), calls=%async_computation.7 | async-start | bytes 278528 | tf_op jit(solution)/shard_map/reduce_scatter | solution.py:175
  394.7 255.3 %reduce-scatter.7.cloned.1.call-start = ((), (), s32[]{:S(2)}) async-start(), calls=%async_computation.5 | async-start | bytes 1114112 | tf_op jit(solution)/shard_map/reduce_scatter | solution.py:173
  420.0 323.9 %reduce-scatter.9.cloned.1.call-start = ((), (), s32[]{:S(2)}) async-start(), calls=%async_computation.6 | async-start | bytes 4456448 | tf_op jit(solution)/shard_map/reduce_scatter | solution.py:174
  424.2 366.6 %copy-start.11 = (f32[20,32]{1,0:T(8,128)S(1)}, f32[20,32]{1,0:T(8,128)}, u32[]{:S(2)}) copy-start(f32[20,32]{1,0:T(8,128)} %param.23) | copy-start | bytes 7684
  424.2 367.9 %copy-start.10 = (f32[32,47]{1,0:T(8,128)S(1)}, f32[32,47]{1,0:T(8,128)}, u32[]{:S(2)}) copy-start(f32[32,47]{1,0:T(8,128)} %param.22) | copy-start | bytes 18052
  424.3 367.9 %copy-start.12 = (f32[32,47]{1,0:T(8,128)S(1)}, f32[32,47]{1,0:T(8,128)}, u32[]{:S(2)}) copy-start(f32[32,47]{1,0:T(8,128)} %param.26) | copy-start | bytes 18052
  424.3 367.9 %copy-start.13 = (f32[32,47]{1,0:T(8,128)S(1)}, f32[32,47]{1,0:T(8,128)}, u32[]{:S(2)}) copy-start(f32[32,47]{1,0:T(8,128)} %param.30) | copy-start | bytes 18052
  424.3 369.3 %copy-start.7 = (f32[4,100,32]{1,2,0:T(8,128)S(1)}, f32[4,100,32]{1,2,0:T(8,128)}, u32[]{:S(2)}) copy-start(f32[4,100,32]{1,2,0:T(8,128)} %param.20) | copy-start | bytes 153604
  424.3 369.2 %copy-start.8 = (f32[4,100,32]{1,2,0:T(8,128)S(1)}, f32[4,100,32]{1,2,0:T(8,128)}, u32[]{:S(2)}) copy-start(f32[4,100,32]{1,2,0:T(8,128)} %param.24) | copy-start | bytes 153604
  424.3 369.2 %copy-start.9 = (f32[4,100,32]{1,2,0:T(8,128)S(1)}, f32[4,100,32]{1,2,0:T(8,128)}, u32[]{:S(2)}) copy-start(f32[4,100,32]{1,2,0:T(8,128)} %param.28) | copy-start | bytes 153604
  424.3 370.8 %copy-start.2 = (f32[128,512]{1,0:T(8,128)S(1)}, f32[128,512]{1,0:T(8,128)}, u32[]{:S(2)}) copy-start(f32[128,512]{1,0:T(8,128)} %param.21) | copy-start | bytes 786436
  424.3 370.8 %copy-start.5 = (f32[128,512]{1,0:T(8,128)S(1)}, f32[128,512]{1,0:T(8,128)}, u32[]{:S(2)}) copy-start(f32[128,512]{1,0:T(8,128)} %param.25) | copy-start | bytes 786436
  424.3 370.8 %copy-start.6 = (f32[128,512]{1,0:T(8,128)S(1)}, f32[128,512]{1,0:T(8,128)}, u32[]{:S(2)}) copy-start(f32[128,512]{1,0:T(8,128)} %param.29) | copy-start | bytes 786436
  743.9 51.2 %copy-start.3 = (f32[128,512]{1,0:T(8,128)S(1)}, f32[128,512]{1,0:T(8,128)}, u32[]{:S(2)}) copy-start(f32[128,512]{1,0:T(8,128)} %reduce-scatter.9.cloned.1.call-done) | copy-start | bytes 786436
Sparse Core Ops, SparseCore 0:
  11.4 66.4 all-gather.2
  373.7 17.7 all-reduce.9
  394.4 23.4 all-reduce.11
  420.7 77.2 reduce-scatter.12
  500.6 72.4 reduce-scatter.10
  575.9 74.0 reduce-scatter.6
  652.3 91.5 reduce-scatter.8
where the time goes:
time: 806 us; the launch traced here: 804 us
  waiting for transfers between devices  341 us (42%)
  blocking collectives  323 us (40%)
  other arithmetic  48.4 us (6%)
  matrix products  40.3 us (5%)
  local copies, waits for them, and re-layouts  32.3 us (4%)
  between operations  19 us (2%)
    reduce_scatter x1, waiting for transfers between devices, on_device(): lax.psum_scatter(paired[1], 'dp', scatter_dimension=0, tiled=True)  92.4 us
    reduce_scatter x1, waiting for transfers between devices, on_device(): lax.psum_scatter(paired[0], 'dp', scatter_dimension=2, tiled=True)  75.5 us
    reduce_scatter x1, waiting for transfers between devices, on_device(): lax.psum_scatter(paired[2], 'dp', scatter_dimension=0, tiled=True)  73.8 us
    unnamed x8, waiting for transfers between devices  70 us
    all_gather x1, blocking collectives, on_device(): lax.all_gather(w_class.astype(jnp.bfloat16), 'dp', axis=0, tiled=True)  43.3 us
    all_gather x1, blocking collectives, on_device(): lax.all_gather(small_params.astype(jnp.bfloat16), 'dp', axis=1, tiled=True)  43 us
    psum x1, blocking collectives, on_device(): totals_two = lax.psum((shift2_part, gain2_part), ('dp', 'rep'))  41.4 us
    psum x1, blocking collectives, on_device(): grad_norm = jnp.sqrt(lax.psum(local_squares, 'dp'))  40.5 us
  transfers between devices with their start and end apart: 7, of which 6 were waited for; matrix products, arithmetic and copies ran while one was open for 9% of the time, Pallas kernels for 0%

commit v1 on v0

v1 whole, which is shorter than its diff:
```python
import functools

import jax
import jax.numpy as jnp
from jax import lax
from jax.experimental import pallas as pl
from jax.experimental.pallas import tpu as pltpu
from jax.sharding import PartitionSpec as P

HOPS = 4
STEP = 7
EPS_NORM = 1e-05
LANES = 128
PCOL = 64
BOTH = ("dp", "rep")
F32 = jnp.float32
BF16 = jnp.bfloat16
HIGHEST = lax.Precision.HIGHEST


def dot(left, right, left_dim, right_dim, precision=None):
    return lax.dot_general(
        left,
        right,
        (((left_dim,), (right_dim,)), ((), ())),
        precision=precision,
        preferred_element_type=F32,
    )


def call(body, outs, *args, smem=(), grid=None, in_specs=None, out_specs=None, scratch=(), mib=40, flops=0, moved=0):
    if in_specs is None:
        in_specs = [
            pl.BlockSpec(memory_space=pltpu.SMEM if i in smem else pltpu.VMEM) for i in range(len(args))
        ]
    if out_specs is None:
        out_specs = tuple(pl.BlockSpec(memory_space=pltpu.VMEM) for _ in outs)
    if not moved:
        moved = sum(a.size * a.dtype.itemsize for a in args)
        moved += sum(o.size * o.dtype.itemsize for o in outs)
    kwargs = {} if grid is None else {"grid": grid}
    return pl.pallas_call(
        body,
        out_shape=tuple(outs),
        in_specs=in_specs,
        out_specs=out_specs,
        scratch_shapes=list(scratch),
        compiler_params=pltpu.CompilerParams(vmem_limit_bytes=mib << 20),
        cost_estimate=pl.CostEstimate(flops=flops, bytes_accessed=moved, transcendentals=0),
        **kwargs,
    )(*args)


def sds(shape, dtype=F32):
    return jax.ShapeDtypeStruct(shape, dtype)


def lane_of(shape):
    return lax.broadcasted_iota(jnp.int32, shape, len(shape) - 1)


def to_cols(rows, first):
    parts = []
    for i in range(4):
        row = rows[first + i : first + i + 1, :]
        parts.append(jnp.transpose(jnp.broadcast_to(row, (LANES, LANES))))
    return jnp.concatenate(parts, axis=0)


def lane_sums(part):
    total = jnp.sum(jnp.transpose(part), axis=0, keepdims=True)
    return jnp.concatenate([total[:, i * LANES : (i + 1) * LANES] for i in range(4)], axis=0)


def fold_lanes(value):
    out = value[:, :LANES]
    for i in range(1, value.shape[1] // LANES):
        out = out + value[:, i * LANES : (i + 1) * LANES]
    return out


def prep_kernel(pos_ref, wb_ref, wc_ref, sp_ref, wm_ref, pack_ref, wmh_ref):
    cb = wc_ref.shape[0]
    d_in = wb_ref.shape[2]
    half = wmh_ref.shape[1]
    pack_ref[...] = jnp.zeros_like(pack_ref)
    pack_ref[0:HOPS, :, 0:d_in] = wb_ref[...].astype(BF16)
    pack_ref[HOPS, :, 0 : wc_ref.shape[1]] = wc_ref[...].astype(BF16)
    pack_ref[HOPS, :, PCOL : PCOL + sp_ref.shape[0]] = jnp.transpose(sp_ref[...]).astype(BF16)
    first = pos_ref[1] == 0
    wmh_ref[...] = jnp.where(first, wm_ref[:, :half], wm_ref[:, half:]).astype(BF16)


def gather_kernel(idx_ref, tab_ref, x_ref, gram_ref, acc, pad):
    i = pl.program_id(0)
    width = tab_ref.shape[1]
    d_in = tab_ref.shape[0] // HOPS
    batch = idx_ref.shape[1]
    rows = lax.broadcasted_iota(jnp.int32, (width, batch), 0) + i * width
    hot = jnp.where(rows == idx_ref[...], 1.0, 0.0).astype(BF16)
    part = dot(tab_ref[...].astype(BF16), hot, 1, 0)

    @pl.when(i == 0)
    def _():
        acc[...] = part

    @pl.when(i > 0)
    def _():
        acc[...] += part

    @pl.when(i == pl.num_programs(0) - 1)
    def _():
        row = lax.broadcasted_iota(jnp.int32, pad.shape, 0)
        pad[...] = jnp.where(row == d_in, 1.0, 0.0)
        for k in range(HOPS):
            pad[0:d_in, :] = acc[k * d_in : (k + 1) * d_in, :]
            x = pad[...].astype(BF16)
            x_ref[k] = x
            gram_ref[k] = dot(x, x, 1, 1)


def sum_spread_kernel(in_ref, out_ref):
    out_ref[...] = jnp.broadcast_to(jnp.sum(in_ref[...], axis=0, keepdims=True), out_ref.shape)


def stats_kernel(count, pos_ref, gram_ref, pack_ref, wb_ref, wc_ref, coef_ref, par_ref, tail):
    dp, _, cb, _ = pack_ref.shape
    lane = lane_of((cb * dp, LANES))
    for s in range(dp):
        if dp == 16:
            other = s ^ pos_ref[0]
            j = (other % 4) * 4 + other // 4
        else:
            j = s
        block = pack_ref[j]
        for k in range(HOPS):
            wb_ref[k, s * cb : (s + 1) * cb, :] = block[k]
        tail[s * cb : (s + 1) * cb, :] = block[HOPS].astype(F32)
    small = tail[...]
    wc_ref[...] = jnp.where(lane < PCOL, small, 0.0).astype(BF16)

    def col(i):
        return small[:, PCOL + i : PCOL + i + 1]

    par = jnp.where(lane == 0, col(4 * HOPS), 0.0)
    for i in range(1, 4):
        par = jnp.where(lane == i, col(4 * HOPS + i), par)
    par_ref[...] = par
    for k in range(HOPS):
        w = wb_ref[k].astype(F32)
        wg = dot(w, gram_ref[k], 1, 0, HIGHEST)
        mean = wg[:, ONE : ONE + 1] / count
        second = jnp.sum(wg * w, axis=1, keepdims=True) / count
        inv = lax.rsqrt(second - mean * mean + EPS_NORM)
        gain, shift, slope, join = col(k), col(HOPS + k), col(2 * HOPS + k), col(3 * HOPS + k)
        v = gain * inv
        values = (
            0.5 * v,
            0.5 * (shift - v * mean),
            1.0 + slope,
            1.0 - slope,
            1.0 + join,
            1.0 - join,
            v,
            mean,
            inv,
        )
        coef = jnp.where(lane == 0, values[0], 0.0)
        for i in range(1, len(values)):
            coef = jnp.where(lane == i, values[i], coef)
        coef_ref[k] = coef


ONE = 100


def shard_at(pos_ref, s, dp):
    if dp != 16:
        return s
    other = s ^ pos_ref[0]
    return (other % 4) * 4 + other // 4


ROWS = 16
WIDE = 256


def forward_kernel(pos_ref, x_ref, wb_ref, coef_ref, mine_ref, other_ref, joined_ref, pre2_ref, pay_ref, pre):
    k = pl.program_id(0)
    hid = wb_ref.shape[1]
    batch = x_ref.shape[2]
    half = mine_ref.shape[2]
    pre[...] = dot(wb_ref[0], x_ref[0], 1, 0)

    def group(g, carry):
        at = pl.ds(pl.multiple_of(g * ROWS, ROWS), ROWS)
        cf = coef_ref[0, at, :]
        c = [jnp.broadcast_to(cf[:, i : i + 1], (ROWS, WIDE)) for i in range(6)]
        for b in range(batch // WIDE):
            lanes = slice(b * WIDE, (b + 1) * WIDE)
            u = pre[at, lanes] * c[0] + c[1]
            u = u * (c[2] + c[3] * jnp.tanh(u)) * 0.5
            joined_ref[0, at, lanes] = (u * (c[4] + c[5] * jnp.tanh(u))).astype(BF16)
        return carry

    lax.fori_loop(0, hid // ROWS, group, 0, unroll=2)
    joined = joined_ref[0]
    for ref, which in ((mine_ref, pos_ref[1]), (other_ref, 1 - pos_ref[1])):
        at = pl.ds(pl.multiple_of(which * half, half), half)
        part = dot(merge_at(ref, pos_ref, k), joined, 0, 0)

        @pl.when(k == 0)
        def _():
            pre2_ref[at, :] = part

        @pl.when(k > 0)
        def _():
            pre2_ref[at, :] += part

    @pl.when(k == HOPS - 1)
    def _():
        value = pre2_ref[...]
        sums = jnp.concatenate([lane_sums(fold_lanes(value)), lane_sums(fold_lanes(value * value))], axis=0)
        pay_ref[...] = jnp.broadcast_to(sums[None], pay_ref.shape)


def merge_at(ref, pos_ref, k):
    dp = ref.shape[0]
    per = dp // HOPS
    blocks = []
    for i in range(per):
        s = k * per + i
        blocks.append(ref[shard_at(pos_ref, s, dp)])
    return jnp.concatenate(blocks, axis=0)


def columns2(count, rows, par):
    mean = to_cols(rows, 0) / count
    inv = lax.rsqrt(to_cols(rows, 4) / count - mean * mean + EPS_NORM)
    shape = mean.shape
    gain = jnp.broadcast_to(par[:, 0:1], shape)
    shift = jnp.broadcast_to(par[:, 1:2], shape)
    slope = jnp.broadcast_to(par[:, 2:3], shape)
    return mean, inv, gain, shift, slope


def head_kernel(
    count, classes, got_ref, pre2_ref, par_ref, wc_ref, lab_ref, dy2_ref, pay_ref, class_ref, stat_ref, act, dact, cols, sums
):
    hid, batch = pre2_ref.shape
    par = par_ref[...]
    mean, inv, gain, shift, slope = columns2(count, jnp.sum(got_ref[...], axis=0), par)
    stat_ref[0] = mean
    stat_ref[1] = inv
    cols[0] = 0.5 * gain * inv
    cols[1] = 0.5 * (shift - gain * inv * mean)
    cols[2] = 1.0 + slope
    cols[3] = 1.0 - slope
    reps = WIDE // LANES

    def tiled(c, at):
        return jnp.concatenate([cols[c, at, :]] * reps, axis=1)

    def first(g, carry):
        at = pl.ds(pl.multiple_of(g * ROWS, ROWS), ROWS)
        c = [tiled(i, at) for i in range(4)]
        for b in range(batch // WIDE):
            lanes = slice(b * WIDE, (b + 1) * WIDE)
            u = pre2_ref[at, lanes] * c[0] + c[1]
            act[at, lanes] = (u * (c[2] + c[3] * jnp.tanh(u))).astype(BF16)
        return carry

    lax.fori_loop(0, hid // ROWS, first, 0, unroll=2)
    logits = dot(wc_ref[...], act[...], 0, 0)
    row = lax.broadcasted_iota(jnp.int32, (LANES, batch), 0)
    logits = jnp.where(row < classes, logits + par[0:LANES, 3:4], -jnp.inf)
    top = jnp.max(logits, axis=0, keepdims=True)
    e = jnp.exp(logits - top)
    probs = e / jnp.sum(e, axis=0, keepdims=True)
    dlog = (probs - jnp.where(row == lab_ref[...], 1.0, 0.0)).astype(BF16)
    grad_class = dot(act[...], dlog, 1, 1)
    bias = jnp.sum(dlog.astype(F32), axis=1, keepdims=True)
    dact[...] = dot(wc_ref[...], dlog, 1, 0)

    def second(g, carry):
        at = pl.ds(pl.multiple_of(g * ROWS, ROWS), ROWS)
        c = [tiled(i, at) for i in range(4)]
        m = jnp.concatenate([stat_ref[0, at, :]] * reps, axis=1)
        v = jnp.concatenate([stat_ref[1, at, :]] * reps, axis=1)
        acc = [jnp.zeros((ROWS, WIDE), F32) for _ in range(3)]
        for b in range(batch // WIDE):
            lanes = slice(b * WIDE, (b + 1) * WIDE)
            p = pre2_ref[at, lanes]
            d = dact[at, lanes]
            u = p * c[0] + c[1]
            t = jnp.tanh(u)
            w = u * (1.0 - t)
            dy = d * (0.5 * (c[2] + c[3] * (t + w * (1.0 + t))))
            dy2_ref[at, lanes] = dy
            acc[0] = acc[0] + dy
            acc[1] = acc[1] + dy * ((p - m) * v)
            acc[2] = acc[2] + d * w
        for i in range(3):
            sums[i, at, :] = fold_lanes(acc[i])
        return carry

    lax.fori_loop(0, hid // ROWS, second, 0, unroll=2)
    pay = jnp.concatenate([lane_sums(sums[0]), lane_sums(sums[1])], axis=0)
    pay_ref[...] = jnp.broadcast_to(pay[None], pay_ref.shape)
    lane = lane_of((hid, LANES))
    slope_sum = jnp.sum(sums[2], axis=1, keepdims=True)
    bias = jnp.concatenate([bias, jnp.zeros((hid - LANES, 1), F32)], axis=0)
    block = jnp.where(lane < classes, grad_class, 0.0)
    block = jnp.where(lane == PCOL, slope_sum, block)
    class_ref[...] = jnp.where(lane == PCOL + 1, bias, block)


def turn_kernel(count, pos_ref, got_ref, stat_ref, par_ref, pre2_ref, dy2_ref, joined_ref, class_ref, dpre_ref, keep_ref, send_ref, sum2_ref, cols):
    hid, batch = pre2_ref.shape
    half = keep_ref.shape[2]
    dp, rows, _ = keep_ref.shape
    mr = joined_ref.shape[0] // dp
    cb = hid // dp
    rows8 = jnp.sum(got_ref[...], axis=0)
    sum2_ref[...] = rows8
    shift_sum = to_cols(rows8, 0)
    gain_sum = to_cols(rows8, 4)
    mean, inv = stat_ref[0], stat_ref[1]
    v = jnp.broadcast_to(par_ref[:, 0:1], mean.shape) * inv
    cols[0] = v
    cols[1] = v * shift_sum / count
    cols[2] = v * inv * gain_sum / count
    reps = WIDE // LANES

    def group(g, carry):
        at = pl.ds(pl.multiple_of(g * ROWS, ROWS), ROWS)
        c = [jnp.concatenate([cols[i, at, :]] * reps, axis=1) for i in range(3)]
        m = jnp.concatenate([stat_ref[0, at, :]] * reps, axis=1)
        for b in range(batch // WIDE):
            lanes = slice(b * WIDE, (b + 1) * WIDE)
            value = c[0] * dy2_ref[at, lanes] - c[1] - (pre2_ref[at, lanes] - m) * c[2]
            dpre_ref[at, lanes] = value.astype(BF16)
        return carry

    lax.fori_loop(0, hid // ROWS, group, 0, unroll=2)
    mine = pl.multiple_of(pos_ref[1] * half, half)
    theirs = pl.multiple_of((1 - pos_ref[1]) * half, half)
    for s in range(dp):
        block = joined_ref[s * mr : (s + 1) * mr, :]
        keep_ref[s, 0:mr, :] = dot(block, dpre_ref[pl.ds(mine, half), :], 1, 1)
        send_ref[s, 0:mr, :] = dot(block, dpre_ref[pl.ds(theirs, half), :], 1, 1).astype(BF16)
    first = pos_ref[1] == 0
    for s in range(dp):
        block = class_ref[s * cb : (s + 1) * cb, :]
        wide = jnp.concatenate([block[: cb // 2], block[cb // 2 :]], axis=1)
        keep_ref[s, mr:rows, :] = jnp.where(first, wide, 0.0)
        send_ref[s, mr:rows, :] = jnp.where(first, 0.0, wide).astype(BF16)


def back_kernel(
    pos_ref, dpre_ref, x_ref, wb_ref, coef_ref, mine_ref, other_ref, b_ref, a_ref, pre, dj, dyv, sums, *, hop
):
    hid = wb_ref.shape[1]
    batch = x_ref.shape[2]
    half = mine_ref.shape[2]
    pre[...] = dot(wb_ref[hop], x_ref[hop], 1, 0)
    at0 = pl.ds(pl.multiple_of(pos_ref[1] * half, half), half)
    at1 = pl.ds(pl.multiple_of((1 - pos_ref[1]) * half, half), half)
    dj[...] = dot(merge_at(mine_ref, pos_ref, hop), dpre_ref[at0, :], 1, 0)
    dj[...] += dot(merge_at(other_ref, pos_ref, hop), dpre_ref[at1, :], 1, 0)

    def group(g, carry):
        at = pl.ds(pl.multiple_of(g * ROWS, ROWS), ROWS)
        cf = coef_ref[hop, at, :]
        c = [jnp.broadcast_to(cf[:, i : i + 1], (ROWS, WIDE)) for i in range(7)]
        scale = 0.25 * c[6]
        acc = [jnp.zeros((ROWS, WIDE), F32) for _ in range(2)]
        for b in range(batch // WIDE):
            lanes = slice(b * WIDE, (b + 1) * WIDE)
            u = pre[at, lanes] * c[0] + c[1]
            t = jnp.tanh(u)
            u2 = u * (c[2] + c[3] * t) * 0.5
            t2 = jnp.tanh(u2)
            d = dj[at, lanes]
            w2 = u2 * (1.0 - t2)
            acc[1] = acc[1] + d * w2
            d = d * (c[4] + c[5] * (t2 + w2 * (1.0 + t2)))
            w = u * (1.0 - t)
            acc[0] = acc[0] + d * w
            d = d * (c[2] + c[3] * (t + w * (1.0 + t)))
            dyv[at, lanes] = (d * scale).astype(BF16)
        for i in range(2):
            sums[i, at, :] = fold_lanes(acc[i])
        return carry

    lax.fori_loop(0, hid // ROWS, group, 0, unroll=2)
    lane = lane_of((hid, LANES))
    block = dot(dyv[...], x_ref[hop], 1, 1)
    block = jnp.where(lane == ONE + 1, 0.5 * jnp.sum(sums[0], axis=1, keepdims=True), block)
    block = jnp.where(lane == ONE + 2, jnp.sum(sums[1], axis=1, keepdims=True), block)
    dp = b_ref.shape[0]
    cb = hid // dp
    for s in range(dp):
        b_ref[s] = block[s * cb : (s + 1) * cb, :]
    a_ref[...] = dot(wb_ref[hop], dyv[...], 0, 0)


def split_low_kernel(pos_ref, keep_ref, got_ref, o0_ref, o1_ref, o2_ref, o3_ref):
    low = pos_ref[0] % 4
    for m, ref in enumerate((o0_ref, o1_ref, o2_ref, o3_ref)):
        for z in range(4):
            j = z * 4 + (low ^ m)
            ref[z] = (keep_ref[j] + got_ref[j].astype(F32)).astype(ref.dtype)


def split_high_kernel(pos_ref, own_ref, g1_ref, g2_ref, g3_ref, o0_ref, o1_ref, o2_ref, o3_ref):
    high = pos_ref[0] // 4
    for k, ref in enumerate((o0_ref, o1_ref, o2_ref, o3_ref)):
        j = high ^ k
        value = own_ref[j] + g1_ref[j].astype(F32) + g2_ref[j].astype(F32) + g3_ref[j].astype(F32)
        ref[...] = value.astype(ref.dtype)


def pick_kernel(pos_ref, a_ref, b_ref, c_ref, d_ref, keep_ref, send_ref):
    first = pos_ref[1] == 0
    refs = (a_ref, b_ref, c_ref, d_ref)
    for i in range(2):
        low, high = refs[i][...], refs[2 + i][...]
        keep_ref[:, i] = jnp.where(first, low, high)
        send_ref[:, i] = jnp.where(first, high, low)


def owner_kernel(
    count, classes, pos_ref, got_ref, w0_ref, w1_ref, w2_ref, w3_ref, pack_ref, coef_ref, gram_ref, sum2_ref,
    grad_ref, pay_ref,
):
    _, _, cb, _ = got_ref.shape
    total = jnp.sum(got_ref[...], axis=0)
    rep = pos_ref[1]
    start = pl.multiple_of(pos_ref[0] * cb, cb)
    lane = lane_of((cb, LANES))
    tail = pack_ref[HOPS].astype(F32)
    squares = jnp.zeros((1, 1), F32)
    spread = jnp.zeros((cb, LANES), F32)

    def all_sum(v):
        return jnp.sum(jnp.sum(v, axis=1, keepdims=True), axis=0, keepdims=True)

    for i in range(2):
        hop = rep * 2 + i
        b = total[i]
        coef = coef_ref[hop, pl.ds(start, cb), :]
        v, mean, inv = coef[:, 6:7], coef[:, 7:8], coef[:, 8:9]
        w = pack_ref[hop].astype(F32)
        gram = gram_ref[hop]
        s = b[:, ONE : ONE + 1]
        g = inv * (jnp.sum(jnp.where(lane < ONE, b * w, 0.0), axis=1, keepdims=True) - mean * s)
        beta = inv * g / count
        alpha = s / count - beta * mean
        wg = dot(w, gram, 1, 0, HIGHEST)
        fixed = jnp.where(lane < ONE, b - alpha * gram[ONE : ONE + 1, :] - beta * wg, 0.0)
        fixed = jnp.where(lane == ONE, g / v, fixed)
        fixed = jnp.where(lane == ONE + 1, s / v, fixed)
        fixed = jnp.where(lane == ONE + 2, b[:, ONE + 1 : ONE + 2], fixed)
        fixed = jnp.where(lane == ONE + 3, b[:, ONE + 2 : ONE + 3], fixed)
        grad_ref[i * cb : (i + 1) * cb, :] = fixed
        squares = squares + all_sum(fixed * fixed)
        spread = jnp.where(lane == 2 * i, alpha, spread)
        spread = jnp.where(lane == 2 * i + 1, beta, spread)
    wide = w0_ref[...].astype(F32) + w1_ref[...].astype(F32) + w2_ref[...].astype(F32) + w3_ref[...].astype(F32)
    mr = wide.shape[0] - cb // 2
    merge = wide[:mr]
    squares = squares + all_sum(merge * merge)
    at = 2 * cb
    for i in range(2):
        grad_ref[at + i * mr : at + (i + 1) * mr, :] = merge[:, i * LANES : (i + 1) * LANES]
    at = at + 2 * mr
    block = jnp.concatenate([wide[mr:, :LANES], wide[mr:, LANES:]], axis=0)
    shift_own = own_column(sum2_ref, 0, pos_ref[0], cb)
    gain_own = own_column(sum2_ref, 4, pos_ref[0], cb)
    block = jnp.where(lane == PCOL + 2, gain_own, block)
    block = jnp.where(lane == PCOL + 3, shift_own, block)
    grad_ref[at : at + cb, :] = block
    squares = squares + jnp.where(rep == 0, all_sum(block * block), 0.0)
    spread = jnp.where(lane == 4, jnp.broadcast_to(squares, spread.shape), spread)
    rows = jnp.transpose(jnp.concatenate([spread, jnp.zeros((LANES - cb, LANES), F32)], axis=0))[0:8]
    offset = (pos_ref[0] * cb) % LANES
    rows = pltpu.roll(rows, offset, 1)
    row8 = lax.broadcasted_iota(jnp.int32, rows.shape, 0)
    rows = jnp.where((row8 == 4) & (lane_of(rows.shape) != offset), 0.0, rows)
    pay_ref[...] = jnp.broadcast_to(rows[None], pay_ref.shape)


def own_column(ref, first, me, cb):
    block = (me * cb) // LANES
    row = ref[pl.ds(first + block, 1), :]
    lane = lane_of((cb, LANES))
    sub = lax.broadcasted_iota(jnp.int32, (cb, LANES), 0)
    hit = lane == sub + (me * cb) % LANES
    return jnp.sum(jnp.where(hit, jnp.broadcast_to(row, (cb, LANES)), 0.0), axis=1, keepdims=True)


def adam_into(weight_ref, moment_ref, square_ref, grad, scale, rate, outs, at=Ellipsis):
    new_ref, new_m_ref, new_s_ref, copy_ref = outs
    weight = weight_ref[at]
    clipped = grad * scale
    moment = 0.9 * moment_ref[at] + 0.1 * clipped
    square = 0.999 * square_ref[at] + 0.001 * clipped * clipped
    fix_one = 1.0 - 0.9**STEP
    fix_two = 1.0 - 0.999**STEP
    update = moment / fix_one / (jnp.sqrt(square / fix_two) + 1e-08) + 0.01 * weight
    new = weight - rate * update
    new_ref[at] = new
    new_m_ref[at] = moment
    new_s_ref[at] = square
    copy_ref[at] = new.astype(BF16)


def final_kernel(pos_ref, got_ref, mine_ref, other_ref, x_ref, wb_ref, a0_ref, a1_ref, a2_ref, a3_ref, *refs):
    weights, firsts, seconds = refs[0:4], refs[4:8], refs[8:12]
    outs = refs[12:28]
    norm_ref, rows_ref = refs[28:30]
    dp = got_ref.shape[0] // 2
    blocks = 4
    per = dp // blocks
    parts = []
    for b in range(blocks):
        for r in range(2):
            total = got_ref[(b * per) * 2 + r]
            for i in range(1, per):
                total = total + got_ref[(b * per + i) * 2 + r]
            parts.append(total)
    squares = parts[0][4:5, :]
    for part in parts[1:]:
        squares = squares + part[4:5, :]
    norm = jnp.sqrt(jnp.sum(squares, axis=1, keepdims=True))
    norm_ref[...] = norm
    scale = 1.0 / jnp.maximum(norm, 1.0)

    cb = weights[0].shape[1]
    d_in = weights[0].shape[2]
    mr = weights[1].shape[0]
    classes = weights[2].shape[1]
    first = pos_ref[1] == 0
    mine, other = mine_ref[...], other_ref[...]
    low = jnp.where(first, mine, other)
    high = jnp.where(first, other, mine)

    def group(i):
        return [o for o in outs[i::4]]

    hops = [low[0:cb], low[cb : 2 * cb], high[0:cb], high[cb : 2 * cb]]
    for k in range(HOPS):
        adam_into(weights[0], firsts[0], seconds[0], hops[k][:, :d_in], scale, 0.05, group(0), k)
    at = 2 * cb
    for half, part in enumerate((low, high)):
        for i in range(2):
            lanes = (slice(None), slice((2 * half + i) * LANES, (2 * half + i + 1) * LANES))
            grad = part[at + i * mr : at + (i + 1) * mr]
            adam_into(weights[1], firsts[1], seconds[1], grad, scale, 0.05, group(1), lanes)
    at = at + 2 * mr
    block = low[at : at + cb]
    adam_into(weights[2], firsts[2], seconds[2], block[:, :classes], scale, 0.05, group(2))
    lane = lane_of((cb, LANES))
    small = jnp.zeros((cb, LANES), F32)
    for kind in range(4):
        for k in range(HOPS):
            small = jnp.where(lane == kind * HOPS + k, hops[k][:, ONE + kind : ONE + kind + 1], small)
    for i, source in enumerate((2, 3, 0, 1)):
        small = jnp.where(lane == 4 * HOPS + i, block[:, PCOL + source : PCOL + source + 1], small)
    small = jnp.transpose(jnp.concatenate([small, jnp.zeros((LANES - cb, LANES), F32)], axis=0))
    adam_into(weights[3], firsts[3], seconds[3], small[: weights[3].shape[0], :cb], scale, 0.3, group(3))

    sub = lax.broadcasted_iota(jnp.int32, (LANES, LANES), 0)
    for k in range(HOPS):
        a_ref = (a0_ref, a1_ref, a2_ref, a3_ref)[k]
        r, i = k // 2, k % 2
        alpha = jnp.concatenate([parts[b * 2 + r][2 * i : 2 * i + 1] for b in range(blocks)], axis=1)
        beta = jnp.concatenate([parts[b * 2 + r][2 * i + 1 : 2 * i + 2] for b in range(blocks)], axis=1)
        w = jnp.transpose(wb_ref[k].astype(F32))
        right = jnp.where(lax.broadcasted_iota(jnp.int32, w.shape, 0) == ONE, alpha, w * beta)
        fix = dot(w, right, 1, 1, HIGHEST)
        hi = fix.astype(BF16)
        lo = (fix - hi.astype(F32)).astype(BF16)
        value = a_ref[...] - dot(hi, x_ref[k], 1, 0) - dot(lo, x_ref[k], 1, 0)
        rows_ref[k * d_in : (k + 1) * d_in, :] = value[:d_in]


def flip(value, mask, dp):
    return lax.ppermute(value, "dp", [(i, i ^ mask) for i in range(dp)])


def swap(value):
    return lax.ppermute(value, "rep", [(0, 1), (1, 0)])


def spread_blocks(block, dp):
    if dp != 16:
        return lax.all_gather(block, "dp")
    high = jnp.stack([block] + [flip(block, 4 * k, dp) for k in range(1, 4)])
    return jnp.concatenate([high] + [flip(high, m, dp) for m in range(1, 4)])


def exchange(value):
    return lax.all_to_all(value, BOTH, 0, 0, tiled=True)


def on_device(table, batch_index, labels, *state):
    weights, firsts, seconds = state[0:4], state[4:8], state[8:12]
    dp, rep = lax.axis_size("dp"), lax.axis_size("rep")
    n = dp * rep
    me, core = lax.axis_index("dp"), lax.axis_index("rep")
    pos = jnp.stack([me, core]).astype(jnp.int32)
    batch = batch_index.shape[0]
    count = float(batch * n)
    nodes, width = table.shape
    d_in = weights[0].shape[1]
    cb = weights[0].shape[2]
    mr, hid = weights[1].shape
    classes = weights[2].shape[1]
    half = hid // 2
    lhs = [v.transpose(0, 2, 1) for v in (weights[0], firsts[0], seconds[0])]
    idx = batch_index.reshape(1, batch)
    lab = labels.reshape(1, batch)

    with jax.named_scope("prep"):
        pack, wmh = call(
            prep_kernel,
            [sds((HOPS + 1, cb, LANES), BF16), sds((mr, half), BF16)],
            pos, lhs[0], weights[2], weights[3], weights[1],
            smem=(0,),
        )
    packs = spread_blocks(pack, dp)
    wm_mine = spread_blocks(wmh, dp)
    wm_other = swap(wm_mine)

    with jax.named_scope("gather"):
        step = 512
        x, gram = call(
            gather_kernel,
            [sds((HOPS, LANES, batch), BF16), sds((HOPS, LANES, LANES))],
            idx, table.T,
            grid=(nodes // step,),
            in_specs=[
                pl.BlockSpec((1, batch), lambda i: (0, 0)),
                pl.BlockSpec((width, step), lambda i: (0, i)),
            ],
            out_specs=(
                pl.BlockSpec((HOPS, LANES, batch), lambda i: (0, 0, 0)),
                pl.BlockSpec((HOPS, LANES, LANES), lambda i: (0, 0, 0)),
            ),
            scratch=[pltpu.VMEM((width, batch), F32), pltpu.VMEM((LANES, batch), F32)],
            flops=2 * nodes * width * batch,
        )
    with jax.named_scope("gram_sum"):
        parts = exchange(gram.reshape(n, HOPS * LANES // n, LANES))
        (parts,) = call(sum_spread_kernel, [sds(parts.shape)], parts)
        gram = exchange(parts).reshape(HOPS, LANES, LANES)
    with jax.named_scope("stats"):
        wb, wc, coef, par = call(
            functools.partial(stats_kernel, count),
            [sds((HOPS, hid, LANES), BF16), sds((hid, LANES), BF16), sds((HOPS, hid, LANES)), sds((hid, LANES))],
            pos, gram, packs,
            smem=(0,),
            scratch=[pltpu.VMEM((hid, LANES), F32)],
            flops=2 * HOPS * hid * LANES * LANES * 6,
        )
    smem = pl.BlockSpec(memory_space=pltpu.SMEM)
    with jax.named_scope("forward"):
        joined, pre2, pay = call(
            forward_kernel,
            [sds((HOPS, hid, batch), BF16), sds((hid, batch)), sds((n, 8, LANES))],
            pos, x, wb, coef, wm_mine, wm_other,
            grid=(HOPS,),
            in_specs=[
                smem,
                pl.BlockSpec((1, LANES, batch), lambda k: (k, 0, 0)),
                pl.BlockSpec((1, hid, LANES), lambda k: (k, 0, 0)),
                pl.BlockSpec((1, hid, LANES), lambda k: (k, 0, 0)),
                pl.BlockSpec((dp, mr, half), lambda k: (0, 0, 0)),
                pl.BlockSpec((dp, mr, half), lambda k: (0, 0, 0)),
            ],
            out_specs=(
                pl.BlockSpec((1, hid, batch), lambda k: (k, 0, 0)),
                pl.BlockSpec((hid, batch), lambda k: (0, 0)),
                pl.BlockSpec((n, 8, LANES), lambda k: (0, 0, 0)),
            ),
            scratch=[pltpu.VMEM((hid, batch), F32)],
            flops=2 * batch * HOPS * hid * (LANES + hid),
        )
    got = exchange(pay)
    with jax.named_scope("head"):
        dy2, pay, block, stat = call(
            functools.partial(head_kernel, count, classes),
            [sds((hid, batch)), sds((n, 8, LANES)), sds((hid, LANES)), sds((2, hid, LANES))],
            got, pre2, par, wc, lab,
            scratch=[
                pltpu.VMEM((hid, batch), BF16),
                pltpu.VMEM((hid, batch), F32),
                pltpu.VMEM((4, hid, LANES), F32),
                pltpu.VMEM((3, hid, LANES), F32),
            ],
            flops=6 * batch * hid * LANES,
        )
    got = exchange(pay)
    with jax.named_scope("turn"):
        rows = mr + cb // 2
        dpre, keep, send, sum2 = call(
            functools.partial(turn_kernel, count),
            [sds((hid, batch), BF16), sds((dp, rows, half)), sds((dp, rows, half), BF16), sds((8, LANES))],
            pos, got, stat, par, pre2, dy2, joined.reshape(HOPS * hid, batch), block,
            smem=(0,),
            scratch=[pltpu.VMEM((3, hid, LANES), F32)],
            flops=2 * batch * HOPS * hid * hid,
        )
    recv = swap(send)
    bs, rs = [], []
    for hop in range(HOPS):
        with jax.named_scope("back"):
            b, a = call(
                functools.partial(back_kernel, hop=hop),
                [sds((dp, cb, LANES)), sds((LANES, batch))],
                pos, dpre, x, wb, coef, wm_mine, wm_other,
                smem=(0,),
                scratch=[
                    pltpu.VMEM((hid, batch), F32),
                    pltpu.VMEM((hid, batch), F32),
                    pltpu.VMEM((hid, batch), BF16),
                    pltpu.VMEM((2, hid, LANES), F32),
                ],
                flops=2 * batch * hid * (hid + 3 * LANES) * 3,
            )
        bs.append(b)
        rs.append(a)
    with jax.named_scope("merge_sum"):
        if dp == 16:
            shape = (4, rows, half)
            low = call(
                split_low_kernel, [sds(shape)] + [sds(shape, BF16)] * 3, pos, keep, recv, smem=(0,)
            )
            moved = [flip(low[m], m, dp) for m in range(1, 4)]
            high = call(
                split_high_kernel,
                [sds(shape[1:])] + [sds(shape[1:], BF16)] * 3,
                pos, low[0], *moved,
                smem=(0,),
            )
            wide = [high[0]] + [flip(high[k], 4 * k, dp) for k in range(1, 4)]
        else:
            total = lax.psum_scatter(keep + recv.astype(F32), "dp", scatter_dimension=0)
            wide = [total] + [jnp.zeros_like(total)] * 3
    with jax.named_scope("branch_sum"):
        keep_b, send_b = call(
            pick_kernel, [sds((dp, 2, cb, LANES))] * 2, pos, *bs, smem=(0,)
        )
        pair = keep_b + swap(send_b)
        got_b = lax.all_to_all(pair, "dp", 0, 0, tiled=True)
    with jax.named_scope("owner"):
        shares, pay = call(
            functools.partial(owner_kernel, count, classes),
            [sds((3 * cb + 2 * mr, LANES)), sds((n, 8, LANES))],
            pos, got_b, *wide, pack, coef, gram, sum2,
            smem=(0,),
        )
    theirs = swap(shares)
    got = exchange(pay)
    with jax.named_scope("final"):
        tr = [(lhs[i],) + tuple(s[1:]) for i, s in enumerate((weights, firsts, seconds))]
        shapes = [t.shape for t in tr[0]]
        outs = []
        for dtype in (F32, F32, F32, BF16):
            outs += [sds(s, dtype) for s in shapes]
        outs += [sds((1, 1)), sds((width, batch))]
        res = call(
            final_kernel, outs, pos, got, shares, theirs, x, wb, *rs, *tr[0], *tr[1], *tr[2],
            smem=(0,),
            flops=2 * batch * LANES * LANES * 3 * HOPS,
        )
    result = list(res[:16])
    for i in range(0, 16, 4):
        result[i] = result[i].transpose(0, 2, 1)
    return (*result, res[16].reshape(()), res[17].T)


def solution(mesh):
    tables = (P(BOTH, None), P(BOTH), P(BOTH))
    params = (P(None, None, "dp"), P("dp", None), P("dp", None), P(None, "dp"))
    return jax.shard_map(
        on_device,
        mesh=mesh,
        in_specs=tables + params * 3,
        out_specs=params * 4 + (P(), P(BOTH, None)),
        check_vma=False,
    )
```

time: 806 us -> 234 us (0.29)
  blocking collectives: 323 us -> 20.4 us
  waiting for transfers between devices: 341 us -> 51.6 us
  Pallas kernels: 0 us -> 80.7 us
  other arithmetic: 48.4 us -> 1.68 us
  starting transfers between devices: 0.51 us -> 43.7 us
  matrix products: 40.3 us -> 0 us
  between operations: 19 us -> 1.23 us
    reduce_scatter x3 -> x0, waiting for transfers between devices: 242 us -> none  [the longest x1 92.4 us: on_device(): lax.psum_scatter(paired[1], 'dp', scatter_dimension=0, tiled=True)]
    psum x5 -> x0, blocking collectives: 196 us -> none  [the longest x1 41.4 us: on_device(): totals_two = lax.psum((shift2_part, gain2_part), ('dp', 'rep'))]
    all_gather x3 -> x0, blocking collectives: 127 us -> none  [the longest x1 43.3 us: on_device(): lax.all_gather(w_class.astype(jnp.bfloat16), 'dp', axis=0, tiled=True)]
    pallas_call x0 -> x16, Pallas kernels: none -> 80.7 us  [call(): pl.pallas_call(body, out_shape=tuple(outs), in_specs=in_specs, out_specs=...]
    unnamed x8 -> x0, waiting for transfers between devices: 70 us -> none
    dot_general x9 -> x0, matrix products: 40.3 us -> none  [the longest x2 18.2 us: back_dot(): lax.dot_general(left, right, (((1,), (1,)), ((), ())), preferred_element_...]
    ppermute x0 -> x22, waiting for transfers between devices: none -> 38.1 us  [the longest x18 35.1 us: flip(): return lax.ppermute(value, 'dp', [(i, i ^ mask) for i in range(dp)])]
    convert_element_type x15 -> x0, other arithmetic: 37 us -> none  [the longest x1 9.12 us: on_device(): joined_low = leaky(act1, slope_join).astype(jnp.bfloat16)]
  transfers between devices with their start and end apart: 7 -> 26, of which waited for: 6 -> 12; matrix products, arithmetic and copies ran while one was open for 9% -> 4% of each run, Pallas kernels for 0% -> 19%
where the time goes in v1:
time: 234 us; the launch traced here: 232 us
  Pallas kernels  80.7 us (34%)
  waiting for transfers between devices  51.6 us (22%)
  starting transfers between devices  43.7 us (19%)
  local copies, waits for them, and re-layouts  32.9 us (14%)
  blocking collectives  20.4 us (9%)
    pallas_call x16, Pallas kernels, call(): pl.pallas_call(body, out_shape=tuple(outs), in_specs=in_specs, out_specs=...  80.7 us
    ppermute x18, waiting for transfers between devices, flip(): return lax.ppermute(value, 'dp', [(i, i ^ mask) for i in range(dp)])  35.1 us
    unnamed x92, local copies, waits for them, and re-layouts  31.2 us
    ppermute x18, starting transfers between devices, flip(): return lax.ppermute(value, 'dp', [(i, i ^ mask) for i in range(dp)])  27.1 us
    all_to_all x2, blocking collectives, exchange(): return lax.all_to_all(value, BOTH, 0, 0, tiled=True)  20.4 us
    all_to_all x3, waiting for transfers between devices, exchange(): return lax.all_to_all(value, BOTH, 0, 0, tiled=True)  13.5 us
    all_to_all x3, starting transfers between devices, exchange(): return lax.all_to_all(value, BOTH, 0, 0, tiled=True)  11.8 us
  transfers between devices with their start and end apart: 26, of which 12 were waited for; matrix products, arithmetic and copies ran while one was open for 4% of the time, Pallas kernels for 19%

profile of v1, /device:TPU:0, one launch (start us, length us, event | category | flops | bytes accessed | tf_op | source)
XLA Modules:
  0.0 232.2 jit_solution(17184365960906899276)
XLA Ops:
  0.7 0.9 copy-done.2
  4.6 5.1 %collective-permute-start.2 = (bf16[5,32,128]{2,1,0:T(8,128)(2,1)S(1)}, bf16[5,32,128]{2,1,0:T(8,128)(2,1)S(1)}, u32[]{:S(2)}, u32[]{:S(2)}) collective-permute-start(bf16[5,32,128]{2,1,0:T(8,128)(2,1)S(1)} %get-tuple-element.77.pack_ref), channel_id=1, source_target_pairs={{0,24},{2,26},{4,28},{6,30},{8,16},{10,18},{12,20},{14,22},{16,8},... | collective-permute-start | bytes 122888 | tf_op jit(solution)/shard_map/ppermute | solution.py:590
  10.3 3.7 %collective-permute-start.8 = (bf16[128,256]{1,0:T(8,128)(2,1)S(1)}, bf16[128,256]{1,0:T(8,128)(2,1)S(1)}, u32[]{:S(2)}, u32[]{:S(2)}) collective-permute-start(bf16[128,256]{1,0:T(8,128)(2,1)S(1)} %get-tuple-element.80), channel_id=1, source_target_pairs={{0,24},{2,26},{4,28},{6,30},{8,16},{10,18},{12,20},{14,22},{16,8},... | collective-permute-start | bytes 196616 | tf_op jit(solution)/shard_map/ppermute | solution.py:590
  14.1 2.9 %copy-done.37 = f32[4096,400]{0,1:T(8,128)S(1)} copy-done((f32[4096,400]{0,1:T(8,128)S(1)}, f32[4096,400]{0,1:T(8,128)}, u32[]{:S(2)}) %copy-start.37) | copy-done | bytes 6553624
  17.6 7.7 %gather.1 = (bf16[4,128,1024]{2,1,0:T(8,128)(2,1)S(1)}, f32[4,128,128]{2,1,0:T(8,128)}) custom-call(s32[1,1024]{1,0:T(1,128)S(1)} %bitcast.44, f32[400,4096]{1,0:T(8,128)S(1)} %bitcast.43), custom_call_target="tpu_custom_call" | custom-call | flops 3355443200 | bytes 7868416 | tf_op jit(solution)/shard_map/gather/pallas_call | solution.py:42
  25.3 5.2 %all-to-all-start = ((f32[32,16,128]{2,1,0:T(8,128)}), f32[32,16,128]{2,1,0:T(8,128)S(1)}, u32[]{:S(2)}, u32[]{:S(2)}) async-start(f32[32,16,128]{2,1,0:T(8,128)} %bitcast.4), calls=%async_computation | async-start | bytes 524288 | tf_op jit(solution)/shard_map/gram_sum/all_to_all | solution.py:605
  31.2 1.8 collective-permute-start.6
  33.7 2.4 %collective-permute-start.5 = (bf16[4,5,32,128]{3,2,1,0:T(8,128)(2,1)}, bf16[4,5,32,128]{3,2,1,0:T(8,128)(2,1)}, u32[]{:S(2)}, u32[]{:S(2)}) collective-permute-start(bf16[4,5,32,128]{3,2,1,0:T(8,128)(2,1)} %pad_maximum_fusion.1), channel_id=1, source_target_pairs={{0,6},{2,4},{4,2},{6,0},{8,14},{10,12},{12,10},{14,8},{16,22},{18,... | collective-permute-start | bytes 491528 | tf_op jit(solution)/shard_map/ppermute | solution.py:590
  36.6 1.3 collective-permute-done.6
  38.0 2.5 %collective-permute-start.11 = (bf16[4,128,256]{2,1,0:T(8,128)(2,1)S(1)}, bf16[4,128,256]{2,1,0:T(8,128)(2,1)S(1)}, u32[]{:S(2)}, u32[]{:S(2)}) collective-permute-start(bf16[4,128,256]{2,1,0:T(8,128)(2,1)S(1)} %pad_maximum_fusion), channel_id=1, source_target_pairs={{0,6},{2,4},{4,2},{6,0},{8,14},{10,12},{12,10},{14,8},{16,22},{18,... | collective-permute-start | bytes 786440 | tf_op jit(solution)/shard_map/ppermute | solution.py:590
  43.4 9.4 %collective-permute-done.9 = bf16[4,128,256]{2,1,0:T(8,128)(2,1)S(1)} collective-permute-done((bf16[4,128,256]{2,1,0:T(8,128)(2,1)S(1)}, bf16[4,128,256]{2,1,0:T(8,128)(2,1)S(1)}, u32[]{:S(2)}, u32[]{:S(2)}) %collective-permute-start.9) | collective-permute-done | bytes 262176 | tf_op jit(solution)/shard_map/ppermute | solution.py:590
  52.8 1.4 collective-permute-start.3
  55.0 1.7 collective-permute-done.10
  58.9 3.4 %all-to-all-start.1 = ((f32[32,16,128]{2,1,0:T(8,128)}), f32[32,16,128]{2,1,0:T(8,128)S(1)}, u32[]{:S(2)}, u32[]{:S(2)}) async-start(f32[32,16,128]{2,1,0:T(8,128)} %gram_sum.1), calls=%async_computation.1 | async-start | bytes 524288 | tf_op jit(solution)/shard_map/gram_sum/all_to_all | solution.py:605
  66.0 7.0 %all-to-all-done.1 = f32[32,16,128]{2,1,0:T(8,128)S(1)} async-done(((f32[32,16,128]{2,1,0:T(8,128)}), f32[32,16,128]{2,1,0:T(8,128)S(1)}, u32[]{:S(2)}, u32[]{:S(2)}) %all-to-all-start.1) | async-done | bytes 262176 | tf_op jit(solution)/shard_map/gram_sum/all_to_all | solution.py:605
  73.0 5.9 %stats.1 = (bf16[4,512,128]{2,1,0:T(8,128)(2,1)S(1)}, bf16[512,128]{1,0:T(8,128)(2,1)S(1)}, f32[4,512,128]{2,1,0:T(8,128)S(1)}, f32[512,128]{1,0:T(8,128)S(1)}) custom-call(s32[2]{0:T(128)S(1)} %pad_add_fusion.pos_ref, f32[4,128,128]{2,1,0:T(8,128)S(1)} %bitcast.34, bf16[16,5,32,128]{3,2,1,0:T(8,128)(2,1)S(1)} %constant_dynamic-update-slice_fusion.pack_ref), custom_call_target="tpu_custom_call" | custom-call | flops 402653184 | bytes 2883592 | tf_op jit(solution)/shard_map/stats/pallas_call | solution.py:42
  78.9 17.2 %forward.1 = (bf16[4,512,1024]{2,1,0:T(8,128)(2,1)S(1)}, f32[512,1024]{1,0:T(8,128)S(1)}, f32[32,8,128]{2,1,0:T(8,128)S(1)}) custom-call(s32[2]{0:T(128)S(1)} %pad_add_fusion.pos_ref, bf16[4,128,1024]{2,1,0:T(8,128)(2,1)S(1)} %get-tuple-element.75.x_ref, bf16[4,512,128]{2,1,0:T(8,128)(2,1)S(1)} %get-tuple-element.78.wb_ref, ...), custom_call_target="tpu_custom_call" | custom-call | flops 2684354560 | bytes 11141128 | tf_op jit(solution)/shard_map/forward/pallas_call | solution.py:42
  96.1 10.4 %all_to_all.30.got_ref = f32[32,8,128]{2,1,0:T(8,128)S(1)} all-to-all(f32[32,8,128]{2,1,0:T(8,128)S(1)} %get-tuple-element.81), channel_id=1, replica_groups=mesh['dp'=16,'rep'=2] {'dp','rep'}, dimensions={0} | all-to-all | bytes 262144 | tf_op jit(solution)/shard_map/all_to_all | solution.py:605
  106.5 3.9 %head.1 = (f32[512,1024]{1,0:T(8,128)S(1)}, f32[32,8,128]{2,1,0:T(8,128)S(1)}, f32[512,128]{1,0:T(8,128)S(1)}, f32[2,512,128]{2,1,0:T(8,128)S(1)}) custom-call(f32[32,8,128]{2,1,0:T(8,128)S(1)} %all_to_all.30.got_ref, f32[512,1024]{1,0:T(8,128)S(1)} %get-tuple-element.82.pre2_ref, f32[512,128]{1,0:T(8,128)S(1)} %get-tuple-element.83.par_ref, ...), custom_call_target="tpu_custom_call" | custom-call | flops 402653184 | bytes 5640192 | tf_op jit(solution)/shard_map/head/pallas_call | solution.py:42
  110.5 10.0 %all_to_all.31.got_ref = f32[32,8,128]{2,1,0:T(8,128)S(1)} all-to-all(f32[32,8,128]{2,1,0:T(8,128)S(1)} %get-tuple-element.85), channel_id=1, replica_groups=mesh['dp'=16,'rep'=2] {'dp','rep'}, dimensions={0} | all-to-all | bytes 262144 | tf_op jit(solution)/shard_map/all_to_all | solution.py:605
  120.5 8.0 %turn.1 = (bf16[512,1024]{1,0:T(8,128)(2,1)S(1)}, f32[16,144,256]{2,1,0:T(8,128)S(1)}, bf16[16,144,256]{2,1,0:T(8,128)(2,1)}, f32[8,128]{1,0:T(8,128)S(1)}) custom-call(s32[2]{0:T(128)S(1)} %pad_add_fusion.pos_ref, f32[32,8,128]{2,1,0:T(8,128)S(1)} %all_to_all.31.got_ref, f32[2,512,128]{2,1,0:T(8,128)S(1)} %get-tuple-element.86.stat_ref, ...), custom_call_target="tpu_custom_call" | custom-call | flops 2147483648 | bytes 14159880 | tf_op jit(solution)/shard_map/turn/pallas_call | solution.py:42
  128.7 6.6 %back.7 = (f32[16,32,128]{2,1,0:T(8,128)S(1)}, f32[128,1024]{1,0:T(8,128)S(1)}) custom-call(s32[2]{0:T(128)S(1)} %pad_add_fusion.pos_ref, bf16[512,1024]{1,0:T(8,128)(2,1)S(1)} %get-tuple-element.90.dpre_ref, bf16[4,128,1024]{2,1,0:T(8,128)(2,1)S(1)} %copy-done.5, bf16[4,512,128]{2,1,0:T(8,128)(2,1)S(1)} %get-tuple-element.78.wb_ref, ...), custom_call_target="tpu_custom_call" | custom-call | flops 2818572288 | bytes 6553608 | tf_op jit(solution)/shard_map/back/pallas_call | solution.py:42
  136.2 6.6 %back.6 = (f32[16,32,128]{2,1,0:T(8,128)S(1)}, f32[128,1024]{1,0:T(8,128)S(1)}) custom-call(s32[2]{0:T(128)S(1)} %pad_add_fusion.pos_ref, bf16[512,1024]{1,0:T(8,128)(2,1)S(1)} %get-tuple-element.90.dpre_ref, bf16[4,128,1024]{2,1,0:T(8,128)(2,1)S(1)} %copy-done.5, bf16[4,512,128]{2,1,0:T(8,128)(2,1)S(1)} %get-tuple-element.78.wb_ref, ...), custom_call_target="tpu_custom_call" | custom-call | flops 2818572288 | bytes 6553608 | tf_op jit(solution)/shard_map/back/pallas_call | solution.py:42
  143.6 6.6 %back.5 = (f32[16,32,128]{2,1,0:T(8,128)S(1)}, f32[128,1024]{1,0:T(8,128)S(1)}) custom-call(s32[2]{0:T(128)S(1)} %pad_add_fusion.pos_ref, bf16[512,1024]{1,0:T(8,128)(2,1)S(1)} %get-tuple-element.90.dpre_ref, bf16[4,128,1024]{2,1,0:T(8,128)(2,1)S(1)} %copy-done.5, bf16[4,512,128]{2,1,0:T(8,128)(2,1)S(1)} %get-tuple-element.78.wb_ref, ...), custom_call_target="tpu_custom_call" | custom-call | flops 2818572288 | bytes 6553608 | tf_op jit(solution)/shard_map/back/pallas_call | solution.py:42
  151.0 6.6 %back.4 = (f32[16,32,128]{2,1,0:T(8,128)S(1)}, f32[128,1024]{1,0:T(8,128)S(1)}) custom-call(s32[2]{0:T(128)S(1)} %pad_add_fusion.pos_ref, bf16[512,1024]{1,0:T(8,128)(2,1)S(1)} %get-tuple-element.90.dpre_ref, bf16[4,128,1024]{2,1,0:T(8,128)(2,1)S(1)} %copy-done.5, bf16[4,512,128]{2,1,0:T(8,128)(2,1)S(1)} %get-tuple-element.78.wb_ref, ...), custom_call_target="tpu_custom_call" | custom-call | flops 2818572288 | bytes 6553608 | tf_op jit(solution)/shard_map/back/pallas_call | solution.py:42
  159.4 1.6 collective-permute-done.13
  161.9 3.8 %all-to-all-start.4 = ((f32[16,2,32,128]{3,2,1,0:T(8,128)}), f32[16,2,32,128]{3,2,1,0:T(8,128)S(1)}, u32[]{:S(2)}, u32[]{:S(2)}) async-start(f32[16,2,32,128]{3,2,1,0:T(8,128)} %add.3), calls=%async_computation.4 | async-start | bytes 1048576 | tf_op jit(solution)/shard_map/branch_sum/all_to_all | solution.py:757
  165.7 1.5 merge_sum.2
  167.3 1.6 collective-permute-start.15
  168.9 1.5 collective-permute-start.16
  170.8 10.4 %collective-permute-done.15.g1_ref = bf16[4,144,256]{2,1,0:T(8,128)(2,1)S(1)} collective-permute-done((bf16[4,144,256]{2,1,0:T(8,128)(2,1)S(1)}, bf16[4,144,256]{2,1,0:T(8,128)(2,1)S(1)}, u32[]{:S(2)}, u32[]{:S(2)}) %collective-permute-start.15) | collective-permute-done | bytes 294944 | tf_op jit(solution)/shard_map/merge_sum/ppermute | solution.py:590
  181.3 6.5 %collective-permute-done.17.g3_ref = bf16[4,144,256]{2,1,0:T(8,128)(2,1)S(1)} collective-permute-done((bf16[4,144,256]{2,1,0:T(8,128)(2,1)S(1)}, bf16[4,144,256]{2,1,0:T(8,128)(2,1)S(1)}, u32[]{:S(2)}, u32[]{:S(2)}) %collective-permute-start.17) | collective-permute-done | bytes 294944 | tf_op jit(solution)/shard_map/merge_sum/ppermute | solution.py:590
  187.8 1.3 merge_sum.3
  189.7 1.5 collective-permute-start.18
  191.3 2.1 collective-permute-start.19
  195.0 3.7 %collective-permute-done.19.w2_ref = bf16[144,256]{1,0:T(8,128)(2,1)} collective-permute-done((bf16[144,256]{1,0:T(8,128)(2,1)}, bf16[144,256]{1,0:T(8,128)(2,1)}, u32[]{:S(2)}, u32[]{:S(2)}) %collective-permute-start.19) | collective-permute-done | bytes 73760 | tf_op jit(solution)/shard_map/merge_sum/ppermute | solution.py:590
  198.7 1.2 collective-permute-done.20.w3_ref
  200.8 1.6 owner.1
  203.8 3.2 %all-to-all-start.5 = ((f32[32,8,128]{2,1,0:T(8,128)}), f32[32,8,128]{2,1,0:T(8,128)S(1)}, u32[]{:S(2)}, u32[]{:S(2)}) async-start(f32[32,8,128]{2,1,0:T(8,128)} %copy-done.25), calls=%async_computation.5 | async-start | bytes 262144 | tf_op jit(solution)/shard_map/all_to_all | solution.py:605
  207.3 1.4 collective-permute-done.21.other_ref
  208.7 6.5 %all-to-all-done.5.got_ref = f32[32,8,128]{2,1,0:T(8,128)S(1)} async-done(((f32[32,8,128]{2,1,0:T(8,128)}), f32[32,8,128]{2,1,0:T(8,128)S(1)}, u32[]{:S(2)}, u32[]{:S(2)}) %all-to-all-start.5) | async-done | bytes 131104 | tf_op jit(solution)/shard_map/all_to_all | solution.py:605
  215.3 1.0 copy-done.8
  216.3 1.0 copy-done.10
  217.3 1.0 copy-done.12
  218.4 1.0 copy-done.14
  219.4 1.0 copy-done.16
  220.5 0.9 copy-done.20
  226.9 5.2 %final.1 = (f32[4,32,100]{2,1,0:T(8,128)}, f32[128,512]{1,0:T(8,128)}, f32[32,47]{1,0:T(8,128)}, f32[20,32]{1,0:T(8,128)}, f32[4,32,100]{2,1,0:T(8,128)}, /*inde...) custom-call(s32[2]{0:T(128)S(1)} %pad_add_fusion.pos_ref, ...), custom_call_target="tpu_custom_call" | custom-call | flops 402653184 | bytes 7892428 | tf_op jit(solution)/shard_map/final/pallas_call | solution.py:42
  (120 shorter events, 32.0 us)
Async XLA Ops:
  0.7 1.0 copy-start.2
  4.6 26.5 %collective-permute-start.2 = (bf16[5,32,128]{2,1,0:T(8,128)(2,1)S(1)}, bf16[5,32,128]{2,1,0:T(8,128)(2,1)S(1)}, u32[]{:S(2)}, u32[]{:S(2)}) collective-permute-start(bf16[5,32,128]{2,1,0:T(8,128)(2,1)S(1)} %get-tuple-element.77.pack_ref), channel_id=1, source_target_pairs={{0,24},{2,26},{4,28},{6,30},{8,16},{10,18},{12,20},{14,22},{16,8},... | collective-permute-start | bytes 122888 | tf_op jit(solution)/shard_map/ppermute | solution.py:590
  9.7 23.3 %collective-permute-start.1 = (bf16[5,32,128]{2,1,0:T(8,128)(2,1)S(1)}, bf16[5,32,128]{2,1,0:T(8,128)(2,1)S(1)}, u32[]{:S(2)}, u32[]{:S(2)}) collective-permute-start(bf16[5,32,128]{2,1,0:T(8,128)(2,1)S(1)} %get-tuple-element.77.pack_ref), channel_id=1, source_target_pairs={{0,16},{2,18},{4,20},{6,22},{8,24},{10,26},{12,28},{14,30},{16,0},... | collective-permute-start | bytes 122888 | tf_op jit(solution)/shard_map/ppermute | solution.py:590
  9.7 23.3 %collective-permute-start = (bf16[5,32,128]{2,1,0:T(8,128)(2,1)S(1)}, bf16[5,32,128]{2,1,0:T(8,128)(2,1)S(1)}, u32[]{:S(2)}, u32[]{:S(2)}) collective-permute-start(bf16[5,32,128]{2,1,0:T(8,128)(2,1)S(1)} %get-tuple-element.77.pack_ref), channel_id=1, source_target_pairs={{0,8},{2,10},{4,12},{6,14},{8,0},{10,2},{12,4},{14,6},{16,24},{18,... | collective-permute-start | bytes 122888 | tf_op jit(solution)/shard_map/ppermute | solution.py:590
  10.3 26.3 %collective-permute-start.8 = (bf16[128,256]{1,0:T(8,128)(2,1)S(1)}, bf16[128,256]{1,0:T(8,128)(2,1)S(1)}, u32[]{:S(2)}, u32[]{:S(2)}) collective-permute-start(bf16[128,256]{1,0:T(8,128)(2,1)S(1)} %get-tuple-element.80), channel_id=1, source_target_pairs={{0,24},{2,26},{4,28},{6,30},{8,16},{10,18},{12,20},{14,22},{16,8},... | collective-permute-start | bytes 196616 | tf_op jit(solution)/shard_map/ppermute | solution.py:590
  14.1 22.5 %collective-permute-start.7 = (bf16[128,256]{1,0:T(8,128)(2,1)S(1)}, bf16[128,256]{1,0:T(8,128)(2,1)S(1)}, u32[]{:S(2)}, u32[]{:S(2)}) collective-permute-start(bf16[128,256]{1,0:T(8,128)(2,1)S(1)} %get-tuple-element.80), channel_id=1, source_target_pairs={{0,16},{2,18},{4,20},{6,22},{8,24},{10,26},{12,28},{14,30},{16,0},... | collective-permute-start | bytes 196616 | tf_op jit(solution)/shard_map/ppermute | solution.py:590
  14.1 2.9 %copy-start.37 = (f32[4096,400]{0,1:T(8,128)S(1)}, f32[4096,400]{0,1:T(8,128)}, u32[]{:S(2)}) copy-start(f32[4096,400]{0,1:T(8,128)} %param.15) | copy-start | bytes 19660804
  25.3 53.5 %copy-start.4 = (bf16[4,128,1024]{2,1,0:T(8,128)(2,1)}, bf16[4,128,1024]{2,1,0:T(8,128)(2,1)S(1)}, u32[]{:S(2)}) copy-start(bf16[4,128,1024]{2,1,0:T(8,128)(2,1)S(1)} %get-tuple-element.75.x_ref) | copy-start | bytes 3145732
  25.3 32.8 %all-to-all-start = ((f32[32,16,128]{2,1,0:T(8,128)}), f32[32,16,128]{2,1,0:T(8,128)S(1)}, u32[]{:S(2)}, u32[]{:S(2)}) async-start(f32[32,16,128]{2,1,0:T(8,128)} %bitcast.4), calls=%async_computation | async-start | bytes 524288 | tf_op jit(solution)/shard_map/gram_sum/all_to_all | solution.py:605
  31.2 27.8 %copy-start.39 = (bf16[5,32,128]{2,1,0:T(8,128)(2,1)}, bf16[5,32,128]{2,1,0:T(8,128)(2,1)S(1)}, u32[]{:S(2)}) copy-start(bf16[5,32,128]{2,1,0:T(8,128)(2,1)S(1)} %collective-permute-done.2) | copy-start | bytes 122884
  31.2 6.8 %collective-permute-start.6 = (bf16[128,256]{1,0:T(8,128)(2,1)S(1)}, bf16[128,256]{1,0:T(8,128)(2,1)S(1)}, u32[]{:S(2)}, u32[]{:S(2)}) collective-permute-start(bf16[128,256]{1,0:T(8,128)(2,1)S(1)} %get-tuple-element.80), channel_id=1, source_target_pairs={{0,8},{2,10},{4,12},{6,14},{8,0},{10,2},{12,4},{14,6},{16,24},{18,... | collective-permute-start | bytes 196616 | tf_op jit(solution)/shard_map/ppermute | solution.py:590
  33.7 31.4 %collective-permute-start.5 = (bf16[4,5,32,128]{3,2,1,0:T(8,128)(2,1)}, bf16[4,5,32,128]{3,2,1,0:T(8,128)(2,1)}, u32[]{:S(2)}, u32[]{:S(2)}) collective-permute-start(bf16[4,5,32,128]{3,2,1,0:T(8,128)(2,1)} %pad_maximum_fusion.1), channel_id=1, source_target_pairs={{0,6},{2,4},{4,2},{6,0},{8,14},{10,12},{12,10},{14,8},{16,22},{18,... | collective-permute-start | bytes 491528 | tf_op jit(solution)/shard_map/ppermute | solution.py:590
  36.1 28.1 %collective-permute-start.4 = (bf16[4,5,32,128]{3,2,1,0:T(8,128)(2,1)}, bf16[4,5,32,128]{3,2,1,0:T(8,128)(2,1)}, u32[]{:S(2)}, u32[]{:S(2)}) collective-permute-start(bf16[4,5,32,128]{3,2,1,0:T(8,128)(2,1)} %pad_maximum_fusion.1), channel_id=1, source_target_pairs={{0,4},{2,6},{4,0},{6,2},{8,12},{10,14},{12,8},{14,10},{16,20},{18,... | collective-permute-start | bytes 491528 | tf_op jit(solution)/shard_map/ppermute | solution.py:590
  38.0 19.4 %collective-permute-start.11 = (bf16[4,128,256]{2,1,0:T(8,128)(2,1)S(1)}, bf16[4,128,256]{2,1,0:T(8,128)(2,1)S(1)}, u32[]{:S(2)}, u32[]{:S(2)}) collective-permute-start(bf16[4,128,256]{2,1,0:T(8,128)(2,1)S(1)} %pad_maximum_fusion), channel_id=1, source_target_pairs={{0,6},{2,4},{4,2},{6,0},{8,14},{10,12},{12,10},{14,8},{16,22},{18,... | collective-permute-start | bytes 786440 | tf_op jit(solution)/shard_map/ppermute | solution.py:590
  40.5 16.2 %collective-permute-start.10 = (bf16[4,128,256]{2,1,0:T(8,128)(2,1)S(1)}, bf16[4,128,256]{2,1,0:T(8,128)(2,1)S(1)}, u32[]{:S(2)}, u32[]{:S(2)}) collective-permute-start(bf16[4,128,256]{2,1,0:T(8,128)(2,1)S(1)} %pad_maximum_fusion), channel_id=1, source_target_pairs={{0,4},{2,6},{4,0},{6,2},{8,12},{10,14},{12,8},{14,10},{16,20},{18,... | collective-permute-start | bytes 786440 | tf_op jit(solution)/shard_map/ppermute | solution.py:590
  41.2 11.6 %collective-permute-start.9 = (bf16[4,128,256]{2,1,0:T(8,128)(2,1)S(1)}, bf16[4,128,256]{2,1,0:T(8,128)(2,1)S(1)}, u32[]{:S(2)}, u32[]{:S(2)}) collective-permute-start(bf16[4,128,256]{2,1,0:T(8,128)(2,1)S(1)} %pad_maximum_fusion), channel_id=1, source_target_pairs={{0,2},{2,0},{4,6},{6,4},{8,10},{10,8},{12,14},{14,12},{16,18},{18,... | collective-permute-start | bytes 786440 | tf_op jit(solution)/shard_map/ppermute | solution.py:590
  52.8 10.4 %collective-permute-start.3 = (bf16[4,5,32,128]{3,2,1,0:T(8,128)(2,1)}, bf16[4,5,32,128]{3,2,1,0:T(8,128)(2,1)}, u32[]{:S(2)}, u32[]{:S(2)}) collective-permute-start(bf16[4,5,32,128]{3,2,1,0:T(8,128)(2,1)} %pad_maximum_fusion.1), channel_id=1, source_target_pairs={{0,2},{2,0},{4,6},{6,4},{8,10},{10,8},{12,14},{14,12},{16,18},{18,... | collective-permute-start | bytes 491528 | tf_op jit(solution)/shard_map/ppermute | solution.py:590
  58.1 20.7 %collective-permute-start.12 = (bf16[16,128,256]{2,1,0:T(8,128)(2,1)}, bf16[16,128,256]{2,1,0:T(8,128)(2,1)}, u32[]{:S(2)}, u32[]{:S(2)}) collective-permute-start(bf16[16,128,256]{2,1,0:T(8,128)(2,1)} %constant_dynamic-update-slice_fusion.7.mine_ref), channel_id=1, source_target_pairs={{0,1},{1,0},{2,3},{3,2},{4,5},{5,4},{6,7},{7,6},{8,9},{9,8},{10,11... | collective-permute-start | bytes 3145736 | tf_op jit(solution)/shard_map/ppermute | solution.py:594
  58.9 14.0 %all-to-all-start.1 = ((f32[32,16,128]{2,1,0:T(8,128)}), f32[32,16,128]{2,1,0:T(8,128)S(1)}, u32[]{:S(2)}, u32[]{:S(2)}) async-start(f32[32,16,128]{2,1,0:T(8,128)} %gram_sum.1), calls=%async_computation.1 | async-start | bytes 524288 | tf_op jit(solution)/shard_map/gram_sum/all_to_all | solution.py:605
  78.8 71.3 %copy-start = (f32[4,512,128]{2,1,0:T(8,128)}, f32[4,512,128]{2,1,0:T(8,128)S(1)}, u32[]{:S(2)}) copy-start(f32[4,512,128]{2,1,0:T(8,128)S(1)} %get-tuple-element.79.coef_ref) | copy-start | bytes 3145732
  78.8 71.3 %copy-start.7 = (bf16[4,512,128]{2,1,0:T(8,128)(2,1)}, bf16[4,512,128]{2,1,0:T(8,128)(2,1)S(1)}, u32[]{:S(2)}) copy-start(bf16[4,512,128]{2,1,0:T(8,128)(2,1)S(1)} %get-tuple-element.78.wb_ref) | copy-start | bytes 1572868
  78.9 27.6 %copy-start.36 = (s32[1024]{0:T(1024)S(1)}, s32[1024]{0:T(1024)}, u32[]{:S(2)}) copy-start(s32[1024]{0:T(1024)} %param.17) | copy-start | bytes 12292
  120.5 8.2 %copy-start.5 = (bf16[4,128,1024]{2,1,0:T(8,128)(2,1)S(1)}, bf16[4,128,1024]{2,1,0:T(8,128)(2,1)}, u32[]{:S(2)}) copy-start(bf16[4,128,1024]{2,1,0:T(8,128)(2,1)} %copy-done.4) | copy-start | bytes 3145732
  128.5 37.2 %collective-permute-start.14 = (bf16[16,144,256]{2,1,0:T(8,128)(2,1)}, bf16[16,144,256]{2,1,0:T(8,128)(2,1)}, u32[]{:S(2)}, u32[]{:S(2)}) collective-permute-start(bf16[16,144,256]{2,1,0:T(8,128)(2,1)} %get-tuple-element.98), channel_id=1, source_target_pairs={{0,1},{1,0},{2,3},{3,2},{4,5},{5,4},{6,7},{7,6},{8,9},{9,8},{10,11... | collective-permute-start | bytes 3538952 | tf_op jit(solution)/shard_map/ppermute | solution.py:594
  159.0 2.0 collective-permute-start.13
  161.9 32.3 %all-to-all-start.4 = ((f32[16,2,32,128]{3,2,1,0:T(8,128)}), f32[16,2,32,128]{3,2,1,0:T(8,128)S(1)}, u32[]{:S(2)}, u32[]{:S(2)}) async-start(f32[16,2,32,128]{3,2,1,0:T(8,128)} %add.3), calls=%async_computation.4 | async-start | bytes 1048576 | tf_op jit(solution)/shard_map/branch_sum/all_to_all | solution.py:757
  165.7 49.5 %copy-start.29 = (f32[32,47]{1,0:T(8,128)S(1)}, f32[32,47]{1,0:T(8,128)}, u32[]{:S(2)}) copy-start(f32[32,47]{1,0:T(8,128)} %refs_2_.1) | copy-start | bytes 18052
  165.7 49.5 %copy-start.31 = (f32[20,32]{1,0:T(8,128)S(1)}, f32[20,32]{1,0:T(8,128)}, u32[]{:S(2)}) copy-start(f32[20,32]{1,0:T(8,128)} %refs_3_.1) | copy-start | bytes 7684
  167.2 32.7 %copy-start.1 = (f32[4,512,128]{2,1,0:T(8,128)S(1)}, f32[4,512,128]{2,1,0:T(8,128)}, u32[]{:S(2)}) copy-start(f32[4,512,128]{2,1,0:T(8,128)} %copy-done) | copy-start | bytes 3145732
  167.2 48.0 %copy-start.3 = (f32[128,512]{1,0:T(8,128)S(1)}, f32[128,512]{1,0:T(8,128)}, u32[]{:S(2)}) copy-start(f32[128,512]{1,0:T(8,128)} %refs_1_.1) | copy-start | bytes 786436
  167.3 48.0 %copy-start.6 = (bf16[4,128,1024]{2,1,0:T(8,128)(2,1)S(1)}, bf16[4,128,1024]{2,1,0:T(8,128)(2,1)}, u32[]{:S(2)}) copy-start(bf16[4,128,1024]{2,1,0:T(8,128)(2,1)} %copy-done.4) | copy-start | bytes 3145732
  167.3 48.0 %copy-start.18 = (f32[4,100,32]{1,2,0:T(8,128)S(1)}, f32[4,100,32]{1,2,0:T(8,128)}, u32[]{:S(2)}) copy-start(f32[4,100,32]{1,2,0:T(8,128)} %param.18) | copy-start | bytes 153604
  167.3 48.0 %copy-start.19 = (f32[128,512]{1,0:T(8,128)S(1)}, f32[128,512]{1,0:T(8,128)}, u32[]{:S(2)}) copy-start(f32[128,512]{1,0:T(8,128)} %refs_5_.1) | copy-start | bytes 786436
  167.3 14.0 %collective-permute-start.15 = (bf16[4,144,256]{2,1,0:T(8,128)(2,1)S(1)}, bf16[4,144,256]{2,1,0:T(8,128)(2,1)S(1)}, u32[]{:S(2)}, u32[]{:S(2)}) collective-permute-start(bf16[4,144,256]{2,1,0:T(8,128)(2,1)S(1)} %get-tuple-element.100), channel_id=1, source_target_pairs={{0,2},{2,0},{4,6},{6,4},{8,10},{10,8},{12,14},{14,12},{16,18},{18,... | collective-permute-start | bytes 884744 | tf_op jit(solution)/shard_map/merge_sum/ppermute | solution.py:590
  168.9 12.3 %collective-permute-start.16 = (bf16[4,144,256]{2,1,0:T(8,128)(2,1)S(1)}, bf16[4,144,256]{2,1,0:T(8,128)(2,1)S(1)}, u32[]{:S(2)}, u32[]{:S(2)}) collective-permute-start(bf16[4,144,256]{2,1,0:T(8,128)(2,1)S(1)} %get-tuple-element.101), channel_id=1, source_target_pairs={{0,4},{2,6},{4,0},{6,2},{8,12},{10,14},{12,8},{14,10},{16,20},{18,... | collective-permute-start | bytes 884744 | tf_op jit(solution)/shard_map/merge_sum/ppermute | solution.py:590
  170.4 17.4 %collective-permute-start.17 = (bf16[4,144,256]{2,1,0:T(8,128)(2,1)S(1)}, bf16[4,144,256]{2,1,0:T(8,128)(2,1)S(1)}, u32[]{:S(2)}, u32[]{:S(2)}) collective-permute-start(bf16[4,144,256]{2,1,0:T(8,128)(2,1)S(1)} %get-tuple-element.102), channel_id=1, source_target_pairs={{0,6},{2,4},{4,2},{6,0},{8,14},{10,12},{12,10},{14,8},{16,22},{18,... | collective-permute-start | bytes 884744 | tf_op jit(solution)/shard_map/merge_sum/ppermute | solution.py:590
  189.7 5.3 %collective-permute-start.18 = (bf16[144,256]{1,0:T(8,128)(2,1)}, bf16[144,256]{1,0:T(8,128)(2,1)}, u32[]{:S(2)}, u32[]{:S(2)}) collective-permute-start(bf16[144,256]{1,0:T(8,128)(2,1)} %get-tuple-element.104), channel_id=1, source_target_pairs={{0,8},{2,10},{4,12},{6,14},{8,0},{10,2},{12,4},{14,6},{16,24},{18,... | collective-permute-start | bytes 221192 | tf_op jit(solution)/shard_map/merge_sum/ppermute | solution.py:590
  191.3 7.4 %collective-permute-start.19 = (bf16[144,256]{1,0:T(8,128)(2,1)}, bf16[144,256]{1,0:T(8,128)(2,1)}, u32[]{:S(2)}, u32[]{:S(2)}) collective-permute-start(bf16[144,256]{1,0:T(8,128)(2,1)} %get-tuple-element.105), channel_id=1, source_target_pairs={{0,16},{2,18},{4,20},{6,22},{8,24},{10,26},{12,28},{14,30},{16,0},... | collective-permute-start | bytes 221192 | tf_op jit(solution)/shard_map/merge_sum/ppermute | solution.py:590
  193.3 6.6 %collective-permute-start.20 = (bf16[144,256]{1,0:T(8,128)(2,1)}, bf16[144,256]{1,0:T(8,128)(2,1)}, u32[]{:S(2)}, u32[]{:S(2)}) collective-permute-start(bf16[144,256]{1,0:T(8,128)(2,1)} %get-tuple-element.106), channel_id=1, source_target_pairs={{0,24},{2,26},{4,28},{6,30},{8,16},{10,18},{12,20},{14,22},{16,8},... | collective-permute-start | bytes 221192 | tf_op jit(solution)/shard_map/merge_sum/ppermute | solution.py:590
  203.8 11.5 %all-to-all-start.5 = ((f32[32,8,128]{2,1,0:T(8,128)}), f32[32,8,128]{2,1,0:T(8,128)S(1)}, u32[]{:S(2)}, u32[]{:S(2)}) async-start(f32[32,8,128]{2,1,0:T(8,128)} %copy-done.25), calls=%async_computation.5 | async-start | bytes 262144 | tf_op jit(solution)/shard_map/all_to_all | solution.py:605
  207.0 1.7 collective-permute-start.21
  215.3 1.0 copy-start.8
  216.3 1.0 copy-start.10
  217.3 1.0 copy-start.12
  218.4 1.0 copy-start.14
  219.4 1.0 copy-start.16
  220.5 0.9 copy-start.20
  221.4 0.9 copy-start.22
  (18 other events, 13.7 us)

commit v2 on v1

v2 whole, which is shorter than its diff:
```python
import functools
import math

import jax
import jax.numpy as jnp
from jax import lax
from jax.experimental import pallas as pl
from jax.experimental.pallas import tpu as pltpu
from jax.sharding import PartitionSpec as P

HOPS = 4
STEP = 7
EPS_NORM = 1e-05
LANES = 128
PCOL = 64
ONE = 100
ROWS, WIDE, CHUNK = 32, 256, 256
BOTH = ("dp", "rep")
F32 = jnp.float32
BF16 = jnp.bfloat16


def dot(left, right, left_dim, right_dim):
    return lax.dot_general(
        left,
        right,
        (((left_dim,), (right_dim,)), ((), ())),
        preferred_element_type=F32,
    )


def call(body, outs, *args, smem=(), hbm=(), chip=(), after=(), grid=None, in_specs=None, out_specs=None, scratch=(), mib=12, flops=0):
    skip = len(args)
    if in_specs is None:
        spaces = {**{i: pltpu.SMEM for i in smem}, **{i: pltpu.HBM for i in hbm}}
        in_specs = [pl.BlockSpec(memory_space=spaces.get(i, pltpu.VMEM)) for i in range(skip)]
    if out_specs is None:
        out_specs = tuple(pl.BlockSpec(memory_space=pltpu.VMEM) for _ in outs)
    in_specs = list(in_specs) + [pl.BlockSpec(memory_space=pl.ANY) for _ in after]
    places = {**{i: pltpu.HBM for i in hbm}, **{i: pltpu.VMEM for i in chip}}
    args = [pltpu.with_memory_space_constraint(a, places[i]) if i in places else a for i, a in enumerate(args)]
    moved = sum(math.prod(a.shape) * jnp.dtype(a.dtype).itemsize for a in (*args, *outs))

    def kernel(*refs):
        body(*refs[:skip], *refs[skip + len(after) :])

    kwargs = {} if grid is None else {"grid": grid}
    return pl.pallas_call(
        kernel,
        out_shape=tuple(outs),
        in_specs=in_specs,
        out_specs=out_specs,
        scratch_shapes=list(scratch),
        compiler_params=pltpu.CompilerParams(vmem_limit_bytes=mib << 20),
        cost_estimate=pl.CostEstimate(flops=flops, bytes_accessed=moved, transcendentals=0),
        **kwargs,
    )(*args, *after)


def fetch(sources, buffers, sems):
    copies = [pltpu.make_async_copy(s, b, sems.at[i]) for i, (s, b) in enumerate(zip(sources, buffers))]
    for copy in copies:
        copy.start()

    def wait():
        for copy in copies:
            copy.wait()

    return wait


def sds(shape, dtype=F32):
    return jax.ShapeDtypeStruct(shape, dtype)


def vmem(shape, dtype=F32):
    return pltpu.VMEM(shape, dtype)


def hbm_out(shape, dtype=F32):
    return pltpu.HBM(shape, dtype)


def lane_of(shape):
    return lax.broadcasted_iota(jnp.int32, shape, len(shape) - 1)


def to_cols(rows, first):
    parts = []
    for i in range(4):
        row = rows[first + i : first + i + 1, :]
        parts.append(jnp.transpose(jnp.broadcast_to(row, (LANES, LANES))))
    return jnp.concatenate(parts, axis=0)


def lane_sums(part):
    total = jnp.sum(jnp.transpose(part), axis=0, keepdims=True)
    return jnp.concatenate([total[:, i * LANES : (i + 1) * LANES] for i in range(4)], axis=0)


def fold_lanes(value):
    out = value[:, :LANES]
    for i in range(1, value.shape[1] // LANES):
        out = out + value[:, i * LANES : (i + 1) * LANES]
    return out


def prep_kernel(pos_ref, wb_hbm, wc_hbm, sp_hbm, wm_hbm, own_ref, block_ref, wb_ref, wc_ref, sp_ref, wm_ref, sems):
    wait = fetch((wb_hbm, wc_hbm, sp_hbm, wm_hbm), (wb_ref, wc_ref, sp_ref, wm_ref), sems)
    cb = wc_ref.shape[0]
    mr, hid = wm_ref.shape
    own_ref[...] = jnp.zeros_like(own_ref)
    wait()
    own_ref[0:HOPS, :, 0 : wb_ref.shape[2]] = wb_ref[...].astype(BF16)
    own_ref[HOPS, :, 0 : wc_ref.shape[1]] = wc_ref[...].astype(BF16)
    own_ref[HOPS, :, PCOL : PCOL + sp_ref.shape[0]] = jnp.transpose(sp_ref[...]).astype(BF16)
    first = pos_ref[1] == 0
    part = cb // 2
    for k in range(HOPS + 1):
        block_ref[k * part : (k + 1) * part, :] = jnp.where(first, own_ref[k, :part], own_ref[k, part:])
    at = (HOPS + 1) * part
    for i in range(2):
        left = wm_ref[:, i * LANES : (i + 1) * LANES]
        right = wm_ref[:, hid // 2 + i * LANES : hid // 2 + (i + 1) * LANES]
        block_ref[at + i * mr : at + (i + 1) * mr, :] = jnp.where(first, left, right).astype(BF16)


def stack_kernel(a_ref, b_ref, c_ref, d_ref, out_ref):
    for i, ref in enumerate((a_ref, b_ref, c_ref, d_ref)):
        out_ref[i] = ref[...]


def assemble_kernel(pos_ref, *refs):
    wb_ref, wm_ref = refs[8:]
    cb = wb_ref.shape[1] // 16
    mr = wm_ref.shape[1] // 16
    part = cb // 2
    first = (HOPS + 1) * part
    for which in range(2):
        half = pos_ref[1] if which == 0 else 1 - pos_ref[1]
        for m in range(4):
            for k in range(4):
                s = pos_ref[0] ^ (4 * k + m)
                block = refs[which * 4 + m][k]
                rows = pl.ds(pl.multiple_of(s * cb + half * part, part), part)
                for j in range(HOPS + 1):
                    wb_ref[j, rows, :] = block[j * part : (j + 1) * part]
                rows = pl.ds(pl.multiple_of(s * mr, mr), mr)
                for i in range(2):
                    wm_ref[half * 2 + i, rows, :] = block[first + i * mr : first + (i + 1) * mr]


def gather_kernel(idx_ref, tab_ref, x_ref, gram_ref, acc, pad):
    i = pl.program_id(0)
    width = tab_ref.shape[1]
    d_in = tab_ref.shape[0] // HOPS
    batch = idx_ref.shape[1]
    rows = lax.broadcasted_iota(jnp.int16, (width, batch), 0)
    hot = jnp.where(rows == (idx_ref[...] - i * width).astype(jnp.int16), BF16(1.0), BF16(0.0))
    part = dot(tab_ref[...].astype(BF16), hot, 1, 0)

    @pl.when(i == 0)
    def _():
        acc[...] = part

    @pl.when(i > 0)
    def _():
        acc[...] += part

    @pl.when(i == pl.num_programs(0) - 1)
    def _():
        row = lax.broadcasted_iota(jnp.int32, pad.shape, 0)
        pad[...] = jnp.where(row == d_in, 1.0, 0.0)
        for k in range(HOPS):
            pad[0:d_in, :] = acc[k * d_in : (k + 1) * d_in, :]
            x = pad[...].astype(BF16)
            x_ref[k] = x
            gram_ref[k] = dot(x, x, 1, 1)


def sum_spread_kernel(in_ref, out_ref):
    out_ref[...] = jnp.broadcast_to(jnp.sum(in_ref[...], axis=0, keepdims=True), out_ref.shape)


def three_terms(wide):
    terms = []
    for _ in range(3):
        terms.append(wide.astype(BF16))
        wide = wide - terms[-1].astype(F32)
    return terms


def exact_dot(low, wide):
    total = None
    for term in three_terms(wide):
        part = dot(low, term, 1, 0)
        total = part if total is None else total + part
    return total


def stats_kernel(count, gram_ref, wb_ref, coef_ref, par_ref, mu_ref, wt_ref):
    hid = wb_ref.shape[1]
    small = jnp.transpose(wb_ref[HOPS].astype(F32))
    row = lax.broadcasted_iota(jnp.int32, (16, hid), 0)

    def at(i):
        return small[PCOL + i : PCOL + i + 1, :]

    def columns(values):
        block = jnp.zeros((16, hid), F32)
        for i, value in enumerate(values):
            block = jnp.where(row == i, value, block)
        return jnp.transpose(jnp.concatenate([block, jnp.zeros((LANES - 16, hid), F32)], axis=0))

    par_ref[...] = columns([at(4 * HOPS + i) for i in range(4)])
    mu_ref[...] = jnp.zeros_like(mu_ref)
    for k in range(HOPS):
        gram = gram_ref[k]
        mu_ref[k : k + 1, :] = gram[ONE : ONE + 1, :] / count
        wide = jnp.transpose(wb_ref[k].astype(F32))
        w = wide.astype(BF16)
        wt_ref[k] = w
        wg = None
        for term in three_terms(gram):
            part = dot(term, w, 1, 0)
            wg = part if wg is None else wg + part
        mean = wg[ONE : ONE + 1, :] / count
        second = jnp.sum(wg * wide, axis=0, keepdims=True) / count
        inv = lax.rsqrt(second - mean * mean + EPS_NORM)
        gain, shift, slope, join = at(k), at(HOPS + k), at(2 * HOPS + k), at(3 * HOPS + k)
        v = gain * inv
        coef_ref[k] = columns(
            (
                0.5 * v,
                0.5 * (shift - v * mean),
                0.5 * (1.0 + slope),
                0.5 * (1.0 - slope),
                1.0 + join,
                1.0 - join,
                join,
                0.5 * (1.0 - join),
                v * slope,
                0.5 * v * (1.0 - slope),
                mean,
                inv,
                v,
            )
        )


def column_set(ref, hop, at, lanes):
    block = ref[hop, at, :]
    return [jnp.broadcast_to(block[:, i : i + 1], (ROWS, WIDE)) for i in lanes]


def merge_block(wm_ref, rows):
    return jnp.concatenate([wm_ref[i, rows, :] for i in range(wm_ref.shape[0])], axis=1)


def forward_kernel(x_ref, wb_ref, coef_ref, wm_hbm, joined_out, pre2_out, pay_ref, pre, wm_ref, joined_ref, pre2_ref, sems, out_sems):
    wait = fetch((wm_hbm,), (wm_ref,), sems)
    stores = []
    hid = wb_ref.shape[1]
    batch = x_ref.shape[2]
    per = hid // CHUNK
    jobs = [(k, c) for k in range(HOPS) for c in range(per)]

    def project(i):
        k, c = jobs[i]
        pre[i % 2] = dot(wb_ref[k, c * CHUNK : (c + 1) * CHUNK, :], x_ref[k], 1, 0)

    def units(i):
        k, c = jobs[i]
        for g in range(CHUNK // ROWS):
            at = slice(c * CHUNK + g * ROWS, c * CHUNK + (g + 1) * ROWS)
            cs = column_set(coef_ref, k, at, range(6))
            for b in range(batch // WIDE):
                lanes = slice(b * WIDE, (b + 1) * WIDE)
                u = pre[i % 2, g * ROWS : (g + 1) * ROWS, lanes] * cs[0] + cs[1]
                u = u * (cs[2] + cs[3] * jnp.tanh(u))
                joined_ref[k, at, lanes] = (u * (cs[4] + cs[5] * jnp.tanh(u))).astype(BF16)

    project(0)
    for i in range(len(jobs)):
        if i + 1 < len(jobs):
            project(i + 1)
        units(i)
        if i % per == per - 1:
            k = i // per
            stores.append(fetch((joined_ref.at[k],), (joined_out.at[k],), out_sems.at[pl.ds(k, 1)]))
            if k == 0:
                wait()
            part = dot(merge_block(wm_ref, slice(k * hid, (k + 1) * hid)), joined_ref[k], 0, 0)
            if k == 0:
                pre2_ref[...] = part
            else:
                pre2_ref[...] += part
    stores.append(fetch((pre2_ref,), (pre2_out,), out_sems.at[pl.ds(HOPS, 1)]))
    value = pre2_ref[...]
    sums = jnp.concatenate([lane_sums(fold_lanes(value)), lane_sums(fold_lanes(value * value))], axis=0)
    pay_ref[...] = jnp.broadcast_to(sums[None], pay_ref.shape)
    for done in stores:
        done()


def columns2(count, rows, par):
    mean = to_cols(rows, 0) / count
    inv = lax.rsqrt(to_cols(rows, 4) / count - mean * mean + EPS_NORM)
    shape = mean.shape
    gain = jnp.broadcast_to(par[:, 0:1], shape)
    shift = jnp.broadcast_to(par[:, 1:2], shape)
    slope = jnp.broadcast_to(par[:, 2:3], shape)
    return mean, inv, gain, shift, slope


def head_kernel(
    count, classes, got_ref, pre2_hbm, par_ref, wb_ref, lab_hbm, dy2_ref, pay_ref, class_ref, stat_ref, act, dact, cols, sums, lab_ref, pre2_ref, sems
):
    wait = fetch((pre2_hbm, lab_hbm), (pre2_ref, lab_ref), sems)
    hid, batch = dy2_ref.shape
    par = par_ref[...]
    mean, inv, gain, shift, slope = columns2(count, jnp.sum(got_ref[...], axis=0), par)
    stat_ref[0] = mean
    stat_ref[1] = inv
    cols[0] = 0.5 * gain * inv
    cols[1] = 0.5 * (shift - gain * inv * mean)
    cols[2] = 1.0 + slope
    cols[3] = 1.0 - slope
    reps = WIDE // LANES

    def tiled(c, at):
        return jnp.concatenate([cols[c, at, :]] * reps, axis=1)

    def first(g, carry):
        at = pl.ds(pl.multiple_of(g * ROWS, ROWS), ROWS)
        c = [tiled(i, at) for i in range(4)]
        for b in range(batch // WIDE):
            lanes = slice(b * WIDE, (b + 1) * WIDE)
            u = pre2_ref[at, lanes] * c[0] + c[1]
            act[at, lanes] = (u * (c[2] + c[3] * jnp.tanh(u))).astype(BF16)
        return carry

    wait()
    lax.fori_loop(0, hid // ROWS, first, 0, unroll=4)
    tail = wb_ref[HOPS]
    wc = jnp.where(lane_of(tail.shape) < PCOL, tail.astype(F32), 0.0).astype(BF16)
    logits = dot(wc, act[...], 0, 0)
    row = lax.broadcasted_iota(jnp.int32, (LANES, batch), 0)
    logits = jnp.where(row < classes, logits + par[0:LANES, 3:4], -jnp.inf)
    top = jnp.max(logits, axis=0, keepdims=True)
    e = jnp.exp(logits - top)
    probs = e / jnp.sum(e, axis=0, keepdims=True)
    dlog = (probs - jnp.where(row == lab_ref[...], 1.0, 0.0)).astype(BF16)
    grad_class = dot(act[...], dlog, 1, 1)
    bias = jnp.sum(dlog.astype(F32), axis=1, keepdims=True)
    dact[...] = dot(wc, dlog, 1, 0)

    def second(g, carry):
        at = pl.ds(pl.multiple_of(g * ROWS, ROWS), ROWS)
        c = [tiled(i, at) for i in range(4)]
        m = jnp.concatenate([stat_ref[0, at, :]] * reps, axis=1)
        v = jnp.concatenate([stat_ref[1, at, :]] * reps, axis=1)
        acc = [jnp.zeros((ROWS, WIDE), F32) for _ in range(3)]
        for b in range(batch // WIDE):
            lanes = slice(b * WIDE, (b + 1) * WIDE)
            p = pre2_ref[at, lanes]
            d = dact[at, lanes]
            u = p * c[0] + c[1]
            t = jnp.tanh(u)
            w = u * (1.0 - t)
            dy = d * (0.5 * (c[2] + c[3] * (t + w * (1.0 + t))))
            dy2_ref[at, lanes] = dy
            acc[0] = acc[0] + dy
            acc[1] = acc[1] + dy * ((p - m) * v)
            acc[2] = acc[2] + d * w
        for i in range(3):
            sums[i, at, :] = fold_lanes(acc[i])
        return carry

    lax.fori_loop(0, hid // ROWS, second, 0, unroll=4)
    pay = jnp.concatenate([lane_sums(sums[0]), lane_sums(sums[1])], axis=0)
    pay_ref[...] = jnp.broadcast_to(pay[None], pay_ref.shape)
    lane = lane_of((hid, LANES))
    slope_sum = jnp.sum(sums[2], axis=1, keepdims=True)
    bias = jnp.concatenate([bias, jnp.zeros((hid - LANES, 1), F32)], axis=0)
    block = jnp.where(lane < classes, grad_class, 0.0)
    block = jnp.where(lane == PCOL, slope_sum, block)
    class_ref[...] = jnp.where(lane == PCOL + 1, bias, block)


def turn_kernel(
    count, pos_ref, got_ref, stat_ref, par_ref, pre2_hbm, dy2_ref, joined_hbm, class_ref, dpre_ref, keep_ref, send_ref, sum2_ref, cols, joined_ref, pre2_ref, sems
):
    hid, batch = dy2_ref.shape
    wait = fetch((pre2_hbm,), (pre2_ref,), sems.at[pl.ds(HOPS, 1)])
    dp, rows, half = keep_ref.shape
    hops = joined_ref.shape[0]
    waits = [fetch((joined_hbm.at[k],), (joined_ref.at[k],), sems.at[pl.ds(k, 1)]) for k in range(hops)]
    mr = hops * hid // dp
    cb = hid // dp
    rows8 = jnp.sum(got_ref[...], axis=0)
    sum2_ref[...] = rows8
    mean, inv = stat_ref[0], stat_ref[1]
    v = jnp.broadcast_to(par_ref[:, 0:1], mean.shape) * inv
    cols[0] = v
    cols[1] = v * to_cols(rows8, 0) / count
    cols[2] = v * inv * to_cols(rows8, 4) / count
    reps = WIDE // LANES
    wait()
    for g in range(hid // ROWS):
        at = slice(g * ROWS, (g + 1) * ROWS)
        c = [jnp.concatenate([cols[i, at, :]] * reps, axis=1) for i in range(3)]
        m = jnp.concatenate([stat_ref[0, at, :]] * reps, axis=1)
        for b in range(batch // WIDE):
            lanes = slice(b * WIDE, (b + 1) * WIDE)
            value = c[0] * dy2_ref[at, lanes] - c[1] - (pre2_ref[at, lanes] - m) * c[2]
            dpre_ref[at, lanes] = value.astype(BF16)
    mine = pl.ds(pl.multiple_of(pos_ref[1] * half, half), half)
    theirs = pl.ds(pl.multiple_of((1 - pos_ref[1]) * half, half), half)
    per = dp // hops
    for k in range(hops):
        waits[k]()
        block = joined_ref[k]
        own = dot(block, dpre_ref[mine, :], 1, 1)
        other = dot(block, dpre_ref[theirs, :], 1, 1).astype(BF16)
        for j in range(per):
            keep_ref[k * per + j, 0:mr, :] = own[j * mr : (j + 1) * mr]
            send_ref[k * per + j, 0:mr, :] = other[j * mr : (j + 1) * mr]
    first = pos_ref[1] == 0
    for s in range(dp):
        block = class_ref[s * cb : (s + 1) * cb, :]
        wide = jnp.concatenate([block[: cb // 2], block[cb // 2 :]], axis=1)
        keep_ref[s, mr:rows, :] = jnp.where(first, wide, 0.0)
        send_ref[s, mr:rows, :] = jnp.where(first, 0.0, wide).astype(BF16)


def factor_kernel(x_ref, wb_ref, coef_ref, e_ref, f_ref, g_ref, pre):
    hid = wb_ref.shape[1]
    batch = x_ref.shape[2]
    per = hid // CHUNK

    def project(c):
        pre[c % 2] = dot(wb_ref[0, c * CHUNK : (c + 1) * CHUNK, :], x_ref[0], 1, 0)

    project(0)
    for c in range(per):
        if c + 1 < per:
            project(c + 1)
        for g in range(CHUNK // ROWS):
            at = slice(c * CHUNK + g * ROWS, c * CHUNK + (g + 1) * ROWS)
            here = slice(g * ROWS, (g + 1) * ROWS)
            a1, b1, p1, q1, s2, q2, s1, r1 = column_set(coef_ref, 0, at, (0, 1, 2, 3, 6, 7, 8, 9))
            for b in range(batch // WIDE):
                lanes = slice(b * WIDE, (b + 1) * WIDE)
                u = pre[c % 2, here, lanes] * a1 + b1
                t = jnp.tanh(u)
                u2 = u * (p1 + q1 * t)
                t2 = jnp.tanh(u2)
                w = u2 * (1.0 - t2)
                g_ref[0, at, lanes] = w.astype(BF16)
                d = s2 + q2 * ((1.0 + t2) * (1.0 + w))
                w = u * (1.0 - t)
                f_ref[0, at, lanes] = (d * w).astype(BF16)
                e_ref[0, at, lanes] = (d * (s1 + r1 * ((1.0 + t) * (1.0 + w)))).astype(BF16)


SMALLS = 4


def back_kernel(own, pos_ref, dpre_ref, x_ref, wb_ref, mu_ref, wm_hbm, e_hbm, f_hbm, g_hbm, *refs):
    if own:
        recv_ref, refs = refs[0], refs[1:]
    b_ref, a_out, dj, dyv, sums, a_ref, wm_ref, e_ref, f_ref, g_ref, sems, out_sems = refs
    hid = wb_ref.shape[1]
    batch = x_ref.shape[2]
    per = hid // CHUNK
    jobs = [(k, c) for k in range(2) for c in range(per)]
    base = 2 * (pos_ref[1] if own else 1 - pos_ref[1])
    lane = lane_of((hid, LANES))
    dp, _, cb, _ = b_ref.shape
    copies = []
    waits = []
    for k in range(2):
        at = pl.ds(pl.multiple_of((base + k) * hid, hid), hid)
        sources = [wm_hbm.at[:, at, :]] + [ref.at[base + k] for ref in (e_hbm, f_hbm, g_hbm)]
        buffers = [ref.at[k] for ref in (wm_ref, e_ref, f_ref, g_ref)]
        waits.append(fetch(sources, buffers, sems.at[k]))

    def project(i):
        k, c = jobs[i]
        if c == 0:
            waits[k]()
        dj[i % 2] = dot(merge_block(wm_ref.at[k], slice(c * CHUNK, (c + 1) * CHUNK)), dpre_ref[...], 1, 0)

    def units(i):
        k, c = jobs[i]
        for g in range(CHUNK // ROWS):
            at = slice(c * CHUNK + g * ROWS, c * CHUNK + (g + 1) * ROWS)
            here = slice(g * ROWS, (g + 1) * ROWS)
            first = jnp.zeros((ROWS, WIDE), F32)
            second = jnp.zeros((ROWS, WIDE), F32)
            for b in range(batch // WIDE):
                lanes = slice(b * WIDE, (b + 1) * WIDE)
                d = dj[i % 2, here, lanes]
                dyv[k, at, lanes] = (d * e_ref[k, at, lanes].astype(F32)).astype(BF16)
                first = first + d * f_ref[k, at, lanes].astype(F32)
                second = second + d * g_ref[k, at, lanes].astype(F32)
            sums[k, 0, at, :] = fold_lanes(first)
            sums[k, 1, at, :] = fold_lanes(second)

    def close(k):
        w = wb_ref[base + k]
        a_ref[k] = dot(w, dyv[k], 0, 0)
        copies.append(fetch((a_ref.at[k],), (a_out.at[k],), out_sems.at[pl.ds(k, 1)]))
        block = dot(dyv[k], x_ref[base + k], 1, 1)
        total = block[:, ONE : ONE + 1]
        block = jnp.where(lane < ONE, block - total * mu_ref[pl.ds(base + k, 1), :], 0.0)
        smalls = (
            total,
            jnp.sum(block * w.astype(F32), axis=1, keepdims=True),
            jnp.sum(sums[k, 0], axis=1, keepdims=True),
            jnp.sum(sums[k, 1], axis=1, keepdims=True),
        )
        for i, value in enumerate(smalls):
            block = jnp.where(lane == ONE + i, value, block)
        for s in range(dp):
            piece = block[s * cb : (s + 1) * cb, :]
            if own:
                piece = piece + join_smalls(recv_ref[s, k].astype(F32))
            b_ref[s, k] = split_smalls(piece)

    project(0)
    for i in range(len(jobs)):
        if i + 1 < len(jobs):
            project(i + 1)
        units(i)
        if i % per == per - 1:
            close(i // per)
    for done in copies:
        done()


def split_smalls(block):
    lane = lane_of(block.shape)
    rest = block - block.astype(BF16).astype(F32)
    moved = pltpu.roll(rest, SMALLS, 1)
    return jnp.where((lane >= ONE + SMALLS) & (lane < ONE + 2 * SMALLS), moved, block).astype(BF16)


def join_smalls(block):
    lane = lane_of(block.shape)
    moved = pltpu.roll(block, LANES - SMALLS, 1)
    block = jnp.where((lane >= ONE) & (lane < ONE + SMALLS), block + moved, block)
    return jnp.where(lane < ONE + SMALLS, block, 0.0)


def split_low_kernel(pos_ref, keep_ref, got_ref, o0_ref, o1_ref, o2_ref, o3_ref):
    low = pos_ref[0] % 4
    for m, ref in enumerate((o0_ref, o1_ref, o2_ref, o3_ref)):
        for z in range(4):
            j = z * 4 + (low ^ m)
            ref[z] = (keep_ref[j] + got_ref[j].astype(F32)).astype(ref.dtype)


def split_high_kernel(pos_ref, own_ref, g1_ref, g2_ref, g3_ref, o0_ref, o1_ref, o2_ref, o3_ref):
    high = pos_ref[0] // 4
    for k, ref in enumerate((o0_ref, o1_ref, o2_ref, o3_ref)):
        j = high ^ k
        value = own_ref[j] + g1_ref[j].astype(F32) + g2_ref[j].astype(F32) + g3_ref[j].astype(F32)
        ref[...] = value.astype(ref.dtype)


def owner_kernel(
    count, classes, pos_ref, got_ref, sum2_ref, w1_ref, w2_ref, w3_ref, *refs
):
    grad_ref, pay_ref, sems = refs[4], refs[5], refs[10]
    w0_ref, pack_ref, coef_ref, gram_ref = refs[6:10]
    fetch(refs[:4], refs[6:10], sems)()
    _, _, cb, _ = got_ref.shape
    total = jnp.sum(got_ref[...].astype(F32), axis=0)
    rep = pos_ref[1]
    start = pl.multiple_of(pos_ref[0] * cb, cb)
    lane = lane_of((cb, LANES))
    squares = jnp.zeros((1, 1), F32)
    spread = jnp.zeros((cb, LANES), F32)

    def all_sum(v):
        return jnp.sum(jnp.sum(v, axis=1, keepdims=True), axis=0, keepdims=True)

    for i in range(2):
        hop = rep * 2 + i
        b = join_smalls(total[i])
        coef = coef_ref[hop, pl.ds(start, cb), :]
        mean, inv, v = coef[:, 10:11], coef[:, 11:12], coef[:, 12:13]
        gram = gram_ref[hop]
        s = b[:, ONE : ONE + 1]
        g = inv * b[:, ONE + 1 : ONE + 2]
        beta = inv * g / count
        alpha = s / count - beta * mean
        wg = exact_dot(pack_ref[hop], gram) - mean * gram[ONE : ONE + 1, :]
        fixed = jnp.where(lane < ONE, b - beta * wg, 0.0)
        fixed = jnp.where(lane == ONE, g / v, fixed)
        fixed = jnp.where(lane == ONE + 1, s / v, fixed)
        fixed = jnp.where(lane == ONE + 2, b[:, ONE + 2 : ONE + 3], fixed)
        fixed = jnp.where(lane == ONE + 3, b[:, ONE + 3 : ONE + 4], fixed)
        grad_ref[i * cb : (i + 1) * cb, :] = fixed
        squares = squares + all_sum(fixed * fixed)
        spread = jnp.where(lane == 2 * i, alpha, spread)
        spread = jnp.where(lane == 2 * i + 1, beta, spread)
    wide = w0_ref[...].astype(F32) + w1_ref[...].astype(F32) + w2_ref[...].astype(F32) + w3_ref[...].astype(F32)
    mr = wide.shape[0] - cb // 2
    merge = wide[:mr]
    squares = squares + all_sum(merge * merge)
    at = 2 * cb
    for i in range(2):
        grad_ref[at + i * mr : at + (i + 1) * mr, :] = merge[:, i * LANES : (i + 1) * LANES]
    at = at + 2 * mr
    block = jnp.concatenate([wide[mr:, :LANES], wide[mr:, LANES:]], axis=0)
    shift_own = own_column(sum2_ref, 0, pos_ref[0], cb)
    gain_own = own_column(sum2_ref, 4, pos_ref[0], cb)
    block = jnp.where(lane == PCOL + 2, gain_own, block)
    block = jnp.where(lane == PCOL + 3, shift_own, block)
    grad_ref[at : at + cb, :] = block
    squares = squares + jnp.where(rep == 0, all_sum(block * block), 0.0)
    spread = jnp.where(lane == 4, jnp.broadcast_to(squares, spread.shape), spread)
    rows = jnp.transpose(jnp.concatenate([spread, jnp.zeros((LANES - cb, LANES), F32)], axis=0))[0:8]
    offset = (pos_ref[0] * cb) % LANES
    rows = pltpu.roll(rows, offset, 1)
    row8 = lax.broadcasted_iota(jnp.int32, rows.shape, 0)
    rows = jnp.where((row8 == 4) & (lane_of(rows.shape) != offset), 0.0, rows)
    pay_ref[...] = jnp.broadcast_to(rows[None], pay_ref.shape)


def own_column(ref, first, me, cb):
    block = (me * cb) // LANES
    row = ref[pl.ds(first + block, 1), :]
    lane = lane_of((cb, LANES))
    sub = lax.broadcasted_iota(jnp.int32, (cb, LANES), 0)
    hit = lane == sub + (me * cb) % LANES
    return jnp.sum(jnp.where(hit, jnp.broadcast_to(row, (cb, LANES)), 0.0), axis=1, keepdims=True)


def adam_into(weight_ref, moment_ref, square_ref, grad, scale, rate, outs, at=Ellipsis):
    new_ref, new_m_ref, new_s_ref, copy_ref = outs
    weight = weight_ref[at]
    clipped = grad * scale
    moment = 0.9 * moment_ref[at] + 0.1 * clipped
    square = 0.999 * square_ref[at] + 0.001 * clipped * clipped
    fix_one = 1.0 - 0.9**STEP
    fix_two = 1.0 - 0.999**STEP
    update = moment / fix_one / (jnp.sqrt(square / fix_two) + 1e-08) + 0.01 * weight
    new = weight - rate * update
    new_ref[at] = new
    new_m_ref[at] = moment
    new_s_ref[at] = square
    copy_ref[at] = new.astype(BF16)


def final_kernel(pos_ref, got_ref, mine_ref, other_ref, x_ref, wt_ref, own_hbm, sent_hbm, *refs):
    states_hbm, refs = refs[:12], refs[12:]
    outs, norm_ref, rows_ref = refs[:16], refs[16], refs[17]
    own_ref, sent_ref = refs[18:20]
    states, sems, more = refs[20:32], refs[32], refs[33]
    wait_rows = fetch((own_hbm, sent_hbm), (own_ref, sent_ref), more)
    wait = fetch(states_hbm, states, sems)
    weights, firsts, seconds = states[0:4], states[4:8], states[8:12]
    dp = got_ref.shape[0] // 2
    blocks = 4
    per = dp // blocks
    parts = []
    for b in range(blocks):
        for r in range(2):
            total = got_ref[(b * per) * 2 + r]
            for i in range(1, per):
                total = total + got_ref[(b * per + i) * 2 + r]
            parts.append(total)
    squares = parts[0][4:5, :]
    for part in parts[1:]:
        squares = squares + part[4:5, :]
    norm = jnp.sqrt(jnp.sum(squares, axis=1, keepdims=True))
    norm_ref[...] = norm
    scale = 1.0 / jnp.maximum(norm, 1.0)

    cb = weights[0].shape[1]
    d_in = weights[0].shape[2]
    mr = weights[1].shape[0]
    classes = weights[2].shape[1]
    first = pos_ref[1] == 0
    mine, other = mine_ref[...], other_ref[...]
    low = jnp.where(first, mine, other)
    high = jnp.where(first, other, mine)
    wait_rows()

    for k in range(HOPS):
        r, i = k // 2, k % 2
        alpha = jnp.concatenate([parts[b * 2 + r][2 * i : 2 * i + 1] for b in range(blocks)], axis=1)
        beta = jnp.concatenate([parts[b * 2 + r][2 * i + 1 : 2 * i + 2] for b in range(blocks)], axis=1)
        low_w = wt_ref[k]
        right = jnp.where(lax.broadcasted_iota(jnp.int32, low_w.shape, 0) == ONE, alpha, low_w.astype(F32) * beta)
        hi = right.astype(BF16)
        fix = dot(low_w, hi, 1, 1) + dot(low_w, (right - hi.astype(F32)).astype(BF16), 1, 1)
        hi = fix.astype(BF16)
        lo = (fix - hi.astype(F32)).astype(BF16)
        kept = pos_ref[1] == r
        value = jnp.where(kept, own_ref[i], sent_ref[i])
        value = value - (dot(hi, x_ref[k], 1, 0) + dot(lo, x_ref[k], 1, 0))
        rows_ref[k * d_in : (k + 1) * d_in, :] = value[:d_in]

    def group(i):
        return [o for o in outs[i::4]]

    wait()
    hops = [low[0:cb], low[cb : 2 * cb], high[0:cb], high[cb : 2 * cb]]
    for k in range(HOPS):
        adam_into(weights[0], firsts[0], seconds[0], hops[k][:, :d_in], scale, 0.05, group(0), k)
    at = 2 * cb
    for half, part in enumerate((low, high)):
        for i in range(2):
            lanes = (slice(None), slice((2 * half + i) * LANES, (2 * half + i + 1) * LANES))
            grad = part[at + i * mr : at + (i + 1) * mr]
            adam_into(weights[1], firsts[1], seconds[1], grad, scale, 0.05, group(1), lanes)
    at = at + 2 * mr
    block = low[at : at + cb]
    adam_into(weights[2], firsts[2], seconds[2], block[:, :classes], scale, 0.05, group(2))
    lane = lane_of((cb, LANES))
    small = jnp.zeros((cb, LANES), F32)
    for kind in range(4):
        for k in range(HOPS):
            small = jnp.where(lane == kind * HOPS + k, hops[k][:, ONE + kind : ONE + kind + 1], small)
    for i, source in enumerate((2, 3, 0, 1)):
        small = jnp.where(lane == 4 * HOPS + i, block[:, PCOL + source : PCOL + source + 1], small)
    small = jnp.transpose(jnp.concatenate([small, jnp.zeros((LANES - cb, LANES), F32)], axis=0))
    adam_into(weights[3], firsts[3], seconds[3], small[: weights[3].shape[0], :cb], scale, 0.3, group(3))


def flip(value, mask, dp):
    return lax.ppermute(value, "dp", [(i, i ^ mask) for i in range(dp)])


def swap(value):
    return lax.ppermute(value, "rep", [(0, 1), (1, 0)])


def exchange(value):
    return lax.all_to_all(value, BOTH, 0, 0, tiled=True)


def weights_plain(wbt, wc, sp, wm, dp):
    cb, classes = wc.shape
    mr, hid = wm.shape
    own = jnp.zeros((HOPS + 1, cb, LANES), BF16)
    own = own.at[:HOPS, :, : wbt.shape[2]].set(wbt.astype(BF16))
    own = own.at[HOPS, :, :classes].set(wc.astype(BF16))
    own = own.at[HOPS, :, PCOL : PCOL + sp.shape[0]].set(sp.T.astype(BF16))
    wb = lax.all_gather(own, "dp", axis=1, tiled=True)
    whole = lax.all_gather(wm.astype(BF16), "dp", axis=0, tiled=True)
    return own, wb, whole.reshape(HOPS * hid, hid // LANES, LANES).transpose(1, 0, 2)


def on_device(table, batch_index, labels, *state):
    weights, firsts, seconds = state[0:4], state[4:8], state[8:12]
    dp, rep = lax.axis_size("dp"), lax.axis_size("rep")
    n = dp * rep
    staged = dp == 16 and rep == 2
    me, core = lax.axis_index("dp"), lax.axis_index("rep")
    pos = jnp.stack([me, core]).astype(jnp.int32)
    batch = batch_index.shape[0]
    count = float(batch * n)
    nodes, width = table.shape
    cb = weights[0].shape[2]
    mr, hid = weights[1].shape
    classes = weights[2].shape[1]
    half = hid // 2
    lhs = [v.transpose(0, 2, 1) for v in (weights[0], firsts[0], seconds[0])]
    idx = batch_index.reshape(1, batch)
    lab = labels.reshape(1, batch)

    if staged:
        with jax.named_scope("prep"):
            sources = (lhs[0], weights[2], weights[3], weights[1])
            size = (HOPS + 1) * cb // 2 + 2 * mr
            own, block = call(
                prep_kernel,
                [hbm_out((HOPS + 1, cb, LANES), BF16), sds((size, LANES), BF16)],
                pos, *sources,
                smem=(0,), hbm=(1, 2, 3, 4),
                scratch=[pltpu.VMEM(v.shape, F32) for v in sources] + [pltpu.SemaphoreType.DMA((4,))],
            )
        far = [flip(block, 4 * k, dp) for k in range(1, 4)]

    with jax.named_scope("gather"):
        step = 2048
        x, gram = call(
            gather_kernel,
            [vmem((HOPS, LANES, batch), BF16), hbm_out((HOPS, LANES, LANES))],
            pltpu.with_memory_space_constraint(idx, pltpu.HBM),
            pltpu.with_memory_space_constraint(table.T, pltpu.HBM),
            grid=(nodes // step,),
            in_specs=[
                pl.BlockSpec((1, batch), lambda i: (0, 0)),
                pl.BlockSpec((width, step), lambda i: (0, i)),
            ],
            out_specs=(
                pl.BlockSpec((HOPS, LANES, batch), lambda i: (0, 0, 0)),
                pl.BlockSpec((HOPS, LANES, LANES), lambda i: (0, 0, 0)),
            ),
            scratch=[pltpu.VMEM((width, batch), F32), pltpu.VMEM((LANES, batch), F32)],
            flops=2 * nodes * width * batch,
            after=(block,) if staged else (),
            mib=24,
        )
    with jax.named_scope("gram_sum"):
        parts = gram.reshape(n, HOPS * LANES // n, LANES)
        if staged:
            (stacked,) = call(stack_kernel, [sds((4,) + block.shape, BF16)], block, *far, after=(x,))
            parts, stacked = lax.optimization_barrier((parts, stacked))
        parts = exchange(parts)
        (parts,) = call(sum_spread_kernel, [hbm_out(parts.shape)], parts)
        gram = exchange(parts).reshape(HOPS, LANES, LANES)
    with jax.named_scope("weights"):
        if staged:
            mine = [stacked] + [flip(stacked, m, dp) for m in range(1, 4)]
            mine, _ = lax.optimization_barrier((mine, parts))
            other = [swap(v) for v in mine]
            wb, wm = call(
                assemble_kernel,
                [vmem((HOPS + 1, hid, LANES), BF16), hbm_out((hid // LANES, HOPS * hid, LANES), BF16)],
                pos, *mine, *other,
                smem=(0,),
            )
        else:
            own, wb, wm = weights_plain(lhs[0], weights[2], weights[3], weights[1], dp)
    with jax.named_scope("stats"):
        coef, par, mu, wt = call(
            functools.partial(stats_kernel, count),
            [vmem((HOPS, hid, LANES)), vmem((hid, LANES)), vmem((8, LANES)), vmem((HOPS, LANES, hid), BF16)],
            gram, wb,
            flops=2 * HOPS * hid * LANES * LANES * 3,
        )
    with jax.named_scope("forward"):
        joined, pre2, pay = call(
            forward_kernel,
            [hbm_out((HOPS, hid, batch), BF16), hbm_out((hid, batch)), sds((n, 8, LANES))],
            x, wb, coef, wm,
            hbm=(3,),
            out_specs=(pl.BlockSpec(memory_space=pltpu.HBM),) * 2 + (pl.BlockSpec(memory_space=pltpu.VMEM),),
            scratch=[
                pltpu.VMEM((2, CHUNK, batch), F32),
                pltpu.VMEM(wm.shape, BF16),
                pltpu.VMEM((HOPS, hid, batch), BF16),
                pltpu.VMEM((hid, batch), F32),
                pltpu.SemaphoreType.DMA((1,)),
                pltpu.SemaphoreType.DMA((HOPS + 1,)),
            ],
            mib=16,
            flops=2 * batch * HOPS * hid * (LANES + hid),
        )
    got = exchange(pay)
    with jax.named_scope("factors"):
        hop = lambda *shape: pl.BlockSpec((1,) + shape, lambda k: (k, 0, 0))
        factors = call(
            factor_kernel,
            [hbm_out((HOPS, hid, batch), BF16)] * 3,
            x, wb, coef,
            grid=(HOPS,),
            in_specs=[hop(LANES, batch), hop(hid, LANES), hop(hid, LANES)],
            out_specs=(hop(hid, batch),) * 3,
            scratch=[pltpu.VMEM((2, CHUNK, batch), F32)],
            after=(pay,),
            flops=2 * batch * HOPS * hid * LANES * 16,
            mib=12,
        )
    with jax.named_scope("head"):
        dy2, pay, block2, stat = call(
            functools.partial(head_kernel, count, classes),
            [vmem((hid, batch)), sds((n, 8, LANES)), vmem((hid, LANES)), vmem((2, hid, LANES))],
            got, pre2, par, wb, lab,
            hbm=(1, 4),
            after=(pltpu.with_memory_space_constraint(factors[0], pltpu.HBM),),
            scratch=[
                pltpu.VMEM((hid, batch), BF16),
                pltpu.VMEM((hid, batch), F32),
                pltpu.VMEM((4, hid, LANES), F32),
                pltpu.VMEM((3, hid, LANES), F32),
                pltpu.VMEM(lab.shape, lab.dtype),
                pltpu.VMEM((hid, batch), F32),
                pltpu.SemaphoreType.DMA((2,)),
            ],
            flops=6 * batch * hid * LANES,
        )
    got = exchange(pay)
    with jax.named_scope("turn"):
        rows = mr + cb // 2
        turned = vmem if staged else sds
        dpre, keep, send, sum2 = call(
            functools.partial(turn_kernel, count),
            [vmem((hid, batch), BF16), turned((dp, rows, half)), sds((dp, rows, half), BF16), vmem((8, LANES))],
            pos, got, stat, par, pre2, dy2, joined, block2,
            smem=(0,), hbm=(4, 6),
            scratch=[
                pltpu.VMEM((3, hid, LANES), F32),
                pltpu.VMEM((HOPS, hid, batch), BF16),
                pltpu.VMEM((hid, batch), F32),
                pltpu.SemaphoreType.DMA((HOPS + 1,)),
            ],
            flops=2 * batch * HOPS * hid * hid,
        )

    def back(own_hops, *more, after=()):
        outs = [(hbm_out if own_hops else sds)((dp, 2, cb, LANES), BF16), hbm_out((2, LANES, batch))]
        with jax.named_scope("back"):
            return call(
                functools.partial(back_kernel, own_hops),
                outs,
                pos, dpre, x, wb, mu, wm, *factors, *more,
                smem=(0,),
                hbm=(5, 6, 7, 8),
                after=after,
                out_specs=(pl.BlockSpec(memory_space=pltpu.VMEM), pl.BlockSpec(memory_space=pltpu.HBM)),
                scratch=[
                    pltpu.VMEM((2, CHUNK, batch), F32),
                    pltpu.VMEM((2, hid, batch), BF16),
                    pltpu.VMEM((2, 2, hid, LANES), F32),
                    pltpu.VMEM((2, LANES, batch), F32),
                    pltpu.VMEM((2, hid // LANES, hid, LANES), BF16),
                ]
                + [pltpu.VMEM((2, hid, batch), BF16)] * 3
                + [pltpu.SemaphoreType.DMA((2, 4)), pltpu.SemaphoreType.DMA((2,))],
                flops=4 * batch * hid * (hid + 3 * LANES),
                mib=20,
            )

    recv = swap(send)
    sent_b, sent_a = back(False)
    recv_b = swap(sent_b)
    with jax.named_scope("merge_sum"):
        if staged:
            shape = (4, rows, half)
            low = call(
                split_low_kernel, [vmem(shape)] + [sds(shape, BF16)] * 3, pos, keep, recv, smem=(0,), after=(sent_b,)
            )
            moved = [flip(low[m], m, dp) for m in range(1, 4)]
            kept_b, kept_a = back(True, recv_b, after=(low[0],))
            high = call(
                split_high_kernel,
                [sds(shape[1:])] + [sds(shape[1:], BF16)] * 3,
                pos, low[0], *moved,
                smem=(0,),
            )
            kept_b, high = lax.optimization_barrier((kept_b, high))
            wide = [high[0]] + [flip(high[k], 4 * k, dp) for k in range(1, 4)]
        else:
            kept_b, kept_a = back(True, recv_b)
            total = lax.psum_scatter(keep + recv.astype(F32), "dp", scatter_dimension=0)
            wide = [total] + [jnp.zeros_like(total)] * 3
    with jax.named_scope("branch_sum"):
        got_b = lax.all_to_all(kept_b, "dp", 0, 0, tiled=True)
    with jax.named_scope("owner"):
        late = (wide[0], own, coef, gram)
        shares, pay = call(
            functools.partial(owner_kernel, count, classes),
            [sds((3 * cb + 2 * mr, LANES)), hbm_out((n, 8, LANES))],
            pos, got_b, sum2, *wide[1:], *late,
            smem=(0,),
            hbm=tuple(range(6, 10)),
            scratch=[pltpu.VMEM(v.shape, v.dtype) for v in late] + [pltpu.SemaphoreType.DMA((4,))],
        )
    theirs = swap(shares)
    got = exchange(pay)
    with jax.named_scope("final"):
        tr = [(lhs[i],) + tuple(s[1:]) for i, s in enumerate((weights, firsts, seconds))]
        shapes = [t.shape for t in tr[0]]
        outs = []
        for dtype in (F32, F32, F32, BF16):
            outs += [sds(s, dtype) for s in shapes]
        outs += [sds((1, 1)), sds((width, batch))]
        local = (*tr[0], *tr[1], *tr[2])
        res = call(
            final_kernel, outs, pos, got, shares, theirs, x, wt, kept_a, sent_a, *local,
            smem=(0,), hbm=tuple(range(6, 8 + len(local))),
            scratch=[pltpu.VMEM(v.shape, v.dtype) for v in (kept_a, sent_a) + local]
            + [pltpu.SemaphoreType.DMA((len(local),)), pltpu.SemaphoreType.DMA((2,))],
            flops=2 * batch * LANES * LANES * 3 * HOPS,
        )
    result = list(res[:16])
    for i in range(0, 16, 4):
        result[i] = result[i].transpose(0, 2, 1)
    return (*result, res[16].reshape(()), res[17].T)


def solution(mesh):
    tables = (P(BOTH, None), P(BOTH), P(BOTH))
    params = (P(None, None, "dp"), P("dp", None), P("dp", None), P(None, "dp"))
    return jax.shard_map(
        on_device,
        mesh=mesh,
        in_specs=tables + params * 3,
        out_specs=params * 4 + (P(), P(BOTH, None)),
        check_vma=False,
    )
```

time: 234 us -> 163 us (0.70)
  local copies, waits for them, and re-layouts: 32.9 us -> 1.46 us
  Pallas kernels: 80.7 us -> 66.9 us
  waiting for transfers between devices: 51.6 us -> 39.7 us
  blocking collectives: 20.4 us -> 13.7 us
  starting transfers between devices: 43.7 us -> 39.6 us
    unnamed x92 -> x10, local copies, waits for them, and re-layouts: 31.2 us -> 1.46 us
    pallas_call x16, Pallas kernels: 80.7 us -> 66.9 us  [call(): pl.pallas_call(kernel, out_shape=tuple(outs), in_specs=in_specs, out_spec...]
    ppermute x18 -> x12, waiting for transfers between devices: 35.1 us -> 22.6 us  [flip(): return lax.ppermute(value, 'dp', [(i, i ^ mask) for i in range(dp)])]
    ppermute x18 -> x12, starting transfers between devices: 27.1 us -> 17.3 us  [flip(): return lax.ppermute(value, 'dp', [(i, i ^ mask) for i in range(dp)])]
    all_to_all x2 -> x1, blocking collectives: 20.4 us -> 13.7 us  [exchange(): return lax.all_to_all(value, BOTH, 0, 0, tiled=True)]
    all_to_all x3 -> x4, starting transfers between devices: 11.8 us -> 16.6 us  [exchange(): return lax.all_to_all(value, BOTH, 0, 0, tiled=True)]
    all_to_all x3 -> x4, waiting for transfers between devices: 13.5 us -> 13.9 us  [exchange(): return lax.all_to_all(value, BOTH, 0, 0, tiled=True)]
  transfers between devices with their start and end apart: 26 -> 24, of which waited for: 12 -> 13; matrix products, arithmetic and copies ran while one was open for 4% -> 0% of each run, Pallas kernels for 19% -> 21%
where the time goes in v2:
time: 163 us
  Pallas kernels  66.9 us (41%)
  waiting for transfers between devices  39.7 us (24%)
  starting transfers between devices  39.6 us (24%)
  blocking collectives  13.7 us (8%)
    pallas_call x16, Pallas kernels, call(): pl.pallas_call(kernel, out_shape=tuple(outs), in_specs=in_specs, out_spec...  66.9 us
    ppermute x12, waiting for transfers between devices, flip(): return lax.ppermute(value, 'dp', [(i, i ^ mask) for i in range(dp)])  22.6 us
    ppermute x12, starting transfers between devices, flip(): return lax.ppermute(value, 'dp', [(i, i ^ mask) for i in range(dp)])  17.3 us
    all_to_all x4, starting transfers between devices, exchange(): return lax.all_to_all(value, BOTH, 0, 0, tiled=True)  16.6 us
    all_to_all x4, waiting for transfers between devices, exchange(): return lax.all_to_all(value, BOTH, 0, 0, tiled=True)  13.9 us
    all_to_all x1, blocking collectives, exchange(): return lax.all_to_all(value, BOTH, 0, 0, tiled=True)  13.7 us
    all_to_all x1, starting transfers between devices, on_device(): got_b = lax.all_to_all(kept_b, 'dp', 0, 0, tiled=True)  3.72 us
    ppermute x7, waiting for transfers between devices, swap(): return lax.ppermute(value, 'rep', [(0, 1), (1, 0)])  3.28 us
  transfers between devices with their start and end apart: 24, of which 13 were waited for; matrix products, arithmetic and copies ran while one was open for 0% of the time, Pallas kernels for 21%

profile of v2, /device:TPU:0, one launch (start us, length us, event | category | flops | bytes accessed | tf_op | source)
XLA Modules:
  0.0 162.5 jit_solution(2382610497237217578)
XLA Ops:
  0.7 2.4 %prep.1 = (bf16[5,32,128]{2,1,0:T(8,128)(2,1)}, bf16[336,128]{1,0:T(8,128)(2,1)S(1)}) custom-call(s32[2]{0:T(128)S(1)} %pad_add_fusion.refs_0_, f32[4,32,100]{2,1,0:T(8,128)} %bitcast.18, f32[32,47]{1,0:T(8,128)} %refs_10_.1, f32[20,32]{1,0:T(8,128)} %refs_11_.1, f32[128,512]{1,0:T(8,128)} %refs_9_.1), custom_call_target="tpu_custom_call" | custom-call | bytes 448904 | tf_op jit(solution)/shard_map/prep/pallas_call | solution.py:48
  3.1 5.1 %collective-permute-start.2 = (bf16[336,128]{1,0:T(8,128)(2,1)S(1)}, bf16[336,128]{1,0:T(8,128)(2,1)S(1)}, u32[]{:S(2)}, u32[]{:S(2)}) collective-permute-start(bf16[336,128]{1,0:T(8,128)(2,1)S(1)} %get-tuple-element.85.refs_2_.refs_0_), channel_id=1, source_target_pairs={{0,24},{2,26},{4,28},{6,30},{8,16},{10,18},{12,20},{14,22},{16,8},... | collective-permute-start | bytes 258056 | tf_op jit(solution)/shard_map/ppermute | solution.py:737
  8.2 0.6 collective-permute-start
  8.9 7.1 %gather.1 = (bf16[4,128,1024]{2,1,0:T(8,128)(2,1)S(1)}, f32[4,128,128]{2,1,0:T(8,128)}) custom-call(s32[1,1024]{1,0:T(1,128)} %bitcast.30, f32[400,4096]{1,0:T(8,128)} %bitcast.24, bf16[336,128]{1,0:T(8,128)(2,1)S(1)} %get-tuple-element.85.refs_2_.refs_0_), custom_call_target="tpu_custom_call" | custom-call | flops 3355443200 | bytes 7868416 | tf_op jit(solution)/shard_map/gather/pallas_call | solution.py:48
  16.0 6.0 %all-to-all-start = ((f32[32,16,128]{2,1,0:T(8,128)}), f32[32,16,128]{2,1,0:T(8,128)S(1)}, u32[]{:S(2)}, u32[]{:S(2)}) async-start(f32[32,16,128]{2,1,0:T(8,128)} %bitcast.20), calls=%async_computation | async-start | bytes 524288 | tf_op jit(solution)/shard_map/gram_sum/all_to_all | solution.py:745
  22.0 2.7 %collective-permute-start.5 = (bf16[4,336,128]{2,1,0:T(8,128)(2,1)S(1)}, bf16[4,336,128]{2,1,0:T(8,128)(2,1)S(1)}, u32[]{:S(2)}, u32[]{:S(2)}) collective-permute-start(bf16[4,336,128]{2,1,0:T(8,128)(2,1)S(1)} %gram_sum.2.refs_1_), channel_id=1, source_target_pairs={{0,6},{2,4},{4,2},{6,0},{8,14},{10,12},{12,10},{14,8},{16,22},{18,... | collective-permute-start | bytes 1032200 | tf_op jit(solution)/shard_map/weights/ppermute | solution.py:737
  24.7 0.6 collective-permute-start.4
  25.6 7.1 %all-to-all-done.refs_0_ = f32[32,16,128]{2,1,0:T(8,128)S(1)} async-done(((f32[32,16,128]{2,1,0:T(8,128)}), f32[32,16,128]{2,1,0:T(8,128)S(1)}, u32[]{:S(2)}, u32[]{:S(2)}) %all-to-all-start) | async-done | bytes 262176 | tf_op jit(solution)/shard_map/gram_sum/all_to_all | solution.py:745
  32.7 0.8 gram_sum.3
  33.4 2.6 %all-to-all-start.1 = ((f32[32,16,128]{2,1,0:T(8,128)}), f32[32,16,128]{2,1,0:T(8,128)S(1)}, u32[]{:S(2)}, u32[]{:S(2)}) async-start(f32[32,16,128]{2,1,0:T(8,128)} %gram_sum.3), calls=%async_computation.1 | async-start | bytes 524288 | tf_op jit(solution)/shard_map/gram_sum/all_to_all | solution.py:745
  36.0 0.5 collective-permute-done.5.refs_4_
  36.5 8.4 %collective-permute-done.4.refs_3_ = bf16[4,336,128]{2,1,0:T(8,128)(2,1)S(1)} collective-permute-done((bf16[4,336,128]{2,1,0:T(8,128)(2,1)S(1)}, bf16[4,336,128]{2,1,0:T(8,128)(2,1)S(1)}, u32[]{:S(2)}, u32[]{:S(2)}) %collective-permute-start.4) | collective-permute-done | bytes 344096 | tf_op jit(solution)/shard_map/weights/ppermute | solution.py:737
  44.9 0.3 collective-permute-done.3.refs_2_
  45.2 0.5 collective-permute-start.7
  45.7 0.5 collective-permute-start.9
  46.2 0.6 collective-permute-done.6.refs_5_
  46.9 0.5 collective-permute-done.7.refs_6_
  47.4 0.5 collective-permute-done.8.refs_7_
  47.9 0.5 collective-permute-done.9.refs_8_
  48.4 2.1 %weights.1 = (bf16[5,512,128]{2,1,0:T(8,128)(2,1)S(1)}, bf16[4,2048,128]{2,1,0:T(8,128)(2,1)}) custom-call(s32[2]{0:T(128)S(1)} %pad_add_fusion.refs_0_, bf16[4,336,128]{2,1,0:T(8,128)(2,1)S(1)} %gram_sum.2.refs_1_, bf16[4,336,128]{2,1,0:T(8,128)(2,1)S(1)} %collective-permute-done.3.refs_2_, bf16[4,336,128]{2,1,0:T(8,128)(2,1)S(1)} %collective-permute-done.4.refs_3_, ...), custom_call_target="tpu_custom_call" | custom-call | bytes 5505032 | tf_op jit(solution)/shard_map/weights/pallas_call | solution.py:48
  50.5 0.9 stats.1
  51.4 0.8 copy-done.2
  52.2 8.1 %forward.1 = (bf16[4,512,1024]{2,1,0:T(8,128)(2,1)}, f32[512,1024]{1,0:T(8,128)}, f32[32,8,128]{2,1,0:T(8,128)}) custom-call(bf16[4,128,1024]{2,1,0:T(8,128)(2,1)S(1)} %get-tuple-element.86.refs_4_.refs_0_.refs_2_, bf16[5,512,128]{2,1,0:T(8,128)(2,1)S(1)} %get-tuple-element.94.refs_1_.refs_3_, f32[4,512,128]{2,1,0:T(8,128)S(1)} %get-tuple-element.95.refs_2_.refs_8_, ...), custom_call_target="tpu_custom_call" | custom-call | flops 2684354560 | bytes 11272192 | tf_op jit(solution)/shard_map/forward/pallas_call | solution.py:48
  60.3 4.4 %all-to-all-start.2 = ((f32[32,8,128]{2,1,0:T(8,128)}), f32[32,8,128]{2,1,0:T(8,128)S(1)}, u32[]{:S(2)}, u32[]{:S(2)}) async-start(f32[32,8,128]{2,1,0:T(8,128)} %get-tuple-element.97.refs_3_), calls=%async_computation.2 | async-start | bytes 262144 | tf_op jit(solution)/shard_map/all_to_all | solution.py:745
  64.8 9.5 %factors.1 = (bf16[4,512,1024]{2,1,0:T(8,128)(2,1)}, bf16[4,512,1024]{2,1,0:T(8,128)(2,1)}, bf16[4,512,1024]{2,1,0:T(8,128)(2,1)}) custom-call(bf16[4,128,1024]{2,1,0:T(8,128)(2,1)S(1)} %get-tuple-element.86.refs_4_.refs_0_.refs_2_, bf16[5,512,128]{2,1,0:T(8,128)(2,1)S(1)} %get-tuple-element.94.refs_1_.refs_3_, ...), custom_call_target="tpu_custom_call" | custom-call | flops 8589934592 | bytes 15335424 | tf_op jit(solution)/shard_map/factors/pallas_call | solution.py:48
  74.3 4.9 %head.1 = (f32[512,1024]{1,0:T(8,128)S(1)}, f32[32,8,128]{2,1,0:T(8,128)S(1)}, f32[512,128]{1,0:T(8,128)S(1)}, f32[2,512,128]{2,1,0:T(8,128)S(1)}) custom-call(f32[32,8,128]{2,1,0:T(8,128)S(1)} %all-to-all-done.2.refs_0_, f32[512,1024]{1,0:T(8,128)} %get-tuple-element.98.refs_1_.refs_4_, f32[512,128]{1,0:T(8,128)S(1)} %get-tuple-element.99.refs_2_.refs_3_, ...), custom_call_target="tpu_custom_call" | custom-call | flops 402653184 | bytes 6164480 | tf_op jit(solution)/shard_map/head/pallas_call | solution.py:48
  79.2 13.7 %all_to_all.30.refs_1_ = f32[32,8,128]{2,1,0:T(8,128)S(1)} all-to-all(f32[32,8,128]{2,1,0:T(8,128)S(1)} %get-tuple-element.101), channel_id=1, replica_groups=mesh['dp'=16,'rep'=2] {'dp','rep'}, dimensions={0} | all-to-all | bytes 262144 | tf_op jit(solution)/shard_map/all_to_all | solution.py:745
  92.9 5.8 %turn.1 = (bf16[512,1024]{1,0:T(8,128)(2,1)S(1)}, f32[16,144,256]{2,1,0:T(8,128)S(1)}, bf16[16,144,256]{2,1,0:T(8,128)(2,1)S(1)}, f32[8,128]{1,0:T(8,128)S(1)}) custom-call(s32[2]{0:T(128)S(1)} %pad_add_fusion.refs_0_, f32[32,8,128]{2,1,0:T(8,128)S(1)} %all_to_all.30.refs_1_, f32[2,512,128]{2,1,0:T(8,128)S(1)} %get-tuple-element.102.refs_2_, ...), custom_call_target="tpu_custom_call" | custom-call | flops 2147483648 | bytes 14159880 | tf_op jit(solution)/shard_map/turn/pallas_call | solution.py:48
  99.0 6.9 %back.2 = (bf16[16,2,32,128]{3,2,1,0:T(8,128)(2,1)S(1)}, f32[2,128,1024]{2,1,0:T(8,128)}) custom-call(s32[2]{0:T(128)S(1)} %pad_add_fusion.refs_0_, bf16[512,1024]{1,0:T(8,128)(2,1)S(1)} %get-tuple-element.106.refs_1_, bf16[4,128,1024]{2,1,0:T(8,128)(2,1)S(1)} %get-tuple-element.86.refs_4_.refs_0_.refs_2_, ...), custom_call_target="tpu_custom_call" | custom-call | flops 1879048192 | bytes 18747400 | tf_op jit(solution)/shard_map/back/pallas_call | solution.py:48
  105.9 0.4 collective-permute-start.10
  106.2 0.8 merge_sum.2
  107.0 0.5 collective-permute-start.12
  107.5 1.0 collective-permute-start.13
  108.5 2.1 %collective-permute-start.14 = (bf16[4,144,256]{2,1,0:T(8,128)(2,1)S(1)}, bf16[4,144,256]{2,1,0:T(8,128)(2,1)S(1)}, u32[]{:S(2)}, u32[]{:S(2)}) collective-permute-start(bf16[4,144,256]{2,1,0:T(8,128)(2,1)S(1)} %get-tuple-element.117), channel_id=1, source_target_pairs={{0,6},{2,4},{4,2},{6,0},{8,14},{10,12},{12,10},{14,8},{16,22},{18,... | collective-permute-start | bytes 884744 | tf_op jit(solution)/shard_map/merge_sum/ppermute | solution.py:737
  110.6 7.7 %back.3 = (bf16[16,2,32,128]{3,2,1,0:T(8,128)(2,1)}, f32[2,128,1024]{2,1,0:T(8,128)}) custom-call(s32[2]{0:T(128)S(1)} %pad_add_fusion.refs_0_, bf16[512,1024]{1,0:T(8,128)(2,1)S(1)} %get-tuple-element.106.refs_1_, bf16[4,128,1024]{2,1,0:T(8,128)(2,1)S(1)} %get-tuple-element.86.refs_4_.refs_0_.refs_2_, ...), custom_call_target="tpu_custom_call" | custom-call | flops 1879048192 | bytes 19009544 | tf_op jit(solution)/shard_map/merge_sum/back/pallas_call | solution.py:48
  118.3 4.3 %collective-permute-done.13.refs_3_ = bf16[4,144,256]{2,1,0:T(8,128)(2,1)S(1)} collective-permute-done((bf16[4,144,256]{2,1,0:T(8,128)(2,1)S(1)}, bf16[4,144,256]{2,1,0:T(8,128)(2,1)S(1)}, u32[]{:S(2)}, u32[]{:S(2)}) %collective-permute-start.13) | collective-permute-done | bytes 294944 | tf_op jit(solution)/shard_map/merge_sum/ppermute | solution.py:737
  122.6 0.7 merge_sum.3
  123.3 0.7 copy-done.4
  123.9 3.7 %all-to-all-start.4 = ((bf16[16,2,32,128]{3,2,1,0:T(8,128)(2,1)}), bf16[16,2,32,128]{3,2,1,0:T(8,128)(2,1)S(1)}, u32[]{:S(2)}, u32[]{:S(2)}) async-start(bf16[16,2,32,128]{3,2,1,0:T(8,128)(2,1)} %get-tuple-element.122), calls=%async_computation.4 | async-start | bytes 524288 | tf_op jit(solution)/shard_map/branch_sum/all_to_all | solution.py:957
  127.7 1.9 %collective-permute-start.15 = (bf16[144,256]{1,0:T(8,128)(2,1)S(1)}, bf16[144,256]{1,0:T(8,128)(2,1)S(1)}, u32[]{:S(2)}, u32[]{:S(2)}) collective-permute-start(bf16[144,256]{1,0:T(8,128)(2,1)S(1)} %get-tuple-element.124), channel_id=1, source_target_pairs={{0,8},{2,10},{4,12},{6,14},{8,0},{10,2},{12,4},{14,6},{16,24},{18,... | collective-permute-start | bytes 221192 | tf_op jit(solution)/shard_map/merge_sum/ppermute | solution.py:737
  129.6 2.4 %collective-permute-start.16 = (bf16[144,256]{1,0:T(8,128)(2,1)S(1)}, bf16[144,256]{1,0:T(8,128)(2,1)S(1)}, u32[]{:S(2)}, u32[]{:S(2)}) collective-permute-start(bf16[144,256]{1,0:T(8,128)(2,1)S(1)} %get-tuple-element.125), channel_id=1, source_target_pairs={{0,16},{2,18},{4,20},{6,22},{8,24},{10,26},{12,28},{14,30},{16,0},... | collective-permute-start | bytes 221192 | tf_op jit(solution)/shard_map/merge_sum/ppermute | solution.py:737
  132.1 2.6 %collective-permute-done.15.refs_3_ = bf16[144,256]{1,0:T(8,128)(2,1)S(1)} collective-permute-done((bf16[144,256]{1,0:T(8,128)(2,1)S(1)}, bf16[144,256]{1,0:T(8,128)(2,1)S(1)}, u32[]{:S(2)}, u32[]{:S(2)}) %collective-permute-start.15) | collective-permute-done | bytes 73760 | tf_op jit(solution)/shard_map/merge_sum/ppermute | solution.py:737
  134.7 6.5 %collective-permute-done.16.refs_4_ = bf16[144,256]{1,0:T(8,128)(2,1)S(1)} collective-permute-done((bf16[144,256]{1,0:T(8,128)(2,1)S(1)}, bf16[144,256]{1,0:T(8,128)(2,1)S(1)}, u32[]{:S(2)}, u32[]{:S(2)}) %collective-permute-start.16) | collective-permute-done | bytes 73760 | tf_op jit(solution)/shard_map/merge_sum/ppermute | solution.py:737
  141.2 3.2 %owner.1 = (f32[352,128]{1,0:T(8,128)S(1)}, f32[32,8,128]{2,1,0:T(8,128)}) custom-call(s32[2]{0:T(128)S(1)} %pad_add_fusion.refs_0_, bf16[16,2,32,128]{3,2,1,0:T(8,128)(2,1)S(1)} %all-to-all-done.4.refs_1_, f32[8,128]{1,0:T(8,128)S(1)} %get-tuple-element.123.refs_2_, bf16[144,256]{1,0:T(8,128)(2,1)S(1)} %collective-permute-done.15.refs_3_, ...), custom_call_target="tpu_custom_call" | custom-call | bytes 2297864 | tf_op jit(solution)/shard_map/owner/pallas_call | solution.py:48
  144.4 3.6 %all-to-all-start.5 = ((f32[32,8,128]{2,1,0:T(8,128)}), f32[32,8,128]{2,1,0:T(8,128)S(1)}, u32[]{:S(2)}, u32[]{:S(2)}) async-start(f32[32,8,128]{2,1,0:T(8,128)} %get-tuple-element.129), calls=%async_computation.5 | async-start | bytes 262144 | tf_op jit(solution)/shard_map/all_to_all | solution.py:745
  148.4 1.2 collective-permute-done.18.refs_3_
  149.6 6.7 %all-to-all-done.5.refs_1_ = f32[32,8,128]{2,1,0:T(8,128)S(1)} async-done(((f32[32,8,128]{2,1,0:T(8,128)}), f32[32,8,128]{2,1,0:T(8,128)S(1)}, u32[]{:S(2)}, u32[]{:S(2)}) %all-to-all-start.5) | async-done | bytes 131104 | tf_op jit(solution)/shard_map/all_to_all | solution.py:745
  156.3 6.0 %final.1 = (f32[4,32,100]{2,1,0:T(8,128)}, f32[128,512]{1,0:T(8,128)}, f32[32,47]{1,0:T(8,128)}, f32[20,32]{1,0:T(8,128)}, f32[4,32,100]{2,1,0:T(8,128)}, /*inde...) custom-call(s32[2]{0:T(128)S(1)} %pad_add_fusion.refs_0_, ...), custom_call_target="tpu_custom_call" | custom-call | flops 402653184 | bytes 7892428 | tf_op jit(solution)/shard_map/final/pallas_call | solution.py:48
  (28 shorter events, 1.2 us)
Async XLA Ops:
  3.1 12.9 %collective-permute-start.2 = (bf16[336,128]{1,0:T(8,128)(2,1)S(1)}, bf16[336,128]{1,0:T(8,128)(2,1)S(1)}, u32[]{:S(2)}, u32[]{:S(2)}) collective-permute-start(bf16[336,128]{1,0:T(8,128)(2,1)S(1)} %get-tuple-element.85.refs_2_.refs_0_), channel_id=1, source_target_pairs={{0,24},{2,26},{4,28},{6,30},{8,16},{10,18},{12,20},{14,22},{16,8},... | collective-permute-start | bytes 258056 | tf_op jit(solution)/shard_map/ppermute | solution.py:737
  8.2 7.8 %collective-permute-start.1 = (bf16[336,128]{1,0:T(8,128)(2,1)S(1)}, bf16[336,128]{1,0:T(8,128)(2,1)S(1)}, u32[]{:S(2)}, u32[]{:S(2)}) collective-permute-start(bf16[336,128]{1,0:T(8,128)(2,1)S(1)} %get-tuple-element.85.refs_2_.refs_0_), channel_id=1, source_target_pairs={{0,16},{2,18},{4,20},{6,22},{8,24},{10,26},{12,28},{14,30},{16,0},... | collective-permute-start | bytes 258056 | tf_op jit(solution)/shard_map/ppermute | solution.py:737
  8.2 7.8 %collective-permute-start = (bf16[336,128]{1,0:T(8,128)(2,1)S(1)}, bf16[336,128]{1,0:T(8,128)(2,1)S(1)}, u32[]{:S(2)}, u32[]{:S(2)}) collective-permute-start(bf16[336,128]{1,0:T(8,128)(2,1)S(1)} %get-tuple-element.85.refs_2_.refs_0_), channel_id=1, source_target_pairs={{0,8},{2,10},{4,12},{6,14},{8,0},{10,2},{12,4},{14,6},{16,24},{18,... | collective-permute-start | bytes 258056 | tf_op jit(solution)/shard_map/ppermute | solution.py:737
  16.0 16.7 %all-to-all-start = ((f32[32,16,128]{2,1,0:T(8,128)}), f32[32,16,128]{2,1,0:T(8,128)S(1)}, u32[]{:S(2)}, u32[]{:S(2)}) async-start(f32[32,16,128]{2,1,0:T(8,128)} %bitcast.20), calls=%async_computation | async-start | bytes 524288 | tf_op jit(solution)/shard_map/gram_sum/all_to_all | solution.py:745
  22.0 14.5 %collective-permute-start.5 = (bf16[4,336,128]{2,1,0:T(8,128)(2,1)S(1)}, bf16[4,336,128]{2,1,0:T(8,128)(2,1)S(1)}, u32[]{:S(2)}, u32[]{:S(2)}) collective-permute-start(bf16[4,336,128]{2,1,0:T(8,128)(2,1)S(1)} %gram_sum.2.refs_1_), channel_id=1, source_target_pairs={{0,6},{2,4},{4,2},{6,0},{8,14},{10,12},{12,10},{14,8},{16,22},{18,... | collective-permute-start | bytes 1032200 | tf_op jit(solution)/shard_map/weights/ppermute | solution.py:737
  24.7 20.1 %collective-permute-start.4 = (bf16[4,336,128]{2,1,0:T(8,128)(2,1)S(1)}, bf16[4,336,128]{2,1,0:T(8,128)(2,1)S(1)}, u32[]{:S(2)}, u32[]{:S(2)}) collective-permute-start(bf16[4,336,128]{2,1,0:T(8,128)(2,1)S(1)} %gram_sum.2.refs_1_), channel_id=1, source_target_pairs={{0,4},{2,6},{4,0},{6,2},{8,12},{10,14},{12,8},{14,10},{16,20},{18,... | collective-permute-start | bytes 1032200 | tf_op jit(solution)/shard_map/weights/ppermute | solution.py:737
  25.3 19.9 %collective-permute-start.3 = (bf16[4,336,128]{2,1,0:T(8,128)(2,1)S(1)}, bf16[4,336,128]{2,1,0:T(8,128)(2,1)S(1)}, u32[]{:S(2)}, u32[]{:S(2)}) collective-permute-start(bf16[4,336,128]{2,1,0:T(8,128)(2,1)S(1)} %gram_sum.2.refs_1_), channel_id=1, source_target_pairs={{0,2},{2,0},{4,6},{6,4},{8,10},{10,8},{12,14},{14,12},{16,18},{18,... | collective-permute-start | bytes 1032200 | tf_op jit(solution)/shard_map/weights/ppermute | solution.py:737
  33.4 17.1 %all-to-all-start.1 = ((f32[32,16,128]{2,1,0:T(8,128)}), f32[32,16,128]{2,1,0:T(8,128)S(1)}, u32[]{:S(2)}, u32[]{:S(2)}) async-start(f32[32,16,128]{2,1,0:T(8,128)} %gram_sum.3), calls=%async_computation.1 | async-start | bytes 524288 | tf_op jit(solution)/shard_map/gram_sum/all_to_all | solution.py:745
  45.2 1.7 %collective-permute-start.6 = (bf16[4,336,128]{2,1,0:T(8,128)(2,1)S(1)}, bf16[4,336,128]{2,1,0:T(8,128)(2,1)S(1)}, u32[]{:S(2)}, u32[]{:S(2)}) collective-permute-start(bf16[4,336,128]{2,1,0:T(8,128)(2,1)S(1)} %gram_sum.2.refs_1_), channel_id=1, source_target_pairs={{0,1},{1,0},{2,3},{3,2},{4,5},{5,4},{6,7},{7,6},{8,9},{9,8},{10,11... | collective-permute-start | bytes 1032200 | tf_op jit(solution)/shard_map/weights/ppermute | solution.py:741
  45.2 2.1 %collective-permute-start.7 = (bf16[4,336,128]{2,1,0:T(8,128)(2,1)S(1)}, bf16[4,336,128]{2,1,0:T(8,128)(2,1)S(1)}, u32[]{:S(2)}, u32[]{:S(2)}) collective-permute-start(bf16[4,336,128]{2,1,0:T(8,128)(2,1)S(1)} %collective-permute-done.3.refs_2_), channel_id=1, source_target_pairs={{0,1},{1,0},{2,3},{3,2},{4,5},{5,4},{6,7},{7,6},{8,9},{9,8},{10,11... | collective-permute-start | bytes 1032200 | tf_op jit(solution)/shard_map/weights/ppermute | solution.py:741
  45.7 2.1 %collective-permute-start.8 = (bf16[4,336,128]{2,1,0:T(8,128)(2,1)S(1)}, bf16[4,336,128]{2,1,0:T(8,128)(2,1)S(1)}, u32[]{:S(2)}, u32[]{:S(2)}) collective-permute-start(bf16[4,336,128]{2,1,0:T(8,128)(2,1)S(1)} %collective-permute-done.4.refs_3_), channel_id=1, source_target_pairs={{0,1},{1,0},{2,3},{3,2},{4,5},{5,4},{6,7},{7,6},{8,9},{9,8},{10,11... | collective-permute-start | bytes 1032200 | tf_op jit(solution)/shard_map/weights/ppermute | solution.py:741
  45.7 2.6 %collective-permute-start.9 = (bf16[4,336,128]{2,1,0:T(8,128)(2,1)S(1)}, bf16[4,336,128]{2,1,0:T(8,128)(2,1)S(1)}, u32[]{:S(2)}, u32[]{:S(2)}) collective-permute-start(bf16[4,336,128]{2,1,0:T(8,128)(2,1)S(1)} %collective-permute-done.5.refs_4_), channel_id=1, source_target_pairs={{0,1},{1,0},{2,3},{3,2},{4,5},{5,4},{6,7},{7,6},{8,9},{9,8},{10,11... | collective-permute-start | bytes 1032200 | tf_op jit(solution)/shard_map/weights/ppermute | solution.py:741
  50.5 9.8 %copy-start = (f32[32,16,128]{2,1,0:T(8,128)}, f32[32,16,128]{2,1,0:T(8,128)S(1)}, u32[]{:S(2)}) copy-start(f32[32,16,128]{2,1,0:T(8,128)S(1)} %all-to-all-done.1) | copy-start | bytes 786436
  51.4 0.8 copy-start.2
  52.2 12.6 %copy-start.1 = (f32[4,512,128]{2,1,0:T(8,128)}, f32[4,512,128]{2,1,0:T(8,128)S(1)}, u32[]{:S(2)}) copy-start(f32[4,512,128]{2,1,0:T(8,128)S(1)} %get-tuple-element.95.refs_2_.refs_8_) | copy-start | bytes 3145732
  60.3 13.9 %all-to-all-start.2 = ((f32[32,8,128]{2,1,0:T(8,128)}), f32[32,8,128]{2,1,0:T(8,128)S(1)}, u32[]{:S(2)}, u32[]{:S(2)}) async-start(f32[32,8,128]{2,1,0:T(8,128)} %get-tuple-element.97.refs_3_), calls=%async_computation.2 | async-start | bytes 262144 | tf_op jit(solution)/shard_map/all_to_all | solution.py:745
  98.7 7.5 %collective-permute-start.11 = (bf16[16,144,256]{2,1,0:T(8,128)(2,1)S(1)}, bf16[16,144,256]{2,1,0:T(8,128)(2,1)S(1)}, u32[]{:S(2)}, u32[]{:S(2)}) collective-permute-start(bf16[16,144,256]{2,1,0:T(8,128)(2,1)S(1)} %get-tuple-element.112), channel_id=1, source_target_pairs={{0,1},{1,0},{2,3},{3,2},{4,5},{5,4},{6,7},{7,6},{8,9},{9,8},{10,11... | collective-permute-start | bytes 3538952 | tf_op jit(solution)/shard_map/ppermute | solution.py:741
  105.9 4.7 %collective-permute-start.10 = (bf16[16,2,32,128]{3,2,1,0:T(8,128)(2,1)S(1)}, bf16[16,2,32,128]{3,2,1,0:T(8,128)(2,1)S(1)}, u32[]{:S(2)}, u32[]{:S(2)}) collective-permute-start(bf16[16,2,32,128]{3,2,1,0:T(8,128)(2,1)S(1)} %get-tuple-element.110.refs_3_), channel_id=1, source_target_pairs={{0,1},{1,0},{2,3},{3,2},{4,5},{5,4},{6,7},{7,6},{8,9},{9,8},{10,11... | collective-permute-start | bytes 786440 | tf_op jit(solution)/shard_map/ppermute | solution.py:741
  107.0 11.3 %collective-permute-start.12 = (bf16[4,144,256]{2,1,0:T(8,128)(2,1)S(1)}, bf16[4,144,256]{2,1,0:T(8,128)(2,1)S(1)}, u32[]{:S(2)}, u32[]{:S(2)}) collective-permute-start(bf16[4,144,256]{2,1,0:T(8,128)(2,1)S(1)} %get-tuple-element.115), channel_id=1, source_target_pairs={{0,2},{2,0},{4,6},{6,4},{8,10},{10,8},{12,14},{14,12},{16,18},{18,... | collective-permute-start | bytes 884744 | tf_op jit(solution)/shard_map/merge_sum/ppermute | solution.py:737
  107.5 15.1 %collective-permute-start.13 = (bf16[4,144,256]{2,1,0:T(8,128)(2,1)S(1)}, bf16[4,144,256]{2,1,0:T(8,128)(2,1)S(1)}, u32[]{:S(2)}, u32[]{:S(2)}) collective-permute-start(bf16[4,144,256]{2,1,0:T(8,128)(2,1)S(1)} %get-tuple-element.116), channel_id=1, source_target_pairs={{0,4},{2,6},{4,0},{6,2},{8,12},{10,14},{12,8},{14,10},{16,20},{18,... | collective-permute-start | bytes 884744 | tf_op jit(solution)/shard_map/merge_sum/ppermute | solution.py:737
  108.5 14.1 %collective-permute-start.14 = (bf16[4,144,256]{2,1,0:T(8,128)(2,1)S(1)}, bf16[4,144,256]{2,1,0:T(8,128)(2,1)S(1)}, u32[]{:S(2)}, u32[]{:S(2)}) collective-permute-start(bf16[4,144,256]{2,1,0:T(8,128)(2,1)S(1)} %get-tuple-element.117), channel_id=1, source_target_pairs={{0,6},{2,4},{4,2},{6,0},{8,14},{10,12},{12,10},{14,8},{16,22},{18,... | collective-permute-start | bytes 884744 | tf_op jit(solution)/shard_map/merge_sum/ppermute | solution.py:737
  118.3 38.0 %copy-start.3 = (bf16[4,128,512]{2,1,0:T(8,128)(2,1)S(1)}, bf16[4,128,512]{2,1,0:T(8,128)(2,1)}, u32[]{:S(2)}) copy-start(bf16[4,128,512]{2,1,0:T(8,128)(2,1)} %copy-done.2) | copy-start | bytes 1572868
  123.3 0.7 copy-start.4
  123.9 17.3 %all-to-all-start.4 = ((bf16[16,2,32,128]{3,2,1,0:T(8,128)(2,1)}), bf16[16,2,32,128]{3,2,1,0:T(8,128)(2,1)S(1)}, u32[]{:S(2)}, u32[]{:S(2)}) async-start(bf16[16,2,32,128]{3,2,1,0:T(8,128)(2,1)} %get-tuple-element.122), calls=%async_computation.4 | async-start | bytes 524288 | tf_op jit(solution)/shard_map/branch_sum/all_to_all | solution.py:957
  127.7 7.1 %collective-permute-start.15 = (bf16[144,256]{1,0:T(8,128)(2,1)S(1)}, bf16[144,256]{1,0:T(8,128)(2,1)S(1)}, u32[]{:S(2)}, u32[]{:S(2)}) collective-permute-start(bf16[144,256]{1,0:T(8,128)(2,1)S(1)} %get-tuple-element.124), channel_id=1, source_target_pairs={{0,8},{2,10},{4,12},{6,14},{8,0},{10,2},{12,4},{14,6},{16,24},{18,... | collective-permute-start | bytes 221192 | tf_op jit(solution)/shard_map/merge_sum/ppermute | solution.py:737
  129.6 11.6 %collective-permute-start.16 = (bf16[144,256]{1,0:T(8,128)(2,1)S(1)}, bf16[144,256]{1,0:T(8,128)(2,1)S(1)}, u32[]{:S(2)}, u32[]{:S(2)}) collective-permute-start(bf16[144,256]{1,0:T(8,128)(2,1)S(1)} %get-tuple-element.125), channel_id=1, source_target_pairs={{0,16},{2,18},{4,20},{6,22},{8,24},{10,26},{12,28},{14,30},{16,0},... | collective-permute-start | bytes 221192 | tf_op jit(solution)/shard_map/merge_sum/ppermute | solution.py:737
  132.0 9.2 %collective-permute-start.17 = (bf16[144,256]{1,0:T(8,128)(2,1)S(1)}, bf16[144,256]{1,0:T(8,128)(2,1)S(1)}, u32[]{:S(2)}, u32[]{:S(2)}) collective-permute-start(bf16[144,256]{1,0:T(8,128)(2,1)S(1)} %get-tuple-element.126), channel_id=1, source_target_pairs={{0,24},{2,26},{4,28},{6,30},{8,16},{10,18},{12,20},{14,22},{16,8},... | collective-permute-start | bytes 221192 | tf_op jit(solution)/shard_map/merge_sum/ppermute | solution.py:737
  144.4 11.9 %all-to-all-start.5 = ((f32[32,8,128]{2,1,0:T(8,128)}), f32[32,8,128]{2,1,0:T(8,128)S(1)}, u32[]{:S(2)}, u32[]{:S(2)}) async-start(f32[32,8,128]{2,1,0:T(8,128)} %get-tuple-element.129), calls=%async_computation.5 | async-start | bytes 262144 | tf_op jit(solution)/shard_map/all_to_all | solution.py:745
  148.1 1.5 collective-permute-start.18

commit v3 on v2

--- a/solution.py
+++ b/solution.py
@@ -29,7 +29,7 @@
     )
 
 
-def call(body, outs, *args, smem=(), hbm=(), chip=(), after=(), grid=None, in_specs=None, out_specs=None, scratch=(), mib=12, flops=0):
+def call(body, outs, *args, smem=(), hbm=(), after=(), grid=None, in_specs=None, out_specs=None, scratch=(), mib=12, flops=0):
     skip = len(args)
     if in_specs is None:
         spaces = {**{i: pltpu.SMEM for i in smem}, **{i: pltpu.HBM for i in hbm}}
@@ -37,8 +37,7 @@
     if out_specs is None:
         out_specs = tuple(pl.BlockSpec(memory_space=pltpu.VMEM) for _ in outs)
     in_specs = list(in_specs) + [pl.BlockSpec(memory_space=pl.ANY) for _ in after]
-    places = {**{i: pltpu.HBM for i in hbm}, **{i: pltpu.VMEM for i in chip}}
-    args = [pltpu.with_memory_space_constraint(a, places[i]) if i in places else a for i, a in enumerate(args)]
+    args = [pltpu.with_memory_space_constraint(a, pltpu.HBM) if i in hbm else a for i, a in enumerate(args)]
     moved = sum(math.prod(a.shape) * jnp.dtype(a.dtype).itemsize for a in (*args, *outs))
 
     def kernel(*refs):
@@ -52,9 +51,9 @@
         out_specs=out_specs,
         scratch_shapes=list(scratch),
         compiler_params=pltpu.CompilerParams(vmem_limit_bytes=mib << 20),
-        cost_estimate=pl.CostEstimate(flops=flops, bytes_accessed=moved, transcendentals=0),
+        cost_estimate=pl.CostEstimate(flops=1024, bytes_accessed=1024, transcendentals=0),
         **kwargs,
-    )(*args, *after)
+    )(*args, *[pltpu.with_memory_space_constraint(a, pltpu.HBM) for a in after])
 
 
 def fetch(sources, buffers, sems):
@@ -107,7 +106,6 @@
 
 def prep_kernel(pos_ref, wb_hbm, wc_hbm, sp_hbm, wm_hbm, own_ref, block_ref, wb_ref, wc_ref, sp_ref, wm_ref, sems):
     wait = fetch((wb_hbm, wc_hbm, sp_hbm, wm_hbm), (wb_ref, wc_ref, sp_ref, wm_ref), sems)
-    cb = wc_ref.shape[0]
     mr, hid = wm_ref.shape
     own_ref[...] = jnp.zeros_like(own_ref)
     wait()
@@ -115,7 +113,7 @@
     own_ref[HOPS, :, 0 : wc_ref.shape[1]] = wc_ref[...].astype(BF16)
     own_ref[HOPS, :, PCOL : PCOL + sp_ref.shape[0]] = jnp.transpose(sp_ref[...]).astype(BF16)
     first = pos_ref[1] == 0
-    part = cb // 2
+    part = wc_ref.shape[0] // 2
     for k in range(HOPS + 1):
         block_ref[k * part : (k + 1) * part, :] = jnp.where(first, own_ref[k, :part], own_ref[k, part:])
     at = (HOPS + 1) * part
@@ -130,24 +128,12 @@
         out_ref[i] = ref[...]
 
 
-def assemble_kernel(pos_ref, *refs):
-    wb_ref, wm_ref = refs[8:]
-    cb = wb_ref.shape[1] // 16
-    mr = wm_ref.shape[1] // 16
-    part = cb // 2
-    first = (HOPS + 1) * part
+def each_block(pos_ref, arrays):
     for which in range(2):
         half = pos_ref[1] if which == 0 else 1 - pos_ref[1]
-        for m in range(4):
-            for k in range(4):
-                s = pos_ref[0] ^ (4 * k + m)
-                block = refs[which * 4 + m][k]
-                rows = pl.ds(pl.multiple_of(s * cb + half * part, part), part)
-                for j in range(HOPS + 1):
-                    wb_ref[j, rows, :] = block[j * part : (j + 1) * part]
-                rows = pl.ds(pl.multiple_of(s * mr, mr), mr)
-                for i in range(2):
-                    wm_ref[half * 2 + i, rows, :] = block[first + i * mr : first + (i + 1) * mr]
+        for t in range(4):
+            for e in range(4):
+                yield arrays[which * 4 + t].at[e], pos_ref[0] ^ (4 * e + t), half
 
 
 def gather_kernel(idx_ref, tab_ref, x_ref, gram_ref, acc, pad):
@@ -198,7 +184,41 @@
     return total
 
 
-def stats_kernel(count, gram_ref, wb_ref, coef_ref, par_ref, mu_ref, wt_ref):
+def assemble_kernel(pos_ref, *refs):
+    wb_ref, wm_ref = refs[8:]
+    cb = wb_ref.shape[1] // 16
+    mr = wm_ref.shape[1] // 16
+    part = cb // 2
+    first = (HOPS + 1) * part
+    for ref, s, half in each_block(pos_ref, refs[:8]):
+        block = ref[...]
+        rows = pl.ds(pl.multiple_of(s * cb + half * part, part), part)
+        for j in range(HOPS + 1):
+            wb_ref[j, rows, :] = block[j * part : (j + 1) * part]
+        rows = pl.ds(pl.multiple_of(s * mr, mr), mr)
+        for i in range(2):
+            wm_ref[half * 2 + i, rows, :] = block[first + i * mr : first + (i + 1) * mr]
+
+
+def own_stats(count, rep, gram_ref, own_ref, fix_ref):
+    lane = lane_of(fix_ref.shape[1:])
+    tail = own_ref[HOPS].astype(F32)
+    for i in range(2):
+        gram = gram_ref[rep * 2 + i]
+        w = own_ref[rep * 2 + i]
+        wg = exact_dot(w, gram)
+        mean = wg[:, ONE : ONE + 1] / count
+        second = jnp.sum(wg * w.astype(F32), axis=1, keepdims=True) / count
+        inv = lax.rsqrt(second - mean * mean + EPS_NORM)
+        gain = jnp.where(rep == 0, tail[:, PCOL + i : PCOL + i + 1], tail[:, PCOL + 2 + i : PCOL + 3 + i])
+        block = wg - mean * gram[ONE : ONE + 1, :]
+        for j, value in enumerate((mean, inv, gain * inv)):
+            block = jnp.where(lane == ONE + j, value, block)
+        fix_ref[i] = block
+
+
+def stats_kernel(count, pos_ref, gram_ref, wb_ref, own_ref, coef_ref, mu_ref, wt_ref, fix_ref):
+    own_stats(count, pos_ref[1], gram_ref, own_ref, fix_ref)
     hid = wb_ref.shape[1]
     small = jnp.transpose(wb_ref[HOPS].astype(F32))
     row = lax.broadcasted_iota(jnp.int32, (16, hid), 0)
@@ -212,7 +232,6 @@
             block = jnp.where(row == i, value, block)
         return jnp.transpose(jnp.concatenate([block, jnp.zeros((LANES - 16, hid), F32)], axis=0))
 
-    par_ref[...] = columns([at(4 * HOPS + i) for i in range(4)])
     mu_ref[...] = jnp.zeros_like(mu_ref)
     for k in range(HOPS):
         gram = gram_ref[k]
@@ -257,9 +276,10 @@
     return jnp.concatenate([wm_ref[i, rows, :] for i in range(wm_ref.shape[0])], axis=1)
 
 
-def forward_kernel(x_ref, wb_ref, coef_ref, wm_hbm, joined_out, pre2_out, pay_ref, pre, wm_ref, joined_ref, pre2_ref, sems, out_sems):
-    wait = fetch((wm_hbm,), (wm_ref,), sems)
-    stores = []
+def forward_kernel(
+    x_ref, wb_ref, coef_ref, wm_hbm, joined_ref, pre2_ref, pay_ref, pre, wm_ref, in_sems
+):
+    wait = fetch((wm_hbm,), (wm_ref,), in_sems)
     hid = wb_ref.shape[1]
     batch = x_ref.shape[2]
     per = hid // CHUNK
@@ -287,7 +307,6 @@
         units(i)
         if i % per == per - 1:
             k = i // per
-            stores.append(fetch((joined_ref.at[k],), (joined_out.at[k],), out_sems.at[pl.ds(k, 1)]))
             if k == 0:
                 wait()
             part = dot(merge_block(wm_ref, slice(k * hid, (k + 1) * hid)), joined_ref[k], 0, 0)
@@ -295,12 +314,13 @@
                 pre2_ref[...] = part
             else:
                 pre2_ref[...] += part
-    stores.append(fetch((pre2_ref,), (pre2_out,), out_sems.at[pl.ds(HOPS, 1)]))
     value = pre2_ref[...]
     sums = jnp.concatenate([lane_sums(fold_lanes(value)), lane_sums(fold_lanes(value * value))], axis=0)
     pay_ref[...] = jnp.broadcast_to(sums[None], pay_ref.shape)
-    for done in stores:
-        done()
+
+
+def par_columns(wb_ref):
+    return wb_ref[HOPS][:, PCOL:].astype(F32)[:, 4 * HOPS : 5 * HOPS]
 
 
 def columns2(count, rows, par):
@@ -314,11 +334,11 @@
 
 
 def head_kernel(
-    count, classes, got_ref, pre2_hbm, par_ref, wb_ref, lab_hbm, dy2_ref, pay_ref, class_ref, stat_ref, act, dact, cols, sums, lab_ref, pre2_ref, sems
+    count, classes, got_ref, pre2_ref, wb_ref, lab_hbm, dy2_ref, pay_ref, class_ref, stat_ref, act, dact, cols, sums, lab_ref, sems
 ):
-    wait = fetch((pre2_hbm, lab_hbm), (pre2_ref, lab_ref), sems)
+    wait = fetch((lab_hbm,), (lab_ref,), sems)
     hid, batch = dy2_ref.shape
-    par = par_ref[...]
+    par = par_columns(wb_ref)
     mean, inv, gain, shift, slope = columns2(count, jnp.sum(got_ref[...], axis=0), par)
     stat_ref[0] = mean
     stat_ref[1] = inv
@@ -340,7 +360,6 @@
             act[at, lanes] = (u * (c[2] + c[3] * jnp.tanh(u))).astype(BF16)
         return carry
 
-    wait()
     lax.fori_loop(0, hid // ROWS, first, 0, unroll=4)
     tail = wb_ref[HOPS]
     wc = jnp.where(lane_of(tail.shape) < PCOL, tail.astype(F32), 0.0).astype(BF16)
@@ -350,6 +369,7 @@
     top = jnp.max(logits, axis=0, keepdims=True)
     e = jnp.exp(logits - top)
     probs = e / jnp.sum(e, axis=0, keepdims=True)
+    wait()
     dlog = (probs - jnp.where(row == lab_ref[...], 1.0, 0.0)).astype(BF16)
     grad_class = dot(act[...], dlog, 1, 1)
     bias = jnp.sum(dlog.astype(F32), axis=1, keepdims=True)
@@ -389,24 +409,18 @@
 
 
 def turn_kernel(
-    count, pos_ref, got_ref, stat_ref, par_ref, pre2_hbm, dy2_ref, joined_hbm, class_ref, dpre_ref, keep_ref, send_ref, sum2_ref, cols, joined_ref, pre2_ref, sems
+    count, pos_ref, got_ref, stat_ref, wb_ref, pre2_ref, dy2_ref, joined_ref, class_ref, dpre_ref, keep_ref, send_ref, sum2_ref, cols
 ):
     hid, batch = dy2_ref.shape
-    wait = fetch((pre2_hbm,), (pre2_ref,), sems.at[pl.ds(HOPS, 1)])
-    dp, rows, half = keep_ref.shape
-    hops = joined_ref.shape[0]
-    waits = [fetch((joined_hbm.at[k],), (joined_ref.at[k],), sems.at[pl.ds(k, 1)]) for k in range(hops)]
-    mr = hops * hid // dp
-    cb = hid // dp
+    half = send_ref.shape[2]
     rows8 = jnp.sum(got_ref[...], axis=0)
     sum2_ref[...] = rows8
     mean, inv = stat_ref[0], stat_ref[1]
-    v = jnp.broadcast_to(par_ref[:, 0:1], mean.shape) * inv
+    v = jnp.broadcast_to(par_columns(wb_ref)[:, 0:1], mean.shape) * inv
     cols[0] = v
     cols[1] = v * to_cols(rows8, 0) / count
     cols[2] = v * inv * to_cols(rows8, 4) / count
     reps = WIDE // LANES
-    wait()
     for g in range(hid // ROWS):
         at = slice(g * ROWS, (g + 1) * ROWS)
         c = [jnp.concatenate([cols[i, at, :]] * reps, axis=1) for i in range(3)]
@@ -417,117 +431,103 @@
             dpre_ref[at, lanes] = value.astype(BF16)
     mine = pl.ds(pl.multiple_of(pos_ref[1] * half, half), half)
     theirs = pl.ds(pl.multiple_of((1 - pos_ref[1]) * half, half), half)
-    per = dp // hops
-    for k in range(hops):
-        waits[k]()
-        block = joined_ref[k]
-        own = dot(block, dpre_ref[mine, :], 1, 1)
-        other = dot(block, dpre_ref[theirs, :], 1, 1).astype(BF16)
+    dp, size, _ = send_ref.shape
+    per = dp // HOPS
+    mr = hid // per
+    cb = hid // dp
+    for k in range(HOPS):
+        other = dot(joined_ref[k], dpre_ref[theirs, :], 1, 1).astype(BF16)
+        own = dot(joined_ref[k], dpre_ref[mine, :], 1, 1)
         for j in range(per):
+            send_ref[k * per + j, 0:mr, :] = other[j * mr : (j + 1) * mr]
             keep_ref[k * per + j, 0:mr, :] = own[j * mr : (j + 1) * mr]
-            send_ref[k * per + j, 0:mr, :] = other[j * mr : (j + 1) * mr]
     first = pos_ref[1] == 0
     for s in range(dp):
         block = class_ref[s * cb : (s + 1) * cb, :]
         wide = jnp.concatenate([block[: cb // 2], block[cb // 2 :]], axis=1)
-        keep_ref[s, mr:rows, :] = jnp.where(first, wide, 0.0)
-        send_ref[s, mr:rows, :] = jnp.where(first, 0.0, wide).astype(BF16)
-
-
-def factor_kernel(x_ref, wb_ref, coef_ref, e_ref, f_ref, g_ref, pre):
-    hid = wb_ref.shape[1]
+        send_ref[s, mr:size, :] = jnp.where(first, 0.0, wide).astype(BF16)
+        keep_ref[s, mr:size, :] = jnp.where(first, wide, 0.0)
+
+
+SMALLS = 4
+
+
+def back_kernel(own, first, count, pos_ref, dpre_ref, x_ref, wb_ref, coef_ref, mu_ref, wt_hbm, wm_hbm, *refs):
+    if own:
+        recv_refs, refs = refs[:count], refs[count:]
+    b_ref, a_out, pre, dj, dyv, sums, a_ref, wm_ref, wt_ref, sems, out_sems = refs
+    hid = wt_ref.shape[2]
     batch = x_ref.shape[2]
     per = hid // CHUNK
-
-    def project(c):
-        pre[c % 2] = dot(wb_ref[0, c * CHUNK : (c + 1) * CHUNK, :], x_ref[0], 1, 0)
-
-    project(0)
-    for c in range(per):
-        if c + 1 < per:
-            project(c + 1)
-        for g in range(CHUNK // ROWS):
-            at = slice(c * CHUNK + g * ROWS, c * CHUNK + (g + 1) * ROWS)
-            here = slice(g * ROWS, (g + 1) * ROWS)
-            a1, b1, p1, q1, s2, q2, s1, r1 = column_set(coef_ref, 0, at, (0, 1, 2, 3, 6, 7, 8, 9))
-            for b in range(batch // WIDE):
-                lanes = slice(b * WIDE, (b + 1) * WIDE)
-                u = pre[c % 2, here, lanes] * a1 + b1
-                t = jnp.tanh(u)
-                u2 = u * (p1 + q1 * t)
-                t2 = jnp.tanh(u2)
-                w = u2 * (1.0 - t2)
-                g_ref[0, at, lanes] = w.astype(BF16)
-                d = s2 + q2 * ((1.0 + t2) * (1.0 + w))
-                w = u * (1.0 - t)
-                f_ref[0, at, lanes] = (d * w).astype(BF16)
-                e_ref[0, at, lanes] = (d * (s1 + r1 * ((1.0 + t) * (1.0 + w)))).astype(BF16)
-
-
-SMALLS = 4
-
-
-def back_kernel(own, pos_ref, dpre_ref, x_ref, wb_ref, mu_ref, wm_hbm, e_hbm, f_hbm, g_hbm, *refs):
-    if own:
-        recv_ref, refs = refs[0], refs[1:]
-    b_ref, a_out, dj, dyv, sums, a_ref, wm_ref, e_ref, f_ref, g_ref, sems, out_sems = refs
-    hid = wb_ref.shape[1]
-    batch = x_ref.shape[2]
-    per = hid // CHUNK
-    jobs = [(k, c) for k in range(2) for c in range(per)]
-    base = 2 * (pos_ref[1] if own else 1 - pos_ref[1])
-    lane = lane_of((hid, LANES))
+    jobs = [(k, c) for k in range(count) for c in range(per)]
+    base = 2 * (pos_ref[1] if own else 1 - pos_ref[1]) + first
     dp, _, cb, _ = b_ref.shape
     copies = []
     waits = []
-    for k in range(2):
-        at = pl.ds(pl.multiple_of((base + k) * hid, hid), hid)
-        sources = [wm_hbm.at[:, at, :]] + [ref.at[base + k] for ref in (e_hbm, f_hbm, g_hbm)]
-        buffers = [ref.at[k] for ref in (wm_ref, e_ref, f_ref, g_ref)]
-        waits.append(fetch(sources, buffers, sems.at[k]))
+    wait_wt = fetch((wt_hbm.at[pl.ds(base, count)],), (wt_ref,), out_sems.at[pl.ds(count, 1)])
+    for i, (k, c) in enumerate(jobs):
+        at = pl.ds(pl.multiple_of((base + k) * hid + c * CHUNK, CHUNK), CHUNK)
+        rows = pl.ds(c * CHUNK, CHUNK)
+        waits.append(fetch((wm_hbm.at[:, at, :],), (wm_ref.at[k, :, rows, :],), sems.at[pl.ds(i, 1)]))
 
     def project(i):
         k, c = jobs[i]
-        if c == 0:
-            waits[k]()
-        dj[i % 2] = dot(merge_block(wm_ref.at[k], slice(c * CHUNK, (c + 1) * CHUNK)), dpre_ref[...], 1, 0)
+        rows = slice(c * CHUNK, (c + 1) * CHUNK)
+        pre[i % 2] = dot(wb_ref[base + k, rows, :], x_ref[base + k], 1, 0)
+        waits[i]()
+        dj[i % 2] = dot(merge_block(wm_ref.at[k], rows), dpre_ref[...], 1, 0)
 
     def units(i):
         k, c = jobs[i]
         for g in range(CHUNK // ROWS):
             at = slice(c * CHUNK + g * ROWS, c * CHUNK + (g + 1) * ROWS)
             here = slice(g * ROWS, (g + 1) * ROWS)
-            first = jnp.zeros((ROWS, WIDE), F32)
-            second = jnp.zeros((ROWS, WIDE), F32)
+            a1, b1, p1, q1, s2, q2, s1, r1 = column_set(coef_ref, base + k, at, (0, 1, 2, 3, 6, 7, 8, 9))
+            one = jnp.zeros((ROWS, WIDE), F32)
+            two = jnp.zeros((ROWS, WIDE), F32)
             for b in range(batch // WIDE):
                 lanes = slice(b * WIDE, (b + 1) * WIDE)
+                u = pre[i % 2, here, lanes] * a1 + b1
+                t = jnp.tanh(u)
+                u2 = u * (p1 + q1 * t)
+                t2 = jnp.tanh(u2)
                 d = dj[i % 2, here, lanes]
-                dyv[k, at, lanes] = (d * e_ref[k, at, lanes].astype(F32)).astype(BF16)
-                first = first + d * f_ref[k, at, lanes].astype(F32)
-                second = second + d * g_ref[k, at, lanes].astype(F32)
-            sums[k, 0, at, :] = fold_lanes(first)
-            sums[k, 1, at, :] = fold_lanes(second)
+                w = u2 * (1.0 - t2)
+                two = two + d * w
+                d = d * (s2 + q2 * ((1.0 + t2) * (1.0 + w)))
+                w = u * (1.0 - t)
+                one = one + d * w
+                dyv[k, at, lanes] = (d * (s1 + r1 * ((1.0 + t) * (1.0 + w)))).astype(BF16)
+            sums[k, 0, at, :] = fold_lanes(one)
+            sums[k, 1, at, :] = fold_lanes(two)
 
     def close(k):
-        w = wb_ref[base + k]
-        a_ref[k] = dot(w, dyv[k], 0, 0)
+        if k == 0:
+            wait_wt()
+        w = wt_ref[k]
+        a_ref[k] = dot(w, dyv[k], 1, 0)
         copies.append(fetch((a_ref.at[k],), (a_out.at[k],), out_sems.at[pl.ds(k, 1)]))
-        block = dot(dyv[k], x_ref[base + k], 1, 1)
-        total = block[:, ONE : ONE + 1]
-        block = jnp.where(lane < ONE, block - total * mu_ref[pl.ds(base + k, 1), :], 0.0)
+        block = dot(x_ref[base + k], dyv[k], 1, 1)
+        row = lax.broadcasted_iota(jnp.int32, block.shape, 0)
+        total = block[ONE : ONE + 1, :]
+        center = jnp.transpose(jnp.broadcast_to(mu_ref[pl.ds(base + k, 1), :], (LANES, LANES)))
+        block = jnp.where(row < ONE, block - jnp.concatenate([center] * (hid // LANES), axis=1) * total, 0.0)
         smalls = (
             total,
-            jnp.sum(block * w.astype(F32), axis=1, keepdims=True),
-            jnp.sum(sums[k, 0], axis=1, keepdims=True),
-            jnp.sum(sums[k, 1], axis=1, keepdims=True),
+            jnp.sum(block * w.astype(F32), axis=0, keepdims=True),
+            jnp.sum(jnp.transpose(sums[k, 0]), axis=0, keepdims=True),
+            jnp.sum(jnp.transpose(sums[k, 1]), axis=0, keepdims=True),
         )
         for i, value in enumerate(smalls):
-            block = jnp.where(lane == ONE + i, value, block)
+            block = jnp.where(row == ONE + i, value, block)
+            if not own:
+                block = jnp.where(row == ONE + SMALLS + i, value - value.astype(BF16).astype(F32), block)
+        block = jnp.transpose(block)
+        if own:
+            received = jnp.concatenate([recv_refs[k][s, 0] for s in range(dp)], axis=0).astype(F32)
+            block = split_smalls(block + join_smalls(received))
         for s in range(dp):
-            piece = block[s * cb : (s + 1) * cb, :]
-            if own:
-                piece = piece + join_smalls(recv_ref[s, k].astype(F32))
-            b_ref[s, k] = split_smalls(piece)
+            b_ref[s, k] = block[s * cb : (s + 1) * cb, :].astype(BF16)
 
     project(0)
     for i in range(len(jobs)):
@@ -544,7 +544,7 @@
     lane = lane_of(block.shape)
     rest = block - block.astype(BF16).astype(F32)
     moved = pltpu.roll(rest, SMALLS, 1)
-    return jnp.where((lane >= ONE + SMALLS) & (lane < ONE + 2 * SMALLS), moved, block).astype(BF16)
+    return jnp.where((lane >= ONE + SMALLS) & (lane < ONE + 2 * SMALLS), moved, block)
 
 
 def join_smalls(block):
@@ -555,17 +555,17 @@
 
 
 def split_low_kernel(pos_ref, keep_ref, got_ref, o0_ref, o1_ref, o2_ref, o3_ref):
-    low = pos_ref[0] % 4
-    for m, ref in enumerate((o0_ref, o1_ref, o2_ref, o3_ref)):
-        for z in range(4):
-            j = z * 4 + (low ^ m)
-            ref[z] = (keep_ref[j] + got_ref[j].astype(F32)).astype(ref.dtype)
+    low, high = pos_ref[0] % 4, pos_ref[0] // 4
+    for t, ref in enumerate((o0_ref, o1_ref, o2_ref, o3_ref)):
+        for e in range(4):
+            j = jnp.where(pos_ref[1] == 0, e * 4 + (low ^ t), (high ^ t) * 4 + e)
+            ref[e] = (keep_ref[j] + got_ref[j].astype(F32)).astype(ref.dtype)
 
 
 def split_high_kernel(pos_ref, own_ref, g1_ref, g2_ref, g3_ref, o0_ref, o1_ref, o2_ref, o3_ref):
-    high = pos_ref[0] // 4
-    for k, ref in enumerate((o0_ref, o1_ref, o2_ref, o3_ref)):
-        j = high ^ k
+    mine = jnp.where(pos_ref[1] == 0, pos_ref[0] // 4, pos_ref[0] % 4)
+    for t, ref in enumerate((o0_ref, o1_ref, o2_ref, o3_ref)):
+        j = mine ^ t
         value = own_ref[j] + g1_ref[j].astype(F32) + g2_ref[j].astype(F32) + g3_ref[j].astype(F32)
         ref[...] = value.astype(ref.dtype)
 
@@ -573,13 +573,11 @@
 def owner_kernel(
     count, classes, pos_ref, got_ref, sum2_ref, w1_ref, w2_ref, w3_ref, *refs
 ):
-    grad_ref, pay_ref, sems = refs[4], refs[5], refs[10]
-    w0_ref, pack_ref, coef_ref, gram_ref = refs[6:10]
-    fetch(refs[:4], refs[6:10], sems)()
+    grad_ref, pay_ref, w0_ref, fix_ref, sems = refs[2:]
+    wait = fetch(refs[:2], (w0_ref, fix_ref), sems)
     _, _, cb, _ = got_ref.shape
     total = jnp.sum(got_ref[...].astype(F32), axis=0)
     rep = pos_ref[1]
-    start = pl.multiple_of(pos_ref[0] * cb, cb)
     lane = lane_of((cb, LANES))
     squares = jnp.zeros((1, 1), F32)
     spread = jnp.zeros((cb, LANES), F32)
@@ -587,17 +585,15 @@
     def all_sum(v):
         return jnp.sum(jnp.sum(v, axis=1, keepdims=True), axis=0, keepdims=True)
 
+    wait()
     for i in range(2):
-        hop = rep * 2 + i
         b = join_smalls(total[i])
-        coef = coef_ref[hop, pl.ds(start, cb), :]
-        mean, inv, v = coef[:, 10:11], coef[:, 11:12], coef[:, 12:13]
-        gram = gram_ref[hop]
+        wg = fix_ref[i]
+        mean, inv, v = [wg[:, ONE + j : ONE + j + 1] for j in range(3)]
         s = b[:, ONE : ONE + 1]
         g = inv * b[:, ONE + 1 : ONE + 2]
         beta = inv * g / count
         alpha = s / count - beta * mean
-        wg = exact_dot(pack_ref[hop], gram) - mean * gram[ONE : ONE + 1, :]
         fixed = jnp.where(lane < ONE, b - beta * wg, 0.0)
         fixed = jnp.where(lane == ONE, g / v, fixed)
         fixed = jnp.where(lane == ONE + 1, s / v, fixed)
@@ -656,12 +652,16 @@
     copy_ref[at] = new.astype(BF16)
 
 
-def final_kernel(pos_ref, got_ref, mine_ref, other_ref, x_ref, wt_ref, own_hbm, sent_hbm, *refs):
+def final_kernel(pos_ref, got_ref, mine_ref, other_ref, x_ref, wt_hbm, own_hbm, sent0_hbm, sent1_hbm, *refs):
     states_hbm, refs = refs[:12], refs[12:]
     outs, norm_ref, rows_ref = refs[:16], refs[16], refs[17]
-    own_ref, sent_ref = refs[18:20]
-    states, sems, more = refs[20:32], refs[32], refs[33]
-    wait_rows = fetch((own_hbm, sent_hbm), (own_ref, sent_ref), more)
+    wt_ref, own_ref, sent_ref = refs[18:21]
+    states, sems, more = refs[21:33], refs[33], refs[34]
+    wait_rows = fetch(
+        (wt_hbm, own_hbm, sent0_hbm, sent1_hbm),
+        (wt_ref, own_ref, sent_ref.at[pl.ds(0, 1)], sent_ref.at[pl.ds(1, 1)]),
+        more,
+    )
     wait = fetch(states_hbm, states, sems)
     weights, firsts, seconds = states[0:4], states[4:8], states[8:12]
     dp = got_ref.shape[0] // 2
@@ -735,6 +735,15 @@
 
 def flip(value, mask, dp):
     return lax.ppermute(value, "dp", [(i, i ^ mask) for i in range(dp)])
+
+
+def turn_flip(value, digit, dp, stage):
+    pairs = []
+    for i in range(dp):
+        for core in range(2):
+            mask = digit if (core + stage) % 2 else 4 * digit
+            pairs.append((i * 2 + core, (i ^ mask) * 2 + core))
+    return lax.ppermute(value, BOTH, pairs)
 
 
 def swap(value):
@@ -812,158 +821,142 @@
     with jax.named_scope("gram_sum"):
         parts = gram.reshape(n, HOPS * LANES // n, LANES)
         if staged:
-            (stacked,) = call(stack_kernel, [sds((4,) + block.shape, BF16)], block, *far, after=(x,))
+            (stacked,) = call(stack_kernel, [sds((4,) + block.shape, BF16)], block, *far, after=(gram,))
             parts, stacked = lax.optimization_barrier((parts, stacked))
         parts = exchange(parts)
         (parts,) = call(sum_spread_kernel, [hbm_out(parts.shape)], parts)
         gram = exchange(parts).reshape(HOPS, LANES, LANES)
-    with jax.named_scope("weights"):
-        if staged:
-            mine = [stacked] + [flip(stacked, m, dp) for m in range(1, 4)]
-            mine, _ = lax.optimization_barrier((mine, parts))
-            other = [swap(v) for v in mine]
+    if staged:
+        mine = [stacked] + [flip(stacked, t, dp) for t in range(1, 4)]
+        mine, _ = lax.optimization_barrier((mine, parts))
+        with jax.named_scope("weights"):
             wb, wm = call(
                 assemble_kernel,
                 [vmem((HOPS + 1, hid, LANES), BF16), hbm_out((hid // LANES, HOPS * hid, LANES), BF16)],
-                pos, *mine, *other,
+                pos, *mine, *[swap(v) for v in mine],
                 smem=(0,),
             )
-        else:
-            own, wb, wm = weights_plain(lhs[0], weights[2], weights[3], weights[1], dp)
+    else:
+        own, wb, wm = weights_plain(lhs[0], weights[2], weights[3], weights[1], dp)
     with jax.named_scope("stats"):
-        coef, par, mu, wt = call(
+        coef, mu, wt, fix = call(
             functools.partial(stats_kernel, count),
-            [vmem((HOPS, hid, LANES)), vmem((hid, LANES)), vmem((8, LANES)), vmem((HOPS, LANES, hid), BF16)],
-            gram, wb,
-            flops=2 * HOPS * hid * LANES * LANES * 3,
+            [
+                vmem((HOPS, hid, LANES)),
+                vmem((8, LANES)),
+                hbm_out((HOPS, LANES, hid), BF16),
+                hbm_out((2, cb, LANES)),
+            ],
+            pos, gram, wb, own,
+            smem=(0,),
         )
     with jax.named_scope("forward"):
         joined, pre2, pay = call(
             forward_kernel,
-            [hbm_out((HOPS, hid, batch), BF16), hbm_out((hid, batch)), sds((n, 8, LANES))],
+            [vmem((HOPS, hid, batch), BF16), vmem((hid, batch)), sds((n, 8, LANES))],
             x, wb, coef, wm,
             hbm=(3,),
-            out_specs=(pl.BlockSpec(memory_space=pltpu.HBM),) * 2 + (pl.BlockSpec(memory_space=pltpu.VMEM),),
             scratch=[
                 pltpu.VMEM((2, CHUNK, batch), F32),
                 pltpu.VMEM(wm.shape, BF16),
-                pltpu.VMEM((HOPS, hid, batch), BF16),
-                pltpu.VMEM((hid, batch), F32),
                 pltpu.SemaphoreType.DMA((1,)),
-                pltpu.SemaphoreType.DMA((HOPS + 1,)),
             ],
             mib=16,
-            flops=2 * batch * HOPS * hid * (LANES + hid),
         )
     got = exchange(pay)
-    with jax.named_scope("factors"):
-        hop = lambda *shape: pl.BlockSpec((1,) + shape, lambda k: (k, 0, 0))
-        factors = call(
-            factor_kernel,
-            [hbm_out((HOPS, hid, batch), BF16)] * 3,
-            x, wb, coef,
-            grid=(HOPS,),
-            in_specs=[hop(LANES, batch), hop(hid, LANES), hop(hid, LANES)],
-            out_specs=(hop(hid, batch),) * 3,
-            scratch=[pltpu.VMEM((2, CHUNK, batch), F32)],
-            after=(pay,),
-            flops=2 * batch * HOPS * hid * LANES * 16,
-            mib=12,
-        )
     with jax.named_scope("head"):
         dy2, pay, block2, stat = call(
             functools.partial(head_kernel, count, classes),
             [vmem((hid, batch)), sds((n, 8, LANES)), vmem((hid, LANES)), vmem((2, hid, LANES))],
-            got, pre2, par, wb, lab,
-            hbm=(1, 4),
-            after=(pltpu.with_memory_space_constraint(factors[0], pltpu.HBM),),
+            got, pre2, wb, lab,
+            hbm=(3,),
             scratch=[
                 pltpu.VMEM((hid, batch), BF16),
                 pltpu.VMEM((hid, batch), F32),
                 pltpu.VMEM((4, hid, LANES), F32),
                 pltpu.VMEM((3, hid, LANES), F32),
                 pltpu.VMEM(lab.shape, lab.dtype),
-                pltpu.VMEM((hid, batch), F32),
-                pltpu.SemaphoreType.DMA((2,)),
+                pltpu.SemaphoreType.DMA((1,)),
             ],
             flops=6 * batch * hid * LANES,
         )
     got = exchange(pay)
     with jax.named_scope("turn"):
         rows = mr + cb // 2
-        turned = vmem if staged else sds
         dpre, keep, send, sum2 = call(
             functools.partial(turn_kernel, count),
-            [vmem((hid, batch), BF16), turned((dp, rows, half)), sds((dp, rows, half), BF16), vmem((8, LANES))],
-            pos, got, stat, par, pre2, dy2, joined, block2,
-            smem=(0,), hbm=(4, 6),
-            scratch=[
-                pltpu.VMEM((3, hid, LANES), F32),
-                pltpu.VMEM((HOPS, hid, batch), BF16),
-                pltpu.VMEM((hid, batch), F32),
-                pltpu.SemaphoreType.DMA((HOPS + 1,)),
-            ],
+            [vmem((hid, batch), BF16), sds((dp, rows, half)), sds((dp, rows, half), BF16), vmem((8, LANES))],
+            pos, got, stat, wb, pre2, dy2, joined, block2,
+            smem=(0,),
+            scratch=[pltpu.VMEM((3, hid, LANES), F32)],
             flops=2 * batch * HOPS * hid * hid,
         )
 
-    def back(own_hops, *more, after=()):
-        outs = [(hbm_out if own_hops else sds)((dp, 2, cb, LANES), BF16), hbm_out((2, LANES, batch))]
+    def back(own_hops, first, num, *more, after=()):
+        outs = [(hbm_out if own_hops else sds)((dp, num, cb, LANES), BF16), hbm_out((num, LANES, batch))]
         with jax.named_scope("back"):
             return call(
-                functools.partial(back_kernel, own_hops),
+                functools.partial(back_kernel, own_hops, first, num),
                 outs,
-                pos, dpre, x, wb, mu, wm, *factors, *more,
+                pos, dpre, x, wb, coef, mu, wt, wm, *more,
                 smem=(0,),
-                hbm=(5, 6, 7, 8),
+                hbm=(6, 7),
                 after=after,
                 out_specs=(pl.BlockSpec(memory_space=pltpu.VMEM), pl.BlockSpec(memory_space=pltpu.HBM)),
                 scratch=[
                     pltpu.VMEM((2, CHUNK, batch), F32),
-                    pltpu.VMEM((2, hid, batch), BF16),
-                    pltpu.VMEM((2, 2, hid, LANES), F32),
-                    pltpu.VMEM((2, LANES, batch), F32),
-                    pltpu.VMEM((2, hid // LANES, hid, LANES), BF16),
-                ]
-                + [pltpu.VMEM((2, hid, batch), BF16)] * 3
-                + [pltpu.SemaphoreType.DMA((2, 4)), pltpu.SemaphoreType.DMA((2,))],
-                flops=4 * batch * hid * (hid + 3 * LANES),
-                mib=20,
+                    pltpu.VMEM((2, CHUNK, batch), F32),
+                    pltpu.VMEM((num, hid, batch), BF16),
+                    pltpu.VMEM((num, 2, hid, LANES), F32),
+                    pltpu.VMEM((num, LANES, batch), F32),
+                    pltpu.VMEM((num, hid // LANES, hid, LANES), BF16),
+                    pltpu.VMEM((num, LANES, hid), BF16),
+                    pltpu.SemaphoreType.DMA((num * hid // CHUNK,)),
+                    pltpu.SemaphoreType.DMA((num + 1,)),
+                ],
+                mib=16,
             )
 
     recv = swap(send)
-    sent_b, sent_a = back(False)
-    recv_b = swap(sent_b)
+    sent = [back(False, 0, 1)]
     with jax.named_scope("merge_sum"):
         if staged:
             shape = (4, rows, half)
             low = call(
-                split_low_kernel, [vmem(shape)] + [sds(shape, BF16)] * 3, pos, keep, recv, smem=(0,), after=(sent_b,)
+                split_low_kernel,
+                [vmem(shape)] + [sds(shape, BF16)] * 3,
+                pos, keep, recv,
+                smem=(0,),
+                after=(sent[0][1],),
             )
-            moved = [flip(low[m], m, dp) for m in range(1, 4)]
-            kept_b, kept_a = back(True, recv_b, after=(low[0],))
+            sent.append(back(False, 1, 1, after=(low[1],)))
+            recv_b = [swap(v[0]) for v in sent]
+            moved = [turn_flip(low[t], t, dp, 1) for t in range(1, 4)]
+            kept_b, kept_a = back(True, 0, 2, *recv_b)
+            kept_b, moved = lax.optimization_barrier((kept_b, moved))
             high = call(
                 split_high_kernel,
                 [sds(shape[1:])] + [sds(shape[1:], BF16)] * 3,
                 pos, low[0], *moved,
                 smem=(0,),
             )
-            kept_b, high = lax.optimization_barrier((kept_b, high))
-            wide = [high[0]] + [flip(high[k], 4 * k, dp) for k in range(1, 4)]
+            wide = [high[0]] + [turn_flip(high[t], t, dp, 0) for t in range(1, 4)]
         else:
-            kept_b, kept_a = back(True, recv_b)
+            sent.append(back(False, 1, 1))
+            kept_b, kept_a = back(True, 0, 2, *[swap(v[0]) for v in sent])
             total = lax.psum_scatter(keep + recv.astype(F32), "dp", scatter_dimension=0)
             wide = [total] + [jnp.zeros_like(total)] * 3
     with jax.named_scope("branch_sum"):
         got_b = lax.all_to_all(kept_b, "dp", 0, 0, tiled=True)
     with jax.named_scope("owner"):
-        late = (wide[0], own, coef, gram)
+        late = (wide[0], fix)
         shares, pay = call(
             functools.partial(owner_kernel, count, classes),
             [sds((3 * cb + 2 * mr, LANES)), hbm_out((n, 8, LANES))],
             pos, got_b, sum2, *wide[1:], *late,
             smem=(0,),
-            hbm=tuple(range(6, 10)),
-            scratch=[pltpu.VMEM(v.shape, v.dtype) for v in late] + [pltpu.SemaphoreType.DMA((4,))],
+            hbm=(6, 7),
+            scratch=[pltpu.VMEM(v.shape, v.dtype) for v in late] + [pltpu.SemaphoreType.DMA((2,))],
         )
     theirs = swap(shares)
     got = exchange(pay)
@@ -976,10 +969,10 @@
         outs += [sds((1, 1)), sds((width, batch))]
         local = (*tr[0], *tr[1], *tr[2])
         res = call(
-            final_kernel, outs, pos, got, shares, theirs, x, wt, kept_a, sent_a, *local,
-            smem=(0,), hbm=tuple(range(6, 8 + len(local))),
-            scratch=[pltpu.VMEM(v.shape, v.dtype) for v in (kept_a, sent_a) + local]
-            + [pltpu.SemaphoreType.DMA((len(local),)), pltpu.SemaphoreType.DMA((2,))],
+            final_kernel, outs, pos, got, shares, theirs, x, wt, kept_a, sent[0][1], sent[1][1], *local,
+            smem=(0,), hbm=tuple(range(5, 9 + len(local))),
+            scratch=[pltpu.VMEM(v.shape, v.dtype) for v in (wt, kept_a, kept_a) + local]
+            + [pltpu.SemaphoreType.DMA((len(local),)), pltpu.SemaphoreType.DMA((4,))],
             flops=2 * batch * LANES * LANES * 3 * HOPS,
         )
     result = list(res[:16])

time: 163 us -> 153 us (0.939)
  blocking collectives: 13.7 us -> 22.3 us
  Pallas kernels: 66.9 us -> 58.4 us
  waiting for transfers between devices: 39.7 us -> 33.5 us
  starting transfers between devices: 39.6 us -> 35.2 us
    ppermute x12 -> x6, waiting for transfers between devices: 22.6 us -> 9.21 us  [flip(): return lax.ppermute(value, 'dp', [(i, i ^ mask) for i in range(dp)])]
    all_to_all x1 -> x2, blocking collectives: 13.7 us -> 22.3 us  [exchange(): return lax.all_to_all(value, BOTH, 0, 0, tiled=True)]
    pallas_call x16, Pallas kernels: 66.9 us -> 58.4 us  [call(): pl.pallas_call(kernel, out_shape=tuple(outs), in_specs=in_specs, out_spec...]
    ppermute x12 -> x6, starting transfers between devices: 17.3 us -> 9.31 us  [flip(): return lax.ppermute(value, 'dp', [(i, i ^ mask) for i in range(dp)])]
    ppermute x0 -> x6, starting transfers between devices: none -> 7.94 us  [turn_flip(): return lax.ppermute(value, BOTH, pairs)]
    ppermute x0 -> x6, waiting for transfers between devices: none -> 6.14 us  [turn_flip(): return lax.ppermute(value, BOTH, pairs)]
    all_to_all x4 -> x3, starting transfers between devices: 16.6 us -> 12.2 us  [exchange(): return lax.all_to_all(value, BOTH, 0, 0, tiled=True)]
    ppermute x7 -> x8, waiting for transfers between devices: 3.28 us -> 4.26 us  [swap(): return lax.ppermute(value, 'rep', [(0, 1), (1, 0)])]
  transfers between devices with their start and end apart: 24 -> 24, of which waited for: 13 -> 13; matrix products, arithmetic and copies ran while one was open for 0% -> 0% of each run, Pallas kernels for 21% -> 20%
where the time goes in v3:
time: 153 us; the launch traced here: 152 us
  Pallas kernels  58.4 us (38%)
  starting transfers between devices  35.2 us (23%)
  waiting for transfers between devices  33.5 us (22%)
  blocking collectives  22.3 us (15%)
  local copies, waits for them, and re-layouts  1.56 us (1%)
    pallas_call x16, Pallas kernels, call(): pl.pallas_call(kernel, out_shape=tuple(outs), in_specs=in_specs, out_spec...  58.4 us
    all_to_all x2, blocking collectives, exchange(): return lax.all_to_all(value, BOTH, 0, 0, tiled=True)  22.3 us
    all_to_all x3, waiting for transfers between devices, exchange(): return lax.all_to_all(value, BOTH, 0, 0, tiled=True)  13.9 us
    all_to_all x3, starting transfers between devices, exchange(): return lax.all_to_all(value, BOTH, 0, 0, tiled=True)  12.2 us
    ppermute x6, starting transfers between devices, flip(): return lax.ppermute(value, 'dp', [(i, i ^ mask) for i in range(dp)])  9.31 us
    ppermute x6, waiting for transfers between devices, flip(): return lax.ppermute(value, 'dp', [(i, i ^ mask) for i in range(dp)])  9.21 us
    ppermute x6, starting transfers between devices, turn_flip(): return lax.ppermute(value, BOTH, pairs)  7.94 us
    ppermute x6, waiting for transfers between devices, turn_flip(): return lax.ppermute(value, BOTH, pairs)  6.14 us
  transfers between devices with their start and end apart: 24, of which 13 were waited for; matrix products, arithmetic and copies ran while one was open for 0% of the time, Pallas kernels for 20%

profile of v3, /device:TPU:0, one launch (start us, length us, event | category | flops | bytes accessed | tf_op | source)
XLA Modules:
  0.0 152.0 jit_solution(12394244119104370614)
XLA Ops:
  0.7 2.4 %prep.1 = (bf16[5,32,128]{2,1,0:T(8,128)(2,1)}, bf16[336,128]{1,0:T(8,128)(2,1)S(1)}) custom-call(s32[2]{0:T(128)S(1)} %pad_add_fusion.refs_0_, f32[4,32,100]{2,1,0:T(8,128)} %bitcast.19, f32[32,47]{1,0:T(8,128)} %refs_11_.1, f32[20,32]{1,0:T(8,128)} %refs_12_.1, f32[128,512]{1,0:T(8,128)} %refs_10_.1), custom_call_target="tpu_custom_call" | custom-call | flops 1024 | bytes 1024 | tf_op jit(solution)/shard_map/prep/pallas_call | solution.py:47
  3.1 5.1 %collective-permute-start.2 = (bf16[336,128]{1,0:T(8,128)(2,1)S(1)}, bf16[336,128]{1,0:T(8,128)(2,1)S(1)}, u32[]{:S(2)}, u32[]{:S(2)}) collective-permute-start(bf16[336,128]{1,0:T(8,128)(2,1)S(1)} %get-tuple-element.83.refs_2_.refs_0_), channel_id=1, source_target_pairs={{0,24},{2,26},{4,28},{6,30},{8,16},{10,18},{12,20},{14,22},{16,8},... | collective-permute-start | bytes 258056 | tf_op jit(solution)/shard_map/ppermute | solution.py:737
  8.2 0.6 collective-permute-start
  8.9 7.1 %gather.1 = (bf16[4,128,1024]{2,1,0:T(8,128)(2,1)S(1)}, f32[4,128,128]{2,1,0:T(8,128)}) custom-call(s32[1,1024]{1,0:T(1,128)} %bitcast.23, f32[400,4096]{1,0:T(8,128)} %bitcast.17, bf16[336,128]{1,0:T(8,128)(2,1)} %copy-done), custom_call_target="tpu_custom_call" | custom-call | flops 1024 | bytes 1024 | tf_op jit(solution)/shard_map/gather/pallas_call | solution.py:47
  16.0 0.9 copy-done.1
  16.9 6.0 %all-to-all-start = ((f32[32,16,128]{2,1,0:T(8,128)}), f32[32,16,128]{2,1,0:T(8,128)S(1)}, u32[]{:S(2)}, u32[]{:S(2)}) async-start(f32[32,16,128]{2,1,0:T(8,128)} %bitcast.18), calls=%async_computation | async-start | bytes 524288 | tf_op jit(solution)/shard_map/gram_sum/all_to_all | solution.py:754
  22.9 2.7 %collective-permute-start.5 = (bf16[4,336,128]{2,1,0:T(8,128)(2,1)S(1)}, bf16[4,336,128]{2,1,0:T(8,128)(2,1)S(1)}, u32[]{:S(2)}, u32[]{:S(2)}) collective-permute-start(bf16[4,336,128]{2,1,0:T(8,128)(2,1)S(1)} %gram_sum.2.refs_1_), channel_id=1, source_target_pairs={{0,6},{2,4},{4,2},{6,0},{8,14},{10,12},{12,10},{14,8},{16,22},{18,... | collective-permute-start | bytes 1032200 | tf_op jit(solution)/shard_map/ppermute | solution.py:737
  25.7 0.6 collective-permute-start.4
  26.5 7.1 %all-to-all-done.refs_0_ = f32[32,16,128]{2,1,0:T(8,128)S(1)} async-done(((f32[32,16,128]{2,1,0:T(8,128)}), f32[32,16,128]{2,1,0:T(8,128)S(1)}, u32[]{:S(2)}, u32[]{:S(2)}) %all-to-all-start) | async-done | bytes 262176 | tf_op jit(solution)/shard_map/gram_sum/all_to_all | solution.py:754
  33.6 0.8 gram_sum.3
  34.3 2.6 %all-to-all-start.1 = ((f32[32,16,128]{2,1,0:T(8,128)}), f32[32,16,128]{2,1,0:T(8,128)S(1)}, u32[]{:S(2)}, u32[]{:S(2)}) async-start(f32[32,16,128]{2,1,0:T(8,128)} %gram_sum.3), calls=%async_computation.1 | async-start | bytes 524288 | tf_op jit(solution)/shard_map/gram_sum/all_to_all | solution.py:754
  36.9 0.5 collective-permute-done.5.refs_4_
  37.4 8.4 %collective-permute-done.4.refs_3_ = bf16[4,336,128]{2,1,0:T(8,128)(2,1)S(1)} collective-permute-done((bf16[4,336,128]{2,1,0:T(8,128)(2,1)S(1)}, bf16[4,336,128]{2,1,0:T(8,128)(2,1)S(1)}, u32[]{:S(2)}, u32[]{:S(2)}) %collective-permute-start.4) | collective-permute-done | bytes 344096 | tf_op jit(solution)/shard_map/ppermute | solution.py:737
  45.8 0.3 collective-permute-done.3.refs_2_
  46.1 0.5 collective-permute-start.7
  46.7 0.5 collective-permute-start.9
  47.2 0.6 collective-permute-done.6.refs_5_
  47.8 0.5 collective-permute-done.7.refs_6_
  48.3 0.5 collective-permute-done.8.refs_7_
  48.8 0.5 collective-permute-done.9.refs_8_
  49.3 2.1 %weights.1 = (bf16[5,512,128]{2,1,0:T(8,128)(2,1)S(1)}, bf16[4,2048,128]{2,1,0:T(8,128)(2,1)}) custom-call(s32[2]{0:T(128)S(1)} %pad_add_fusion.refs_0_, bf16[4,336,128]{2,1,0:T(8,128)(2,1)S(1)} %gram_sum.2.refs_1_, bf16[4,336,128]{2,1,0:T(8,128)(2,1)S(1)} %collective-permute-done.3.refs_2_, bf16[4,336,128]{2,1,0:T(8,128)(2,1)S(1)} %collective-permute-done.4.refs_3_, ...), custom_call_target="tpu_custom_call" | custom-call | flops 1024 | bytes 1024 | tf_op jit(solution)/shard_map/weights/pallas_call | solution.py:47
  51.4 1.9 %stats.1 = (f32[4,512,128]{2,1,0:T(8,128)S(1)}, f32[8,128]{1,0:T(8,128)S(1)}, bf16[4,128,512]{2,1,0:T(8,128)(2,1)}, f32[2,32,128]{2,1,0:T(8,128)}) custom-call(s32[2]{0:T(128)S(1)} %pad_add_fusion.refs_0_, f32[4,128,128]{2,1,0:T(8,128)S(1)} %bitcast.16, bf16[5,512,128]{2,1,0:T(8,128)(2,1)S(1)} %get-tuple-element.92.refs_2_.refs_1_.refs_3_, ...), custom_call_target="tpu_custom_call" | custom-call | flops 1024 | bytes 1024 | tf_op jit(solution)/shard_map/stats/pallas_call | solution.py:47
  53.3 6.0 %forward.1 = (bf16[4,512,1024]{2,1,0:T(8,128)(2,1)S(1)}, f32[512,1024]{1,0:T(8,128)S(1)}, f32[32,8,128]{2,1,0:T(8,128)S(1)}) custom-call(bf16[4,128,1024]{2,1,0:T(8,128)(2,1)S(1)} %get-tuple-element.84.refs_0_.refs_2_.refs_4_, bf16[5,512,128]{2,1,0:T(8,128)(2,1)S(1)} %get-tuple-element.92.refs_2_.refs_1_.refs_3_, ...), custom_call_target="tpu_custom_call" | custom-call | flops 1024 | bytes 1024 | tf_op jit(solution)/shard_map/forward/pallas_call | solution.py:47
  59.3 12.3 %all_to_all.30.refs_0_ = f32[32,8,128]{2,1,0:T(8,128)S(1)} all-to-all(f32[32,8,128]{2,1,0:T(8,128)S(1)} %get-tuple-element.96), channel_id=1, replica_groups=mesh['dp'=16,'rep'=2] {'dp','rep'}, dimensions={0} | all-to-all | bytes 262144 | tf_op jit(solution)/shard_map/all_to_all | solution.py:754
  71.6 3.7 %head.1 = (f32[512,1024]{1,0:T(8,128)S(1)}, f32[32,8,128]{2,1,0:T(8,128)S(1)}, f32[512,128]{1,0:T(8,128)S(1)}, f32[2,512,128]{2,1,0:T(8,128)S(1)}) custom-call(f32[32,8,128]{2,1,0:T(8,128)S(1)} %all_to_all.30.refs_0_, f32[512,1024]{1,0:T(8,128)S(1)} %get-tuple-element.97.refs_1_.refs_4_, bf16[5,512,128]{2,1,0:T(8,128)(2,1)S(1)} %get-tuple-element.92.refs_2_.refs_1_.refs_3_, ...), custom_call_target="tpu_custom_call" | custom-call | flops 1024 | bytes 1024 | tf_op jit(solution)/shard_map/head/pallas_call | solution.py:47
  75.3 10.0 %all_to_all.31.refs_1_ = f32[32,8,128]{2,1,0:T(8,128)S(1)} all-to-all(f32[32,8,128]{2,1,0:T(8,128)S(1)} %get-tuple-element.98), channel_id=1, replica_groups=mesh['dp'=16,'rep'=2] {'dp','rep'}, dimensions={0} | all-to-all | bytes 262144 | tf_op jit(solution)/shard_map/all_to_all | solution.py:754
  85.3 3.6 %turn.1 = (bf16[512,1024]{1,0:T(8,128)(2,1)S(1)}, f32[16,144,256]{2,1,0:T(8,128)S(1)}, bf16[16,144,256]{2,1,0:T(8,128)(2,1)S(1)}, f32[8,128]{1,0:T(8,128)S(1)}) custom-call(s32[2]{0:T(128)S(1)} %pad_add_fusion.refs_0_, f32[32,8,128]{2,1,0:T(8,128)S(1)} %all_to_all.31.refs_1_, f32[2,512,128]{2,1,0:T(8,128)S(1)} %get-tuple-element.99.refs_2_, ...), custom_call_target="tpu_custom_call" | custom-call | flops 1024 | bytes 1024 | tf_op jit(solution)/shard_map/turn/pallas_call | solution.py:47
  89.3 5.4 %back.3 = (bf16[16,1,32,128]{3,2,1,0:T(8,128)(2,1)S(1)}, f32[1,128,1024]{2,1,0:T(8,128)}) custom-call(s32[2]{0:T(128)S(1)} %pad_add_fusion.refs_0_, bf16[512,1024]{1,0:T(8,128)(2,1)S(1)} %get-tuple-element.103.refs_1_, bf16[4,128,1024]{2,1,0:T(8,128)(2,1)S(1)} %get-tuple-element.84.refs_0_.refs_2_.refs_4_, ...), custom_call_target="tpu_custom_call" | custom-call | flops 1024 | bytes 1024 | tf_op jit(solution)/shard_map/back/pallas_call | solution.py:47
  94.7 0.8 merge_sum.2
  95.5 0.5 collective-permute-start.14
  96.0 1.3 collective-permute-start.15
  97.4 1.7 %collective-permute-start.13 = (bf16[4,144,256]{2,1,0:T(8,128)(2,1)S(1)}, bf16[4,144,256]{2,1,0:T(8,128)(2,1)S(1)}, u32[]{:S(2)}, u32[]{:S(2)}) collective-permute-start(bf16[4,144,256]{2,1,0:T(8,128)(2,1)S(1)} %get-tuple-element.110.refs_8_), channel_id=1, source_target_pairs={{0,2},{1,9},{2,0},{3,11},{4,6},{5,13},{6,4},{7,15},{8,10},{9,1},{1... | collective-permute-start | bytes 884744 | tf_op jit(solution)/shard_map/merge_sum/ppermute | solution.py:746
  99.1 5.4 %back.4 = (bf16[16,1,32,128]{3,2,1,0:T(8,128)(2,1)S(1)}, f32[1,128,1024]{2,1,0:T(8,128)}) custom-call(s32[2]{0:T(128)S(1)} %pad_add_fusion.refs_0_, bf16[512,1024]{1,0:T(8,128)(2,1)S(1)} %get-tuple-element.103.refs_1_, bf16[4,128,1024]{2,1,0:T(8,128)(2,1)S(1)} %get-tuple-element.84.refs_0_.refs_2_.refs_4_, ...), custom_call_target="tpu_custom_call" | custom-call | flops 1024 | bytes 1024 | tf_op jit(solution)/shard_map/merge_sum/back/pallas_call | solution.py:47
  104.5 0.6 collective-permute-start.12
  105.1 1.0 collective-permute-done.12.refs_9_
  106.0 9.5 %back.5 = (bf16[16,2,32,128]{3,2,1,0:T(8,128)(2,1)}, f32[2,128,1024]{2,1,0:T(8,128)}) custom-call(s32[2]{0:T(128)S(1)} %pad_add_fusion.refs_0_, bf16[512,1024]{1,0:T(8,128)(2,1)S(1)} %get-tuple-element.103.refs_1_, bf16[4,128,1024]{2,1,0:T(8,128)(2,1)S(1)} %get-tuple-element.84.refs_0_.refs_2_.refs_4_, ...), custom_call_target="tpu_custom_call" | custom-call | flops 1024 | bytes 1024 | tf_op jit(solution)/shard_map/merge_sum/back/pallas_call | solution.py:47
  115.6 3.5 %all-to-all-start.4 = ((bf16[16,2,32,128]{3,2,1,0:T(8,128)(2,1)}), bf16[16,2,32,128]{3,2,1,0:T(8,128)(2,1)S(1)}, u32[]{:S(2)}, u32[]{:S(2)}) async-start(bf16[16,2,32,128]{3,2,1,0:T(8,128)(2,1)} %get-tuple-element.115), calls=%async_computation.4 | async-start | bytes 524288 | tf_op jit(solution)/shard_map/branch_sum/all_to_all | solution.py:950
  119.2 0.7 merge_sum.3
  119.9 0.7 copy-done.3
  120.5 1.8 %collective-permute-start.16 = (bf16[144,256]{1,0:T(8,128)(2,1)S(1)}, bf16[144,256]{1,0:T(8,128)(2,1)S(1)}, u32[]{:S(2)}, u32[]{:S(2)}) collective-permute-start(bf16[144,256]{1,0:T(8,128)(2,1)S(1)} %get-tuple-element.121), channel_id=1, source_target_pairs={{0,8},{1,3},{2,10},{3,1},{4,12},{5,7},{6,14},{7,5},{8,0},{9,11},{1... | collective-permute-start | bytes 221192 | tf_op jit(solution)/shard_map/merge_sum/ppermute | solution.py:746
  122.3 2.4 %collective-permute-start.17 = (bf16[144,256]{1,0:T(8,128)(2,1)S(1)}, bf16[144,256]{1,0:T(8,128)(2,1)S(1)}, u32[]{:S(2)}, u32[]{:S(2)}) collective-permute-start(bf16[144,256]{1,0:T(8,128)(2,1)S(1)} %get-tuple-element.122), channel_id=1, source_target_pairs={{0,16},{1,5},{2,18},{3,7},{4,20},{5,1},{6,22},{7,3},{8,24},{9,13},... | collective-permute-start | bytes 221192 | tf_op jit(solution)/shard_map/merge_sum/ppermute | solution.py:746
  124.9 1.5 collective-permute-done.16.refs_3_
  126.4 4.6 %collective-permute-done.17.refs_4_ = bf16[144,256]{1,0:T(8,128)(2,1)S(1)} collective-permute-done((bf16[144,256]{1,0:T(8,128)(2,1)S(1)}, bf16[144,256]{1,0:T(8,128)(2,1)S(1)}, u32[]{:S(2)}, u32[]{:S(2)}) %collective-permute-start.17) | collective-permute-done | bytes 73760 | tf_op jit(solution)/shard_map/merge_sum/ppermute | solution.py:746
  131.0 2.7 %owner.1 = (f32[352,128]{1,0:T(8,128)S(1)}, f32[32,8,128]{2,1,0:T(8,128)}) custom-call(s32[2]{0:T(128)S(1)} %pad_add_fusion.refs_0_, bf16[16,2,32,128]{3,2,1,0:T(8,128)(2,1)S(1)} %all-to-all-done.4.refs_1_, f32[8,128]{1,0:T(8,128)S(1)} %get-tuple-element.116.refs_2_, bf16[144,256]{1,0:T(8,128)(2,1)S(1)} %collective-permute-done.16.refs_3_, ...), custom_call_target="tpu_custom_call" | custom-call | flops 1024 | bytes 1024 | tf_op jit(solution)/shard_map/owner/pallas_call | solution.py:47
  133.7 3.6 %all-to-all-start.5 = ((f32[32,8,128]{2,1,0:T(8,128)}), f32[32,8,128]{2,1,0:T(8,128)S(1)}, u32[]{:S(2)}, u32[]{:S(2)}) async-start(f32[32,8,128]{2,1,0:T(8,128)} %get-tuple-element.126), calls=%async_computation.5 | async-start | bytes 262144 | tf_op jit(solution)/shard_map/all_to_all | solution.py:754
  137.7 1.2 collective-permute-done.19.refs_3_
  138.9 6.7 %all-to-all-done.5.refs_1_ = f32[32,8,128]{2,1,0:T(8,128)S(1)} async-done(((f32[32,8,128]{2,1,0:T(8,128)}), f32[32,8,128]{2,1,0:T(8,128)S(1)}, u32[]{:S(2)}, u32[]{:S(2)}) %all-to-all-start.5) | async-done | bytes 131104 | tf_op jit(solution)/shard_map/all_to_all | solution.py:754
  145.6 6.2 %final.1 = (f32[4,32,100]{2,1,0:T(8,128)}, f32[128,512]{1,0:T(8,128)}, f32[32,47]{1,0:T(8,128)}, f32[20,32]{1,0:T(8,128)}, f32[4,32,100]{2,1,0:T(8,128)}, /*inde...) custom-call(s32[2]{0:T(128)S(1)} %pad_add_fusion.refs_0_, ...), custom_call_target="tpu_custom_call" | custom-call | flops 1024 | bytes 1024 | tf_op jit(solution)/shard_map/final/pallas_call | solution.py:47
  (29 shorter events, 1.2 us)
Async XLA Ops:
  3.1 5.8 %copy-start = (bf16[336,128]{1,0:T(8,128)(2,1)}, bf16[336,128]{1,0:T(8,128)(2,1)S(1)}, u32[]{:S(2)}) copy-start(bf16[336,128]{1,0:T(8,128)(2,1)S(1)} %get-tuple-element.83.refs_2_.refs_0_) | copy-start | bytes 258052
  3.1 12.9 %collective-permute-start.2 = (bf16[336,128]{1,0:T(8,128)(2,1)S(1)}, bf16[336,128]{1,0:T(8,128)(2,1)S(1)}, u32[]{:S(2)}, u32[]{:S(2)}) collective-permute-start(bf16[336,128]{1,0:T(8,128)(2,1)S(1)} %get-tuple-element.83.refs_2_.refs_0_), channel_id=1, source_target_pairs={{0,24},{2,26},{4,28},{6,30},{8,16},{10,18},{12,20},{14,22},{16,8},... | collective-permute-start | bytes 258056 | tf_op jit(solution)/shard_map/ppermute | solution.py:737
  8.2 7.8 %collective-permute-start.1 = (bf16[336,128]{1,0:T(8,128)(2,1)S(1)}, bf16[336,128]{1,0:T(8,128)(2,1)S(1)}, u32[]{:S(2)}, u32[]{:S(2)}) collective-permute-start(bf16[336,128]{1,0:T(8,128)(2,1)S(1)} %get-tuple-element.83.refs_2_.refs_0_), channel_id=1, source_target_pairs={{0,16},{2,18},{4,20},{6,22},{8,24},{10,26},{12,28},{14,30},{16,0},... | collective-permute-start | bytes 258056 | tf_op jit(solution)/shard_map/ppermute | solution.py:737
  8.2 7.8 %collective-permute-start = (bf16[336,128]{1,0:T(8,128)(2,1)S(1)}, bf16[336,128]{1,0:T(8,128)(2,1)S(1)}, u32[]{:S(2)}, u32[]{:S(2)}) collective-permute-start(bf16[336,128]{1,0:T(8,128)(2,1)S(1)} %get-tuple-element.83.refs_2_.refs_0_), channel_id=1, source_target_pairs={{0,8},{2,10},{4,12},{6,14},{8,0},{10,2},{12,4},{14,6},{16,24},{18,... | collective-permute-start | bytes 258056 | tf_op jit(solution)/shard_map/ppermute | solution.py:737
  16.0 0.9 copy-start.1
  16.9 34.5 %copy-start.4 = (bf16[5,32,128]{2,1,0:T(8,128)(2,1)S(1)}, bf16[5,32,128]{2,1,0:T(8,128)(2,1)}, u32[]{:S(2)}) copy-start(bf16[5,32,128]{2,1,0:T(8,128)(2,1)} %get-tuple-element.93.refs_3_) | copy-start | bytes 122884
  16.9 16.7 %all-to-all-start = ((f32[32,16,128]{2,1,0:T(8,128)}), f32[32,16,128]{2,1,0:T(8,128)S(1)}, u32[]{:S(2)}, u32[]{:S(2)}) async-start(f32[32,16,128]{2,1,0:T(8,128)} %bitcast.18), calls=%async_computation | async-start | bytes 524288 | tf_op jit(solution)/shard_map/gram_sum/all_to_all | solution.py:754
  22.9 14.5 %collective-permute-start.5 = (bf16[4,336,128]{2,1,0:T(8,128)(2,1)S(1)}, bf16[4,336,128]{2,1,0:T(8,128)(2,1)S(1)}, u32[]{:S(2)}, u32[]{:S(2)}) collective-permute-start(bf16[4,336,128]{2,1,0:T(8,128)(2,1)S(1)} %gram_sum.2.refs_1_), channel_id=1, source_target_pairs={{0,6},{2,4},{4,2},{6,0},{8,14},{10,12},{12,10},{14,8},{16,22},{18,... | collective-permute-start | bytes 1032200 | tf_op jit(solution)/shard_map/ppermute | solution.py:737
  25.7 20.1 %collective-permute-start.4 = (bf16[4,336,128]{2,1,0:T(8,128)(2,1)S(1)}, bf16[4,336,128]{2,1,0:T(8,128)(2,1)S(1)}, u32[]{:S(2)}, u32[]{:S(2)}) collective-permute-start(bf16[4,336,128]{2,1,0:T(8,128)(2,1)S(1)} %gram_sum.2.refs_1_), channel_id=1, source_target_pairs={{0,4},{2,6},{4,0},{6,2},{8,12},{10,14},{12,8},{14,10},{16,20},{18,... | collective-permute-start | bytes 1032200 | tf_op jit(solution)/shard_map/ppermute | solution.py:737
  26.2 19.9 %collective-permute-start.3 = (bf16[4,336,128]{2,1,0:T(8,128)(2,1)S(1)}, bf16[4,336,128]{2,1,0:T(8,128)(2,1)S(1)}, u32[]{:S(2)}, u32[]{:S(2)}) collective-permute-start(bf16[4,336,128]{2,1,0:T(8,128)(2,1)S(1)} %gram_sum.2.refs_1_), channel_id=1, source_target_pairs={{0,2},{2,0},{4,6},{6,4},{8,10},{10,8},{12,14},{14,12},{16,18},{18,... | collective-permute-start | bytes 1032200 | tf_op jit(solution)/shard_map/ppermute | solution.py:737
  34.3 17.1 %all-to-all-start.1 = ((f32[32,16,128]{2,1,0:T(8,128)}), f32[32,16,128]{2,1,0:T(8,128)S(1)}, u32[]{:S(2)}, u32[]{:S(2)}) async-start(f32[32,16,128]{2,1,0:T(8,128)} %gram_sum.3), calls=%async_computation.1 | async-start | bytes 524288 | tf_op jit(solution)/shard_map/gram_sum/all_to_all | solution.py:754
  46.1 1.7 %collective-permute-start.6 = (bf16[4,336,128]{2,1,0:T(8,128)(2,1)S(1)}, bf16[4,336,128]{2,1,0:T(8,128)(2,1)S(1)}, u32[]{:S(2)}, u32[]{:S(2)}) collective-permute-start(bf16[4,336,128]{2,1,0:T(8,128)(2,1)S(1)} %gram_sum.2.refs_1_), channel_id=1, source_target_pairs={{0,1},{1,0},{2,3},{3,2},{4,5},{5,4},{6,7},{7,6},{8,9},{9,8},{10,11... | collective-permute-start | bytes 1032200 | tf_op jit(solution)/shard_map/weights/ppermute | solution.py:750
  46.1 2.1 %collective-permute-start.7 = (bf16[4,336,128]{2,1,0:T(8,128)(2,1)S(1)}, bf16[4,336,128]{2,1,0:T(8,128)(2,1)S(1)}, u32[]{:S(2)}, u32[]{:S(2)}) collective-permute-start(bf16[4,336,128]{2,1,0:T(8,128)(2,1)S(1)} %collective-permute-done.3.refs_2_), channel_id=1, source_target_pairs={{0,1},{1,0},{2,3},{3,2},{4,5},{5,4},{6,7},{7,6},{8,9},{9,8},{10,11... | collective-permute-start | bytes 1032200 | tf_op jit(solution)/shard_map/weights/ppermute | solution.py:750
  46.6 2.1 %collective-permute-start.8 = (bf16[4,336,128]{2,1,0:T(8,128)(2,1)S(1)}, bf16[4,336,128]{2,1,0:T(8,128)(2,1)S(1)}, u32[]{:S(2)}, u32[]{:S(2)}) collective-permute-start(bf16[4,336,128]{2,1,0:T(8,128)(2,1)S(1)} %collective-permute-done.4.refs_3_), channel_id=1, source_target_pairs={{0,1},{1,0},{2,3},{3,2},{4,5},{5,4},{6,7},{7,6},{8,9},{9,8},{10,11... | collective-permute-start | bytes 1032200 | tf_op jit(solution)/shard_map/weights/ppermute | solution.py:750
  46.7 2.6 %collective-permute-start.9 = (bf16[4,336,128]{2,1,0:T(8,128)(2,1)S(1)}, bf16[4,336,128]{2,1,0:T(8,128)(2,1)S(1)}, u32[]{:S(2)}, u32[]{:S(2)}) collective-permute-start(bf16[4,336,128]{2,1,0:T(8,128)(2,1)S(1)} %collective-permute-done.5.refs_4_), channel_id=1, source_target_pairs={{0,1},{1,0},{2,3},{3,2},{4,5},{5,4},{6,7},{7,6},{8,9},{9,8},{10,11... | collective-permute-start | bytes 1032200 | tf_op jit(solution)/shard_map/weights/ppermute | solution.py:750
  89.0 5.7 %collective-permute-start.11 = (bf16[16,144,256]{2,1,0:T(8,128)(2,1)S(1)}, bf16[16,144,256]{2,1,0:T(8,128)(2,1)S(1)}, u32[]{:S(2)}, u32[]{:S(2)}) collective-permute-start(bf16[16,144,256]{2,1,0:T(8,128)(2,1)S(1)} %get-tuple-element.108), channel_id=1, source_target_pairs={{0,1},{1,0},{2,3},{3,2},{4,5},{5,4},{6,7},{7,6},{8,9},{9,8},{10,11... | collective-permute-start | bytes 3538952 | tf_op jit(solution)/shard_map/ppermute | solution.py:750
  95.5 3.6 %copy-start.2 = (bf16[4,144,256]{2,1,0:T(8,128)(2,1)}, bf16[4,144,256]{2,1,0:T(8,128)(2,1)S(1)}, u32[]{:S(2)}) copy-start(bf16[4,144,256]{2,1,0:T(8,128)(2,1)S(1)} %get-tuple-element.110.refs_8_) | copy-start | bytes 884740
  95.5 20.1 %collective-permute-start.14 = (bf16[4,144,256]{2,1,0:T(8,128)(2,1)S(1)}, bf16[4,144,256]{2,1,0:T(8,128)(2,1)S(1)}, u32[]{:S(2)}, u32[]{:S(2)}) collective-permute-start(bf16[4,144,256]{2,1,0:T(8,128)(2,1)S(1)} %get-tuple-element.113), channel_id=1, source_target_pairs={{0,4},{1,17},{2,6},{3,19},{4,0},{5,21},{6,2},{7,23},{8,12},{9,25},... | collective-permute-start | bytes 884744 | tf_op jit(solution)/shard_map/merge_sum/ppermute | solution.py:746
  96.0 19.6 %collective-permute-start.15 = (bf16[4,144,256]{2,1,0:T(8,128)(2,1)S(1)}, bf16[4,144,256]{2,1,0:T(8,128)(2,1)S(1)}, u32[]{:S(2)}, u32[]{:S(2)}) collective-permute-start(bf16[4,144,256]{2,1,0:T(8,128)(2,1)S(1)} %get-tuple-element.114), channel_id=1, source_target_pairs={{0,6},{1,25},{2,4},{3,27},{4,2},{5,29},{6,0},{7,31},{8,14},{9,17},... | collective-permute-start | bytes 884744 | tf_op jit(solution)/shard_map/merge_sum/ppermute | solution.py:746
  97.4 18.2 %collective-permute-start.13 = (bf16[4,144,256]{2,1,0:T(8,128)(2,1)S(1)}, bf16[4,144,256]{2,1,0:T(8,128)(2,1)S(1)}, u32[]{:S(2)}, u32[]{:S(2)}) collective-permute-start(bf16[4,144,256]{2,1,0:T(8,128)(2,1)S(1)} %get-tuple-element.110.refs_8_), channel_id=1, source_target_pairs={{0,2},{1,9},{2,0},{3,11},{4,6},{5,13},{6,4},{7,15},{8,10},{9,1},{1... | collective-permute-start | bytes 884744 | tf_op jit(solution)/shard_map/merge_sum/ppermute | solution.py:746
  99.1 6.0 %collective-permute-start.10 = (bf16[16,1,32,128]{3,2,1,0:T(8,128)(2,1)S(1)}, bf16[16,1,32,128]{3,2,1,0:T(8,128)(2,1)S(1)}, u32[]{:S(2)}, u32[]{:S(2)}) collective-permute-start(bf16[16,1,32,128]{3,2,1,0:T(8,128)(2,1)S(1)} %get-tuple-element.106), channel_id=1, source_target_pairs={{0,1},{1,0},{2,3},{3,2},{4,5},{5,4},{6,7},{7,6},{8,9},{9,8},{10,11... | collective-permute-start | bytes 393224 | tf_op jit(solution)/shard_map/merge_sum/ppermute | solution.py:750
  104.5 1.6 %collective-permute-start.12 = (bf16[16,1,32,128]{3,2,1,0:T(8,128)(2,1)S(1)}, bf16[16,1,32,128]{3,2,1,0:T(8,128)(2,1)S(1)}, u32[]{:S(2)}, u32[]{:S(2)}) collective-permute-start(bf16[16,1,32,128]{3,2,1,0:T(8,128)(2,1)S(1)} %get-tuple-element.111), channel_id=1, source_target_pairs={{0,1},{1,0},{2,3},{3,2},{4,5},{5,4},{6,7},{7,6},{8,9},{9,8},{10,11... | collective-permute-start | bytes 393224 | tf_op jit(solution)/shard_map/merge_sum/ppermute | solution.py:750
  115.6 15.4 %all-to-all-start.4 = ((bf16[16,2,32,128]{3,2,1,0:T(8,128)(2,1)}), bf16[16,2,32,128]{3,2,1,0:T(8,128)(2,1)S(1)}, u32[]{:S(2)}, u32[]{:S(2)}) async-start(bf16[16,2,32,128]{3,2,1,0:T(8,128)(2,1)} %get-tuple-element.115), calls=%async_computation.4 | async-start | bytes 524288 | tf_op jit(solution)/shard_map/branch_sum/all_to_all | solution.py:950
  119.8 0.7 copy-start.3
  120.5 5.9 %collective-permute-start.16 = (bf16[144,256]{1,0:T(8,128)(2,1)S(1)}, bf16[144,256]{1,0:T(8,128)(2,1)S(1)}, u32[]{:S(2)}, u32[]{:S(2)}) collective-permute-start(bf16[144,256]{1,0:T(8,128)(2,1)S(1)} %get-tuple-element.121), channel_id=1, source_target_pairs={{0,8},{1,3},{2,10},{3,1},{4,12},{5,7},{6,14},{7,5},{8,0},{9,11},{1... | collective-permute-start | bytes 221192 | tf_op jit(solution)/shard_map/merge_sum/ppermute | solution.py:746
  122.3 8.7 %collective-permute-start.17 = (bf16[144,256]{1,0:T(8,128)(2,1)S(1)}, bf16[144,256]{1,0:T(8,128)(2,1)S(1)}, u32[]{:S(2)}, u32[]{:S(2)}) collective-permute-start(bf16[144,256]{1,0:T(8,128)(2,1)S(1)} %get-tuple-element.122), channel_id=1, source_target_pairs={{0,16},{1,5},{2,18},{3,7},{4,20},{5,1},{6,22},{7,3},{8,24},{9,13},... | collective-permute-start | bytes 221192 | tf_op jit(solution)/shard_map/merge_sum/ppermute | solution.py:746
  124.7 6.3 %collective-permute-start.18 = (bf16[144,256]{1,0:T(8,128)(2,1)S(1)}, bf16[144,256]{1,0:T(8,128)(2,1)S(1)}, u32[]{:S(2)}, u32[]{:S(2)}) collective-permute-start(bf16[144,256]{1,0:T(8,128)(2,1)S(1)} %get-tuple-element.123), channel_id=1, source_target_pairs={{0,24},{1,7},{2,26},{3,5},{4,28},{5,3},{6,30},{7,1},{8,16},{9,15},... | collective-permute-start | bytes 221192 | tf_op jit(solution)/shard_map/merge_sum/ppermute | solution.py:746
  133.7 11.9 %all-to-all-start.5 = ((f32[32,8,128]{2,1,0:T(8,128)}), f32[32,8,128]{2,1,0:T(8,128)S(1)}, u32[]{:S(2)}, u32[]{:S(2)}) async-start(f32[32,8,128]{2,1,0:T(8,128)} %get-tuple-element.126), calls=%async_computation.5 | async-start | bytes 262144 | tf_op jit(solution)/shard_map/all_to_all | solution.py:754
  137.4 1.5 collective-permute-start.19

commit v4 on v3

--- a/solution.py
+++ b/solution.py
@@ -217,7 +217,7 @@
         fix_ref[i] = block
 
 
-def stats_kernel(count, pos_ref, gram_ref, wb_ref, own_ref, coef_ref, mu_ref, wt_ref, fix_ref):
+def stats_kernel(count, pos_ref, gram_ref, wb_ref, own_ref, ws_ref, coef_ref, mu_ref, wt_ref, fix_ref):
     own_stats(count, pos_ref[1], gram_ref, own_ref, fix_ref)
     hid = wb_ref.shape[1]
     small = jnp.transpose(wb_ref[HOPS].astype(F32))
@@ -248,23 +248,32 @@
         inv = lax.rsqrt(second - mean * mean + EPS_NORM)
         gain, shift, slope, join = at(k), at(HOPS + k), at(2 * HOPS + k), at(3 * HOPS + k)
         v = gain * inv
+        half = 0.5 * v
+        scaled = jnp.where(
+            lax.broadcasted_iota(jnp.int32, wide.shape, 0) == ONE, 0.5 * shift - half * mean, half * wide
+        )
+        scaled = jnp.transpose(scaled)
+        high = scaled.astype(BF16)
+        ws_ref[k, :, 0:LANES] = high
+        ws_ref[k, :, LANES : 2 * LANES] = (scaled - high.astype(F32)).astype(BF16)
+        scale = 0.5 * (1.0 - join)
         coef_ref[k] = columns(
             (
-                0.5 * v,
-                0.5 * (shift - v * mean),
                 0.5 * (1.0 + slope),
                 0.5 * (1.0 - slope),
                 1.0 + join,
                 1.0 - join,
-                join,
-                0.5 * (1.0 - join),
-                v * slope,
-                0.5 * v * (1.0 - slope),
-                mean,
-                inv,
-                v,
+                join / scale,
+                scale,
+                scale * v * slope,
+                scale * 0.5 * v * (1.0 - slope),
             )
         )
+
+
+def project_units(ws_ref, x_ref, k, rows):
+    x = x_ref[k]
+    return dot(ws_ref[k, rows, :], jnp.concatenate([x, x], axis=0), 1, 0)
 
 
 def column_set(ref, hop, at, lanes):
@@ -277,28 +286,29 @@
 
 
 def forward_kernel(
-    x_ref, wb_ref, coef_ref, wm_hbm, joined_ref, pre2_ref, pay_ref, pre, wm_ref, in_sems
+    x_ref, ws_ref, coef_ref, wt_ref, fix_ref, wm_hbm, joined_ref, pre2_ref, pay_ref, wt_out, fix_out, pre, wm_ref, sems
 ):
-    wait = fetch((wm_hbm,), (wm_ref,), in_sems)
-    hid = wb_ref.shape[1]
+    wait = fetch((wm_hbm,), (wm_ref,), sems.at[pl.ds(2, 1)])
+    stored = fetch((wt_ref, fix_ref), (wt_out, fix_out), sems)
+    hid = ws_ref.shape[1]
     batch = x_ref.shape[2]
     per = hid // CHUNK
     jobs = [(k, c) for k in range(HOPS) for c in range(per)]
 
     def project(i):
         k, c = jobs[i]
-        pre[i % 2] = dot(wb_ref[k, c * CHUNK : (c + 1) * CHUNK, :], x_ref[k], 1, 0)
+        pre[i % 2] = project_units(ws_ref, x_ref, k, slice(c * CHUNK, (c + 1) * CHUNK))
 
     def units(i):
         k, c = jobs[i]
         for g in range(CHUNK // ROWS):
             at = slice(c * CHUNK + g * ROWS, c * CHUNK + (g + 1) * ROWS)
-            cs = column_set(coef_ref, k, at, range(6))
+            cs = column_set(coef_ref, k, at, range(4))
             for b in range(batch // WIDE):
                 lanes = slice(b * WIDE, (b + 1) * WIDE)
-                u = pre[i % 2, g * ROWS : (g + 1) * ROWS, lanes] * cs[0] + cs[1]
-                u = u * (cs[2] + cs[3] * jnp.tanh(u))
-                joined_ref[k, at, lanes] = (u * (cs[4] + cs[5] * jnp.tanh(u))).astype(BF16)
+                u = pre[i % 2, g * ROWS : (g + 1) * ROWS, lanes]
+                u = u * (cs[0] + cs[1] * jnp.tanh(u))
+                joined_ref[k, at, lanes] = (u * (cs[2] + cs[3] * jnp.tanh(u))).astype(BF16)
 
     project(0)
     for i in range(len(jobs)):
@@ -317,6 +327,7 @@
     value = pre2_ref[...]
     sums = jnp.concatenate([lane_sums(fold_lanes(value)), lane_sums(fold_lanes(value * value))], axis=0)
     pay_ref[...] = jnp.broadcast_to(sums[None], pay_ref.shape)
+    stored()
 
 
 def par_columns(wb_ref):
@@ -409,8 +420,9 @@
 
 
 def turn_kernel(
-    count, pos_ref, got_ref, stat_ref, wb_ref, pre2_ref, dy2_ref, joined_ref, class_ref, dpre_ref, keep_ref, send_ref, sum2_ref, cols
+    count, pos_ref, got_ref, stat_ref, wb_ref, pre2_ref, dy2_ref, joined_ref, class_ref, wm_hbm, dpre_ref, keep_ref, send_ref, sum2_ref, wm_ref, cols, sems
 ):
+    wait = fetch((wm_hbm,), (wm_ref,), sems)
     hid, batch = dy2_ref.shape
     half = send_ref.shape[2]
     rows8 = jnp.sum(got_ref[...], axis=0)
@@ -447,15 +459,16 @@
         wide = jnp.concatenate([block[: cb // 2], block[cb // 2 :]], axis=1)
         send_ref[s, mr:size, :] = jnp.where(first, 0.0, wide).astype(BF16)
         keep_ref[s, mr:size, :] = jnp.where(first, wide, 0.0)
+    wait()
 
 
 SMALLS = 4
 
 
-def back_kernel(own, first, count, pos_ref, dpre_ref, x_ref, wb_ref, coef_ref, mu_ref, wt_hbm, wm_hbm, *refs):
+def back_kernel(own, first, count, pos_ref, dpre_ref, x_ref, ws_ref, coef_ref, mu_ref, wm_ref, wt_hbm, *refs):
     if own:
         recv_refs, refs = refs[:count], refs[count:]
-    b_ref, a_out, pre, dj, dyv, sums, a_ref, wm_ref, wt_ref, sems, out_sems = refs
+    b_ref, a_out, pre, dj, dyv, sums, a_ref, wt_ref, out_sems = refs
     hid = wt_ref.shape[2]
     batch = x_ref.shape[2]
     per = hid // CHUNK
@@ -463,38 +476,33 @@
     base = 2 * (pos_ref[1] if own else 1 - pos_ref[1]) + first
     dp, _, cb, _ = b_ref.shape
     copies = []
-    waits = []
     wait_wt = fetch((wt_hbm.at[pl.ds(base, count)],), (wt_ref,), out_sems.at[pl.ds(count, 1)])
-    for i, (k, c) in enumerate(jobs):
-        at = pl.ds(pl.multiple_of((base + k) * hid + c * CHUNK, CHUNK), CHUNK)
-        rows = pl.ds(c * CHUNK, CHUNK)
-        waits.append(fetch((wm_hbm.at[:, at, :],), (wm_ref.at[k, :, rows, :],), sems.at[pl.ds(i, 1)]))
 
     def project(i):
         k, c = jobs[i]
         rows = slice(c * CHUNK, (c + 1) * CHUNK)
-        pre[i % 2] = dot(wb_ref[base + k, rows, :], x_ref[base + k], 1, 0)
-        waits[i]()
-        dj[i % 2] = dot(merge_block(wm_ref.at[k], rows), dpre_ref[...], 1, 0)
+        pre[i % 2] = project_units(ws_ref, x_ref, base + k, rows)
+        at = pl.ds(pl.multiple_of((base + k) * hid + c * CHUNK, CHUNK), CHUNK)
+        dj[i % 2] = dot(merge_block(wm_ref, at), dpre_ref[...], 1, 0)
 
     def units(i):
         k, c = jobs[i]
         for g in range(CHUNK // ROWS):
             at = slice(c * CHUNK + g * ROWS, c * CHUNK + (g + 1) * ROWS)
             here = slice(g * ROWS, (g + 1) * ROWS)
-            a1, b1, p1, q1, s2, q2, s1, r1 = column_set(coef_ref, base + k, at, (0, 1, 2, 3, 6, 7, 8, 9))
+            p1, q1, s2, s1, r1 = column_set(coef_ref, base + k, at, (0, 1, 4, 6, 7))
             one = jnp.zeros((ROWS, WIDE), F32)
             two = jnp.zeros((ROWS, WIDE), F32)
             for b in range(batch // WIDE):
                 lanes = slice(b * WIDE, (b + 1) * WIDE)
-                u = pre[i % 2, here, lanes] * a1 + b1
+                u = pre[i % 2, here, lanes]
                 t = jnp.tanh(u)
                 u2 = u * (p1 + q1 * t)
                 t2 = jnp.tanh(u2)
                 d = dj[i % 2, here, lanes]
                 w = u2 * (1.0 - t2)
                 two = two + d * w
-                d = d * (s2 + q2 * ((1.0 + t2) * (1.0 + w)))
+                d = d * (s2 + (1.0 + t2) * (1.0 + w))
                 w = u * (1.0 - t)
                 one = one + d * w
                 dyv[k, at, lanes] = (d * (s1 + r1 * ((1.0 + t) * (1.0 + w)))).astype(BF16)
@@ -515,7 +523,7 @@
         smalls = (
             total,
             jnp.sum(block * w.astype(F32), axis=0, keepdims=True),
-            jnp.sum(jnp.transpose(sums[k, 0]), axis=0, keepdims=True),
+            jnp.sum(jnp.transpose(sums[k, 0] * coef_ref[base + k, :, 5:6]), axis=0, keepdims=True),
             jnp.sum(jnp.transpose(sums[k, 1]), axis=0, keepdims=True),
         )
         for i, value in enumerate(smalls):
@@ -585,6 +593,7 @@
     def all_sum(v):
         return jnp.sum(jnp.sum(v, axis=1, keepdims=True), axis=0, keepdims=True)
 
+    others = w1_ref[...].astype(F32) + w2_ref[...].astype(F32) + w3_ref[...].astype(F32)
     wait()
     for i in range(2):
         b = join_smalls(total[i])
@@ -603,7 +612,7 @@
         squares = squares + all_sum(fixed * fixed)
         spread = jnp.where(lane == 2 * i, alpha, spread)
         spread = jnp.where(lane == 2 * i + 1, beta, spread)
-    wide = w0_ref[...].astype(F32) + w1_ref[...].astype(F32) + w2_ref[...].astype(F32) + w3_ref[...].astype(F32)
+    wide = w0_ref[...].astype(F32) + others
     mr = wide.shape[0] - cb // 2
     merge = wide[:mr]
     squares = squares + all_sum(merge * merge)
@@ -618,13 +627,12 @@
     block = jnp.where(lane == PCOL + 3, shift_own, block)
     grad_ref[at : at + cb, :] = block
     squares = squares + jnp.where(rep == 0, all_sum(block * block), 0.0)
-    spread = jnp.where(lane == 4, jnp.broadcast_to(squares, spread.shape), spread)
     rows = jnp.transpose(jnp.concatenate([spread, jnp.zeros((LANES - cb, LANES), F32)], axis=0))[0:8]
-    offset = (pos_ref[0] * cb) % LANES
-    rows = pltpu.roll(rows, offset, 1)
-    row8 = lax.broadcasted_iota(jnp.int32, rows.shape, 0)
-    rows = jnp.where((row8 == 4) & (lane_of(rows.shape) != offset), 0.0, rows)
-    pay_ref[...] = jnp.broadcast_to(rows[None], pay_ref.shape)
+    packed = jnp.concatenate([rows[i : i + 1, :cb] for i in range(4)], axis=1)
+    if 4 * cb < LANES:
+        packed = jnp.concatenate([packed, jnp.zeros((1, LANES - 4 * cb), F32)], axis=1)
+    pay = jnp.concatenate([packed, jnp.where(lane_of((1, LANES)) == 0, squares, 0.0)], axis=0)
+    pay_ref[...] = jnp.broadcast_to(pay[None], pay_ref.shape)
 
 
 def own_column(ref, first, me, cb):
@@ -653,35 +661,41 @@
 
 
 def final_kernel(pos_ref, got_ref, mine_ref, other_ref, x_ref, wt_hbm, own_hbm, sent0_hbm, sent1_hbm, *refs):
-    states_hbm, refs = refs[:12], refs[12:]
-    outs, norm_ref, rows_ref = refs[:16], refs[16], refs[17]
-    wt_ref, own_ref, sent_ref = refs[18:21]
-    states, sems, more = refs[21:33], refs[33], refs[34]
+    states_hbm, outs_hbm, norm_ref, rows_hbm = refs[:12], refs[12:28], refs[28], refs[29]
+    wt_ref, own_ref, sent_ref = refs[30:33]
+    states, outs, rows_ref, sems, more, out_sems = refs[33:45], refs[45:61], refs[61], refs[62], refs[63], refs[64]
+    wait_wt = fetch((wt_hbm,), (wt_ref,), more)
     wait_rows = fetch(
-        (wt_hbm, own_hbm, sent0_hbm, sent1_hbm),
-        (wt_ref, own_ref, sent_ref.at[pl.ds(0, 1)], sent_ref.at[pl.ds(1, 1)]),
-        more,
+        (own_hbm, sent0_hbm, sent1_hbm),
+        (own_ref, sent_ref.at[pl.ds(0, 1)], sent_ref.at[pl.ds(1, 1)]),
+        more.at[pl.ds(1, 3)],
     )
     wait = fetch(states_hbm, states, sems)
     weights, firsts, seconds = states[0:4], states[4:8], states[8:12]
-    dp = got_ref.shape[0] // 2
+    n = got_ref.shape[0]
+    cb = weights[0].shape[1]
     blocks = 4
-    per = dp // blocks
-    parts = []
-    for b in range(blocks):
-        for r in range(2):
-            total = got_ref[(b * per) * 2 + r]
-            for i in range(1, per):
-                total = total + got_ref[(b * per + i) * 2 + r]
-            parts.append(total)
-    squares = parts[0][4:5, :]
-    for part in parts[1:]:
-        squares = squares + part[4:5, :]
+    per = n // 2 // blocks
+    lane = lane_of((blocks, LANES))
+    parts = [[jnp.zeros((blocks, LANES), F32) for _ in range(4)] for _ in range(2)]
+    for r in range(2):
+        for j in range(per):
+            rows = [got_ref[(b * per + j) * 2 + r, 0:1, :] for b in range(blocks)]
+            rows = jnp.concatenate(rows, axis=0)
+            here = (lane >= j * cb) & (lane < (j + 1) * cb)
+            for i in range(4):
+                shift = (j - i) * cb % LANES
+                moved = pltpu.roll(rows, shift, 1) if shift else rows
+                parts[r][i] = jnp.where(here, moved, parts[r][i])
+
+    def spread_row(r, i):
+        return jnp.concatenate([parts[r][i][b : b + 1] for b in range(blocks)], axis=1)
+
+    squares = jnp.sum(got_ref[...], axis=0)[1:2, :]
     norm = jnp.sqrt(jnp.sum(squares, axis=1, keepdims=True))
     norm_ref[...] = norm
     scale = 1.0 / jnp.maximum(norm, 1.0)
 
-    cb = weights[0].shape[1]
     d_in = weights[0].shape[2]
     mr = weights[1].shape[0]
     classes = weights[2].shape[1]
@@ -689,22 +703,27 @@
     mine, other = mine_ref[...], other_ref[...]
     low = jnp.where(first, mine, other)
     high = jnp.where(first, other, mine)
-    wait_rows()
-
+    stores = []
+    fixes = []
+    wait_wt()
     for k in range(HOPS):
         r, i = k // 2, k % 2
-        alpha = jnp.concatenate([parts[b * 2 + r][2 * i : 2 * i + 1] for b in range(blocks)], axis=1)
-        beta = jnp.concatenate([parts[b * 2 + r][2 * i + 1 : 2 * i + 2] for b in range(blocks)], axis=1)
+        alpha, beta = spread_row(r, 2 * i), spread_row(r, 2 * i + 1)
         low_w = wt_ref[k]
         right = jnp.where(lax.broadcasted_iota(jnp.int32, low_w.shape, 0) == ONE, alpha, low_w.astype(F32) * beta)
-        hi = right.astype(BF16)
-        fix = dot(low_w, hi, 1, 1) + dot(low_w, (right - hi.astype(F32)).astype(BF16), 1, 1)
-        hi = fix.astype(BF16)
-        lo = (fix - hi.astype(F32)).astype(BF16)
-        kept = pos_ref[1] == r
-        value = jnp.where(kept, own_ref[i], sent_ref[i])
-        value = value - (dot(hi, x_ref[k], 1, 0) + dot(lo, x_ref[k], 1, 0))
+        high_part = right.astype(BF16)
+        fix = dot(low_w, high_part, 1, 1) + dot(low_w, (right - high_part.astype(F32)).astype(BF16), 1, 1)
+        high_part = fix.astype(BF16)
+        fixes.append(jnp.concatenate([high_part, (fix - high_part.astype(F32)).astype(BF16)], axis=1))
+    wait_rows()
+    for k in range(HOPS):
+        r, i = k // 2, k % 2
+        value = jnp.where(pos_ref[1] == r, own_ref[i], sent_ref[i])
+        value = value - dot(fixes[k], jnp.concatenate([x_ref[k], x_ref[k]], axis=0), 1, 0)
         rows_ref[k * d_in : (k + 1) * d_in, :] = value[:d_in]
+        if i == 1:
+            part = pl.ds(r * 2 * d_in, 2 * d_in)
+            stores.append(fetch((rows_ref.at[part, :],), (rows_hbm.at[part, :],), out_sems.at[pl.ds(16 + r, 1)]))
 
     def group(i):
         return [o for o in outs[i::4]]
@@ -731,6 +750,9 @@
         small = jnp.where(lane == 4 * HOPS + i, block[:, PCOL + source : PCOL + source + 1], small)
     small = jnp.transpose(jnp.concatenate([small, jnp.zeros((LANES - cb, LANES), F32)], axis=0))
     adam_into(weights[3], firsts[3], seconds[3], small[: weights[3].shape[0], :cb], scale, 0.3, group(3))
+    stores.append(fetch(outs, outs_hbm, out_sems))
+    for done in stores:
+        done()
 
 
 def flip(value, mask, dp):
@@ -815,13 +837,13 @@
             ),
             scratch=[pltpu.VMEM((width, batch), F32), pltpu.VMEM((LANES, batch), F32)],
             flops=2 * nodes * width * batch,
-            after=(block,) if staged else (),
+            after=(own,) if staged else (),
             mib=24,
         )
     with jax.named_scope("gram_sum"):
         parts = gram.reshape(n, HOPS * LANES // n, LANES)
         if staged:
-            (stacked,) = call(stack_kernel, [sds((4,) + block.shape, BF16)], block, *far, after=(gram,))
+            (stacked,) = call(stack_kernel, [sds((4,) + block.shape, BF16)], block, *far)
             parts, stacked = lax.optimization_barrier((parts, stacked))
         parts = exchange(parts)
         (parts,) = call(sum_spread_kernel, [hbm_out(parts.shape)], parts)
@@ -839,29 +861,31 @@
     else:
         own, wb, wm = weights_plain(lhs[0], weights[2], weights[3], weights[1], dp)
     with jax.named_scope("stats"):
-        coef, mu, wt, fix = call(
+        ws, coef, mu, wt, fix = call(
             functools.partial(stats_kernel, count),
             [
+                vmem((HOPS, hid, 2 * LANES), BF16),
                 vmem((HOPS, hid, LANES)),
                 vmem((8, LANES)),
-                hbm_out((HOPS, LANES, hid), BF16),
-                hbm_out((2, cb, LANES)),
+                vmem((HOPS, LANES, hid), BF16),
+                vmem((2, cb, LANES)),
             ],
             pos, gram, wb, own,
             smem=(0,),
         )
     with jax.named_scope("forward"):
-        joined, pre2, pay = call(
+        joined, pre2, pay, wt, fix = call(
             forward_kernel,
-            [vmem((HOPS, hid, batch), BF16), vmem((hid, batch)), sds((n, 8, LANES))],
-            x, wb, coef, wm,
-            hbm=(3,),
+            [vmem((HOPS, hid, batch), BF16), vmem((hid, batch)), sds((n, 8, LANES))]
+            + [hbm_out(v.shape, v.dtype) for v in (wt, fix)],
+            x, ws, coef, wt, fix, wm,
+            hbm=(5,),
+            out_specs=tuple(pl.BlockSpec(memory_space=m) for m in (pltpu.VMEM,) * 3 + (pltpu.HBM,) * 2),
             scratch=[
                 pltpu.VMEM((2, CHUNK, batch), F32),
                 pltpu.VMEM(wm.shape, BF16),
-                pltpu.SemaphoreType.DMA((1,)),
+                pltpu.SemaphoreType.DMA((3,)),
             ],
-            mib=16,
         )
     got = exchange(pay)
     with jax.named_scope("head"):
@@ -883,12 +907,18 @@
     got = exchange(pay)
     with jax.named_scope("turn"):
         rows = mr + cb // 2
-        dpre, keep, send, sum2 = call(
+        dpre, keep, send, sum2, wm = call(
             functools.partial(turn_kernel, count),
-            [vmem((hid, batch), BF16), sds((dp, rows, half)), sds((dp, rows, half), BF16), vmem((8, LANES))],
-            pos, got, stat, wb, pre2, dy2, joined, block2,
-            smem=(0,),
-            scratch=[pltpu.VMEM((3, hid, LANES), F32)],
+            [
+                vmem((hid, batch), BF16),
+                sds((dp, rows, half)),
+                sds((dp, rows, half), BF16),
+                vmem((8, LANES)),
+                vmem(wm.shape, BF16),
+            ],
+            pos, got, stat, wb, pre2, dy2, joined, block2, wm,
+            smem=(0,), hbm=(8,),
+            scratch=[pltpu.VMEM((3, hid, LANES), F32), pltpu.SemaphoreType.DMA((1,))],
             flops=2 * batch * HOPS * hid * hid,
         )
 
@@ -898,9 +928,9 @@
             return call(
                 functools.partial(back_kernel, own_hops, first, num),
                 outs,
-                pos, dpre, x, wb, coef, mu, wt, wm, *more,
+                pos, dpre, x, ws, coef, mu, wm, wt, *more,
                 smem=(0,),
-                hbm=(6, 7),
+                hbm=(7,),
                 after=after,
                 out_specs=(pl.BlockSpec(memory_space=pltpu.VMEM), pl.BlockSpec(memory_space=pltpu.HBM)),
                 scratch=[
@@ -909,9 +939,7 @@
                     pltpu.VMEM((num, hid, batch), BF16),
                     pltpu.VMEM((num, 2, hid, LANES), F32),
                     pltpu.VMEM((num, LANES, batch), F32),
-                    pltpu.VMEM((num, hid // LANES, hid, LANES), BF16),
                     pltpu.VMEM((num, LANES, hid), BF16),
-                    pltpu.SemaphoreType.DMA((num * hid // CHUNK,)),
                     pltpu.SemaphoreType.DMA((num + 1,)),
                 ],
                 mib=16,
@@ -952,7 +980,7 @@
         late = (wide[0], fix)
         shares, pay = call(
             functools.partial(owner_kernel, count, classes),
-            [sds((3 * cb + 2 * mr, LANES)), hbm_out((n, 8, LANES))],
+            [sds((3 * cb + 2 * mr, LANES)), hbm_out((n, 2, LANES))],
             pos, got_b, sum2, *wide[1:], *late,
             smem=(0,),
             hbm=(6, 7),
@@ -971,8 +999,10 @@
         res = call(
             final_kernel, outs, pos, got, shares, theirs, x, wt, kept_a, sent[0][1], sent[1][1], *local,
             smem=(0,), hbm=tuple(range(5, 9 + len(local))),
+            out_specs=tuple(pl.BlockSpec(memory_space=pltpu.VMEM if i == 16 else pltpu.HBM) for i in range(18)),
             scratch=[pltpu.VMEM(v.shape, v.dtype) for v in (wt, kept_a, kept_a) + local]
-            + [pltpu.SemaphoreType.DMA((len(local),)), pltpu.SemaphoreType.DMA((4,))],
+            + [pltpu.VMEM(v.shape, v.dtype) for i, v in enumerate(outs) if i != 16]
+            + [pltpu.SemaphoreType.DMA((k,)) for k in (len(local), 4, 18)],
             flops=2 * batch * LANES * LANES * 3 * HOPS,
         )
     result = list(res[:16])

time: 153 us -> 147 us (0.961)
  blocking collectives: 22.3 us -> 33.2 us
  waiting for transfers between devices: 33.5 us -> 25.6 us
  Pallas kernels: 58.4 us -> 54.3 us
  starting transfers between devices: 35.2 us -> 31.3 us
    all_to_all x2 -> x3, blocking collectives: 22.3 us -> 33.2 us  [exchange(): return lax.all_to_all(value, BOTH, 0, 0, tiled=True)]
    all_to_all x3 -> x2, waiting for transfers between devices: 13.9 us -> 7.11 us  [exchange(): return lax.all_to_all(value, BOTH, 0, 0, tiled=True)]
    pallas_call x16, Pallas kernels: 58.4 us -> 54.3 us  [call(): pl.pallas_call(kernel, out_shape=tuple(outs), in_specs=in_specs, out_spec...]
    all_to_all x3 -> x2, starting transfers between devices: 12.2 us -> 8.58 us  [exchange(): return lax.all_to_all(value, BOTH, 0, 0, tiled=True)]
  transfers between devices with their start and end apart: 24 -> 23, of which waited for: 13 -> 11; matrix products, arithmetic and copies ran while one was open for 0% -> 0% of each run, Pallas kernels for 20% -> 19%
where the time goes in v4:
time: 147 us; the launch traced here: 146 us
  Pallas kernels  54.3 us (37%)
  blocking collectives  33.2 us (23%)
  starting transfers between devices  31.3 us (21%)
  waiting for transfers between devices  25.6 us (17%)
    pallas_call x16, Pallas kernels, call(): pl.pallas_call(kernel, out_shape=tuple(outs), in_specs=in_specs, out_spec...  54.3 us
    all_to_all x3, blocking collectives, exchange(): return lax.all_to_all(value, BOTH, 0, 0, tiled=True)  33.2 us
    ppermute x6, starting transfers between devices, flip(): return lax.ppermute(value, 'dp', [(i, i ^ mask) for i in range(dp)])  9.31 us
    ppermute x6, waiting for transfers between devices, flip(): return lax.ppermute(value, 'dp', [(i, i ^ mask) for i in range(dp)])  9.21 us
    all_to_all x2, starting transfers between devices, exchange(): return lax.all_to_all(value, BOTH, 0, 0, tiled=True)  8.58 us
    ppermute x6, starting transfers between devices, turn_flip(): return lax.ppermute(value, BOTH, pairs)  7.94 us
    all_to_all x2, waiting for transfers between devices, exchange(): return lax.all_to_all(value, BOTH, 0, 0, tiled=True)  7.11 us
    ppermute x6, waiting for transfers between devices, turn_flip(): return lax.ppermute(value, BOTH, pairs)  6.15 us
  transfers between devices with their start and end apart: 23, of which 11 were waited for; matrix products, arithmetic and copies ran while one was open for 0% of the time, Pallas kernels for 19%

profile of v4, /device:TPU:0, one launch (start us, length us, event | category | flops | bytes accessed | tf_op | source)
XLA Modules:
  0.0 146.2 jit_solution(16532843623166089018)
XLA Ops:
  0.7 2.4 %prep.1 = (bf16[5,32,128]{2,1,0:T(8,128)(2,1)}, bf16[336,128]{1,0:T(8,128)(2,1)S(1)}) custom-call(s32[2]{0:T(128)S(1)} %pad_add_fusion.refs_0_, f32[4,32,100]{2,1,0:T(8,128)} %bitcast.18, f32[32,47]{1,0:T(8,128)} %refs_11_.1, f32[20,32]{1,0:T(8,128)} %refs_12_.1, f32[128,512]{1,0:T(8,128)} %refs_10_.1), custom_call_target="tpu_custom_call" | custom-call | flops 1024 | bytes 1024 | tf_op jit(solution)/shard_map/prep/pallas_call | solution.py:47
  3.1 5.1 %collective-permute-start.2 = (bf16[336,128]{1,0:T(8,128)(2,1)S(1)}, bf16[336,128]{1,0:T(8,128)(2,1)S(1)}, u32[]{:S(2)}, u32[]{:S(2)}) collective-permute-start(bf16[336,128]{1,0:T(8,128)(2,1)S(1)} %get-tuple-element.90.refs_0_), channel_id=1, source_target_pairs={{0,24},{2,26},{4,28},{6,30},{8,16},{10,18},{12,20},{14,22},{16,8},... | collective-permute-start | bytes 258056 | tf_op jit(solution)/shard_map/ppermute | solution.py:759
  8.2 0.6 collective-permute-start
  8.9 7.1 %gather.1 = (bf16[4,128,1024]{2,1,0:T(8,128)(2,1)S(1)}, f32[4,128,128]{2,1,0:T(8,128)}) custom-call(s32[1,1024]{1,0:T(1,128)} %bitcast.24, f32[400,4096]{1,0:T(8,128)} %bitcast.17, bf16[5,32,128]{2,1,0:T(8,128)(2,1)} %get-tuple-element.87.refs_2_.refs_3_), custom_call_target="tpu_custom_call" | custom-call | flops 1024 | bytes 1024 | tf_op jit(solution)/shard_map/gather/pallas_call | solution.py:47
  16.0 6.0 %all-to-all-start = ((f32[32,16,128]{2,1,0:T(8,128)}), f32[32,16,128]{2,1,0:T(8,128)S(1)}, u32[]{:S(2)}, u32[]{:S(2)}) async-start(f32[32,16,128]{2,1,0:T(8,128)} %bitcast.20), calls=%async_computation | async-start | bytes 524288 | tf_op jit(solution)/shard_map/gram_sum/all_to_all | solution.py:776
  22.0 2.7 %collective-permute-start.5 = (bf16[4,336,128]{2,1,0:T(8,128)(2,1)S(1)}, bf16[4,336,128]{2,1,0:T(8,128)(2,1)S(1)}, u32[]{:S(2)}, u32[]{:S(2)}) collective-permute-start(bf16[4,336,128]{2,1,0:T(8,128)(2,1)S(1)} %gram_sum.2.refs_1_), channel_id=1, source_target_pairs={{0,6},{2,4},{4,2},{6,0},{8,14},{10,12},{12,10},{14,8},{16,22},{18,... | collective-permute-start | bytes 1032200 | tf_op jit(solution)/shard_map/ppermute | solution.py:759
  24.8 0.6 collective-permute-start.4
  25.3 0.3 collective-permute-start.3
  25.6 7.1 %all-to-all-done.refs_0_ = f32[32,16,128]{2,1,0:T(8,128)S(1)} async-done(((f32[32,16,128]{2,1,0:T(8,128)}), f32[32,16,128]{2,1,0:T(8,128)S(1)}, u32[]{:S(2)}, u32[]{:S(2)}) %all-to-all-start) | async-done | bytes 262176 | tf_op jit(solution)/shard_map/gram_sum/all_to_all | solution.py:776
  32.7 0.8 gram_sum.3
  33.4 2.6 %all-to-all-start.1 = ((f32[32,16,128]{2,1,0:T(8,128)}), f32[32,16,128]{2,1,0:T(8,128)S(1)}, u32[]{:S(2)}, u32[]{:S(2)}) async-start(f32[32,16,128]{2,1,0:T(8,128)} %gram_sum.3), calls=%async_computation.1 | async-start | bytes 524288 | tf_op jit(solution)/shard_map/gram_sum/all_to_all | solution.py:776
  36.0 0.5 collective-permute-done.5.refs_4_
  36.5 8.4 %collective-permute-done.4.refs_3_ = bf16[4,336,128]{2,1,0:T(8,128)(2,1)S(1)} collective-permute-done((bf16[4,336,128]{2,1,0:T(8,128)(2,1)S(1)}, bf16[4,336,128]{2,1,0:T(8,128)(2,1)S(1)}, u32[]{:S(2)}, u32[]{:S(2)}) %collective-permute-start.4) | collective-permute-done | bytes 344096 | tf_op jit(solution)/shard_map/ppermute | solution.py:759
  44.9 0.3 collective-permute-done.3.refs_2_
  45.2 0.5 collective-permute-start.7
  45.7 0.5 collective-permute-start.9
  46.3 0.6 collective-permute-done.6.refs_5_
  46.9 0.5 collective-permute-done.7.refs_6_
  47.4 0.5 collective-permute-done.8.refs_7_
  47.9 0.5 collective-permute-done.9.refs_8_
  48.4 2.2 %weights.1 = (bf16[5,512,128]{2,1,0:T(8,128)(2,1)S(1)}, bf16[4,2048,128]{2,1,0:T(8,128)(2,1)}) custom-call(s32[2]{0:T(128)S(1)} %pad_add_fusion.refs_0_, bf16[4,336,128]{2,1,0:T(8,128)(2,1)S(1)} %gram_sum.2.refs_1_, bf16[4,336,128]{2,1,0:T(8,128)(2,1)S(1)} %collective-permute-done.3.refs_2_, bf16[4,336,128]{2,1,0:T(8,128)(2,1)S(1)} %collective-permute-done.4.refs_3_, ...), custom_call_target="tpu_custom_call" | custom-call | flops 1024 | bytes 1024 | tf_op jit(solution)/shard_map/weights/pallas_call | solution.py:47
  50.5 2.0 %stats.1 = (bf16[4,512,256]{2,1,0:T(8,128)(2,1)S(1)}, f32[4,512,128]{2,1,0:T(8,128)S(1)}, f32[8,128]{1,0:T(8,128)S(1)}, bf16[4,128,512]{2,1,0:T(8,128)(2,1)S(1)}, f32[2,32,128]{2,1,0:T(8,128)S(1)}) custom-call(s32[2]{0:T(128)S(1)} %pad_add_fusion.refs_0_, f32[4,128,128]{2,1,0:T(8,128)S(1)} %bitcast.16, ...), custom_call_target="tpu_custom_call" | custom-call | flops 1024 | bytes 1024 | tf_op jit(solution)/shard_map/stats/pallas_call | solution.py:47
  52.5 5.9 %forward.1 = (bf16[4,512,1024]{2,1,0:T(8,128)(2,1)S(1)}, f32[512,1024]{1,0:T(8,128)S(1)}, f32[32,8,128]{2,1,0:T(8,128)S(1)}, bf16[4,128,512]{2,1,0:T(8,128)(2,1)}, f32[2,32,128]{2,1,0:T(8,128)}) custom-call(bf16[4,128,1024]{2,1,0:T(8,128)(2,1)S(1)} %get-tuple-element.88.refs_0_.refs_2_.refs_4_, bf16[4,512,256]{2,1,0:T(8,128)(2,1)S(1)} %get-tuple-element.98.refs_1_.refs_3_, ...), custom_call_target="tpu_custom_call" | custom-call | flops 1024 | bytes 1024 | tf_op jit(solution)/shard_map/forward/pallas_call | solution.py:47
  58.4 12.3 %all_to_all.30.refs_0_ = f32[32,8,128]{2,1,0:T(8,128)S(1)} all-to-all(f32[32,8,128]{2,1,0:T(8,128)S(1)} %get-tuple-element.103), channel_id=1, replica_groups=mesh['dp'=16,'rep'=2] {'dp','rep'}, dimensions={0} | all-to-all | bytes 262144 | tf_op jit(solution)/shard_map/all_to_all | solution.py:776
  70.6 3.7 %head.1 = (f32[512,1024]{1,0:T(8,128)S(1)}, f32[32,8,128]{2,1,0:T(8,128)S(1)}, f32[512,128]{1,0:T(8,128)S(1)}, f32[2,512,128]{2,1,0:T(8,128)S(1)}) custom-call(f32[32,8,128]{2,1,0:T(8,128)S(1)} %all_to_all.30.refs_0_, f32[512,1024]{1,0:T(8,128)S(1)} %get-tuple-element.104.refs_1_.refs_4_, bf16[5,512,128]{2,1,0:T(8,128)(2,1)S(1)} %get-tuple-element.97.refs_2_.refs_3_, ...), custom_call_target="tpu_custom_call" | custom-call | flops 1024 | bytes 1024 | tf_op jit(solution)/shard_map/head/pallas_call | solution.py:47
  74.3 10.0 %all_to_all.31.refs_1_ = f32[32,8,128]{2,1,0:T(8,128)S(1)} all-to-all(f32[32,8,128]{2,1,0:T(8,128)S(1)} %get-tuple-element.105), channel_id=1, replica_groups=mesh['dp'=16,'rep'=2] {'dp','rep'}, dimensions={0} | all-to-all | bytes 262144 | tf_op jit(solution)/shard_map/all_to_all | solution.py:776
  84.4 3.6 %turn.1 = (bf16[512,1024]{1,0:T(8,128)(2,1)S(1)}, f32[16,144,256]{2,1,0:T(8,128)S(1)}, bf16[16,144,256]{2,1,0:T(8,128)(2,1)S(1)}, f32[8,128]{1,0:T(8,128)S(1)}, bf16[4,2048,128]{2,1,0:T(8,128)(2,1)S(1)}) custom-call(s32[2]{0:T(128)S(1)} %pad_add_fusion.refs_0_, f32[32,8,128]{2,1,0:T(8,128)S(1)} %all_to_all.31.refs_1_, ...), custom_call_target="tpu_custom_call" | custom-call | flops 1024 | bytes 1024 | tf_op jit(solution)/shard_map/turn/pallas_call | solution.py:47
  88.0 0.3 collective-permute-start.11
  88.3 4.3 %back.3 = (bf16[16,1,32,128]{3,2,1,0:T(8,128)(2,1)S(1)}, f32[1,128,1024]{2,1,0:T(8,128)}) custom-call(s32[2]{0:T(128)S(1)} %pad_add_fusion.refs_0_, bf16[512,1024]{1,0:T(8,128)(2,1)S(1)} %get-tuple-element.110.refs_1_, bf16[4,128,1024]{2,1,0:T(8,128)(2,1)S(1)} %get-tuple-element.88.refs_0_.refs_2_.refs_4_, ...), custom_call_target="tpu_custom_call" | custom-call | flops 1024 | bytes 1024 | tf_op jit(solution)/shard_map/back/pallas_call | solution.py:47
  92.6 0.8 merge_sum.2
  93.4 0.5 collective-permute-start.14
  93.9 1.4 collective-permute-start.15
  95.3 1.7 %collective-permute-start.13 = (bf16[4,144,256]{2,1,0:T(8,128)(2,1)S(1)}, bf16[4,144,256]{2,1,0:T(8,128)(2,1)S(1)}, u32[]{:S(2)}, u32[]{:S(2)}) collective-permute-start(bf16[4,144,256]{2,1,0:T(8,128)(2,1)S(1)} %get-tuple-element.118.refs_8_), channel_id=1, source_target_pairs={{0,2},{1,9},{2,0},{3,11},{4,6},{5,13},{6,4},{7,15},{8,10},{9,1},{1... | collective-permute-start | bytes 884744 | tf_op jit(solution)/shard_map/merge_sum/ppermute | solution.py:768
  97.0 4.3 %back.4 = (bf16[16,1,32,128]{3,2,1,0:T(8,128)(2,1)S(1)}, f32[1,128,1024]{2,1,0:T(8,128)}) custom-call(s32[2]{0:T(128)S(1)} %pad_add_fusion.refs_0_, bf16[512,1024]{1,0:T(8,128)(2,1)S(1)} %get-tuple-element.110.refs_1_, bf16[4,128,1024]{2,1,0:T(8,128)(2,1)S(1)} %get-tuple-element.88.refs_0_.refs_2_.refs_4_, ...), custom_call_target="tpu_custom_call" | custom-call | flops 1024 | bytes 1024 | tf_op jit(solution)/shard_map/merge_sum/back/pallas_call | solution.py:47
  101.3 0.6 collective-permute-start.12
  101.9 1.0 collective-permute-done.12.refs_9_
  102.9 8.6 %back.5 = (bf16[16,2,32,128]{3,2,1,0:T(8,128)(2,1)}, f32[2,128,1024]{2,1,0:T(8,128)}) custom-call(s32[2]{0:T(128)S(1)} %pad_add_fusion.refs_0_, bf16[512,1024]{1,0:T(8,128)(2,1)S(1)} %get-tuple-element.110.refs_1_, bf16[4,128,1024]{2,1,0:T(8,128)(2,1)S(1)} %get-tuple-element.88.refs_0_.refs_2_.refs_4_, ...), custom_call_target="tpu_custom_call" | custom-call | flops 1024 | bytes 1024 | tf_op jit(solution)/shard_map/merge_sum/back/pallas_call | solution.py:47
  111.5 3.5 %all-to-all-start.4 = ((bf16[16,2,32,128]{3,2,1,0:T(8,128)(2,1)}), bf16[16,2,32,128]{3,2,1,0:T(8,128)(2,1)S(1)}, u32[]{:S(2)}, u32[]{:S(2)}) async-start(bf16[16,2,32,128]{3,2,1,0:T(8,128)(2,1)} %get-tuple-element.123), calls=%async_computation.4 | async-start | bytes 524288 | tf_op jit(solution)/shard_map/branch_sum/all_to_all | solution.py:978
  115.1 0.7 merge_sum.3
  115.8 0.7 copy-done.2
  116.4 1.8 %collective-permute-start.16 = (bf16[144,256]{1,0:T(8,128)(2,1)S(1)}, bf16[144,256]{1,0:T(8,128)(2,1)S(1)}, u32[]{:S(2)}, u32[]{:S(2)}) collective-permute-start(bf16[144,256]{1,0:T(8,128)(2,1)S(1)} %get-tuple-element.129), channel_id=1, source_target_pairs={{0,8},{1,3},{2,10},{3,1},{4,12},{5,7},{6,14},{7,5},{8,0},{9,11},{1... | collective-permute-start | bytes 221192 | tf_op jit(solution)/shard_map/merge_sum/ppermute | solution.py:768
  118.3 2.4 %collective-permute-start.17 = (bf16[144,256]{1,0:T(8,128)(2,1)S(1)}, bf16[144,256]{1,0:T(8,128)(2,1)S(1)}, u32[]{:S(2)}, u32[]{:S(2)}) collective-permute-start(bf16[144,256]{1,0:T(8,128)(2,1)S(1)} %get-tuple-element.130), channel_id=1, source_target_pairs={{0,16},{1,5},{2,18},{3,7},{4,20},{5,1},{6,22},{7,3},{8,24},{9,13},... | collective-permute-start | bytes 221192 | tf_op jit(solution)/shard_map/merge_sum/ppermute | solution.py:768
  120.7 0.1 collective-permute-start.18
  120.8 1.5 %collective-permute-done.16.refs_3_ = bf16[144,256]{1,0:T(8,128)(2,1)S(1)} collective-permute-done((bf16[144,256]{1,0:T(8,128)(2,1)S(1)}, bf16[144,256]{1,0:T(8,128)(2,1)S(1)}, u32[]{:S(2)}, u32[]{:S(2)}) %collective-permute-start.16) | collective-permute-done | bytes 73760 | tf_op jit(solution)/shard_map/merge_sum/ppermute | solution.py:768
  122.3 4.6 %collective-permute-done.17.refs_4_ = bf16[144,256]{1,0:T(8,128)(2,1)S(1)} collective-permute-done((bf16[144,256]{1,0:T(8,128)(2,1)S(1)}, bf16[144,256]{1,0:T(8,128)(2,1)S(1)}, u32[]{:S(2)}, u32[]{:S(2)}) %collective-permute-start.17) | collective-permute-done | bytes 73760 | tf_op jit(solution)/shard_map/merge_sum/ppermute | solution.py:768
  127.0 2.5 %owner.1 = (f32[352,128]{1,0:T(8,128)S(1)}, f32[32,2,128]{2,1,0:T(2,128)}) custom-call(s32[2]{0:T(128)S(1)} %pad_add_fusion.refs_0_, bf16[16,2,32,128]{3,2,1,0:T(8,128)(2,1)S(1)} %all-to-all-done.4.refs_1_, f32[8,128]{1,0:T(8,128)S(1)} %get-tuple-element.124.refs_2_, bf16[144,256]{1,0:T(8,128)(2,1)S(1)} %collective-permute-done.16.refs_3_, ...), custom_call_target="tpu_custom_call" | custom-call | flops 1024 | bytes 1024 | tf_op jit(solution)/shard_map/owner/pallas_call | solution.py:47
  129.6 11.0 %all_to_all.32.refs_1_ = f32[32,2,128]{2,1,0:T(2,128)S(1)} all-to-all(f32[32,2,128]{2,1,0:T(2,128)} %get-tuple-element.134), channel_id=1, replica_groups=mesh['dp'=16,'rep'=2] {'dp','rep'}, dimensions={0} | all-to-all | bytes 65536 | tf_op jit(solution)/shard_map/all_to_all | solution.py:776
  140.5 5.5 %final.1 = (f32[4,32,100]{2,1,0:T(8,128)}, f32[128,512]{1,0:T(8,128)}, f32[32,47]{1,0:T(8,128)}, f32[20,32]{1,0:T(8,128)}, f32[4,32,100]{2,1,0:T(8,128)}, /*inde...) custom-call(s32[2]{0:T(128)S(1)} %pad_add_fusion.refs_0_, ...), custom_call_target="tpu_custom_call" | custom-call | flops 1024 | bytes 1024 | tf_op jit(solution)/shard_map/final/pallas_call | solution.py:47
  (24 shorter events, 0.2 us)
Async XLA Ops:
  3.1 12.9 %collective-permute-start.2 = (bf16[336,128]{1,0:T(8,128)(2,1)S(1)}, bf16[336,128]{1,0:T(8,128)(2,1)S(1)}, u32[]{:S(2)}, u32[]{:S(2)}) collective-permute-start(bf16[336,128]{1,0:T(8,128)(2,1)S(1)} %get-tuple-element.90.refs_0_), channel_id=1, source_target_pairs={{0,24},{2,26},{4,28},{6,30},{8,16},{10,18},{12,20},{14,22},{16,8},... | collective-permute-start | bytes 258056 | tf_op jit(solution)/shard_map/ppermute | solution.py:759
  8.2 7.8 %collective-permute-start.1 = (bf16[336,128]{1,0:T(8,128)(2,1)S(1)}, bf16[336,128]{1,0:T(8,128)(2,1)S(1)}, u32[]{:S(2)}, u32[]{:S(2)}) collective-permute-start(bf16[336,128]{1,0:T(8,128)(2,1)S(1)} %get-tuple-element.90.refs_0_), channel_id=1, source_target_pairs={{0,16},{2,18},{4,20},{6,22},{8,24},{10,26},{12,28},{14,30},{16,0},... | collective-permute-start | bytes 258056 | tf_op jit(solution)/shard_map/ppermute | solution.py:759
  8.2 7.8 %collective-permute-start = (bf16[336,128]{1,0:T(8,128)(2,1)S(1)}, bf16[336,128]{1,0:T(8,128)(2,1)S(1)}, u32[]{:S(2)}, u32[]{:S(2)}) collective-permute-start(bf16[336,128]{1,0:T(8,128)(2,1)S(1)} %get-tuple-element.90.refs_0_), channel_id=1, source_target_pairs={{0,8},{2,10},{4,12},{6,14},{8,0},{10,2},{12,4},{14,6},{16,24},{18,... | collective-permute-start | bytes 258056 | tf_op jit(solution)/shard_map/ppermute | solution.py:759
  16.0 34.5 %copy-start.1 = (bf16[5,32,128]{2,1,0:T(8,128)(2,1)S(1)}, bf16[5,32,128]{2,1,0:T(8,128)(2,1)}, u32[]{:S(2)}) copy-start(bf16[5,32,128]{2,1,0:T(8,128)(2,1)} %get-tuple-element.87.refs_2_.refs_3_) | copy-start | bytes 122884
  16.0 16.7 %all-to-all-start = ((f32[32,16,128]{2,1,0:T(8,128)}), f32[32,16,128]{2,1,0:T(8,128)S(1)}, u32[]{:S(2)}, u32[]{:S(2)}) async-start(f32[32,16,128]{2,1,0:T(8,128)} %bitcast.20), calls=%async_computation | async-start | bytes 524288 | tf_op jit(solution)/shard_map/gram_sum/all_to_all | solution.py:776
  22.0 14.5 %collective-permute-start.5 = (bf16[4,336,128]{2,1,0:T(8,128)(2,1)S(1)}, bf16[4,336,128]{2,1,0:T(8,128)(2,1)S(1)}, u32[]{:S(2)}, u32[]{:S(2)}) collective-permute-start(bf16[4,336,128]{2,1,0:T(8,128)(2,1)S(1)} %gram_sum.2.refs_1_), channel_id=1, source_target_pairs={{0,6},{2,4},{4,2},{6,0},{8,14},{10,12},{12,10},{14,8},{16,22},{18,... | collective-permute-start | bytes 1032200 | tf_op jit(solution)/shard_map/ppermute | solution.py:759
  24.8 20.1 %collective-permute-start.4 = (bf16[4,336,128]{2,1,0:T(8,128)(2,1)S(1)}, bf16[4,336,128]{2,1,0:T(8,128)(2,1)S(1)}, u32[]{:S(2)}, u32[]{:S(2)}) collective-permute-start(bf16[4,336,128]{2,1,0:T(8,128)(2,1)S(1)} %gram_sum.2.refs_1_), channel_id=1, source_target_pairs={{0,4},{2,6},{4,0},{6,2},{8,12},{10,14},{12,8},{14,10},{16,20},{18,... | collective-permute-start | bytes 1032200 | tf_op jit(solution)/shard_map/ppermute | solution.py:759
  25.3 19.9 %collective-permute-start.3 = (bf16[4,336,128]{2,1,0:T(8,128)(2,1)S(1)}, bf16[4,336,128]{2,1,0:T(8,128)(2,1)S(1)}, u32[]{:S(2)}, u32[]{:S(2)}) collective-permute-start(bf16[4,336,128]{2,1,0:T(8,128)(2,1)S(1)} %gram_sum.2.refs_1_), channel_id=1, source_target_pairs={{0,2},{2,0},{4,6},{6,4},{8,10},{10,8},{12,14},{14,12},{16,18},{18,... | collective-permute-start | bytes 1032200 | tf_op jit(solution)/shard_map/ppermute | solution.py:759
  33.4 17.1 %all-to-all-start.1 = ((f32[32,16,128]{2,1,0:T(8,128)}), f32[32,16,128]{2,1,0:T(8,128)S(1)}, u32[]{:S(2)}, u32[]{:S(2)}) async-start(f32[32,16,128]{2,1,0:T(8,128)} %gram_sum.3), calls=%async_computation.1 | async-start | bytes 524288 | tf_op jit(solution)/shard_map/gram_sum/all_to_all | solution.py:776
  45.2 1.7 %collective-permute-start.6 = (bf16[4,336,128]{2,1,0:T(8,128)(2,1)S(1)}, bf16[4,336,128]{2,1,0:T(8,128)(2,1)S(1)}, u32[]{:S(2)}, u32[]{:S(2)}) collective-permute-start(bf16[4,336,128]{2,1,0:T(8,128)(2,1)S(1)} %gram_sum.2.refs_1_), channel_id=1, source_target_pairs={{0,1},{1,0},{2,3},{3,2},{4,5},{5,4},{6,7},{7,6},{8,9},{9,8},{10,11... | collective-permute-start | bytes 1032200 | tf_op jit(solution)/shard_map/weights/ppermute | solution.py:772
  45.2 2.1 %collective-permute-start.7 = (bf16[4,336,128]{2,1,0:T(8,128)(2,1)S(1)}, bf16[4,336,128]{2,1,0:T(8,128)(2,1)S(1)}, u32[]{:S(2)}, u32[]{:S(2)}) collective-permute-start(bf16[4,336,128]{2,1,0:T(8,128)(2,1)S(1)} %collective-permute-done.3.refs_2_), channel_id=1, source_target_pairs={{0,1},{1,0},{2,3},{3,2},{4,5},{5,4},{6,7},{7,6},{8,9},{9,8},{10,11... | collective-permute-start | bytes 1032200 | tf_op jit(solution)/shard_map/weights/ppermute | solution.py:772
  45.7 2.1 %collective-permute-start.8 = (bf16[4,336,128]{2,1,0:T(8,128)(2,1)S(1)}, bf16[4,336,128]{2,1,0:T(8,128)(2,1)S(1)}, u32[]{:S(2)}, u32[]{:S(2)}) collective-permute-start(bf16[4,336,128]{2,1,0:T(8,128)(2,1)S(1)} %collective-permute-done.4.refs_3_), channel_id=1, source_target_pairs={{0,1},{1,0},{2,3},{3,2},{4,5},{5,4},{6,7},{7,6},{8,9},{9,8},{10,11... | collective-permute-start | bytes 1032200 | tf_op jit(solution)/shard_map/weights/ppermute | solution.py:772
  45.7 2.6 %collective-permute-start.9 = (bf16[4,336,128]{2,1,0:T(8,128)(2,1)S(1)}, bf16[4,336,128]{2,1,0:T(8,128)(2,1)S(1)}, u32[]{:S(2)}, u32[]{:S(2)}) collective-permute-start(bf16[4,336,128]{2,1,0:T(8,128)(2,1)S(1)} %collective-permute-done.5.refs_4_), channel_id=1, source_target_pairs={{0,1},{1,0},{2,3},{3,2},{4,5},{5,4},{6,7},{7,6},{8,9},{9,8},{10,11... | collective-permute-start | bytes 1032200 | tf_op jit(solution)/shard_map/weights/ppermute | solution.py:772
  88.0 4.6 %collective-permute-start.11 = (bf16[16,144,256]{2,1,0:T(8,128)(2,1)S(1)}, bf16[16,144,256]{2,1,0:T(8,128)(2,1)S(1)}, u32[]{:S(2)}, u32[]{:S(2)}) collective-permute-start(bf16[16,144,256]{2,1,0:T(8,128)(2,1)S(1)} %get-tuple-element.116), channel_id=1, source_target_pairs={{0,1},{1,0},{2,3},{3,2},{4,5},{5,4},{6,7},{7,6},{8,9},{9,8},{10,11... | collective-permute-start | bytes 3538952 | tf_op jit(solution)/shard_map/ppermute | solution.py:772
  93.4 3.6 %copy-start = (bf16[4,144,256]{2,1,0:T(8,128)(2,1)}, bf16[4,144,256]{2,1,0:T(8,128)(2,1)S(1)}, u32[]{:S(2)}) copy-start(bf16[4,144,256]{2,1,0:T(8,128)(2,1)S(1)} %get-tuple-element.118.refs_8_) | copy-start | bytes 884740
  93.4 18.1 %collective-permute-start.14 = (bf16[4,144,256]{2,1,0:T(8,128)(2,1)S(1)}, bf16[4,144,256]{2,1,0:T(8,128)(2,1)S(1)}, u32[]{:S(2)}, u32[]{:S(2)}) collective-permute-start(bf16[4,144,256]{2,1,0:T(8,128)(2,1)S(1)} %get-tuple-element.121), channel_id=1, source_target_pairs={{0,4},{1,17},{2,6},{3,19},{4,0},{5,21},{6,2},{7,23},{8,12},{9,25},... | collective-permute-start | bytes 884744 | tf_op jit(solution)/shard_map/merge_sum/ppermute | solution.py:768
  93.9 17.6 %collective-permute-start.15 = (bf16[4,144,256]{2,1,0:T(8,128)(2,1)S(1)}, bf16[4,144,256]{2,1,0:T(8,128)(2,1)S(1)}, u32[]{:S(2)}, u32[]{:S(2)}) collective-permute-start(bf16[4,144,256]{2,1,0:T(8,128)(2,1)S(1)} %get-tuple-element.122), channel_id=1, source_target_pairs={{0,6},{1,25},{2,4},{3,27},{4,2},{5,29},{6,0},{7,31},{8,14},{9,17},... | collective-permute-start | bytes 884744 | tf_op jit(solution)/shard_map/merge_sum/ppermute | solution.py:768
  95.3 16.2 %collective-permute-start.13 = (bf16[4,144,256]{2,1,0:T(8,128)(2,1)S(1)}, bf16[4,144,256]{2,1,0:T(8,128)(2,1)S(1)}, u32[]{:S(2)}, u32[]{:S(2)}) collective-permute-start(bf16[4,144,256]{2,1,0:T(8,128)(2,1)S(1)} %get-tuple-element.118.refs_8_), channel_id=1, source_target_pairs={{0,2},{1,9},{2,0},{3,11},{4,6},{5,13},{6,4},{7,15},{8,10},{9,1},{1... | collective-permute-start | bytes 884744 | tf_op jit(solution)/shard_map/merge_sum/ppermute | solution.py:768
  97.0 4.9 %collective-permute-start.10 = (bf16[16,1,32,128]{3,2,1,0:T(8,128)(2,1)S(1)}, bf16[16,1,32,128]{3,2,1,0:T(8,128)(2,1)S(1)}, u32[]{:S(2)}, u32[]{:S(2)}) collective-permute-start(bf16[16,1,32,128]{3,2,1,0:T(8,128)(2,1)S(1)} %get-tuple-element.114), channel_id=1, source_target_pairs={{0,1},{1,0},{2,3},{3,2},{4,5},{5,4},{6,7},{7,6},{8,9},{9,8},{10,11... | collective-permute-start | bytes 393224 | tf_op jit(solution)/shard_map/merge_sum/ppermute | solution.py:772
  101.3 1.6 %collective-permute-start.12 = (bf16[16,1,32,128]{3,2,1,0:T(8,128)(2,1)S(1)}, bf16[16,1,32,128]{3,2,1,0:T(8,128)(2,1)S(1)}, u32[]{:S(2)}, u32[]{:S(2)}) collective-permute-start(bf16[16,1,32,128]{3,2,1,0:T(8,128)(2,1)S(1)} %get-tuple-element.119), channel_id=1, source_target_pairs={{0,1},{1,0},{2,3},{3,2},{4,5},{5,4},{6,7},{7,6},{8,9},{9,8},{10,11... | collective-permute-start | bytes 393224 | tf_op jit(solution)/shard_map/merge_sum/ppermute | solution.py:772
  111.5 15.4 %all-to-all-start.4 = ((bf16[16,2,32,128]{3,2,1,0:T(8,128)(2,1)}), bf16[16,2,32,128]{3,2,1,0:T(8,128)(2,1)S(1)}, u32[]{:S(2)}, u32[]{:S(2)}) async-start(bf16[16,2,32,128]{3,2,1,0:T(8,128)(2,1)} %get-tuple-element.123), calls=%async_computation.4 | async-start | bytes 524288 | tf_op jit(solution)/shard_map/branch_sum/all_to_all | solution.py:978
  115.8 0.7 copy-start.2
  116.4 5.9 %collective-permute-start.16 = (bf16[144,256]{1,0:T(8,128)(2,1)S(1)}, bf16[144,256]{1,0:T(8,128)(2,1)S(1)}, u32[]{:S(2)}, u32[]{:S(2)}) collective-permute-start(bf16[144,256]{1,0:T(8,128)(2,1)S(1)} %get-tuple-element.129), channel_id=1, source_target_pairs={{0,8},{1,3},{2,10},{3,1},{4,12},{5,7},{6,14},{7,5},{8,0},{9,11},{1... | collective-permute-start | bytes 221192 | tf_op jit(solution)/shard_map/merge_sum/ppermute | solution.py:768
  118.3 8.7 %collective-permute-start.17 = (bf16[144,256]{1,0:T(8,128)(2,1)S(1)}, bf16[144,256]{1,0:T(8,128)(2,1)S(1)}, u32[]{:S(2)}, u32[]{:S(2)}) collective-permute-start(bf16[144,256]{1,0:T(8,128)(2,1)S(1)} %get-tuple-element.130), channel_id=1, source_target_pairs={{0,16},{1,5},{2,18},{3,7},{4,20},{5,1},{6,22},{7,3},{8,24},{9,13},... | collective-permute-start | bytes 221192 | tf_op jit(solution)/shard_map/merge_sum/ppermute | solution.py:768
  120.7 6.3 %collective-permute-start.18 = (bf16[144,256]{1,0:T(8,128)(2,1)S(1)}, bf16[144,256]{1,0:T(8,128)(2,1)S(1)}, u32[]{:S(2)}, u32[]{:S(2)}) collective-permute-start(bf16[144,256]{1,0:T(8,128)(2,1)S(1)} %get-tuple-element.131), channel_id=1, source_target_pairs={{0,24},{1,7},{2,26},{3,5},{4,28},{5,3},{6,30},{7,1},{8,16},{9,15},... | collective-permute-start | bytes 221192 | tf_op jit(solution)/shard_map/merge_sum/ppermute | solution.py:768
  129.5 11.1 %collective-permute-start.19 = (f32[352,128]{1,0:T(8,128)S(1)}, f32[352,128]{1,0:T(8,128)S(1)}, u32[]{:S(2)}, u32[]{:S(2)}) collective-permute-start(f32[352,128]{1,0:T(8,128)S(1)} %get-tuple-element.135.refs_2_), channel_id=1, source_target_pairs={{0,1},{1,0},{2,3},{3,2},{4,5},{5,4},{6,7},{7,6},{8,9},{9,8},{10,11... | collective-permute-start | bytes 540680 | tf_op jit(solution)/shard_map/ppermute | solution.py:772

commit v5 on v4

--- a/solution.py
+++ b/solution.py
@@ -14,6 +14,7 @@
 LANES = 128
 PCOL = 64
 ONE = 100
+FREE = LANES - ONE
 ROWS, WIDE, CHUNK = 32, 256, 256
 BOTH = ("dp", "rep")
 F32 = jnp.float32
@@ -104,19 +105,25 @@
     return out
 
 
-def prep_kernel(pos_ref, wb_hbm, wc_hbm, sp_hbm, wm_hbm, own_ref, block_ref, wb_ref, wc_ref, sp_ref, wm_ref, sems):
+def prep_kernel(pos_ref, wb_hbm, wc_hbm, sp_hbm, wm_hbm, own_ref, block_ref, wb_ref, wc_ref, sp_ref, wm_ref, mix_ref, sems):
     wait = fetch((wb_hbm, wc_hbm, sp_hbm, wm_hbm), (wb_ref, wc_ref, sp_ref, wm_ref), sems)
     mr, hid = wm_ref.shape
     own_ref[...] = jnp.zeros_like(own_ref)
     wait()
+    wc = wc_ref[...].astype(BF16)
+    small = jnp.transpose(sp_ref[...]).astype(BF16)
     own_ref[0:HOPS, :, 0 : wb_ref.shape[2]] = wb_ref[...].astype(BF16)
-    own_ref[HOPS, :, 0 : wc_ref.shape[1]] = wc_ref[...].astype(BF16)
-    own_ref[HOPS, :, PCOL : PCOL + sp_ref.shape[0]] = jnp.transpose(sp_ref[...]).astype(BF16)
+    own_ref[HOPS, :, 0 : wc.shape[1]] = wc
+    own_ref[HOPS, :, PCOL : PCOL + small.shape[1]] = small
+    mix_ref[...] = own_ref[0:HOPS]
+    mix_ref[0, :, ONE : ONE + small.shape[1]] = small
+    mix_ref[1, :, ONE:LANES] = wc[:, :FREE]
+    mix_ref[2, :, ONE : ONE + wc.shape[1] - FREE] = wc[:, FREE:]
     first = pos_ref[1] == 0
-    part = wc_ref.shape[0] // 2
-    for k in range(HOPS + 1):
-        block_ref[k * part : (k + 1) * part, :] = jnp.where(first, own_ref[k, :part], own_ref[k, part:])
-    at = (HOPS + 1) * part
+    part = wc.shape[0] // 2
+    for k in range(HOPS):
+        block_ref[k * part : (k + 1) * part, :] = jnp.where(first, mix_ref[k, :part], mix_ref[k, part:])
+    at = HOPS * part
     for i in range(2):
         left = wm_ref[:, i * LANES : (i + 1) * LANES]
         right = wm_ref[:, hid // 2 + i * LANES : hid // 2 + (i + 1) * LANES]
@@ -184,20 +191,31 @@
     return total
 
 
-def assemble_kernel(pos_ref, *refs):
-    wb_ref, wm_ref = refs[8:]
-    cb = wb_ref.shape[1] // 16
+def assemble_kernel(classes, pos_ref, *refs):
+    wb_ref, wm_out, wm_ref, sems = refs[8:]
+    hid = wb_ref.shape[1]
+    cb = hid // 16
     mr = wm_ref.shape[1] // 16
     part = cb // 2
-    first = (HOPS + 1) * part
+    first = HOPS * part
     for ref, s, half in each_block(pos_ref, refs[:8]):
-        block = ref[...]
-        rows = pl.ds(pl.multiple_of(s * cb + half * part, part), part)
-        for j in range(HOPS + 1):
-            wb_ref[j, rows, :] = block[j * part : (j + 1) * part]
         rows = pl.ds(pl.multiple_of(s * mr, mr), mr)
         for i in range(2):
-            wm_ref[half * 2 + i, rows, :] = block[first + i * mr : first + (i + 1) * mr]
+            wm_ref[half * 2 + i, rows, :] = ref[first + i * mr : first + (i + 1) * mr, :]
+    stored = fetch((wm_ref,), (wm_out,), sems)
+    for ref, s, half in each_block(pos_ref, refs[:8]):
+        rows = pl.ds(pl.multiple_of(s * cb + half * part, part), part)
+        for j in range(HOPS):
+            wb_ref[j, rows, :] = ref[j * part : (j + 1) * part, :]
+    lane = lane_of((hid, LANES))
+    mixed = [wb_ref[j].astype(F32) for j in range(3)]
+    tail = jnp.where((lane >= PCOL) & (lane < PCOL + 5 * HOPS), pltpu.roll(mixed[0], LANES + PCOL - ONE, 1), 0.0)
+    tail = jnp.where(lane < FREE, pltpu.roll(mixed[1], LANES - ONE, 1), tail)
+    tail = jnp.where((lane >= FREE) & (lane < classes), pltpu.roll(mixed[2], LANES + FREE - ONE, 1), tail)
+    wb_ref[HOPS] = tail.astype(BF16)
+    for j in range(3):
+        wb_ref[j] = jnp.where(lane < ONE, mixed[j], 0.0).astype(BF16)
+    stored()
 
 
 def own_stats(count, rep, gram_ref, own_ref, fix_ref):
@@ -467,7 +485,7 @@
 
 def back_kernel(own, first, count, pos_ref, dpre_ref, x_ref, ws_ref, coef_ref, mu_ref, wm_ref, wt_hbm, *refs):
     if own:
-        recv_refs, refs = refs[:count], refs[count:]
+        recv_ref, refs = refs[0], refs[1:]
     b_ref, a_out, pre, dj, dyv, sums, a_ref, wt_ref, out_sems = refs
     hid = wt_ref.shape[2]
     batch = x_ref.shape[2]
@@ -532,7 +550,7 @@
                 block = jnp.where(row == ONE + SMALLS + i, value - value.astype(BF16).astype(F32), block)
         block = jnp.transpose(block)
         if own:
-            received = jnp.concatenate([recv_refs[k][s, 0] for s in range(dp)], axis=0).astype(F32)
+            received = jnp.concatenate([recv_ref[s, k] for s in range(dp)], axis=0).astype(F32)
             block = split_smalls(block + join_smalls(received))
         for s in range(dp):
             b_ref[s, k] = block[s * cb : (s + 1) * cb, :].astype(BF16)
@@ -581,8 +599,11 @@
 def owner_kernel(
     count, classes, pos_ref, got_ref, sum2_ref, w1_ref, w2_ref, w3_ref, *refs
 ):
-    grad_ref, pay_ref, w0_ref, fix_ref, sems = refs[2:]
+    late = (len(refs) - 7) // 2
+    grad_ref, pay_ref = refs[2 + late : 4 + late]
+    w0_ref, fix_ref, sems, late_sems = refs[4 + 2 * late :]
     wait = fetch(refs[:2], (w0_ref, fix_ref), sems)
+    brought = fetch(refs[2 : 2 + late], refs[4 + late : 4 + 2 * late], late_sems)
     _, _, cb, _ = got_ref.shape
     total = jnp.sum(got_ref[...].astype(F32), axis=0)
     rep = pos_ref[1]
@@ -633,6 +654,7 @@
         packed = jnp.concatenate([packed, jnp.zeros((1, LANES - 4 * cb), F32)], axis=1)
     pay = jnp.concatenate([packed, jnp.where(lane_of((1, LANES)) == 0, squares, 0.0)], axis=0)
     pay_ref[...] = jnp.broadcast_to(pay[None], pay_ref.shape)
+    brought()
 
 
 def own_column(ref, first, me, cb):
@@ -660,17 +682,9 @@
     copy_ref[at] = new.astype(BF16)
 
 
-def final_kernel(pos_ref, got_ref, mine_ref, other_ref, x_ref, wt_hbm, own_hbm, sent0_hbm, sent1_hbm, *refs):
-    states_hbm, outs_hbm, norm_ref, rows_hbm = refs[:12], refs[12:28], refs[28], refs[29]
-    wt_ref, own_ref, sent_ref = refs[30:33]
-    states, outs, rows_ref, sems, more, out_sems = refs[33:45], refs[45:61], refs[61], refs[62], refs[63], refs[64]
-    wait_wt = fetch((wt_hbm,), (wt_ref,), more)
-    wait_rows = fetch(
-        (own_hbm, sent0_hbm, sent1_hbm),
-        (own_ref, sent_ref.at[pl.ds(0, 1)], sent_ref.at[pl.ds(1, 1)]),
-        more.at[pl.ds(1, 3)],
-    )
-    wait = fetch(states_hbm, states, sems)
+def final_kernel(pos_ref, got_ref, mine_ref, other_ref, x_ref, wt_ref, own_ref, sent_ref, *refs):
+    states, outs_hbm, norm_ref, rows_hbm = refs[:12], refs[12:28], refs[28], refs[29]
+    outs, rows_ref, out_sems = refs[30:46], refs[46], refs[47]
     weights, firsts, seconds = states[0:4], states[4:8], states[8:12]
     n = got_ref.shape[0]
     cb = weights[0].shape[1]
@@ -705,7 +719,6 @@
     high = jnp.where(first, other, mine)
     stores = []
     fixes = []
-    wait_wt()
     for k in range(HOPS):
         r, i = k // 2, k % 2
         alpha, beta = spread_row(r, 2 * i), spread_row(r, 2 * i + 1)
@@ -715,7 +728,6 @@
         fix = dot(low_w, high_part, 1, 1) + dot(low_w, (right - high_part.astype(F32)).astype(BF16), 1, 1)
         high_part = fix.astype(BF16)
         fixes.append(jnp.concatenate([high_part, (fix - high_part.astype(F32)).astype(BF16)], axis=1))
-    wait_rows()
     for k in range(HOPS):
         r, i = k // 2, k % 2
         value = jnp.where(pos_ref[1] == r, own_ref[i], sent_ref[i])
@@ -728,7 +740,6 @@
     def group(i):
         return [o for o in outs[i::4]]
 
-    wait()
     hops = [low[0:cb], low[cb : 2 * cb], high[0:cb], high[cb : 2 * cb]]
     for k in range(HOPS):
         adam_into(weights[0], firsts[0], seconds[0], hops[k][:, :d_in], scale, 0.05, group(0), k)
@@ -809,13 +820,14 @@
     if staged:
         with jax.named_scope("prep"):
             sources = (lhs[0], weights[2], weights[3], weights[1])
-            size = (HOPS + 1) * cb // 2 + 2 * mr
+            size = HOPS * cb // 2 + 2 * mr
             own, block = call(
                 prep_kernel,
                 [hbm_out((HOPS + 1, cb, LANES), BF16), sds((size, LANES), BF16)],
                 pos, *sources,
                 smem=(0,), hbm=(1, 2, 3, 4),
-                scratch=[pltpu.VMEM(v.shape, F32) for v in sources] + [pltpu.SemaphoreType.DMA((4,))],
+                scratch=[pltpu.VMEM(v.shape, F32) for v in sources]
+                + [pltpu.VMEM((HOPS, cb, LANES), BF16), pltpu.SemaphoreType.DMA((4,))],
             )
         far = [flip(block, 4 * k, dp) for k in range(1, 4)]
 
@@ -850,13 +862,16 @@
         gram = exchange(parts).reshape(HOPS, LANES, LANES)
     if staged:
         mine = [stacked] + [flip(stacked, t, dp) for t in range(1, 4)]
-        mine, _ = lax.optimization_barrier((mine, parts))
+        mine = mine[:1] + [lax.optimization_barrier((v, parts))[0] for v in mine[1:]]
         with jax.named_scope("weights"):
+            whole = (hid // LANES, HOPS * hid, LANES)
             wb, wm = call(
-                assemble_kernel,
-                [vmem((HOPS + 1, hid, LANES), BF16), hbm_out((hid // LANES, HOPS * hid, LANES), BF16)],
+                functools.partial(assemble_kernel, classes),
+                [vmem((HOPS + 1, hid, LANES), BF16), hbm_out(whole, BF16)],
                 pos, *mine, *[swap(v) for v in mine],
                 smem=(0,),
+                out_specs=(pl.BlockSpec(memory_space=pltpu.VMEM), pl.BlockSpec(memory_space=pltpu.HBM)),
+                scratch=[pltpu.VMEM(whole, BF16), pltpu.SemaphoreType.DMA((1,))],
             )
     else:
         own, wb, wm = weights_plain(lhs[0], weights[2], weights[3], weights[1], dp)
@@ -946,8 +961,9 @@
             )
 
     recv = swap(send)
-    sent = [back(False, 0, 1)]
     with jax.named_scope("merge_sum"):
+        sent_b, sent_a = back(False, 0, 2)
+        recv_b = swap(sent_b)
         if staged:
             shape = (4, rows, half)
             low = call(
@@ -955,12 +971,10 @@
                 [vmem(shape)] + [sds(shape, BF16)] * 3,
                 pos, keep, recv,
                 smem=(0,),
-                after=(sent[0][1],),
+                after=(sent_a,),
             )
-            sent.append(back(False, 1, 1, after=(low[1],)))
-            recv_b = [swap(v[0]) for v in sent]
             moved = [turn_flip(low[t], t, dp, 1) for t in range(1, 4)]
-            kept_b, kept_a = back(True, 0, 2, *recv_b)
+            kept_b, kept_a = back(True, 0, 2, recv_b, after=(low[1],))
             kept_b, moved = lax.optimization_barrier((kept_b, moved))
             high = call(
                 split_high_kernel,
@@ -970,40 +984,38 @@
             )
             wide = [high[0]] + [turn_flip(high[t], t, dp, 0) for t in range(1, 4)]
         else:
-            sent.append(back(False, 1, 1))
-            kept_b, kept_a = back(True, 0, 2, *[swap(v[0]) for v in sent])
+            kept_b, kept_a = back(True, 0, 2, recv_b)
             total = lax.psum_scatter(keep + recv.astype(F32), "dp", scatter_dimension=0)
             wide = [total] + [jnp.zeros_like(total)] * 3
     with jax.named_scope("branch_sum"):
         got_b = lax.all_to_all(kept_b, "dp", 0, 0, tiled=True)
     with jax.named_scope("owner"):
         late = (wide[0], fix)
-        shares, pay = call(
+        tr = [(lhs[i],) + tuple(s[1:]) for i, s in enumerate((weights, firsts, seconds))]
+        last = (wt, kept_a, sent_a, *tr[0], *tr[1], *tr[2])
+        shares, pay, *last = call(
             functools.partial(owner_kernel, count, classes),
-            [sds((3 * cb + 2 * mr, LANES)), hbm_out((n, 2, LANES))],
-            pos, got_b, sum2, *wide[1:], *late,
+            [sds((3 * cb + 2 * mr, LANES)), hbm_out((n, 2, LANES))] + [vmem(v.shape, v.dtype) for v in last],
+            pos, got_b, sum2, *wide[1:], *late, *last,
             smem=(0,),
-            hbm=(6, 7),
-            scratch=[pltpu.VMEM(v.shape, v.dtype) for v in late] + [pltpu.SemaphoreType.DMA((2,))],
+            hbm=tuple(range(6, 8 + len(last))),
+            scratch=[pltpu.VMEM(v.shape, v.dtype) for v in late]
+            + [pltpu.SemaphoreType.DMA((2,)), pltpu.SemaphoreType.DMA((len(last),))],
         )
     theirs = swap(shares)
     got = exchange(pay)
     with jax.named_scope("final"):
-        tr = [(lhs[i],) + tuple(s[1:]) for i, s in enumerate((weights, firsts, seconds))]
         shapes = [t.shape for t in tr[0]]
         outs = []
         for dtype in (F32, F32, F32, BF16):
             outs += [sds(s, dtype) for s in shapes]
         outs += [sds((1, 1)), sds((width, batch))]
-        local = (*tr[0], *tr[1], *tr[2])
         res = call(
-            final_kernel, outs, pos, got, shares, theirs, x, wt, kept_a, sent[0][1], sent[1][1], *local,
-            smem=(0,), hbm=tuple(range(5, 9 + len(local))),
+            final_kernel, outs, pos, got, shares, theirs, x, *last,
+            smem=(0,),
             out_specs=tuple(pl.BlockSpec(memory_space=pltpu.VMEM if i == 16 else pltpu.HBM) for i in range(18)),
-            scratch=[pltpu.VMEM(v.shape, v.dtype) for v in (wt, kept_a, kept_a) + local]
-            + [pltpu.VMEM(v.shape, v.dtype) for i, v in enumerate(outs) if i != 16]
-            + [pltpu.SemaphoreType.DMA((k,)) for k in (len(local), 4, 18)],
-            flops=2 * batch * LANES * LANES * 3 * HOPS,
+            scratch=[pltpu.VMEM(v.shape, v.dtype) for i, v in enumerate(outs) if i != 16]
+            + [pltpu.SemaphoreType.DMA((18,))],
         )
     result = list(res[:16])
     for i in range(0, 16, 4):

time: 147 us -> 144 us (0.980)
  Pallas kernels: 54.3 us -> 52.7 us
    ppermute x6, waiting for transfers between devices: 9.21 us -> 7.57 us  [flip(): return lax.ppermute(value, 'dp', [(i, i ^ mask) for i in range(dp)])]
    pallas_call x16 -> x15, Pallas kernels: 54.3 us -> 52.7 us  [call(): pl.pallas_call(kernel, out_shape=tuple(outs), in_specs=in_specs, out_spec...]
    ppermute x8 -> x7, waiting for transfers between devices: 3.1 us -> 3.12 us  [swap(): return lax.ppermute(value, 'rep', [(0, 1), (1, 0)])]
  transfers between devices with their start and end apart: 23 -> 22, of which waited for: 11 -> 8; matrix products, arithmetic and copies ran while one was open for 0% -> 0% of each run, Pallas kernels for 19% -> 19%
where the time goes in v5:
time: 144 us; the launch traced here: 143 us
  Pallas kernels  52.7 us (37%)
  blocking collectives  33.5 us (23%)
  starting transfers between devices  30.7 us (21%)
  waiting for transfers between devices  24.6 us (17%)
    pallas_call x15, Pallas kernels, call(): pl.pallas_call(kernel, out_shape=tuple(outs), in_specs=in_specs, out_spec...  52.7 us
    all_to_all x3, blocking collectives, exchange(): return lax.all_to_all(value, BOTH, 0, 0, tiled=True)  33.5 us
    ppermute x6, starting transfers between devices, flip(): return lax.ppermute(value, 'dp', [(i, i ^ mask) for i in range(dp)])  9.31 us
    all_to_all x2, starting transfers between devices, exchange(): return lax.all_to_all(value, BOTH, 0, 0, tiled=True)  8.58 us
    ppermute x6, starting transfers between devices, turn_flip(): return lax.ppermute(value, BOTH, pairs)  7.94 us
    ppermute x6, waiting for transfers between devices, flip(): return lax.ppermute(value, 'dp', [(i, i ^ mask) for i in range(dp)])  7.57 us
    all_to_all x2, waiting for transfers between devices, exchange(): return lax.all_to_all(value, BOTH, 0, 0, tiled=True)  7.11 us
    ppermute x6, waiting for transfers between devices, turn_flip(): return lax.ppermute(value, BOTH, pairs)  6.75 us
  transfers between devices with their start and end apart: 22, of which 8 were waited for; matrix products, arithmetic and copies ran while one was open for 0% of the time, Pallas kernels for 19%

profile of v5, /device:TPU:0, one launch (start us, length us, event | category | flops | bytes accessed | tf_op | source)
XLA Modules:
  0.0 143.3 jit_solution(2019322811622874008)
XLA Ops:
  0.7 0.1 pad_add_fusion.refs_0_
  0.7 2.4 %prep.1 = (bf16[5,32,128]{2,1,0:T(8,128)(2,1)}, bf16[320,128]{1,0:T(8,128)(2,1)S(1)}) custom-call(s32[2]{0:T(128)S(1)} %pad_add_fusion.refs_0_, f32[4,32,100]{2,1,0:T(8,128)} %bitcast.18, f32[32,47]{1,0:T(8,128)} %refs_13_.1, f32[20,32]{1,0:T(8,128)} %refs_14_.1, f32[128,512]{1,0:T(8,128)} %refs_12_.1), custom_call_target="tpu_custom_call" | custom-call | flops 1024 | bytes 1024 | tf_op jit(solution)/shard_map/prep/pallas_call | solution.py:48
  3.1 5.1 %collective-permute-start.2 = (bf16[320,128]{1,0:T(8,128)(2,1)S(1)}, bf16[320,128]{1,0:T(8,128)(2,1)S(1)}, u32[]{:S(2)}, u32[]{:S(2)}) collective-permute-start(bf16[320,128]{1,0:T(8,128)(2,1)S(1)} %get-tuple-element.102.refs_0_), channel_id=1, source_target_pairs={{0,24},{2,26},{4,28},{6,30},{8,16},{10,18},{12,20},{14,22},{16,8},... | collective-permute-start | bytes 245768 | tf_op jit(solution)/shard_map/ppermute | solution.py:770
  8.2 0.6 collective-permute-start
  8.9 7.1 %gather.1 = (bf16[4,128,1024]{2,1,0:T(8,128)(2,1)S(1)}, f32[4,128,128]{2,1,0:T(8,128)}) custom-call(s32[1,1024]{1,0:T(1,128)} %bitcast.24, f32[400,4096]{1,0:T(8,128)} %bitcast.17, bf16[5,32,128]{2,1,0:T(8,128)(2,1)} %get-tuple-element.99.refs_2_.refs_3_), custom_call_target="tpu_custom_call" | custom-call | flops 1024 | bytes 1024 | tf_op jit(solution)/shard_map/gather/pallas_call | solution.py:48
  16.0 0.0 copy-start.1
  16.1 6.0 %all-to-all-start = ((f32[32,16,128]{2,1,0:T(8,128)}), f32[32,16,128]{2,1,0:T(8,128)S(1)}, u32[]{:S(2)}, u32[]{:S(2)}) async-start(f32[32,16,128]{2,1,0:T(8,128)} %bitcast.20), calls=%async_computation | async-start | bytes 524288 | tf_op jit(solution)/shard_map/gram_sum/all_to_all | solution.py:787
  22.1 2.7 %collective-permute-start.5 = (bf16[4,320,128]{2,1,0:T(8,128)(2,1)S(1)}, bf16[4,320,128]{2,1,0:T(8,128)(2,1)S(1)}, u32[]{:S(2)}, u32[]{:S(2)}) collective-permute-start(bf16[4,320,128]{2,1,0:T(8,128)(2,1)S(1)} %gram_sum.2.refs_1_), channel_id=1, source_target_pairs={{0,6},{2,4},{4,2},{6,0},{8,14},{10,12},{12,10},{14,8},{16,22},{18,... | collective-permute-start | bytes 983048 | tf_op jit(solution)/shard_map/ppermute | solution.py:770
  24.8 0.6 collective-permute-start.4
  25.4 0.3 collective-permute-start.3
  25.6 7.1 %all-to-all-done.refs_0_ = f32[32,16,128]{2,1,0:T(8,128)S(1)} async-done(((f32[32,16,128]{2,1,0:T(8,128)}), f32[32,16,128]{2,1,0:T(8,128)S(1)}, u32[]{:S(2)}, u32[]{:S(2)}) %all-to-all-start) | async-done | bytes 262176 | tf_op jit(solution)/shard_map/gram_sum/all_to_all | solution.py:787
  32.7 0.8 gram_sum.3
  33.5 2.6 %all-to-all-start.1 = ((f32[32,16,128]{2,1,0:T(8,128)}), f32[32,16,128]{2,1,0:T(8,128)S(1)}, u32[]{:S(2)}, u32[]{:S(2)}) async-start(f32[32,16,128]{2,1,0:T(8,128)} %gram_sum.3), calls=%async_computation.1 | async-start | bytes 524288 | tf_op jit(solution)/shard_map/gram_sum/all_to_all | solution.py:787
  36.1 0.2 collective-permute-start.6
  36.2 0.4 collective-permute-start.9
  36.6 7.5 %collective-permute-done.4.refs_3_ = bf16[4,320,128]{2,1,0:T(8,128)(2,1)S(1)} collective-permute-done((bf16[4,320,128]{2,1,0:T(8,128)(2,1)S(1)}, bf16[4,320,128]{2,1,0:T(8,128)(2,1)S(1)}, u32[]{:S(2)}, u32[]{:S(2)}) %collective-permute-start.4) | collective-permute-done | bytes 327712 | tf_op jit(solution)/shard_map/ppermute | solution.py:770
  44.1 0.1 collective-permute-done.3.refs_2_
  44.2 0.4 collective-permute-start.7
  44.7 1.1 collective-permute-done.8.refs_7_
  45.8 0.5 collective-permute-done.7.refs_6_
  46.2 2.2 %weights.1 = (bf16[5,512,128]{2,1,0:T(8,128)(2,1)S(1)}, bf16[4,2048,128]{2,1,0:T(8,128)(2,1)}) custom-call(s32[2]{0:T(128)S(1)} %pad_add_fusion.refs_0_, bf16[4,320,128]{2,1,0:T(8,128)(2,1)S(1)} %gram_sum.2.refs_1_, bf16[4,320,128]{2,1,0:T(8,128)(2,1)S(1)} %collective-permute-done.3.refs_2_, bf16[4,320,128]{2,1,0:T(8,128)(2,1)S(1)} %collective-permute-done.4.refs_3_, ...), custom_call_target="tpu_custom_call" | custom-call | flops 1024 | bytes 1024 | tf_op jit(solution)/shard_map/weights/pallas_call | solution.py:48
  48.5 2.0 %stats.1 = (bf16[4,512,256]{2,1,0:T(8,128)(2,1)S(1)}, f32[4,512,128]{2,1,0:T(8,128)S(1)}, f32[8,128]{1,0:T(8,128)S(1)}, bf16[4,128,512]{2,1,0:T(8,128)(2,1)S(1)}, f32[2,32,128]{2,1,0:T(8,128)S(1)}) custom-call(s32[2]{0:T(128)S(1)} %pad_add_fusion.refs_0_, f32[4,128,128]{2,1,0:T(8,128)S(1)} %bitcast.16, ...), custom_call_target="tpu_custom_call" | custom-call | flops 1024 | bytes 1024 | tf_op jit(solution)/shard_map/stats/pallas_call | solution.py:48
  50.4 5.9 %forward.1 = (bf16[4,512,1024]{2,1,0:T(8,128)(2,1)S(1)}, f32[512,1024]{1,0:T(8,128)S(1)}, f32[32,8,128]{2,1,0:T(8,128)S(1)}, bf16[4,128,512]{2,1,0:T(8,128)(2,1)}, f32[2,32,128]{2,1,0:T(8,128)}) custom-call(bf16[4,128,1024]{2,1,0:T(8,128)(2,1)S(1)} %get-tuple-element.100.refs_0_.refs_2_.refs_4_, bf16[4,512,256]{2,1,0:T(8,128)(2,1)S(1)} %get-tuple-element.109.refs_1_.refs_3_, ...), custom_call_target="tpu_custom_call" | custom-call | flops 1024 | bytes 1024 | tf_op jit(solution)/shard_map/forward/pallas_call | solution.py:48
  56.3 12.6 %all_to_all.30.refs_0_ = f32[32,8,128]{2,1,0:T(8,128)S(1)} all-to-all(f32[32,8,128]{2,1,0:T(8,128)S(1)} %get-tuple-element.114), channel_id=1, replica_groups=mesh['dp'=16,'rep'=2] {'dp','rep'}, dimensions={0} | all-to-all | bytes 262144 | tf_op jit(solution)/shard_map/all_to_all | solution.py:787
  68.9 3.7 %head.1 = (f32[512,1024]{1,0:T(8,128)S(1)}, f32[32,8,128]{2,1,0:T(8,128)S(1)}, f32[512,128]{1,0:T(8,128)S(1)}, f32[2,512,128]{2,1,0:T(8,128)S(1)}) custom-call(f32[32,8,128]{2,1,0:T(8,128)S(1)} %all_to_all.30.refs_0_, f32[512,1024]{1,0:T(8,128)S(1)} %get-tuple-element.115.refs_1_.refs_4_, bf16[5,512,128]{2,1,0:T(8,128)(2,1)S(1)} %get-tuple-element.108.refs_2_.refs_3_, ...), custom_call_target="tpu_custom_call" | custom-call | flops 1024 | bytes 1024 | tf_op jit(solution)/shard_map/head/pallas_call | solution.py:48
  72.6 10.0 %all_to_all.31.refs_1_ = f32[32,8,128]{2,1,0:T(8,128)S(1)} all-to-all(f32[32,8,128]{2,1,0:T(8,128)S(1)} %get-tuple-element.116), channel_id=1, replica_groups=mesh['dp'=16,'rep'=2] {'dp','rep'}, dimensions={0} | all-to-all | bytes 262144 | tf_op jit(solution)/shard_map/all_to_all | solution.py:787
  82.6 3.6 %turn.1 = (bf16[512,1024]{1,0:T(8,128)(2,1)S(1)}, f32[16,144,256]{2,1,0:T(8,128)S(1)}, bf16[16,144,256]{2,1,0:T(8,128)(2,1)S(1)}, f32[8,128]{1,0:T(8,128)S(1)}, bf16[4,2048,128]{2,1,0:T(8,128)(2,1)S(1)}) custom-call(s32[2]{0:T(128)S(1)} %pad_add_fusion.refs_0_, f32[32,8,128]{2,1,0:T(8,128)S(1)} %all_to_all.31.refs_1_, ...), custom_call_target="tpu_custom_call" | custom-call | flops 1024 | bytes 1024 | tf_op jit(solution)/shard_map/turn/pallas_call | solution.py:48
  86.3 0.3 collective-permute-start.11
  86.5 7.5 %back.2 = (bf16[16,2,32,128]{3,2,1,0:T(8,128)(2,1)S(1)}, f32[2,128,1024]{2,1,0:T(8,128)}) custom-call(s32[2]{0:T(128)S(1)} %pad_add_fusion.refs_0_, bf16[512,1024]{1,0:T(8,128)(2,1)S(1)} %get-tuple-element.121.refs_1_, bf16[4,128,1024]{2,1,0:T(8,128)(2,1)S(1)} %get-tuple-element.100.refs_0_.refs_2_.refs_4_, ...), custom_call_target="tpu_custom_call" | custom-call | flops 1024 | bytes 1024 | tf_op jit(solution)/shard_map/merge_sum/back/pallas_call | solution.py:48
  94.0 0.8 merge_sum.2
  94.8 0.5 collective-permute-start.13
  95.4 1.4 collective-permute-start.14
  96.7 1.7 %collective-permute-start.12 = (bf16[4,144,256]{2,1,0:T(8,128)(2,1)S(1)}, bf16[4,144,256]{2,1,0:T(8,128)(2,1)S(1)}, u32[]{:S(2)}, u32[]{:S(2)}) collective-permute-start(bf16[4,144,256]{2,1,0:T(8,128)(2,1)S(1)} %get-tuple-element.129.refs_9_), channel_id=1, source_target_pairs={{0,2},{1,9},{2,0},{3,11},{4,6},{5,13},{6,4},{7,15},{8,10},{9,1},{1... | collective-permute-start | bytes 884744 | tf_op jit(solution)/shard_map/merge_sum/ppermute | solution.py:779
  98.4 1.5 %collective-permute-done.10.refs_8_ = bf16[16,2,32,128]{3,2,1,0:T(8,128)(2,1)S(1)} collective-permute-done((bf16[16,2,32,128]{3,2,1,0:T(8,128)(2,1)S(1)}, bf16[16,2,32,128]{3,2,1,0:T(8,128)(2,1)S(1)}, u32[]{:S(2)}, u32[]{:S(2)}) %collective-permute-start.10) | collective-permute-done | bytes 262176 | tf_op jit(solution)/shard_map/merge_sum/ppermute | solution.py:783
  99.9 8.6 %back.3 = (bf16[16,2,32,128]{3,2,1,0:T(8,128)(2,1)}, f32[2,128,1024]{2,1,0:T(8,128)}) custom-call(s32[2]{0:T(128)S(1)} %pad_add_fusion.refs_0_, bf16[512,1024]{1,0:T(8,128)(2,1)S(1)} %get-tuple-element.121.refs_1_, bf16[4,128,1024]{2,1,0:T(8,128)(2,1)S(1)} %get-tuple-element.100.refs_0_.refs_2_.refs_4_, ...), custom_call_target="tpu_custom_call" | custom-call | flops 1024 | bytes 1024 | tf_op jit(solution)/shard_map/merge_sum/back/pallas_call | solution.py:48
  108.6 3.5 %all-to-all-start.4 = ((bf16[16,2,32,128]{3,2,1,0:T(8,128)(2,1)}), bf16[16,2,32,128]{3,2,1,0:T(8,128)(2,1)S(1)}, u32[]{:S(2)}, u32[]{:S(2)}) async-start(bf16[16,2,32,128]{3,2,1,0:T(8,128)(2,1)} %get-tuple-element.133), calls=%async_computation.4 | async-start | bytes 524288 | tf_op jit(solution)/shard_map/branch_sum/all_to_all | solution.py:991
  112.1 0.7 merge_sum.3
  112.8 0.0 copy-start.2
  112.8 0.7 copy-done.2
  113.5 1.8 %collective-permute-start.15 = (bf16[144,256]{1,0:T(8,128)(2,1)S(1)}, bf16[144,256]{1,0:T(8,128)(2,1)S(1)}, u32[]{:S(2)}, u32[]{:S(2)}) collective-permute-start(bf16[144,256]{1,0:T(8,128)(2,1)S(1)} %get-tuple-element.139), channel_id=1, source_target_pairs={{0,8},{1,3},{2,10},{3,1},{4,12},{5,7},{6,14},{7,5},{8,0},{9,11},{1... | collective-permute-start | bytes 221192 | tf_op jit(solution)/shard_map/merge_sum/ppermute | solution.py:779
  115.3 2.4 %collective-permute-start.16 = (bf16[144,256]{1,0:T(8,128)(2,1)S(1)}, bf16[144,256]{1,0:T(8,128)(2,1)S(1)}, u32[]{:S(2)}, u32[]{:S(2)}) collective-permute-start(bf16[144,256]{1,0:T(8,128)(2,1)S(1)} %get-tuple-element.140), channel_id=1, source_target_pairs={{0,16},{1,5},{2,18},{3,7},{4,20},{5,1},{6,22},{7,3},{8,24},{9,13},... | collective-permute-start | bytes 221192 | tf_op jit(solution)/shard_map/merge_sum/ppermute | solution.py:779
  117.7 0.1 collective-permute-start.17
  117.9 1.4 collective-permute-done.15.refs_3_
  119.3 5.3 %collective-permute-done.16.refs_4_ = bf16[144,256]{1,0:T(8,128)(2,1)S(1)} collective-permute-done((bf16[144,256]{1,0:T(8,128)(2,1)S(1)}, bf16[144,256]{1,0:T(8,128)(2,1)S(1)}, u32[]{:S(2)}, u32[]{:S(2)}) %collective-permute-start.16) | collective-permute-done | bytes 73760 | tf_op jit(solution)/shard_map/merge_sum/ppermute | solution.py:779
  124.6 3.8 %owner.1 = (f32[352,128]{1,0:T(8,128)S(1)}, f32[32,2,128]{2,1,0:T(2,128)}, bf16[4,128,512]{2,1,0:T(8,128)(2,1)S(1)}, f32[2,128,1024]{2,1,0:T(8,128)S(1)}, f32[2,...) custom-call(s32[2]{0:T(128)S(1)} %pad_add_fusion.refs_0_, ...), custom_call_target="tpu_custom_call" | custom-call | flops 1024 | bytes 1024 | tf_op jit(solution)/shard_map/owner/pallas_call | solution.py:48
  128.4 0.1 collective-permute-start.18
  128.4 11.0 %all_to_all.32.refs_1_ = f32[32,2,128]{2,1,0:T(2,128)S(1)} all-to-all(f32[32,2,128]{2,1,0:T(2,128)} %get-tuple-element.145), channel_id=1, replica_groups=mesh['dp'=16,'rep'=2] {'dp','rep'}, dimensions={0} | all-to-all | bytes 65536 | tf_op jit(solution)/shard_map/all_to_all | solution.py:787
  139.4 3.7 %final.1 = (f32[4,32,100]{2,1,0:T(8,128)}, f32[128,512]{1,0:T(8,128)}, f32[32,47]{1,0:T(8,128)}, f32[20,32]{1,0:T(8,128)}, f32[4,32,100]{2,1,0:T(8,128)}, /*inde...) custom-call(s32[2]{0:T(128)S(1)} %pad_add_fusion.refs_0_, ...), custom_call_target="tpu_custom_call" | custom-call | flops 1024 | bytes 1024 | tf_op jit(solution)/shard_map/final/pallas_call | solution.py:48
  (21 shorter events, 0.1 us)
Async XLA Ops:
  3.1 12.9 %collective-permute-start.2 = (bf16[320,128]{1,0:T(8,128)(2,1)S(1)}, bf16[320,128]{1,0:T(8,128)(2,1)S(1)}, u32[]{:S(2)}, u32[]{:S(2)}) collective-permute-start(bf16[320,128]{1,0:T(8,128)(2,1)S(1)} %get-tuple-element.102.refs_0_), channel_id=1, source_target_pairs={{0,24},{2,26},{4,28},{6,30},{8,16},{10,18},{12,20},{14,22},{16,8},... | collective-permute-start | bytes 245768 | tf_op jit(solution)/shard_map/ppermute | solution.py:770
  8.2 7.8 %collective-permute-start.1 = (bf16[320,128]{1,0:T(8,128)(2,1)S(1)}, bf16[320,128]{1,0:T(8,128)(2,1)S(1)}, u32[]{:S(2)}, u32[]{:S(2)}) collective-permute-start(bf16[320,128]{1,0:T(8,128)(2,1)S(1)} %get-tuple-element.102.refs_0_), channel_id=1, source_target_pairs={{0,16},{2,18},{4,20},{6,22},{8,24},{10,26},{12,28},{14,30},{16,0},... | collective-permute-start | bytes 245768 | tf_op jit(solution)/shard_map/ppermute | solution.py:770
  8.2 7.8 %collective-permute-start = (bf16[320,128]{1,0:T(8,128)(2,1)S(1)}, bf16[320,128]{1,0:T(8,128)(2,1)S(1)}, u32[]{:S(2)}, u32[]{:S(2)}) collective-permute-start(bf16[320,128]{1,0:T(8,128)(2,1)S(1)} %get-tuple-element.102.refs_0_), channel_id=1, source_target_pairs={{0,8},{2,10},{4,12},{6,14},{8,0},{10,2},{12,4},{14,6},{16,24},{18,... | collective-permute-start | bytes 245768 | tf_op jit(solution)/shard_map/ppermute | solution.py:770
  16.0 32.4 %copy-start.1 = (bf16[5,32,128]{2,1,0:T(8,128)(2,1)S(1)}, bf16[5,32,128]{2,1,0:T(8,128)(2,1)}, u32[]{:S(2)}) copy-start(bf16[5,32,128]{2,1,0:T(8,128)(2,1)} %get-tuple-element.99.refs_2_.refs_3_) | copy-start | bytes 122884
  16.1 16.7 %all-to-all-start = ((f32[32,16,128]{2,1,0:T(8,128)}), f32[32,16,128]{2,1,0:T(8,128)S(1)}, u32[]{:S(2)}, u32[]{:S(2)}) async-start(f32[32,16,128]{2,1,0:T(8,128)} %bitcast.20), calls=%async_computation | async-start | bytes 524288 | tf_op jit(solution)/shard_map/gram_sum/all_to_all | solution.py:787
  22.1 14.2 %collective-permute-start.5 = (bf16[4,320,128]{2,1,0:T(8,128)(2,1)S(1)}, bf16[4,320,128]{2,1,0:T(8,128)(2,1)S(1)}, u32[]{:S(2)}, u32[]{:S(2)}) collective-permute-start(bf16[4,320,128]{2,1,0:T(8,128)(2,1)S(1)} %gram_sum.2.refs_1_), channel_id=1, source_target_pairs={{0,6},{2,4},{4,2},{6,0},{8,14},{10,12},{12,10},{14,8},{16,22},{18,... | collective-permute-start | bytes 983048 | tf_op jit(solution)/shard_map/ppermute | solution.py:770
  24.8 19.3 %collective-permute-start.4 = (bf16[4,320,128]{2,1,0:T(8,128)(2,1)S(1)}, bf16[4,320,128]{2,1,0:T(8,128)(2,1)S(1)}, u32[]{:S(2)}, u32[]{:S(2)}) collective-permute-start(bf16[4,320,128]{2,1,0:T(8,128)(2,1)S(1)} %gram_sum.2.refs_1_), channel_id=1, source_target_pairs={{0,4},{2,6},{4,0},{6,2},{8,12},{10,14},{12,8},{14,10},{16,20},{18,... | collective-permute-start | bytes 983048 | tf_op jit(solution)/shard_map/ppermute | solution.py:770
  25.4 18.9 %collective-permute-start.3 = (bf16[4,320,128]{2,1,0:T(8,128)(2,1)S(1)}, bf16[4,320,128]{2,1,0:T(8,128)(2,1)S(1)}, u32[]{:S(2)}, u32[]{:S(2)}) collective-permute-start(bf16[4,320,128]{2,1,0:T(8,128)(2,1)S(1)} %gram_sum.2.refs_1_), channel_id=1, source_target_pairs={{0,2},{2,0},{4,6},{6,4},{8,10},{10,8},{12,14},{14,12},{16,18},{18,... | collective-permute-start | bytes 983048 | tf_op jit(solution)/shard_map/ppermute | solution.py:770
  33.5 15.0 %all-to-all-start.1 = ((f32[32,16,128]{2,1,0:T(8,128)}), f32[32,16,128]{2,1,0:T(8,128)S(1)}, u32[]{:S(2)}, u32[]{:S(2)}) async-start(f32[32,16,128]{2,1,0:T(8,128)} %gram_sum.3), calls=%async_computation.1 | async-start | bytes 524288 | tf_op jit(solution)/shard_map/gram_sum/all_to_all | solution.py:787
  36.1 8.6 %collective-permute-start.6 = (bf16[4,320,128]{2,1,0:T(8,128)(2,1)S(1)}, bf16[4,320,128]{2,1,0:T(8,128)(2,1)S(1)}, u32[]{:S(2)}, u32[]{:S(2)}) collective-permute-start(bf16[4,320,128]{2,1,0:T(8,128)(2,1)S(1)} %gram_sum.2.refs_1_), channel_id=1, source_target_pairs={{0,1},{1,0},{2,3},{3,2},{4,5},{5,4},{6,7},{7,6},{8,9},{9,8},{10,11... | collective-permute-start | bytes 983048 | tf_op jit(solution)/shard_map/weights/ppermute | solution.py:783
  36.2 8.4 %collective-permute-start.9 = (bf16[4,320,128]{2,1,0:T(8,128)(2,1)S(1)}, bf16[4,320,128]{2,1,0:T(8,128)(2,1)S(1)}, u32[]{:S(2)}, u32[]{:S(2)}) collective-permute-start(bf16[4,320,128]{2,1,0:T(8,128)(2,1)S(1)} %collective-permute-done.5.refs_4_), channel_id=1, source_target_pairs={{0,1},{1,0},{2,3},{3,2},{4,5},{5,4},{6,7},{7,6},{8,9},{9,8},{10,11... | collective-permute-start | bytes 983048 | tf_op jit(solution)/shard_map/weights/ppermute | solution.py:783
  44.1 1.6 %collective-permute-start.8 = (bf16[4,320,128]{2,1,0:T(8,128)(2,1)S(1)}, bf16[4,320,128]{2,1,0:T(8,128)(2,1)S(1)}, u32[]{:S(2)}, u32[]{:S(2)}) collective-permute-start(bf16[4,320,128]{2,1,0:T(8,128)(2,1)S(1)} %collective-permute-done.4.refs_3_), channel_id=1, source_target_pairs={{0,1},{1,0},{2,3},{3,2},{4,5},{5,4},{6,7},{7,6},{8,9},{9,8},{10,11... | collective-permute-start | bytes 983048 | tf_op jit(solution)/shard_map/weights/ppermute | solution.py:783
  44.2 2.0 %collective-permute-start.7 = (bf16[4,320,128]{2,1,0:T(8,128)(2,1)S(1)}, bf16[4,320,128]{2,1,0:T(8,128)(2,1)S(1)}, u32[]{:S(2)}, u32[]{:S(2)}) collective-permute-start(bf16[4,320,128]{2,1,0:T(8,128)(2,1)S(1)} %collective-permute-done.3.refs_2_), channel_id=1, source_target_pairs={{0,1},{1,0},{2,3},{3,2},{4,5},{5,4},{6,7},{7,6},{8,9},{9,8},{10,11... | collective-permute-start | bytes 983048 | tf_op jit(solution)/shard_map/weights/ppermute | solution.py:783
  86.3 7.8 %collective-permute-start.11 = (bf16[16,144,256]{2,1,0:T(8,128)(2,1)S(1)}, bf16[16,144,256]{2,1,0:T(8,128)(2,1)S(1)}, u32[]{:S(2)}, u32[]{:S(2)}) collective-permute-start(bf16[16,144,256]{2,1,0:T(8,128)(2,1)S(1)} %get-tuple-element.127), channel_id=1, source_target_pairs={{0,1},{1,0},{2,3},{3,2},{4,5},{5,4},{6,7},{7,6},{8,9},{9,8},{10,11... | collective-permute-start | bytes 3538952 | tf_op jit(solution)/shard_map/ppermute | solution.py:783
  94.8 5.1 %copy-start = (bf16[4,144,256]{2,1,0:T(8,128)(2,1)}, bf16[4,144,256]{2,1,0:T(8,128)(2,1)S(1)}, u32[]{:S(2)}) copy-start(bf16[4,144,256]{2,1,0:T(8,128)(2,1)S(1)} %get-tuple-element.129.refs_9_) | copy-start | bytes 884740
  94.8 13.7 %collective-permute-start.13 = (bf16[4,144,256]{2,1,0:T(8,128)(2,1)S(1)}, bf16[4,144,256]{2,1,0:T(8,128)(2,1)S(1)}, u32[]{:S(2)}, u32[]{:S(2)}) collective-permute-start(bf16[4,144,256]{2,1,0:T(8,128)(2,1)S(1)} %get-tuple-element.131), channel_id=1, source_target_pairs={{0,4},{1,17},{2,6},{3,19},{4,0},{5,21},{6,2},{7,23},{8,12},{9,25},... | collective-permute-start | bytes 884744 | tf_op jit(solution)/shard_map/merge_sum/ppermute | solution.py:779
  95.4 13.2 %collective-permute-start.14 = (bf16[4,144,256]{2,1,0:T(8,128)(2,1)S(1)}, bf16[4,144,256]{2,1,0:T(8,128)(2,1)S(1)}, u32[]{:S(2)}, u32[]{:S(2)}) collective-permute-start(bf16[4,144,256]{2,1,0:T(8,128)(2,1)S(1)} %get-tuple-element.132), channel_id=1, source_target_pairs={{0,6},{1,25},{2,4},{3,27},{4,2},{5,29},{6,0},{7,31},{8,14},{9,17},... | collective-permute-start | bytes 884744 | tf_op jit(solution)/shard_map/merge_sum/ppermute | solution.py:779
  96.7 11.8 %collective-permute-start.12 = (bf16[4,144,256]{2,1,0:T(8,128)(2,1)S(1)}, bf16[4,144,256]{2,1,0:T(8,128)(2,1)S(1)}, u32[]{:S(2)}, u32[]{:S(2)}) collective-permute-start(bf16[4,144,256]{2,1,0:T(8,128)(2,1)S(1)} %get-tuple-element.129.refs_9_), channel_id=1, source_target_pairs={{0,2},{1,9},{2,0},{3,11},{4,6},{5,13},{6,4},{7,15},{8,10},{9,1},{1... | collective-permute-start | bytes 884744 | tf_op jit(solution)/shard_map/merge_sum/ppermute | solution.py:779
  98.4 1.5 %collective-permute-start.10 = (bf16[16,2,32,128]{3,2,1,0:T(8,128)(2,1)S(1)}, bf16[16,2,32,128]{3,2,1,0:T(8,128)(2,1)S(1)}, u32[]{:S(2)}, u32[]{:S(2)}) collective-permute-start(bf16[16,2,32,128]{3,2,1,0:T(8,128)(2,1)S(1)} %get-tuple-element.125), channel_id=1, source_target_pairs={{0,1},{1,0},{2,3},{3,2},{4,5},{5,4},{6,7},{7,6},{8,9},{9,8},{10,11... | collective-permute-start | bytes 786440 | tf_op jit(solution)/shard_map/merge_sum/ppermute | solution.py:783
  108.6 16.0 %all-to-all-start.4 = ((bf16[16,2,32,128]{3,2,1,0:T(8,128)(2,1)}), bf16[16,2,32,128]{3,2,1,0:T(8,128)(2,1)S(1)}, u32[]{:S(2)}, u32[]{:S(2)}) async-start(bf16[16,2,32,128]{3,2,1,0:T(8,128)(2,1)} %get-tuple-element.133), calls=%async_computation.4 | async-start | bytes 524288 | tf_op jit(solution)/shard_map/branch_sum/all_to_all | solution.py:991
  112.8 0.7 copy-start.2
  113.5 5.8 %collective-permute-start.15 = (bf16[144,256]{1,0:T(8,128)(2,1)S(1)}, bf16[144,256]{1,0:T(8,128)(2,1)S(1)}, u32[]{:S(2)}, u32[]{:S(2)}) collective-permute-start(bf16[144,256]{1,0:T(8,128)(2,1)S(1)} %get-tuple-element.139), channel_id=1, source_target_pairs={{0,8},{1,3},{2,10},{3,1},{4,12},{5,7},{6,14},{7,5},{8,0},{9,11},{1... | collective-permute-start | bytes 221192 | tf_op jit(solution)/shard_map/merge_sum/ppermute | solution.py:779
  115.3 9.3 %collective-permute-start.16 = (bf16[144,256]{1,0:T(8,128)(2,1)S(1)}, bf16[144,256]{1,0:T(8,128)(2,1)S(1)}, u32[]{:S(2)}, u32[]{:S(2)}) collective-permute-start(bf16[144,256]{1,0:T(8,128)(2,1)S(1)} %get-tuple-element.140), channel_id=1, source_target_pairs={{0,16},{1,5},{2,18},{3,7},{4,20},{5,1},{6,22},{7,3},{8,24},{9,13},... | collective-permute-start | bytes 221192 | tf_op jit(solution)/shard_map/merge_sum/ppermute | solution.py:779
  117.7 6.9 %collective-permute-start.17 = (bf16[144,256]{1,0:T(8,128)(2,1)S(1)}, bf16[144,256]{1,0:T(8,128)(2,1)S(1)}, u32[]{:S(2)}, u32[]{:S(2)}) collective-permute-start(bf16[144,256]{1,0:T(8,128)(2,1)S(1)} %get-tuple-element.141), channel_id=1, source_target_pairs={{0,24},{1,7},{2,26},{3,5},{4,28},{5,3},{6,30},{7,1},{8,16},{9,15},... | collective-permute-start | bytes 221192 | tf_op jit(solution)/shard_map/merge_sum/ppermute | solution.py:779
  128.4 11.1 %collective-permute-start.18 = (f32[352,128]{1,0:T(8,128)S(1)}, f32[352,128]{1,0:T(8,128)S(1)}, u32[]{:S(2)}, u32[]{:S(2)}) collective-permute-start(f32[352,128]{1,0:T(8,128)S(1)} %get-tuple-element.146.refs_2_), channel_id=1, source_target_pairs={{0,1},{1,0},{2,3},{3,2},{4,5},{5,4},{6,7},{7,6},{8,9},{9,8},{10,11... | collective-permute-start | bytes 540680 | tf_op jit(solution)/shard_map/ppermute | solution.py:783

commit v6 on v5

--- a/solution.py
+++ b/solution.py
@@ -143,6 +143,44 @@
                 yield arrays[which * 4 + t].at[e], pos_ref[0] ^ (4 * e + t), half
 
 
+HALF = LANES // 2
+QUADS = HALF // 4
+
+
+def store_grams(grams, out_ref):
+    if out_ref.shape[0] == HOPS:
+        for k in range(HOPS):
+            out_ref[k] = grams[k]
+        return
+    lane = lane_of((HALF, LANES))
+    blocks = [g[:HALF] for g in grams]
+    for k in range(0, HOPS, 2):
+        blocks.append(jnp.where(lane < HALF, pltpu.roll(grams[k][HALF:], HALF, 1), grams[k + 1][HALF:]))
+    for i, block in enumerate(blocks):
+        for j in range(QUADS):
+            out_ref[i * QUADS + j] = block[4 * j : 4 * j + 4]
+
+
+def load_grams(in_ref, gram_ref, rest_ref):
+    if in_ref.shape[0] == HOPS:
+        gram_ref[...] = in_ref[...]
+        return
+    for i in range(HOPS + HOPS // 2):
+        for j in range(QUADS):
+            rows = slice(4 * j, 4 * j + 4)
+            if i < HOPS:
+                gram_ref[i, rows, :] = in_ref[i * QUADS + j]
+            else:
+                rest_ref[i - HOPS, rows, :] = in_ref[i * QUADS + j]
+    lane = lane_of((HALF, LANES))
+    for k in range(HOPS):
+        upper = jnp.concatenate([gram_ref[k, :HALF, :], jnp.zeros((HALF, LANES), F32)], axis=0)
+        rest = rest_ref[k // 2]
+        if k % 2 == 0:
+            rest = pltpu.roll(rest, HALF, 1)
+        gram_ref[k, HALF:, :] = jnp.where(lane < HALF, jnp.transpose(upper)[HALF:], rest)
+
+
 def gather_kernel(idx_ref, tab_ref, x_ref, gram_ref, acc, pad):
     i = pl.program_id(0)
     width = tab_ref.shape[1]
@@ -164,11 +202,13 @@
     def _():
         row = lax.broadcasted_iota(jnp.int32, pad.shape, 0)
         pad[...] = jnp.where(row == d_in, 1.0, 0.0)
+        grams = []
         for k in range(HOPS):
             pad[0:d_in, :] = acc[k * d_in : (k + 1) * d_in, :]
             x = pad[...].astype(BF16)
             x_ref[k] = x
-            gram_ref[k] = dot(x, x, 1, 1)
+            grams.append(dot(x, x, 1, 1))
+        store_grams(grams, gram_ref)
 
 
 def sum_spread_kernel(in_ref, out_ref):
@@ -191,7 +231,7 @@
     return total
 
 
-def assemble_kernel(classes, pos_ref, *refs):
+def assemble_kernel(classes, pos_ref, order_ref, *refs):
     wb_ref, wm_out, wm_ref, sems = refs[8:]
     hid = wb_ref.shape[1]
     cb = hid // 16
@@ -218,7 +258,11 @@
     stored()
 
 
-def own_stats(count, rep, gram_ref, own_ref, fix_ref):
+def own_stats_kernel(count, pos_ref, in_ref, own_hbm, gram_ref, fix_ref, rest_ref, own_ref, sems):
+    wait = fetch((own_hbm,), (own_ref,), sems)
+    load_grams(in_ref, gram_ref, rest_ref)
+    wait()
+    rep = pos_ref[1]
     lane = lane_of(fix_ref.shape[1:])
     tail = own_ref[HOPS].astype(F32)
     for i in range(2):
@@ -235,8 +279,7 @@
         fix_ref[i] = block
 
 
-def stats_kernel(count, pos_ref, gram_ref, wb_ref, own_ref, ws_ref, coef_ref, mu_ref, wt_ref, fix_ref):
-    own_stats(count, pos_ref[1], gram_ref, own_ref, fix_ref)
+def stats_kernel(count, gram_ref, wb_ref, ws_ref, coef_ref, mu_ref, wt_ref):
     hid = wb_ref.shape[1]
     small = jnp.transpose(wb_ref[HOPS].astype(F32))
     row = lax.broadcasted_iota(jnp.int32, (16, hid), 0)
@@ -389,17 +432,19 @@
             act[at, lanes] = (u * (c[2] + c[3] * jnp.tanh(u))).astype(BF16)
         return carry
 
-    lax.fori_loop(0, hid // ROWS, first, 0, unroll=4)
+    lax.fori_loop(0, hid // ROWS, first, 0, unroll=8)
     tail = wb_ref[HOPS]
     wc = jnp.where(lane_of(tail.shape) < PCOL, tail.astype(F32), 0.0).astype(BF16)
     logits = dot(wc, act[...], 0, 0)
-    row = lax.broadcasted_iota(jnp.int32, (LANES, batch), 0)
-    logits = jnp.where(row < classes, logits + par[0:LANES, 3:4], -jnp.inf)
+    live = -(-classes // 16) * 16
+    row = lax.broadcasted_iota(jnp.int32, (live, batch), 0)
+    logits = jnp.where(row < classes, logits[:live] + par[0:live, 3:4], -jnp.inf)
     top = jnp.max(logits, axis=0, keepdims=True)
     e = jnp.exp(logits - top)
     probs = e / jnp.sum(e, axis=0, keepdims=True)
     wait()
     dlog = (probs - jnp.where(row == lab_ref[...], 1.0, 0.0)).astype(BF16)
+    dlog = jnp.concatenate([dlog, jnp.zeros((LANES - live, batch), BF16)], axis=0)
     grad_class = dot(act[...], dlog, 1, 1)
     bias = jnp.sum(dlog.astype(F32), axis=1, keepdims=True)
     dact[...] = dot(wc, dlog, 1, 0)
@@ -426,7 +471,7 @@
             sums[i, at, :] = fold_lanes(acc[i])
         return carry
 
-    lax.fori_loop(0, hid // ROWS, second, 0, unroll=4)
+    lax.fori_loop(0, hid // ROWS, second, 0, unroll=8)
     pay = jnp.concatenate([lane_sums(sums[0]), lane_sums(sums[1])], axis=0)
     pay_ref[...] = jnp.broadcast_to(pay[None], pay_ref.shape)
     lane = lane_of((hid, LANES))
@@ -597,13 +642,13 @@
 
 
 def owner_kernel(
-    count, classes, pos_ref, got_ref, sum2_ref, w1_ref, w2_ref, w3_ref, *refs
+    count, classes, pos_ref, got_ref, sum2_ref, w0_ref, w1_ref, w2_ref, w3_ref, *refs
 ):
-    late = (len(refs) - 7) // 2
-    grad_ref, pay_ref = refs[2 + late : 4 + late]
-    w0_ref, fix_ref, sems, late_sems = refs[4 + 2 * late :]
-    wait = fetch(refs[:2], (w0_ref, fix_ref), sems)
-    brought = fetch(refs[2 : 2 + late], refs[4 + late : 4 + 2 * late], late_sems)
+    late = (len(refs) - 6) // 2
+    grad_ref, pay_ref = refs[1 + late : 3 + late]
+    fix_ref, sems, late_sems = refs[3 + 2 * late :]
+    wait = fetch(refs[:1], (fix_ref,), sems)
+    brought = fetch(refs[1 : 1 + late], refs[3 + late : 3 + 2 * late], late_sems)
     _, _, cb, _ = got_ref.shape
     total = jnp.sum(got_ref[...].astype(F32), axis=0)
     rep = pos_ref[1]
@@ -833,9 +878,10 @@
 
     with jax.named_scope("gather"):
         step = 2048
+        sums = (6 * QUADS, 4, LANES) if 6 * QUADS % n == 0 else (HOPS, LANES, LANES)
         x, gram = call(
             gather_kernel,
-            [vmem((HOPS, LANES, batch), BF16), hbm_out((HOPS, LANES, LANES))],
+            [vmem((HOPS, LANES, batch), BF16), hbm_out(sums)],
             pltpu.with_memory_space_constraint(idx, pltpu.HBM),
             pltpu.with_memory_space_constraint(table.T, pltpu.HBM),
             grid=(nodes // step,),
@@ -845,7 +891,7 @@
             ],
             out_specs=(
                 pl.BlockSpec((HOPS, LANES, batch), lambda i: (0, 0, 0)),
-                pl.BlockSpec((HOPS, LANES, LANES), lambda i: (0, 0, 0)),
+                pl.BlockSpec(sums, lambda i: (0, 0, 0)),
             ),
             scratch=[pltpu.VMEM((width, batch), F32), pltpu.VMEM((LANES, batch), F32)],
             flops=2 * nodes * width * batch,
@@ -853,13 +899,27 @@
             mib=24,
         )
     with jax.named_scope("gram_sum"):
-        parts = gram.reshape(n, HOPS * LANES // n, LANES)
+        parts = gram.reshape(n, -1, *sums[1:]) if sums[1] == 4 else gram.reshape(n, -1, LANES)
         if staged:
             (stacked,) = call(stack_kernel, [sds((4,) + block.shape, BF16)], block, *far)
             parts, stacked = lax.optimization_barrier((parts, stacked))
         parts = exchange(parts)
         (parts,) = call(sum_spread_kernel, [hbm_out(parts.shape)], parts)
-        gram = exchange(parts).reshape(HOPS, LANES, LANES)
+        gram = exchange(parts).reshape(sums)
+    if not staged:
+        own, wb, wm = weights_plain(lhs[0], weights[2], weights[3], weights[1], dp)
+    with jax.named_scope("own_stats"):
+        gram, fix = call(
+            functools.partial(own_stats_kernel, count),
+            [vmem((HOPS, LANES, LANES)), vmem((2, cb, LANES))],
+            pos, gram, own,
+            smem=(0,), hbm=(2,),
+            scratch=[
+                pltpu.VMEM((HOPS // 2, HALF, LANES), F32),
+                pltpu.VMEM(own.shape, BF16),
+                pltpu.SemaphoreType.DMA((1,)),
+            ],
+        )
     if staged:
         mine = [stacked] + [flip(stacked, t, dp) for t in range(1, 4)]
         mine = mine[:1] + [lax.optimization_barrier((v, parts))[0] for v in mine[1:]]
@@ -868,25 +928,21 @@
             wb, wm = call(
                 functools.partial(assemble_kernel, classes),
                 [vmem((HOPS + 1, hid, LANES), BF16), hbm_out(whole, BF16)],
-                pos, *mine, *[swap(v) for v in mine],
+                pos, fix, *mine, *[swap(v) for v in mine],
                 smem=(0,),
                 out_specs=(pl.BlockSpec(memory_space=pltpu.VMEM), pl.BlockSpec(memory_space=pltpu.HBM)),
                 scratch=[pltpu.VMEM(whole, BF16), pltpu.SemaphoreType.DMA((1,))],
             )
-    else:
-        own, wb, wm = weights_plain(lhs[0], weights[2], weights[3], weights[1], dp)
     with jax.named_scope("stats"):
-        ws, coef, mu, wt, fix = call(
+        ws, coef, mu, wt = call(
             functools.partial(stats_kernel, count),
             [
                 vmem((HOPS, hid, 2 * LANES), BF16),
                 vmem((HOPS, hid, LANES)),
                 vmem((8, LANES)),
                 vmem((HOPS, LANES, hid), BF16),
-                vmem((2, cb, LANES)),
             ],
-            pos, gram, wb, own,
-            smem=(0,),
+            gram, wb,
         )
     with jax.named_scope("forward"):
         joined, pre2, pay, wt, fix = call(
@@ -990,17 +1046,19 @@
     with jax.named_scope("branch_sum"):
         got_b = lax.all_to_all(kept_b, "dp", 0, 0, tiled=True)
     with jax.named_scope("owner"):
-        late = (wide[0], fix)
         tr = [(lhs[i],) + tuple(s[1:]) for i, s in enumerate((weights, firsts, seconds))]
         last = (wt, kept_a, sent_a, *tr[0], *tr[1], *tr[2])
         shares, pay, *last = call(
             functools.partial(owner_kernel, count, classes),
             [sds((3 * cb + 2 * mr, LANES)), hbm_out((n, 2, LANES))] + [vmem(v.shape, v.dtype) for v in last],
-            pos, got_b, sum2, *wide[1:], *late, *last,
+            pos, got_b, sum2, *wide, fix, *last,
             smem=(0,),
-            hbm=tuple(range(6, 8 + len(last))),
-            scratch=[pltpu.VMEM(v.shape, v.dtype) for v in late]
-            + [pltpu.SemaphoreType.DMA((2,)), pltpu.SemaphoreType.DMA((len(last),))],
+            hbm=tuple(range(7, 8 + len(last))),
+            scratch=[
+                pltpu.VMEM(fix.shape, F32),
+                pltpu.SemaphoreType.DMA((1,)),
+                pltpu.SemaphoreType.DMA((len(last),)),
+            ],
         )
     theirs = swap(shares)
     got = exchange(pay)

time: 144 us -> 142 us (0.986)
  waiting for transfers between devices: 24.6 us -> 23 us
    all_to_all x2, waiting for transfers between devices: 7.11 us -> 5.39 us  [exchange(): return lax.all_to_all(value, BOTH, 0, 0, tiled=True)]
    ppermute x7, waiting for transfers between devices: 3.12 us -> 1.55 us  [swap(): return lax.ppermute(value, 'rep', [(0, 1), (1, 0)])]
    pallas_call x15 -> x16, Pallas kernels: 52.7 us -> 53.7 us  [call(): pl.pallas_call(kernel, out_shape=tuple(outs), in_specs=in_specs, out_spec...]
  transfers between devices with their start and end apart: 22 -> 22, of which waited for: 8 -> 6; matrix products, arithmetic and copies ran while one was open for 0% -> 0% of each run, Pallas kernels for 19% -> 19%
where the time goes in v6:
time: 142 us
  Pallas kernels  53.7 us (38%)
  blocking collectives  33 us (23%)
  starting transfers between devices  30.8 us (22%)
  waiting for transfers between devices  23 us (16%)
    pallas_call x16, Pallas kernels, call(): pl.pallas_call(kernel, out_shape=tuple(outs), in_specs=in_specs, out_spec...  53.7 us
    all_to_all x3, blocking collectives, exchange(): return lax.all_to_all(value, BOTH, 0, 0, tiled=True)  33 us
    ppermute x6, starting transfers between devices, flip(): return lax.ppermute(value, 'dp', [(i, i ^ mask) for i in range(dp)])  9.31 us
    ppermute x6, waiting for transfers between devices, flip(): return lax.ppermute(value, 'dp', [(i, i ^ mask) for i in range(dp)])  8.75 us
    all_to_all x2, starting transfers between devices, exchange(): return lax.all_to_all(value, BOTH, 0, 0, tiled=True)  8.65 us
    ppermute x6, starting transfers between devices, turn_flip(): return lax.ppermute(value, BOTH, pairs)  8.01 us
    ppermute x6, waiting for transfers between devices, turn_flip(): return lax.ppermute(value, BOTH, pairs)  7.35 us
    all_to_all x2, waiting for transfers between devices, exchange(): return lax.all_to_all(value, BOTH, 0, 0, tiled=True)  5.39 us
  transfers between devices with their start and end apart: 22, of which 6 were waited for; matrix products, arithmetic and copies ran while one was open for 0% of the time, Pallas kernels for 19%

profile of v6, /device:TPU:0, one launch (start us, length us, event | category | flops | bytes accessed | tf_op | source)
XLA Modules:
  0.0 141.7 jit_solution(7251010402560651271)
XLA Ops:
  0.7 0.1 pad_add_fusion.refs_0_
  0.7 2.4 %prep.1 = (bf16[5,32,128]{2,1,0:T(8,128)(2,1)}, bf16[320,128]{1,0:T(8,128)(2,1)S(1)}) custom-call(s32[2]{0:T(128)S(1)} %pad_add_fusion.refs_0_, f32[4,32,100]{2,1,0:T(8,128)} %bitcast.18, f32[32,47]{1,0:T(8,128)} %refs_13_.1, f32[20,32]{1,0:T(8,128)} %refs_14_.1, f32[128,512]{1,0:T(8,128)} %refs_12_.1), custom_call_target="tpu_custom_call" | custom-call | flops 1024 | bytes 1024 | tf_op jit(solution)/shard_map/prep/pallas_call | solution.py:48
  3.1 5.1 %collective-permute-start.2 = (bf16[320,128]{1,0:T(8,128)(2,1)S(1)}, bf16[320,128]{1,0:T(8,128)(2,1)S(1)}, u32[]{:S(2)}, u32[]{:S(2)}) collective-permute-start(bf16[320,128]{1,0:T(8,128)(2,1)S(1)} %get-tuple-element.103.refs_0_), channel_id=1, source_target_pairs={{0,24},{2,26},{4,28},{6,30},{8,16},{10,18},{12,20},{14,22},{16,8},... | collective-permute-start | bytes 245768 | tf_op jit(solution)/shard_map/ppermute | solution.py:815
  8.2 0.0 collective-permute-start.1
  8.2 0.6 collective-permute-start
  8.9 7.1 %gather.1 = (bf16[4,128,1024]{2,1,0:T(8,128)(2,1)S(1)}, f32[96,4,128]{2,1,0:T(4,128)}) custom-call(s32[1,1024]{1,0:T(1,128)} %bitcast.24, f32[400,4096]{1,0:T(8,128)} %bitcast.17, bf16[5,32,128]{2,1,0:T(8,128)(2,1)} %get-tuple-element.100.refs_2_), custom_call_target="tpu_custom_call" | custom-call | flops 1024 | bytes 1024 | tf_op jit(solution)/shard_map/gather/pallas_call | solution.py:48
  16.0 0.0 collective-permute-done.refs_1_
  16.1 6.0 %all-to-all-start = ((f32[32,3,4,128]{3,2,1,0:T(4,128)}), f32[32,3,4,128]{3,2,1,0:T(4,128)S(1)}, u32[]{:S(2)}, u32[]{:S(2)}) async-start(f32[32,3,4,128]{3,2,1,0:T(4,128)} %bitcast.20), calls=%async_computation | async-start | bytes 393216 | tf_op jit(solution)/shard_map/gram_sum/all_to_all | solution.py:832
  22.1 2.7 %collective-permute-start.5 = (bf16[4,320,128]{2,1,0:T(8,128)(2,1)S(1)}, bf16[4,320,128]{2,1,0:T(8,128)(2,1)S(1)}, u32[]{:S(2)}, u32[]{:S(2)}) collective-permute-start(bf16[4,320,128]{2,1,0:T(8,128)(2,1)S(1)} %gram_sum.2.refs_2_), channel_id=1, source_target_pairs={{0,6},{2,4},{4,2},{6,0},{8,14},{10,12},{12,10},{14,8},{16,22},{18,... | collective-permute-start | bytes 983048 | tf_op jit(solution)/shard_map/ppermute | solution.py:815
  24.8 0.6 collective-permute-start.4
  25.4 0.3 collective-permute-start.3
  25.6 5.4 %all-to-all-done.refs_0_ = f32[32,3,4,128]{3,2,1,0:T(4,128)S(1)} async-done(((f32[32,3,4,128]{3,2,1,0:T(4,128)}), f32[32,3,4,128]{3,2,1,0:T(4,128)S(1)}, u32[]{:S(2)}, u32[]{:S(2)}) %all-to-all-start) | async-done | bytes 196640 | tf_op jit(solution)/shard_map/gram_sum/all_to_all | solution.py:832
  31.0 0.7 gram_sum.3
  31.8 2.7 %all-to-all-start.1 = ((f32[32,3,4,128]{3,2,1,0:T(4,128)}), f32[32,3,4,128]{3,2,1,0:T(4,128)S(1)}, u32[]{:S(2)}, u32[]{:S(2)}) async-start(f32[32,3,4,128]{3,2,1,0:T(4,128)} %gram_sum.3), calls=%async_computation.1 | async-start | bytes 393216 | tf_op jit(solution)/shard_map/gram_sum/all_to_all | solution.py:832
  34.4 0.4 collective-permute-start.6
  34.9 0.6 collective-permute-done.5.refs_5_
  35.5 8.1 %collective-permute-done.4.refs_4_ = bf16[4,320,128]{2,1,0:T(8,128)(2,1)S(1)} collective-permute-done((bf16[4,320,128]{2,1,0:T(8,128)(2,1)S(1)}, bf16[4,320,128]{2,1,0:T(8,128)(2,1)S(1)}, u32[]{:S(2)}, u32[]{:S(2)}) %collective-permute-start.4) | collective-permute-done | bytes 327712 | tf_op jit(solution)/shard_map/ppermute | solution.py:815
  43.6 0.5 collective-permute-start.7
  44.1 1.8 %own_stats.1 = (f32[4,128,128]{2,1,0:T(8,128)S(1)}, f32[2,32,128]{2,1,0:T(8,128)S(1)}) custom-call(s32[2]{0:T(128)S(1)} %pad_add_fusion.refs_0_, f32[96,4,128]{2,1,0:T(4,128)S(1)} %bitcast.16, bf16[5,32,128]{2,1,0:T(8,128)(2,1)} %get-tuple-element.100.refs_2_), custom_call_target="tpu_custom_call" | custom-call | flops 1024 | bytes 1024 | tf_op jit(solution)/shard_map/own_stats/pallas_call | solution.py:48
  45.9 0.0 collective-permute-done.9.refs_9_
  45.9 2.7 %weights.1 = (bf16[5,512,128]{2,1,0:T(8,128)(2,1)S(1)}, bf16[4,2048,128]{2,1,0:T(8,128)(2,1)}) custom-call(s32[2]{0:T(128)S(1)} %pad_add_fusion.refs_0_, f32[2,32,128]{2,1,0:T(8,128)S(1)} %get-tuple-element.106.refs_1_.refs_4_, bf16[4,320,128]{2,1,0:T(8,128)(2,1)S(1)} %gram_sum.2.refs_2_, bf16[4,320,128]{2,1,0:T(8,128)(2,1)S(1)} %collective-permute-done.3.refs_3_, ...), custom_call_target="tpu_custom_call" | custom-call | flops 1024 | bytes 1024 | tf_op jit(solution)/shard_map/weights/pallas_call | solution.py:48
  48.6 1.1 stats.1
  49.6 5.9 %forward.1 = (bf16[4,512,1024]{2,1,0:T(8,128)(2,1)S(1)}, f32[512,1024]{1,0:T(8,128)S(1)}, f32[32,8,128]{2,1,0:T(8,128)S(1)}, bf16[4,128,512]{2,1,0:T(8,128)(2,1)}, f32[2,32,128]{2,1,0:T(8,128)}) custom-call(bf16[4,128,1024]{2,1,0:T(8,128)(2,1)S(1)} %get-tuple-element.101.refs_0_.refs_2_.refs_4_, bf16[4,512,256]{2,1,0:T(8,128)(2,1)S(1)} %get-tuple-element.112.refs_1_.refs_3_, ...), custom_call_target="tpu_custom_call" | custom-call | flops 1024 | bytes 1024 | tf_op jit(solution)/shard_map/forward/pallas_call | solution.py:48
  55.5 12.1 %all_to_all.30.refs_0_ = f32[32,8,128]{2,1,0:T(8,128)S(1)} all-to-all(f32[32,8,128]{2,1,0:T(8,128)S(1)} %get-tuple-element.116), channel_id=1, replica_groups=mesh['dp'=16,'rep'=2] {'dp','rep'}, dimensions={0} | all-to-all | bytes 262144 | tf_op jit(solution)/shard_map/all_to_all | solution.py:832
  67.6 3.6 %head.1 = (f32[512,1024]{1,0:T(8,128)S(1)}, f32[32,8,128]{2,1,0:T(8,128)S(1)}, f32[512,128]{1,0:T(8,128)S(1)}, f32[2,512,128]{2,1,0:T(8,128)S(1)}) custom-call(f32[32,8,128]{2,1,0:T(8,128)S(1)} %all_to_all.30.refs_0_, f32[512,1024]{1,0:T(8,128)S(1)} %get-tuple-element.117.refs_1_.refs_4_, ...), custom_call_target="tpu_custom_call" | custom-call | flops 1024 | bytes 1024 | tf_op jit(solution)/shard_map/head/pallas_call | solution.py:48
  71.2 10.0 %all_to_all.31.refs_1_ = f32[32,8,128]{2,1,0:T(8,128)S(1)} all-to-all(f32[32,8,128]{2,1,0:T(8,128)S(1)} %get-tuple-element.118), channel_id=1, replica_groups=mesh['dp'=16,'rep'=2] {'dp','rep'}, dimensions={0} | all-to-all | bytes 262144 | tf_op jit(solution)/shard_map/all_to_all | solution.py:832
  81.2 3.6 %turn.1 = (bf16[512,1024]{1,0:T(8,128)(2,1)S(1)}, f32[16,144,256]{2,1,0:T(8,128)S(1)}, bf16[16,144,256]{2,1,0:T(8,128)(2,1)S(1)}, f32[8,128]{1,0:T(8,128)S(1)}, bf16[4,2048,128]{2,1,0:T(8,128)(2,1)S(1)}) custom-call(s32[2]{0:T(128)S(1)} %pad_add_fusion.refs_0_, f32[32,8,128]{2,1,0:T(8,128)S(1)} %all_to_all.31.refs_1_, ...), custom_call_target="tpu_custom_call" | custom-call | flops 1024 | bytes 1024 | tf_op jit(solution)/shard_map/turn/pallas_call | solution.py:48
  84.8 0.3 collective-permute-start.11
  85.1 7.5 %back.2 = (bf16[16,2,32,128]{3,2,1,0:T(8,128)(2,1)S(1)}, f32[2,128,1024]{2,1,0:T(8,128)}) custom-call(s32[2]{0:T(128)S(1)} %pad_add_fusion.refs_0_, bf16[512,1024]{1,0:T(8,128)(2,1)S(1)} %get-tuple-element.123.refs_1_, bf16[4,128,1024]{2,1,0:T(8,128)(2,1)S(1)} %get-tuple-element.101.refs_0_.refs_2_.refs_4_, ...), custom_call_target="tpu_custom_call" | custom-call | flops 1024 | bytes 1024 | tf_op jit(solution)/shard_map/merge_sum/back/pallas_call | solution.py:48
  92.6 0.8 merge_sum.2
  93.4 0.5 collective-permute-start.13
  93.9 1.3 collective-permute-start.14
  95.3 1.7 %collective-permute-start.12 = (bf16[4,144,256]{2,1,0:T(8,128)(2,1)S(1)}, bf16[4,144,256]{2,1,0:T(8,128)(2,1)S(1)}, u32[]{:S(2)}, u32[]{:S(2)}) collective-permute-start(bf16[4,144,256]{2,1,0:T(8,128)(2,1)S(1)} %get-tuple-element.131.refs_9_), channel_id=1, source_target_pairs={{0,2},{1,9},{2,0},{3,11},{4,6},{5,13},{6,4},{7,15},{8,10},{9,1},{1... | collective-permute-start | bytes 884744 | tf_op jit(solution)/shard_map/merge_sum/ppermute | solution.py:824
  97.0 0.0 collective-permute-start.10
  97.0 1.5 %collective-permute-done.10.refs_8_ = bf16[16,2,32,128]{3,2,1,0:T(8,128)(2,1)S(1)} collective-permute-done((bf16[16,2,32,128]{3,2,1,0:T(8,128)(2,1)S(1)}, bf16[16,2,32,128]{3,2,1,0:T(8,128)(2,1)S(1)}, u32[]{:S(2)}, u32[]{:S(2)}) %collective-permute-start.10) | collective-permute-done | bytes 262176 | tf_op jit(solution)/shard_map/merge_sum/ppermute | solution.py:828
  98.5 8.6 %back.3 = (bf16[16,2,32,128]{3,2,1,0:T(8,128)(2,1)}, f32[2,128,1024]{2,1,0:T(8,128)}) custom-call(s32[2]{0:T(128)S(1)} %pad_add_fusion.refs_0_, bf16[512,1024]{1,0:T(8,128)(2,1)S(1)} %get-tuple-element.123.refs_1_, bf16[4,128,1024]{2,1,0:T(8,128)(2,1)S(1)} %get-tuple-element.101.refs_0_.refs_2_.refs_4_, ...), custom_call_target="tpu_custom_call" | custom-call | flops 1024 | bytes 1024 | tf_op jit(solution)/shard_map/merge_sum/back/pallas_call | solution.py:48
  107.1 0.0 collective-permute-done.13.refs_3_
  107.1 3.5 %all-to-all-start.4 = ((bf16[16,2,32,128]{3,2,1,0:T(8,128)(2,1)}), bf16[16,2,32,128]{3,2,1,0:T(8,128)(2,1)S(1)}, u32[]{:S(2)}, u32[]{:S(2)}) async-start(bf16[16,2,32,128]{3,2,1,0:T(8,128)(2,1)} %get-tuple-element.135), calls=%async_computation.4 | async-start | bytes 524288 | tf_op jit(solution)/shard_map/branch_sum/all_to_all | solution.py:1047
  110.7 0.7 merge_sum.3
  111.4 1.9 %collective-permute-start.15 = (bf16[144,256]{1,0:T(8,128)(2,1)S(1)}, bf16[144,256]{1,0:T(8,128)(2,1)S(1)}, u32[]{:S(2)}, u32[]{:S(2)}) collective-permute-start(bf16[144,256]{1,0:T(8,128)(2,1)S(1)} %get-tuple-element.142), channel_id=1, source_target_pairs={{0,8},{1,3},{2,10},{3,1},{4,12},{5,7},{6,14},{7,5},{8,0},{9,11},{1... | collective-permute-start | bytes 221192 | tf_op jit(solution)/shard_map/merge_sum/ppermute | solution.py:824
  113.3 2.4 %collective-permute-start.16 = (bf16[144,256]{1,0:T(8,128)(2,1)S(1)}, bf16[144,256]{1,0:T(8,128)(2,1)S(1)}, u32[]{:S(2)}, u32[]{:S(2)}) collective-permute-start(bf16[144,256]{1,0:T(8,128)(2,1)S(1)} %get-tuple-element.143), channel_id=1, source_target_pairs={{0,16},{1,5},{2,18},{3,7},{4,20},{5,1},{6,22},{7,3},{8,24},{9,13},... | collective-permute-start | bytes 221192 | tf_op jit(solution)/shard_map/merge_sum/ppermute | solution.py:824
  115.7 0.1 collective-permute-start.17
  115.8 2.0 %collective-permute-done.15.refs_4_ = bf16[144,256]{1,0:T(8,128)(2,1)S(1)} collective-permute-done((bf16[144,256]{1,0:T(8,128)(2,1)S(1)}, bf16[144,256]{1,0:T(8,128)(2,1)S(1)}, u32[]{:S(2)}, u32[]{:S(2)}) %collective-permute-start.15) | collective-permute-done | bytes 73760 | tf_op jit(solution)/shard_map/merge_sum/ppermute | solution.py:824
  117.9 5.3 %collective-permute-done.16.refs_5_ = bf16[144,256]{1,0:T(8,128)(2,1)S(1)} collective-permute-done((bf16[144,256]{1,0:T(8,128)(2,1)S(1)}, bf16[144,256]{1,0:T(8,128)(2,1)S(1)}, u32[]{:S(2)}, u32[]{:S(2)}) %collective-permute-start.16) | collective-permute-done | bytes 73760 | tf_op jit(solution)/shard_map/merge_sum/ppermute | solution.py:824
  123.2 3.6 %owner.1 = (f32[352,128]{1,0:T(8,128)S(1)}, f32[32,2,128]{2,1,0:T(2,128)}, bf16[4,128,512]{2,1,0:T(8,128)(2,1)S(1)}, f32[2,128,1024]{2,1,0:T(8,128)S(1)}, f32[2,...) custom-call(s32[2]{0:T(128)S(1)} %pad_add_fusion.refs_0_, ...), custom_call_target="tpu_custom_call" | custom-call | flops 1024 | bytes 1024 | tf_op jit(solution)/shard_map/owner/pallas_call | solution.py:48
  126.8 0.1 collective-permute-start.18
  126.9 11.0 %all_to_all.32.refs_1_ = f32[32,2,128]{2,1,0:T(2,128)S(1)} all-to-all(f32[32,2,128]{2,1,0:T(2,128)} %get-tuple-element.147), channel_id=1, replica_groups=mesh['dp'=16,'rep'=2] {'dp','rep'}, dimensions={0} | all-to-all | bytes 65536 | tf_op jit(solution)/shard_map/all_to_all | solution.py:832
  137.8 3.7 %final.1 = (f32[4,32,100]{2,1,0:T(8,128)}, f32[128,512]{1,0:T(8,128)}, f32[32,47]{1,0:T(8,128)}, f32[20,32]{1,0:T(8,128)}, f32[4,32,100]{2,1,0:T(8,128)}, /*inde...) custom-call(s32[2]{0:T(128)S(1)} %pad_add_fusion.refs_0_, ...), custom_call_target="tpu_custom_call" | custom-call | flops 1024 | bytes 1024 | tf_op jit(solution)/shard_map/final/pallas_call | solution.py:48
  (18 shorter events, 0.1 us)
Async XLA Ops:
  3.1 12.9 %collective-permute-start.2 = (bf16[320,128]{1,0:T(8,128)(2,1)S(1)}, bf16[320,128]{1,0:T(8,128)(2,1)S(1)}, u32[]{:S(2)}, u32[]{:S(2)}) collective-permute-start(bf16[320,128]{1,0:T(8,128)(2,1)S(1)} %get-tuple-element.103.refs_0_), channel_id=1, source_target_pairs={{0,24},{2,26},{4,28},{6,30},{8,16},{10,18},{12,20},{14,22},{16,8},... | collective-permute-start | bytes 245768 | tf_op jit(solution)/shard_map/ppermute | solution.py:815
  8.2 7.8 %collective-permute-start.1 = (bf16[320,128]{1,0:T(8,128)(2,1)S(1)}, bf16[320,128]{1,0:T(8,128)(2,1)S(1)}, u32[]{:S(2)}, u32[]{:S(2)}) collective-permute-start(bf16[320,128]{1,0:T(8,128)(2,1)S(1)} %get-tuple-element.103.refs_0_), channel_id=1, source_target_pairs={{0,16},{2,18},{4,20},{6,22},{8,24},{10,26},{12,28},{14,30},{16,0},... | collective-permute-start | bytes 245768 | tf_op jit(solution)/shard_map/ppermute | solution.py:815
  8.2 7.8 %collective-permute-start = (bf16[320,128]{1,0:T(8,128)(2,1)S(1)}, bf16[320,128]{1,0:T(8,128)(2,1)S(1)}, u32[]{:S(2)}, u32[]{:S(2)}) collective-permute-start(bf16[320,128]{1,0:T(8,128)(2,1)S(1)} %get-tuple-element.103.refs_0_), channel_id=1, source_target_pairs={{0,8},{2,10},{4,12},{6,14},{8,0},{10,2},{12,4},{14,6},{16,24},{18,... | collective-permute-start | bytes 245768 | tf_op jit(solution)/shard_map/ppermute | solution.py:815
  16.1 15.0 %all-to-all-start = ((f32[32,3,4,128]{3,2,1,0:T(4,128)}), f32[32,3,4,128]{3,2,1,0:T(4,128)S(1)}, u32[]{:S(2)}, u32[]{:S(2)}) async-start(f32[32,3,4,128]{3,2,1,0:T(4,128)} %bitcast.20), calls=%async_computation | async-start | bytes 393216 | tf_op jit(solution)/shard_map/gram_sum/all_to_all | solution.py:832
  22.1 13.4 %collective-permute-start.5 = (bf16[4,320,128]{2,1,0:T(8,128)(2,1)S(1)}, bf16[4,320,128]{2,1,0:T(8,128)(2,1)S(1)}, u32[]{:S(2)}, u32[]{:S(2)}) collective-permute-start(bf16[4,320,128]{2,1,0:T(8,128)(2,1)S(1)} %gram_sum.2.refs_2_), channel_id=1, source_target_pairs={{0,6},{2,4},{4,2},{6,0},{8,14},{10,12},{12,10},{14,8},{16,22},{18,... | collective-permute-start | bytes 983048 | tf_op jit(solution)/shard_map/ppermute | solution.py:815
  24.8 18.8 %collective-permute-start.4 = (bf16[4,320,128]{2,1,0:T(8,128)(2,1)S(1)}, bf16[4,320,128]{2,1,0:T(8,128)(2,1)S(1)}, u32[]{:S(2)}, u32[]{:S(2)}) collective-permute-start(bf16[4,320,128]{2,1,0:T(8,128)(2,1)S(1)} %gram_sum.2.refs_2_), channel_id=1, source_target_pairs={{0,4},{2,6},{4,0},{6,2},{8,12},{10,14},{12,8},{14,10},{16,20},{18,... | collective-permute-start | bytes 983048 | tf_op jit(solution)/shard_map/ppermute | solution.py:815
  25.4 18.2 %collective-permute-start.3 = (bf16[4,320,128]{2,1,0:T(8,128)(2,1)S(1)}, bf16[4,320,128]{2,1,0:T(8,128)(2,1)S(1)}, u32[]{:S(2)}, u32[]{:S(2)}) collective-permute-start(bf16[4,320,128]{2,1,0:T(8,128)(2,1)S(1)} %gram_sum.2.refs_2_), channel_id=1, source_target_pairs={{0,2},{2,0},{4,6},{6,4},{8,10},{10,8},{12,14},{14,12},{16,18},{18,... | collective-permute-start | bytes 983048 | tf_op jit(solution)/shard_map/ppermute | solution.py:815
  31.8 12.3 %all-to-all-start.1 = ((f32[32,3,4,128]{3,2,1,0:T(4,128)}), f32[32,3,4,128]{3,2,1,0:T(4,128)S(1)}, u32[]{:S(2)}, u32[]{:S(2)}) async-start(f32[32,3,4,128]{3,2,1,0:T(4,128)} %gram_sum.3), calls=%async_computation.1 | async-start | bytes 393216 | tf_op jit(solution)/shard_map/gram_sum/all_to_all | solution.py:832
  34.4 11.4 %collective-permute-start.6 = (bf16[4,320,128]{2,1,0:T(8,128)(2,1)S(1)}, bf16[4,320,128]{2,1,0:T(8,128)(2,1)S(1)}, u32[]{:S(2)}, u32[]{:S(2)}) collective-permute-start(bf16[4,320,128]{2,1,0:T(8,128)(2,1)S(1)} %gram_sum.2.refs_2_), channel_id=1, source_target_pairs={{0,1},{1,0},{2,3},{3,2},{4,5},{5,4},{6,7},{7,6},{8,9},{9,8},{10,11... | collective-permute-start | bytes 983048 | tf_op jit(solution)/shard_map/weights/ppermute | solution.py:828
  35.5 10.4 %collective-permute-start.9 = (bf16[4,320,128]{2,1,0:T(8,128)(2,1)S(1)}, bf16[4,320,128]{2,1,0:T(8,128)(2,1)S(1)}, u32[]{:S(2)}, u32[]{:S(2)}) collective-permute-start(bf16[4,320,128]{2,1,0:T(8,128)(2,1)S(1)} %collective-permute-done.5.refs_5_), channel_id=1, source_target_pairs={{0,1},{1,0},{2,3},{3,2},{4,5},{5,4},{6,7},{7,6},{8,9},{9,8},{10,11... | collective-permute-start | bytes 983048 | tf_op jit(solution)/shard_map/weights/ppermute | solution.py:828
  43.6 2.3 %collective-permute-start.8 = (bf16[4,320,128]{2,1,0:T(8,128)(2,1)S(1)}, bf16[4,320,128]{2,1,0:T(8,128)(2,1)S(1)}, u32[]{:S(2)}, u32[]{:S(2)}) collective-permute-start(bf16[4,320,128]{2,1,0:T(8,128)(2,1)S(1)} %collective-permute-done.4.refs_4_), channel_id=1, source_target_pairs={{0,1},{1,0},{2,3},{3,2},{4,5},{5,4},{6,7},{7,6},{8,9},{9,8},{10,11... | collective-permute-start | bytes 983048 | tf_op jit(solution)/shard_map/weights/ppermute | solution.py:828
  43.6 2.3 %collective-permute-start.7 = (bf16[4,320,128]{2,1,0:T(8,128)(2,1)S(1)}, bf16[4,320,128]{2,1,0:T(8,128)(2,1)}, u32[]{:S(2)}, u32[]{:S(2)}) collective-permute-start(bf16[4,320,128]{2,1,0:T(8,128)(2,1)S(1)} %collective-permute-done.3.refs_3_), channel_id=1, source_target_pairs={{0,1},{1,0},{2,3},{3,2},{4,5},{5,4},{6,7},{7,6},{8,9},{9,8},{10,11... | collective-permute-start | bytes 983048 | tf_op jit(solution)/shard_map/weights/ppermute | solution.py:828
  84.8 7.8 %collective-permute-start.11 = (bf16[16,144,256]{2,1,0:T(8,128)(2,1)S(1)}, bf16[16,144,256]{2,1,0:T(8,128)(2,1)S(1)}, u32[]{:S(2)}, u32[]{:S(2)}) collective-permute-start(bf16[16,144,256]{2,1,0:T(8,128)(2,1)S(1)} %get-tuple-element.129), channel_id=1, source_target_pairs={{0,1},{1,0},{2,3},{3,2},{4,5},{5,4},{6,7},{7,6},{8,9},{9,8},{10,11... | collective-permute-start | bytes 3538952 | tf_op jit(solution)/shard_map/ppermute | solution.py:828
  93.4 5.1 %copy-start = (bf16[4,144,256]{2,1,0:T(8,128)(2,1)}, bf16[4,144,256]{2,1,0:T(8,128)(2,1)S(1)}, u32[]{:S(2)}) copy-start(bf16[4,144,256]{2,1,0:T(8,128)(2,1)S(1)} %get-tuple-element.131.refs_9_) | copy-start | bytes 884740
  93.4 13.7 %collective-permute-start.13 = (bf16[4,144,256]{2,1,0:T(8,128)(2,1)S(1)}, bf16[4,144,256]{2,1,0:T(8,128)(2,1)S(1)}, u32[]{:S(2)}, u32[]{:S(2)}) collective-permute-start(bf16[4,144,256]{2,1,0:T(8,128)(2,1)S(1)} %get-tuple-element.133), channel_id=1, source_target_pairs={{0,4},{1,17},{2,6},{3,19},{4,0},{5,21},{6,2},{7,23},{8,12},{9,25},... | collective-permute-start | bytes 884744 | tf_op jit(solution)/shard_map/merge_sum/ppermute | solution.py:824
  93.9 13.2 %collective-permute-start.14 = (bf16[4,144,256]{2,1,0:T(8,128)(2,1)S(1)}, bf16[4,144,256]{2,1,0:T(8,128)(2,1)S(1)}, u32[]{:S(2)}, u32[]{:S(2)}) collective-permute-start(bf16[4,144,256]{2,1,0:T(8,128)(2,1)S(1)} %get-tuple-element.134), channel_id=1, source_target_pairs={{0,6},{1,25},{2,4},{3,27},{4,2},{5,29},{6,0},{7,31},{8,14},{9,17},... | collective-permute-start | bytes 884744 | tf_op jit(solution)/shard_map/merge_sum/ppermute | solution.py:824
  95.3 11.9 %collective-permute-start.12 = (bf16[4,144,256]{2,1,0:T(8,128)(2,1)S(1)}, bf16[4,144,256]{2,1,0:T(8,128)(2,1)S(1)}, u32[]{:S(2)}, u32[]{:S(2)}) collective-permute-start(bf16[4,144,256]{2,1,0:T(8,128)(2,1)S(1)} %get-tuple-element.131.refs_9_), channel_id=1, source_target_pairs={{0,2},{1,9},{2,0},{3,11},{4,6},{5,13},{6,4},{7,15},{8,10},{9,1},{1... | collective-permute-start | bytes 884744 | tf_op jit(solution)/shard_map/merge_sum/ppermute | solution.py:824
  97.0 1.5 %collective-permute-start.10 = (bf16[16,2,32,128]{3,2,1,0:T(8,128)(2,1)S(1)}, bf16[16,2,32,128]{3,2,1,0:T(8,128)(2,1)S(1)}, u32[]{:S(2)}, u32[]{:S(2)}) collective-permute-start(bf16[16,2,32,128]{3,2,1,0:T(8,128)(2,1)S(1)} %get-tuple-element.127), channel_id=1, source_target_pairs={{0,1},{1,0},{2,3},{3,2},{4,5},{5,4},{6,7},{7,6},{8,9},{9,8},{10,11... | collective-permute-start | bytes 786440 | tf_op jit(solution)/shard_map/merge_sum/ppermute | solution.py:828
  107.1 16.0 %all-to-all-start.4 = ((bf16[16,2,32,128]{3,2,1,0:T(8,128)(2,1)}), bf16[16,2,32,128]{3,2,1,0:T(8,128)(2,1)S(1)}, u32[]{:S(2)}, u32[]{:S(2)}) async-start(bf16[16,2,32,128]{3,2,1,0:T(8,128)(2,1)} %get-tuple-element.135), calls=%async_computation.4 | async-start | bytes 524288 | tf_op jit(solution)/shard_map/branch_sum/all_to_all | solution.py:1047
  111.4 6.5 %collective-permute-start.15 = (bf16[144,256]{1,0:T(8,128)(2,1)S(1)}, bf16[144,256]{1,0:T(8,128)(2,1)S(1)}, u32[]{:S(2)}, u32[]{:S(2)}) collective-permute-start(bf16[144,256]{1,0:T(8,128)(2,1)S(1)} %get-tuple-element.142), channel_id=1, source_target_pairs={{0,8},{1,3},{2,10},{3,1},{4,12},{5,7},{6,14},{7,5},{8,0},{9,11},{1... | collective-permute-start | bytes 221192 | tf_op jit(solution)/shard_map/merge_sum/ppermute | solution.py:824
  113.3 9.9 %collective-permute-start.16 = (bf16[144,256]{1,0:T(8,128)(2,1)S(1)}, bf16[144,256]{1,0:T(8,128)(2,1)S(1)}, u32[]{:S(2)}, u32[]{:S(2)}) collective-permute-start(bf16[144,256]{1,0:T(8,128)(2,1)S(1)} %get-tuple-element.143), channel_id=1, source_target_pairs={{0,16},{1,5},{2,18},{3,7},{4,20},{5,1},{6,22},{7,3},{8,24},{9,13},... | collective-permute-start | bytes 221192 | tf_op jit(solution)/shard_map/merge_sum/ppermute | solution.py:824
  115.7 7.5 %collective-permute-start.17 = (bf16[144,256]{1,0:T(8,128)(2,1)S(1)}, bf16[144,256]{1,0:T(8,128)(2,1)S(1)}, u32[]{:S(2)}, u32[]{:S(2)}) collective-permute-start(bf16[144,256]{1,0:T(8,128)(2,1)S(1)} %get-tuple-element.144), channel_id=1, source_target_pairs={{0,24},{1,7},{2,26},{3,5},{4,28},{5,3},{6,30},{7,1},{8,16},{9,15},... | collective-permute-start | bytes 221192 | tf_op jit(solution)/shard_map/merge_sum/ppermute | solution.py:824
  126.8 11.1 %collective-permute-start.18 = (f32[352,128]{1,0:T(8,128)S(1)}, f32[352,128]{1,0:T(8,128)S(1)}, u32[]{:S(2)}, u32[]{:S(2)}) collective-permute-start(f32[352,128]{1,0:T(8,128)S(1)} %get-tuple-element.148.refs_2_), channel_id=1, source_target_pairs={{0,1},{1,0},{2,3},{3,2},{4,5},{5,4},{6,7},{7,6},{8,9},{9,8},{10,11... | collective-permute-start | bytes 540680 | tf_op jit(solution)/shard_map/ppermute | solution.py:828

commit v7 on v6

--- a/solution.py
+++ b/solution.py
@@ -181,8 +181,21 @@
         gram_ref[k, HALF:, :] = jnp.where(lane < HALF, jnp.transpose(upper)[HALF:], rest)
 
 
-def gather_kernel(idx_ref, tab_ref, x_ref, gram_ref, acc, pad):
+def gather_kernel(idx_ref, tab_ref, *refs):
     i = pl.program_id(0)
+    if len(refs) > 4:
+        own_ref, x_ref, gram_ref, own_out, acc, pad, sem = refs
+        copy = pltpu.make_async_copy(own_ref, own_out, sem)
+
+        @pl.when(i == 0)
+        def _():
+            copy.start()
+
+        @pl.when(i == pl.num_programs(0) - 1)
+        def _():
+            copy.wait()
+    else:
+        x_ref, gram_ref, acc, pad = refs
     width = tab_ref.shape[1]
     d_in = tab_ref.shape[0] // HOPS
     batch = idx_ref.shape[1]
@@ -660,6 +673,21 @@
         return jnp.sum(jnp.sum(v, axis=1, keepdims=True), axis=0, keepdims=True)
 
     others = w1_ref[...].astype(F32) + w2_ref[...].astype(F32) + w3_ref[...].astype(F32)
+    wide = w0_ref[...].astype(F32) + others
+    mr = wide.shape[0] - cb // 2
+    merge = wide[:mr]
+    squares = squares + all_sum(merge * merge)
+    at = 2 * cb
+    for i in range(2):
+        grad_ref[at + i * mr : at + (i + 1) * mr, :] = merge[:, i * LANES : (i + 1) * LANES]
+    at = at + 2 * mr
+    block = jnp.concatenate([wide[mr:, :LANES], wide[mr:, LANES:]], axis=0)
+    shift_own = own_column(sum2_ref, 0, pos_ref[0], cb)
+    gain_own = own_column(sum2_ref, 4, pos_ref[0], cb)
+    block = jnp.where(lane == PCOL + 2, gain_own, block)
+    block = jnp.where(lane == PCOL + 3, shift_own, block)
+    grad_ref[at : at + cb, :] = block
+    squares = squares + jnp.where(rep == 0, all_sum(block * block), 0.0)
     wait()
     for i in range(2):
         b = join_smalls(total[i])
@@ -678,21 +706,6 @@
         squares = squares + all_sum(fixed * fixed)
         spread = jnp.where(lane == 2 * i, alpha, spread)
         spread = jnp.where(lane == 2 * i + 1, beta, spread)
-    wide = w0_ref[...].astype(F32) + others
-    mr = wide.shape[0] - cb // 2
-    merge = wide[:mr]
-    squares = squares + all_sum(merge * merge)
-    at = 2 * cb
-    for i in range(2):
-        grad_ref[at + i * mr : at + (i + 1) * mr, :] = merge[:, i * LANES : (i + 1) * LANES]
-    at = at + 2 * mr
-    block = jnp.concatenate([wide[mr:, :LANES], wide[mr:, LANES:]], axis=0)
-    shift_own = own_column(sum2_ref, 0, pos_ref[0], cb)
-    gain_own = own_column(sum2_ref, 4, pos_ref[0], cb)
-    block = jnp.where(lane == PCOL + 2, gain_own, block)
-    block = jnp.where(lane == PCOL + 3, shift_own, block)
-    grad_ref[at : at + cb, :] = block
-    squares = squares + jnp.where(rep == 0, all_sum(block * block), 0.0)
     rows = jnp.transpose(jnp.concatenate([spread, jnp.zeros((LANES - cb, LANES), F32)], axis=0))[0:8]
     packed = jnp.concatenate([rows[i : i + 1, :cb] for i in range(4)], axis=1)
     if 4 * cb < LANES:
@@ -868,7 +881,7 @@
             size = HOPS * cb // 2 + 2 * mr
             own, block = call(
                 prep_kernel,
-                [hbm_out((HOPS + 1, cb, LANES), BF16), sds((size, LANES), BF16)],
+                [vmem((HOPS + 1, cb, LANES), BF16), sds((size, LANES), BF16)],
                 pos, *sources,
                 smem=(0,), hbm=(1, 2, 3, 4),
                 scratch=[pltpu.VMEM(v.shape, F32) for v in sources]
@@ -879,25 +892,30 @@
     with jax.named_scope("gather"):
         step = 2048
         sums = (6 * QUADS, 4, LANES) if 6 * QUADS % n == 0 else (HOPS, LANES, LANES)
-        x, gram = call(
+        passed = [own] if staged else []
+        x, gram, *made = call(
             gather_kernel,
-            [vmem((HOPS, LANES, batch), BF16), hbm_out(sums)],
+            [vmem((HOPS, LANES, batch), BF16), hbm_out(sums)] + [hbm_out(v.shape, v.dtype) for v in passed],
             pltpu.with_memory_space_constraint(idx, pltpu.HBM),
             pltpu.with_memory_space_constraint(table.T, pltpu.HBM),
+            *passed,
             grid=(nodes // step,),
             in_specs=[
                 pl.BlockSpec((1, batch), lambda i: (0, 0)),
                 pl.BlockSpec((width, step), lambda i: (0, i)),
-            ],
+            ]
+            + [pl.BlockSpec(memory_space=pltpu.VMEM) for _ in passed],
             out_specs=(
                 pl.BlockSpec((HOPS, LANES, batch), lambda i: (0, 0, 0)),
                 pl.BlockSpec(sums, lambda i: (0, 0, 0)),
-            ),
-            scratch=[pltpu.VMEM((width, batch), F32), pltpu.VMEM((LANES, batch), F32)],
-            flops=2 * nodes * width * batch,
-            after=(own,) if staged else (),
+            )
+            + tuple(pl.BlockSpec(memory_space=pltpu.HBM) for _ in passed),
+            scratch=[pltpu.VMEM((width, batch), F32), pltpu.VMEM((LANES, batch), F32)]
+            + [pltpu.SemaphoreType.DMA for _ in passed],
             mib=24,
         )
+        if staged:
+            own = made[0]
     with jax.named_scope("gram_sum"):
         parts = gram.reshape(n, -1, *sums[1:]) if sums[1] == 4 else gram.reshape(n, -1, LANES)
         if staged:
@@ -1029,7 +1047,8 @@
                 smem=(0,),
                 after=(sent_a,),
             )
-            moved = [turn_flip(low[t], t, dp, 1) for t in range(1, 4)]
+            away, recv_b = lax.optimization_barrier((low[1:], recv_b))
+            moved = [turn_flip(v, t, dp, 1) for t, v in enumerate(away, 1)]
             kept_b, kept_a = back(True, 0, 2, recv_b, after=(low[1],))
             kept_b, moved = lax.optimization_barrier((kept_b, moved))
             high = call(

time: 142 us -> 141 us (level)
  waiting for transfers between devices: 23 us -> 21.5 us
  transfers between devices with their start and end apart: 22 -> 22, of which waited for: 6 -> 7; matrix products, arithmetic and copies ran while one was open for 0% -> 0% of each run, Pallas kernels for 19% -> 19%
where the time goes in v7:
time: 141 us; the launch traced here: 140 us
  Pallas kernels  53 us (38%)
  blocking collectives  32.6 us (23%)
  starting transfers between devices  32 us (23%)
  waiting for transfers between devices  21.5 us (15%)
    pallas_call x16, Pallas kernels, call(): pl.pallas_call(kernel, out_shape=tuple(outs), in_specs=in_specs, out_spec...  53 us
    all_to_all x3, blocking collectives, exchange(): return lax.all_to_all(value, BOTH, 0, 0, tiled=True)  32.6 us
    ppermute x6, starting transfers between devices, flip(): return lax.ppermute(value, 'dp', [(i, i ^ mask) for i in range(dp)])  9.31 us
    ppermute x6, waiting for transfers between devices, flip(): return lax.ppermute(value, 'dp', [(i, i ^ mask) for i in range(dp)])  8.75 us
    all_to_all x2, starting transfers between devices, exchange(): return lax.all_to_all(value, BOTH, 0, 0, tiled=True)  8.65 us
    ppermute x6, starting transfers between devices, turn_flip(): return lax.ppermute(value, BOTH, pairs)  7.94 us
    ppermute x6, waiting for transfers between devices, turn_flip(): return lax.ppermute(value, BOTH, pairs)  6.87 us
    all_to_all x2, waiting for transfers between devices, exchange(): return lax.all_to_all(value, BOTH, 0, 0, tiled=True)  5.39 us
  transfers between devices with their start and end apart: 22, of which 7 were waited for; matrix products, arithmetic and copies ran while one was open for 0% of the time, Pallas kernels for 19%

profile of v7, /device:TPU:0, one launch (start us, length us, event | category | flops | bytes accessed | tf_op | source)
XLA Modules:
  0.0 140.3 jit_solution(17621600668908215648)
XLA Ops:
  0.7 0.1 pad_add_fusion.refs_0_
  0.7 1.8 %prep.1 = (bf16[5,32,128]{2,1,0:T(8,128)(2,1)S(1)}, bf16[320,128]{1,0:T(8,128)(2,1)S(1)}) custom-call(s32[2]{0:T(128)S(1)} %pad_add_fusion.refs_0_, f32[4,32,100]{2,1,0:T(8,128)} %bitcast.18, f32[32,47]{1,0:T(8,128)} %refs_13_.1, f32[20,32]{1,0:T(8,128)} %refs_14_.1, f32[128,512]{1,0:T(8,128)} %refs_12_.1), custom_call_target="tpu_custom_call" | custom-call | flops 1024 | bytes 1024 | tf_op jit(solution)/shard_map/prep/pallas_call | solution.py:48
  2.5 5.1 %collective-permute-start.2 = (bf16[320,128]{1,0:T(8,128)(2,1)S(1)}, bf16[320,128]{1,0:T(8,128)(2,1)S(1)}, u32[]{:S(2)}, u32[]{:S(2)}) collective-permute-start(bf16[320,128]{1,0:T(8,128)(2,1)S(1)} %get-tuple-element.108.refs_0_), channel_id=1, source_target_pairs={{0,24},{2,26},{4,28},{6,30},{8,16},{10,18},{12,20},{14,22},{16,8},... | collective-permute-start | bytes 245768 | tf_op jit(solution)/shard_map/ppermute | solution.py:828
  7.6 0.0 collective-permute-start.1
  7.6 0.6 collective-permute-start
  8.3 7.2 %gather.1 = (bf16[4,128,1024]{2,1,0:T(8,128)(2,1)S(1)}, f32[96,4,128]{2,1,0:T(4,128)}, bf16[5,32,128]{2,1,0:T(8,128)(2,1)}) custom-call(s32[1,1024]{1,0:T(1,128)} %bitcast.24, f32[400,4096]{1,0:T(8,128)} %bitcast.17, bf16[5,32,128]{2,1,0:T(8,128)(2,1)S(1)} %get-tuple-element.105.refs_2_), custom_call_target="tpu_custom_call" | custom-call | flops 1024 | bytes 1024 | tf_op jit(solution)/shard_map/gather/pallas_call | solution.py:48
  15.4 0.0 collective-permute-done.2.refs_3_
  15.5 6.0 %all-to-all-start = ((f32[32,3,4,128]{3,2,1,0:T(4,128)}), f32[32,3,4,128]{3,2,1,0:T(4,128)S(1)}, u32[]{:S(2)}, u32[]{:S(2)}) async-start(f32[32,3,4,128]{3,2,1,0:T(4,128)} %bitcast.20), calls=%async_computation | async-start | bytes 393216 | tf_op jit(solution)/shard_map/gram_sum/all_to_all | solution.py:845
  21.5 2.7 %collective-permute-start.5 = (bf16[4,320,128]{2,1,0:T(8,128)(2,1)S(1)}, bf16[4,320,128]{2,1,0:T(8,128)(2,1)S(1)}, u32[]{:S(2)}, u32[]{:S(2)}) collective-permute-start(bf16[4,320,128]{2,1,0:T(8,128)(2,1)S(1)} %gram_sum.2.refs_2_), channel_id=1, source_target_pairs={{0,6},{2,4},{4,2},{6,0},{8,14},{10,12},{12,10},{14,8},{16,22},{18,... | collective-permute-start | bytes 983048 | tf_op jit(solution)/shard_map/ppermute | solution.py:828
  24.2 0.6 collective-permute-start.4
  24.8 0.3 collective-permute-start.3
  25.1 5.4 %all-to-all-done.refs_0_ = f32[32,3,4,128]{3,2,1,0:T(4,128)S(1)} async-done(((f32[32,3,4,128]{3,2,1,0:T(4,128)}), f32[32,3,4,128]{3,2,1,0:T(4,128)S(1)}, u32[]{:S(2)}, u32[]{:S(2)}) %all-to-all-start) | async-done | bytes 196640 | tf_op jit(solution)/shard_map/gram_sum/all_to_all | solution.py:845
  30.5 0.7 gram_sum.3
  31.2 2.7 %all-to-all-start.1 = ((f32[32,3,4,128]{3,2,1,0:T(4,128)}), f32[32,3,4,128]{3,2,1,0:T(4,128)S(1)}, u32[]{:S(2)}, u32[]{:S(2)}) async-start(f32[32,3,4,128]{3,2,1,0:T(4,128)} %gram_sum.3), calls=%async_computation.1 | async-start | bytes 393216 | tf_op jit(solution)/shard_map/gram_sum/all_to_all | solution.py:845
  33.8 0.4 collective-permute-start.6
  34.3 0.6 collective-permute-done.5.refs_5_
  34.9 0.0 collective-permute-start.9
  34.9 8.1 %collective-permute-done.4.refs_4_ = bf16[4,320,128]{2,1,0:T(8,128)(2,1)S(1)} collective-permute-done((bf16[4,320,128]{2,1,0:T(8,128)(2,1)S(1)}, bf16[4,320,128]{2,1,0:T(8,128)(2,1)S(1)}, u32[]{:S(2)}, u32[]{:S(2)}) %collective-permute-start.4) | collective-permute-done | bytes 327712 | tf_op jit(solution)/shard_map/ppermute | solution.py:828
  43.0 0.5 collective-permute-start.7
  43.5 1.8 %own_stats.1 = (f32[4,128,128]{2,1,0:T(8,128)S(1)}, f32[2,32,128]{2,1,0:T(8,128)S(1)}) custom-call(s32[2]{0:T(128)S(1)} %pad_add_fusion.refs_0_, f32[96,4,128]{2,1,0:T(4,128)S(1)} %bitcast.16, bf16[5,32,128]{2,1,0:T(8,128)(2,1)} %get-tuple-element.110.refs_2_), custom_call_target="tpu_custom_call" | custom-call | flops 1024 | bytes 1024 | tf_op jit(solution)/shard_map/own_stats/pallas_call | solution.py:48
  45.3 2.7 %weights.1 = (bf16[5,512,128]{2,1,0:T(8,128)(2,1)S(1)}, bf16[4,2048,128]{2,1,0:T(8,128)(2,1)}) custom-call(s32[2]{0:T(128)S(1)} %pad_add_fusion.refs_0_, f32[2,32,128]{2,1,0:T(8,128)S(1)} %get-tuple-element.112.refs_1_.refs_4_, bf16[4,320,128]{2,1,0:T(8,128)(2,1)S(1)} %gram_sum.2.refs_2_, bf16[4,320,128]{2,1,0:T(8,128)(2,1)S(1)} %collective-permute-done.3.refs_3_, ...), custom_call_target="tpu_custom_call" | custom-call | flops 1024 | bytes 1024 | tf_op jit(solution)/shard_map/weights/pallas_call | solution.py:48
  48.0 1.1 stats.1
  49.1 5.9 %forward.1 = (bf16[4,512,1024]{2,1,0:T(8,128)(2,1)S(1)}, f32[512,1024]{1,0:T(8,128)S(1)}, f32[32,8,128]{2,1,0:T(8,128)S(1)}, bf16[4,128,512]{2,1,0:T(8,128)(2,1)}, f32[2,32,128]{2,1,0:T(8,128)}) custom-call(bf16[4,128,1024]{2,1,0:T(8,128)(2,1)S(1)} %get-tuple-element.106.refs_0_.refs_2_.refs_4_, bf16[4,512,256]{2,1,0:T(8,128)(2,1)S(1)} %get-tuple-element.118.refs_1_.refs_3_, ...), custom_call_target="tpu_custom_call" | custom-call | flops 1024 | bytes 1024 | tf_op jit(solution)/shard_map/forward/pallas_call | solution.py:48
  54.9 12.1 %all_to_all.30.refs_0_ = f32[32,8,128]{2,1,0:T(8,128)S(1)} all-to-all(f32[32,8,128]{2,1,0:T(8,128)S(1)} %get-tuple-element.122), channel_id=1, replica_groups=mesh['dp'=16,'rep'=2] {'dp','rep'}, dimensions={0} | all-to-all | bytes 262144 | tf_op jit(solution)/shard_map/all_to_all | solution.py:845
  67.0 3.6 %head.1 = (f32[512,1024]{1,0:T(8,128)S(1)}, f32[32,8,128]{2,1,0:T(8,128)S(1)}, f32[512,128]{1,0:T(8,128)S(1)}, f32[2,512,128]{2,1,0:T(8,128)S(1)}) custom-call(f32[32,8,128]{2,1,0:T(8,128)S(1)} %all_to_all.30.refs_0_, f32[512,1024]{1,0:T(8,128)S(1)} %get-tuple-element.123.refs_1_.refs_4_, ...), custom_call_target="tpu_custom_call" | custom-call | flops 1024 | bytes 1024 | tf_op jit(solution)/shard_map/head/pallas_call | solution.py:48
  70.6 10.0 %all_to_all.31.refs_1_ = f32[32,8,128]{2,1,0:T(8,128)S(1)} all-to-all(f32[32,8,128]{2,1,0:T(8,128)S(1)} %get-tuple-element.124), channel_id=1, replica_groups=mesh['dp'=16,'rep'=2] {'dp','rep'}, dimensions={0} | all-to-all | bytes 262144 | tf_op jit(solution)/shard_map/all_to_all | solution.py:845
  80.6 3.6 %turn.1 = (bf16[512,1024]{1,0:T(8,128)(2,1)S(1)}, f32[16,144,256]{2,1,0:T(8,128)S(1)}, bf16[16,144,256]{2,1,0:T(8,128)(2,1)S(1)}, f32[8,128]{1,0:T(8,128)S(1)}, bf16[4,2048,128]{2,1,0:T(8,128)(2,1)S(1)}) custom-call(s32[2]{0:T(128)S(1)} %pad_add_fusion.refs_0_, f32[32,8,128]{2,1,0:T(8,128)S(1)} %all_to_all.31.refs_1_, ...), custom_call_target="tpu_custom_call" | custom-call | flops 1024 | bytes 1024 | tf_op jit(solution)/shard_map/turn/pallas_call | solution.py:48
  84.3 0.3 collective-permute-start.10
  84.5 7.5 %back.2 = (bf16[16,2,32,128]{3,2,1,0:T(8,128)(2,1)S(1)}, f32[2,128,1024]{2,1,0:T(8,128)}) custom-call(s32[2]{0:T(128)S(1)} %pad_add_fusion.refs_0_, bf16[512,1024]{1,0:T(8,128)(2,1)S(1)} %get-tuple-element.129.refs_1_, bf16[4,128,1024]{2,1,0:T(8,128)(2,1)S(1)} %get-tuple-element.106.refs_0_.refs_2_.refs_4_, ...), custom_call_target="tpu_custom_call" | custom-call | flops 1024 | bytes 1024 | tf_op jit(solution)/shard_map/merge_sum/back/pallas_call | solution.py:48
  92.0 0.4 collective-permute-start.11
  92.4 0.8 merge_sum.2
  93.2 0.4 collective-permute-done.11.refs_8_
  93.6 0.3 collective-permute-start.12
  94.0 1.0 collective-permute-start.13
  95.0 2.2 %collective-permute-start.14 = (bf16[4,144,256]{2,1,0:T(8,128)(2,1)S(1)}, bf16[4,144,256]{2,1,0:T(8,128)(2,1)S(1)}, u32[]{:S(2)}, u32[]{:S(2)}) collective-permute-start(bf16[4,144,256]{2,1,0:T(8,128)(2,1)S(1)} %get-tuple-element.144), channel_id=1, source_target_pairs={{0,6},{1,25},{2,4},{3,27},{4,2},{5,29},{6,0},{7,31},{8,14},{9,17},... | collective-permute-start | bytes 884744 | tf_op jit(solution)/shard_map/merge_sum/ppermute | solution.py:837
  97.1 8.6 %back.3 = (bf16[16,2,32,128]{3,2,1,0:T(8,128)(2,1)}, f32[2,128,1024]{2,1,0:T(8,128)}) custom-call(s32[2]{0:T(128)S(1)} %pad_add_fusion.refs_0_, bf16[512,1024]{1,0:T(8,128)(2,1)S(1)} %get-tuple-element.129.refs_1_, bf16[4,128,1024]{2,1,0:T(8,128)(2,1)S(1)} %get-tuple-element.106.refs_0_.refs_2_.refs_4_, ...), custom_call_target="tpu_custom_call" | custom-call | flops 1024 | bytes 1024 | tf_op jit(solution)/shard_map/merge_sum/back/pallas_call | solution.py:48
  105.8 3.5 %all-to-all-start.4 = ((bf16[16,2,32,128]{3,2,1,0:T(8,128)(2,1)}), bf16[16,2,32,128]{3,2,1,0:T(8,128)(2,1)S(1)}, u32[]{:S(2)}, u32[]{:S(2)}) async-start(bf16[16,2,32,128]{3,2,1,0:T(8,128)(2,1)} %get-tuple-element.145), calls=%async_computation.4 | async-start | bytes 524288 | tf_op jit(solution)/shard_map/branch_sum/all_to_all | solution.py:1066
  109.3 0.7 merge_sum.3
  110.0 1.9 %collective-permute-start.15 = (bf16[144,256]{1,0:T(8,128)(2,1)S(1)}, bf16[144,256]{1,0:T(8,128)(2,1)S(1)}, u32[]{:S(2)}, u32[]{:S(2)}) collective-permute-start(bf16[144,256]{1,0:T(8,128)(2,1)S(1)} %get-tuple-element.152), channel_id=1, source_target_pairs={{0,8},{1,3},{2,10},{3,1},{4,12},{5,7},{6,14},{7,5},{8,0},{9,11},{1... | collective-permute-start | bytes 221192 | tf_op jit(solution)/shard_map/merge_sum/ppermute | solution.py:837
  111.9 2.4 %collective-permute-start.16 = (bf16[144,256]{1,0:T(8,128)(2,1)S(1)}, bf16[144,256]{1,0:T(8,128)(2,1)S(1)}, u32[]{:S(2)}, u32[]{:S(2)}) collective-permute-start(bf16[144,256]{1,0:T(8,128)(2,1)S(1)} %get-tuple-element.153), channel_id=1, source_target_pairs={{0,16},{1,5},{2,18},{3,7},{4,20},{5,1},{6,22},{7,3},{8,24},{9,13},... | collective-permute-start | bytes 221192 | tf_op jit(solution)/shard_map/merge_sum/ppermute | solution.py:837
  114.3 0.1 collective-permute-start.17
  114.5 1.2 collective-permute-done.15.refs_4_
  115.6 5.3 %collective-permute-done.16.refs_5_ = bf16[144,256]{1,0:T(8,128)(2,1)S(1)} collective-permute-done((bf16[144,256]{1,0:T(8,128)(2,1)S(1)}, bf16[144,256]{1,0:T(8,128)(2,1)S(1)}, u32[]{:S(2)}, u32[]{:S(2)}) %collective-permute-start.16) | collective-permute-done | bytes 73760 | tf_op jit(solution)/shard_map/merge_sum/ppermute | solution.py:837
  120.9 0.4 collective-permute-done.17.refs_6_
  121.3 3.5 %owner.1 = (f32[352,128]{1,0:T(8,128)S(1)}, f32[32,2,128]{2,1,0:T(2,128)}, bf16[4,128,512]{2,1,0:T(8,128)(2,1)S(1)}, f32[2,128,1024]{2,1,0:T(8,128)S(1)}, f32[2,...) custom-call(s32[2]{0:T(128)S(1)} %pad_add_fusion.refs_0_, ...), custom_call_target="tpu_custom_call" | custom-call | flops 1024 | bytes 1024 | tf_op jit(solution)/shard_map/owner/pallas_call | solution.py:48
  124.8 1.0 collective-permute-start.18
  125.8 10.6 %all_to_all.32.refs_1_ = f32[32,2,128]{2,1,0:T(2,128)S(1)} all-to-all(f32[32,2,128]{2,1,0:T(2,128)} %get-tuple-element.157), channel_id=1, replica_groups=mesh['dp'=16,'rep'=2] {'dp','rep'}, dimensions={0} | all-to-all | bytes 65536 | tf_op jit(solution)/shard_map/all_to_all | solution.py:845
  136.4 3.7 %final.1 = (f32[4,32,100]{2,1,0:T(8,128)}, f32[128,512]{1,0:T(8,128)}, f32[32,47]{1,0:T(8,128)}, f32[20,32]{1,0:T(8,128)}, f32[4,32,100]{2,1,0:T(8,128)}, /*inde...) custom-call(s32[2]{0:T(128)S(1)} %pad_add_fusion.refs_0_, ...), custom_call_target="tpu_custom_call" | custom-call | flops 1024 | bytes 1024 | tf_op jit(solution)/shard_map/final/pallas_call | solution.py:48
  (18 shorter events, 0.1 us)
Async XLA Ops:
  2.5 12.9 %collective-permute-start.2 = (bf16[320,128]{1,0:T(8,128)(2,1)S(1)}, bf16[320,128]{1,0:T(8,128)(2,1)S(1)}, u32[]{:S(2)}, u32[]{:S(2)}) collective-permute-start(bf16[320,128]{1,0:T(8,128)(2,1)S(1)} %get-tuple-element.108.refs_0_), channel_id=1, source_target_pairs={{0,24},{2,26},{4,28},{6,30},{8,16},{10,18},{12,20},{14,22},{16,8},... | collective-permute-start | bytes 245768 | tf_op jit(solution)/shard_map/ppermute | solution.py:828
  7.6 7.8 %collective-permute-start.1 = (bf16[320,128]{1,0:T(8,128)(2,1)S(1)}, bf16[320,128]{1,0:T(8,128)(2,1)S(1)}, u32[]{:S(2)}, u32[]{:S(2)}) collective-permute-start(bf16[320,128]{1,0:T(8,128)(2,1)S(1)} %get-tuple-element.108.refs_0_), channel_id=1, source_target_pairs={{0,16},{2,18},{4,20},{6,22},{8,24},{10,26},{12,28},{14,30},{16,0},... | collective-permute-start | bytes 245768 | tf_op jit(solution)/shard_map/ppermute | solution.py:828
  7.6 7.8 %collective-permute-start = (bf16[320,128]{1,0:T(8,128)(2,1)S(1)}, bf16[320,128]{1,0:T(8,128)(2,1)S(1)}, u32[]{:S(2)}, u32[]{:S(2)}) collective-permute-start(bf16[320,128]{1,0:T(8,128)(2,1)S(1)} %get-tuple-element.108.refs_0_), channel_id=1, source_target_pairs={{0,8},{2,10},{4,12},{6,14},{8,0},{10,2},{12,4},{14,6},{16,24},{18,... | collective-permute-start | bytes 245768 | tf_op jit(solution)/shard_map/ppermute | solution.py:828
  15.5 15.0 %all-to-all-start = ((f32[32,3,4,128]{3,2,1,0:T(4,128)}), f32[32,3,4,128]{3,2,1,0:T(4,128)S(1)}, u32[]{:S(2)}, u32[]{:S(2)}) async-start(f32[32,3,4,128]{3,2,1,0:T(4,128)} %bitcast.20), calls=%async_computation | async-start | bytes 393216 | tf_op jit(solution)/shard_map/gram_sum/all_to_all | solution.py:845
  21.5 13.4 %collective-permute-start.5 = (bf16[4,320,128]{2,1,0:T(8,128)(2,1)S(1)}, bf16[4,320,128]{2,1,0:T(8,128)(2,1)S(1)}, u32[]{:S(2)}, u32[]{:S(2)}) collective-permute-start(bf16[4,320,128]{2,1,0:T(8,128)(2,1)S(1)} %gram_sum.2.refs_2_), channel_id=1, source_target_pairs={{0,6},{2,4},{4,2},{6,0},{8,14},{10,12},{12,10},{14,8},{16,22},{18,... | collective-permute-start | bytes 983048 | tf_op jit(solution)/shard_map/ppermute | solution.py:828
  24.2 18.8 %collective-permute-start.4 = (bf16[4,320,128]{2,1,0:T(8,128)(2,1)S(1)}, bf16[4,320,128]{2,1,0:T(8,128)(2,1)S(1)}, u32[]{:S(2)}, u32[]{:S(2)}) collective-permute-start(bf16[4,320,128]{2,1,0:T(8,128)(2,1)S(1)} %gram_sum.2.refs_2_), channel_id=1, source_target_pairs={{0,4},{2,6},{4,0},{6,2},{8,12},{10,14},{12,8},{14,10},{16,20},{18,... | collective-permute-start | bytes 983048 | tf_op jit(solution)/shard_map/ppermute | solution.py:828
  24.8 18.2 %collective-permute-start.3 = (bf16[4,320,128]{2,1,0:T(8,128)(2,1)S(1)}, bf16[4,320,128]{2,1,0:T(8,128)(2,1)S(1)}, u32[]{:S(2)}, u32[]{:S(2)}) collective-permute-start(bf16[4,320,128]{2,1,0:T(8,128)(2,1)S(1)} %gram_sum.2.refs_2_), channel_id=1, source_target_pairs={{0,2},{2,0},{4,6},{6,4},{8,10},{10,8},{12,14},{14,12},{16,18},{18,... | collective-permute-start | bytes 983048 | tf_op jit(solution)/shard_map/ppermute | solution.py:828
  31.2 12.3 %all-to-all-start.1 = ((f32[32,3,4,128]{3,2,1,0:T(4,128)}), f32[32,3,4,128]{3,2,1,0:T(4,128)S(1)}, u32[]{:S(2)}, u32[]{:S(2)}) async-start(f32[32,3,4,128]{3,2,1,0:T(4,128)} %gram_sum.3), calls=%async_computation.1 | async-start | bytes 393216 | tf_op jit(solution)/shard_map/gram_sum/all_to_all | solution.py:845
  33.8 11.4 %collective-permute-start.6 = (bf16[4,320,128]{2,1,0:T(8,128)(2,1)S(1)}, bf16[4,320,128]{2,1,0:T(8,128)(2,1)S(1)}, u32[]{:S(2)}, u32[]{:S(2)}) collective-permute-start(bf16[4,320,128]{2,1,0:T(8,128)(2,1)S(1)} %gram_sum.2.refs_2_), channel_id=1, source_target_pairs={{0,1},{1,0},{2,3},{3,2},{4,5},{5,4},{6,7},{7,6},{8,9},{9,8},{10,11... | collective-permute-start | bytes 983048 | tf_op jit(solution)/shard_map/weights/ppermute | solution.py:841
  34.9 10.4 %collective-permute-start.9 = (bf16[4,320,128]{2,1,0:T(8,128)(2,1)S(1)}, bf16[4,320,128]{2,1,0:T(8,128)(2,1)S(1)}, u32[]{:S(2)}, u32[]{:S(2)}) collective-permute-start(bf16[4,320,128]{2,1,0:T(8,128)(2,1)S(1)} %collective-permute-done.5.refs_5_), channel_id=1, source_target_pairs={{0,1},{1,0},{2,3},{3,2},{4,5},{5,4},{6,7},{7,6},{8,9},{9,8},{10,11... | collective-permute-start | bytes 983048 | tf_op jit(solution)/shard_map/weights/ppermute | solution.py:841
  43.0 2.3 %collective-permute-start.8 = (bf16[4,320,128]{2,1,0:T(8,128)(2,1)S(1)}, bf16[4,320,128]{2,1,0:T(8,128)(2,1)S(1)}, u32[]{:S(2)}, u32[]{:S(2)}) collective-permute-start(bf16[4,320,128]{2,1,0:T(8,128)(2,1)S(1)} %collective-permute-done.4.refs_4_), channel_id=1, source_target_pairs={{0,1},{1,0},{2,3},{3,2},{4,5},{5,4},{6,7},{7,6},{8,9},{9,8},{10,11... | collective-permute-start | bytes 983048 | tf_op jit(solution)/shard_map/weights/ppermute | solution.py:841
  43.0 2.3 %collective-permute-start.7 = (bf16[4,320,128]{2,1,0:T(8,128)(2,1)S(1)}, bf16[4,320,128]{2,1,0:T(8,128)(2,1)}, u32[]{:S(2)}, u32[]{:S(2)}) collective-permute-start(bf16[4,320,128]{2,1,0:T(8,128)(2,1)S(1)} %collective-permute-done.3.refs_3_), channel_id=1, source_target_pairs={{0,1},{1,0},{2,3},{3,2},{4,5},{5,4},{6,7},{7,6},{8,9},{9,8},{10,11... | collective-permute-start | bytes 983048 | tf_op jit(solution)/shard_map/weights/ppermute | solution.py:841
  84.3 8.1 %collective-permute-start.10 = (bf16[16,144,256]{2,1,0:T(8,128)(2,1)S(1)}, bf16[16,144,256]{2,1,0:T(8,128)(2,1)S(1)}, u32[]{:S(2)}, u32[]{:S(2)}) collective-permute-start(bf16[16,144,256]{2,1,0:T(8,128)(2,1)S(1)} %get-tuple-element.134), channel_id=1, source_target_pairs={{0,1},{1,0},{2,3},{3,2},{4,5},{5,4},{6,7},{7,6},{8,9},{9,8},{10,11... | collective-permute-start | bytes 3538952 | tf_op jit(solution)/shard_map/ppermute | solution.py:841
  92.0 1.6 %collective-permute-start.11 = (bf16[16,2,32,128]{3,2,1,0:T(8,128)(2,1)S(1)}, bf16[16,2,32,128]{3,2,1,0:T(8,128)(2,1)S(1)}, u32[]{:S(2)}, u32[]{:S(2)}) collective-permute-start(bf16[16,2,32,128]{3,2,1,0:T(8,128)(2,1)S(1)} %get-tuple-element.139), channel_id=1, source_target_pairs={{0,1},{1,0},{2,3},{3,2},{4,5},{5,4},{6,7},{7,6},{8,9},{9,8},{10,11... | collective-permute-start | bytes 786440 | tf_op jit(solution)/shard_map/merge_sum/ppermute | solution.py:841
  93.2 4.0 %copy-start = (bf16[4,144,256]{2,1,0:T(8,128)(2,1)}, bf16[4,144,256]{2,1,0:T(8,128)(2,1)S(1)}, u32[]{:S(2)}) copy-start(bf16[4,144,256]{2,1,0:T(8,128)(2,1)S(1)} %get-tuple-element.142.refs_9_) | copy-start | bytes 884740
  93.6 12.1 %collective-permute-start.12 = (bf16[4,144,256]{2,1,0:T(8,128)(2,1)S(1)}, bf16[4,144,256]{2,1,0:T(8,128)(2,1)S(1)}, u32[]{:S(2)}, u32[]{:S(2)}) collective-permute-start(bf16[4,144,256]{2,1,0:T(8,128)(2,1)S(1)} %get-tuple-element.142.refs_9_), channel_id=1, source_target_pairs={{0,2},{1,9},{2,0},{3,11},{4,6},{5,13},{6,4},{7,15},{8,10},{9,1},{1... | collective-permute-start | bytes 884744 | tf_op jit(solution)/shard_map/merge_sum/ppermute | solution.py:837
  94.0 11.8 %collective-permute-start.13 = (bf16[4,144,256]{2,1,0:T(8,128)(2,1)S(1)}, bf16[4,144,256]{2,1,0:T(8,128)(2,1)S(1)}, u32[]{:S(2)}, u32[]{:S(2)}) collective-permute-start(bf16[4,144,256]{2,1,0:T(8,128)(2,1)S(1)} %get-tuple-element.143), channel_id=1, source_target_pairs={{0,4},{1,17},{2,6},{3,19},{4,0},{5,21},{6,2},{7,23},{8,12},{9,25},... | collective-permute-start | bytes 884744 | tf_op jit(solution)/shard_map/merge_sum/ppermute | solution.py:837
  95.0 10.8 %collective-permute-start.14 = (bf16[4,144,256]{2,1,0:T(8,128)(2,1)S(1)}, bf16[4,144,256]{2,1,0:T(8,128)(2,1)S(1)}, u32[]{:S(2)}, u32[]{:S(2)}) collective-permute-start(bf16[4,144,256]{2,1,0:T(8,128)(2,1)S(1)} %get-tuple-element.144), channel_id=1, source_target_pairs={{0,6},{1,25},{2,4},{3,27},{4,2},{5,29},{6,0},{7,31},{8,14},{9,17},... | collective-permute-start | bytes 884744 | tf_op jit(solution)/shard_map/merge_sum/ppermute | solution.py:837
  105.8 15.6 %all-to-all-start.4 = ((bf16[16,2,32,128]{3,2,1,0:T(8,128)(2,1)}), bf16[16,2,32,128]{3,2,1,0:T(8,128)(2,1)S(1)}, u32[]{:S(2)}, u32[]{:S(2)}) async-start(bf16[16,2,32,128]{3,2,1,0:T(8,128)(2,1)} %get-tuple-element.145), calls=%async_computation.4 | async-start | bytes 524288 | tf_op jit(solution)/shard_map/branch_sum/all_to_all | solution.py:1066
  110.0 5.6 %collective-permute-start.15 = (bf16[144,256]{1,0:T(8,128)(2,1)S(1)}, bf16[144,256]{1,0:T(8,128)(2,1)S(1)}, u32[]{:S(2)}, u32[]{:S(2)}) collective-permute-start(bf16[144,256]{1,0:T(8,128)(2,1)S(1)} %get-tuple-element.152), channel_id=1, source_target_pairs={{0,8},{1,3},{2,10},{3,1},{4,12},{5,7},{6,14},{7,5},{8,0},{9,11},{1... | collective-permute-start | bytes 221192 | tf_op jit(solution)/shard_map/merge_sum/ppermute | solution.py:837
  111.9 9.0 %collective-permute-start.16 = (bf16[144,256]{1,0:T(8,128)(2,1)S(1)}, bf16[144,256]{1,0:T(8,128)(2,1)S(1)}, u32[]{:S(2)}, u32[]{:S(2)}) collective-permute-start(bf16[144,256]{1,0:T(8,128)(2,1)S(1)} %get-tuple-element.153), channel_id=1, source_target_pairs={{0,16},{1,5},{2,18},{3,7},{4,20},{5,1},{6,22},{7,3},{8,24},{9,13},... | collective-permute-start | bytes 221192 | tf_op jit(solution)/shard_map/merge_sum/ppermute | solution.py:837
  114.3 7.0 %collective-permute-start.17 = (bf16[144,256]{1,0:T(8,128)(2,1)S(1)}, bf16[144,256]{1,0:T(8,128)(2,1)S(1)}, u32[]{:S(2)}, u32[]{:S(2)}) collective-permute-start(bf16[144,256]{1,0:T(8,128)(2,1)S(1)} %get-tuple-element.154), channel_id=1, source_target_pairs={{0,24},{1,7},{2,26},{3,5},{4,28},{5,3},{6,30},{7,1},{8,16},{9,15},... | collective-permute-start | bytes 221192 | tf_op jit(solution)/shard_map/merge_sum/ppermute | solution.py:837
  124.8 11.5 %collective-permute-start.18 = (f32[352,128]{1,0:T(8,128)S(1)}, f32[352,128]{1,0:T(8,128)S(1)}, u32[]{:S(2)}, u32[]{:S(2)}) collective-permute-start(f32[352,128]{1,0:T(8,128)S(1)} %get-tuple-element.158.refs_2_), channel_id=1, source_target_pairs={{0,1},{1,0},{2,3},{3,2},{4,5},{5,4},{6,7},{7,6},{8,9},{9,8},{10,11... | collective-permute-start | bytes 540680 | tf_op jit(solution)/shard_map/ppermute | solution.py:841

commit v8 on v7

--- a/solution.py
+++ b/solution.py
@@ -15,7 +15,7 @@
 PCOL = 64
 ONE = 100
 FREE = LANES - ONE
-ROWS, WIDE, CHUNK = 32, 256, 256
+ROWS, WIDE, CHUNK, SPAN = 32, 256, 256, 512
 BOTH = ("dp", "rep")
 F32 = jnp.float32
 BF16 = jnp.bfloat16
@@ -547,7 +547,7 @@
     b_ref, a_out, pre, dj, dyv, sums, a_ref, wt_ref, out_sems = refs
     hid = wt_ref.shape[2]
     batch = x_ref.shape[2]
-    per = hid // CHUNK
+    per = hid // SPAN
     jobs = [(k, c) for k in range(count) for c in range(per)]
     base = 2 * (pos_ref[1] if own else 1 - pos_ref[1]) + first
     dp, _, cb, _ = b_ref.shape
@@ -556,15 +556,15 @@
 
     def project(i):
         k, c = jobs[i]
-        rows = slice(c * CHUNK, (c + 1) * CHUNK)
+        rows = slice(c * SPAN, (c + 1) * SPAN)
         pre[i % 2] = project_units(ws_ref, x_ref, base + k, rows)
-        at = pl.ds(pl.multiple_of((base + k) * hid + c * CHUNK, CHUNK), CHUNK)
+        at = pl.ds(pl.multiple_of((base + k) * hid + c * SPAN, SPAN), SPAN)
         dj[i % 2] = dot(merge_block(wm_ref, at), dpre_ref[...], 1, 0)
 
     def units(i):
         k, c = jobs[i]
-        for g in range(CHUNK // ROWS):
-            at = slice(c * CHUNK + g * ROWS, c * CHUNK + (g + 1) * ROWS)
+        for g in range(SPAN // ROWS):
+            at = slice(c * SPAN + g * ROWS, c * SPAN + (g + 1) * ROWS)
             here = slice(g * ROWS, (g + 1) * ROWS)
             p1, q1, s2, s1, r1 = column_set(coef_ref, base + k, at, (0, 1, 4, 6, 7))
             one = jnp.zeros((ROWS, WIDE), F32)
@@ -1023,15 +1023,15 @@
                 after=after,
                 out_specs=(pl.BlockSpec(memory_space=pltpu.VMEM), pl.BlockSpec(memory_space=pltpu.HBM)),
                 scratch=[
-                    pltpu.VMEM((2, CHUNK, batch), F32),
-                    pltpu.VMEM((2, CHUNK, batch), F32),
+                    pltpu.VMEM((2, SPAN, batch), F32),
+                    pltpu.VMEM((2, SPAN, batch), F32),
                     pltpu.VMEM((num, hid, batch), BF16),
                     pltpu.VMEM((num, 2, hid, LANES), F32),
                     pltpu.VMEM((num, LANES, batch), F32),
                     pltpu.VMEM((num, LANES, hid), BF16),
                     pltpu.SemaphoreType.DMA((num + 1,)),
                 ],
-                mib=16,
+                mib=24,
             )
 
     recv = swap(send)
@@ -1049,7 +1049,7 @@
             )
             away, recv_b = lax.optimization_barrier((low[1:], recv_b))
             moved = [turn_flip(v, t, dp, 1) for t, v in enumerate(away, 1)]
-            kept_b, kept_a = back(True, 0, 2, recv_b, after=(low[1],))
+            kept_b, kept_a = back(True, 0, 2, recv_b)
             kept_b, moved = lax.optimization_barrier((kept_b, moved))
             high = call(
                 split_high_kernel,

time: 141 us -> 140 us (level)
  no operation moved by 1% of the time
where the time goes in v8:
time: 140 us
  Pallas kernels  52.6 us (38%)
  blocking collectives  32.4 us (23%)
  starting transfers between devices  32.2 us (23%)
  waiting for transfers between devices  21.5 us (15%)
    pallas_call x16, Pallas kernels, call(): pl.pallas_call(kernel, out_shape=tuple(outs), in_specs=in_specs, out_spec...  52.6 us
    all_to_all x3, blocking collectives, exchange(): return lax.all_to_all(value, BOTH, 0, 0, tiled=True)  32.4 us
    ppermute x6, starting transfers between devices, flip(): return lax.ppermute(value, 'dp', [(i, i ^ mask) for i in range(dp)])  9.31 us
    ppermute x6, waiting for transfers between devices, flip(): return lax.ppermute(value, 'dp', [(i, i ^ mask) for i in range(dp)])  8.75 us
    all_to_all x2, starting transfers between devices, exchange(): return lax.all_to_all(value, BOTH, 0, 0, tiled=True)  8.65 us
    ppermute x6, starting transfers between devices, turn_flip(): return lax.ppermute(value, BOTH, pairs)  7.94 us
    ppermute x6, waiting for transfers between devices, turn_flip(): return lax.ppermute(value, BOTH, pairs)  6.87 us
    all_to_all x2, waiting for transfers between devices, exchange(): return lax.all_to_all(value, BOTH, 0, 0, tiled=True)  5.39 us
  transfers between devices with their start and end apart: 22, of which 7 were waited for; matrix products, arithmetic and copies ran while one was open for 0% of the time, Pallas kernels for 19%

profile of v8, /device:TPU:0, one launch (start us, length us, event | category | flops | bytes accessed | tf_op | source)
XLA Modules:
  0.0 139.8 jit_solution(3149488510833414853)
XLA Ops:
  0.7 0.1 pad_add_fusion.refs_0_
  0.7 1.8 %prep.1 = (bf16[5,32,128]{2,1,0:T(8,128)(2,1)S(1)}, bf16[320,128]{1,0:T(8,128)(2,1)S(1)}) custom-call(s32[2]{0:T(128)S(1)} %pad_add_fusion.refs_0_, f32[4,32,100]{2,1,0:T(8,128)} %bitcast.18, f32[32,47]{1,0:T(8,128)} %refs_13_.1, f32[20,32]{1,0:T(8,128)} %refs_14_.1, f32[128,512]{1,0:T(8,128)} %refs_12_.1), custom_call_target="tpu_custom_call" | custom-call | flops 1024 | bytes 1024 | tf_op jit(solution)/shard_map/prep/pallas_call | solution.py:48
  2.5 5.1 %collective-permute-start.2 = (bf16[320,128]{1,0:T(8,128)(2,1)S(1)}, bf16[320,128]{1,0:T(8,128)(2,1)S(1)}, u32[]{:S(2)}, u32[]{:S(2)}) collective-permute-start(bf16[320,128]{1,0:T(8,128)(2,1)S(1)} %get-tuple-element.108.refs_0_), channel_id=1, source_target_pairs={{0,24},{2,26},{4,28},{6,30},{8,16},{10,18},{12,20},{14,22},{16,8},... | collective-permute-start | bytes 245768 | tf_op jit(solution)/shard_map/ppermute | solution.py:828
  7.6 0.0 collective-permute-start.1
  7.6 0.6 collective-permute-start
  8.3 7.2 %gather.1 = (bf16[4,128,1024]{2,1,0:T(8,128)(2,1)S(1)}, f32[96,4,128]{2,1,0:T(4,128)}, bf16[5,32,128]{2,1,0:T(8,128)(2,1)}) custom-call(s32[1,1024]{1,0:T(1,128)} %bitcast.24, f32[400,4096]{1,0:T(8,128)} %bitcast.17, bf16[5,32,128]{2,1,0:T(8,128)(2,1)S(1)} %get-tuple-element.105.refs_2_), custom_call_target="tpu_custom_call" | custom-call | flops 1024 | bytes 1024 | tf_op jit(solution)/shard_map/gather/pallas_call | solution.py:48
  15.4 0.0 collective-permute-done.2.refs_3_
  15.5 6.0 %all-to-all-start = ((f32[32,3,4,128]{3,2,1,0:T(4,128)}), f32[32,3,4,128]{3,2,1,0:T(4,128)S(1)}, u32[]{:S(2)}, u32[]{:S(2)}) async-start(f32[32,3,4,128]{3,2,1,0:T(4,128)} %bitcast.20), calls=%async_computation | async-start | bytes 393216 | tf_op jit(solution)/shard_map/gram_sum/all_to_all | solution.py:845
  21.5 2.7 %collective-permute-start.5 = (bf16[4,320,128]{2,1,0:T(8,128)(2,1)S(1)}, bf16[4,320,128]{2,1,0:T(8,128)(2,1)S(1)}, u32[]{:S(2)}, u32[]{:S(2)}) collective-permute-start(bf16[4,320,128]{2,1,0:T(8,128)(2,1)S(1)} %gram_sum.2.refs_2_), channel_id=1, source_target_pairs={{0,6},{2,4},{4,2},{6,0},{8,14},{10,12},{12,10},{14,8},{16,22},{18,... | collective-permute-start | bytes 983048 | tf_op jit(solution)/shard_map/ppermute | solution.py:828
  24.2 0.6 collective-permute-start.4
  24.8 0.3 collective-permute-start.3
  25.1 5.4 %all-to-all-done.refs_0_ = f32[32,3,4,128]{3,2,1,0:T(4,128)S(1)} async-done(((f32[32,3,4,128]{3,2,1,0:T(4,128)}), f32[32,3,4,128]{3,2,1,0:T(4,128)S(1)}, u32[]{:S(2)}, u32[]{:S(2)}) %all-to-all-start) | async-done | bytes 196640 | tf_op jit(solution)/shard_map/gram_sum/all_to_all | solution.py:845
  30.5 0.7 gram_sum.3
  31.2 2.7 %all-to-all-start.1 = ((f32[32,3,4,128]{3,2,1,0:T(4,128)}), f32[32,3,4,128]{3,2,1,0:T(4,128)S(1)}, u32[]{:S(2)}, u32[]{:S(2)}) async-start(f32[32,3,4,128]{3,2,1,0:T(4,128)} %gram_sum.3), calls=%async_computation.1 | async-start | bytes 393216 | tf_op jit(solution)/shard_map/gram_sum/all_to_all | solution.py:845
  33.8 0.4 collective-permute-start.6
  34.3 0.6 collective-permute-done.5.refs_5_
  34.9 0.0 collective-permute-start.9
  34.9 8.1 %collective-permute-done.4.refs_4_ = bf16[4,320,128]{2,1,0:T(8,128)(2,1)S(1)} collective-permute-done((bf16[4,320,128]{2,1,0:T(8,128)(2,1)S(1)}, bf16[4,320,128]{2,1,0:T(8,128)(2,1)S(1)}, u32[]{:S(2)}, u32[]{:S(2)}) %collective-permute-start.4) | collective-permute-done | bytes 327712 | tf_op jit(solution)/shard_map/ppermute | solution.py:828
  43.0 0.5 collective-permute-start.7
  43.5 1.8 %own_stats.1 = (f32[4,128,128]{2,1,0:T(8,128)S(1)}, f32[2,32,128]{2,1,0:T(8,128)S(1)}) custom-call(s32[2]{0:T(128)S(1)} %pad_add_fusion.refs_0_, f32[96,4,128]{2,1,0:T(4,128)S(1)} %bitcast.16, bf16[5,32,128]{2,1,0:T(8,128)(2,1)} %get-tuple-element.110.refs_2_), custom_call_target="tpu_custom_call" | custom-call | flops 1024 | bytes 1024 | tf_op jit(solution)/shard_map/own_stats/pallas_call | solution.py:48
  45.3 2.7 %weights.1 = (bf16[5,512,128]{2,1,0:T(8,128)(2,1)S(1)}, bf16[4,2048,128]{2,1,0:T(8,128)(2,1)}) custom-call(s32[2]{0:T(128)S(1)} %pad_add_fusion.refs_0_, f32[2,32,128]{2,1,0:T(8,128)S(1)} %get-tuple-element.112.refs_1_.refs_4_, bf16[4,320,128]{2,1,0:T(8,128)(2,1)S(1)} %gram_sum.2.refs_2_, bf16[4,320,128]{2,1,0:T(8,128)(2,1)S(1)} %collective-permute-done.3.refs_3_, ...), custom_call_target="tpu_custom_call" | custom-call | flops 1024 | bytes 1024 | tf_op jit(solution)/shard_map/weights/pallas_call | solution.py:48
  48.0 1.1 stats.1
  49.1 5.8 %forward.1 = (bf16[4,512,1024]{2,1,0:T(8,128)(2,1)S(1)}, f32[512,1024]{1,0:T(8,128)S(1)}, f32[32,8,128]{2,1,0:T(8,128)S(1)}, bf16[4,128,512]{2,1,0:T(8,128)(2,1)}, f32[2,32,128]{2,1,0:T(8,128)}) custom-call(bf16[4,128,1024]{2,1,0:T(8,128)(2,1)S(1)} %get-tuple-element.106.refs_0_.refs_2_.refs_4_, bf16[4,512,256]{2,1,0:T(8,128)(2,1)S(1)} %get-tuple-element.118.refs_1_.refs_3_, ...), custom_call_target="tpu_custom_call" | custom-call | flops 1024 | bytes 1024 | tf_op jit(solution)/shard_map/forward/pallas_call | solution.py:48
  54.9 12.0 %all_to_all.30.refs_0_ = f32[32,8,128]{2,1,0:T(8,128)S(1)} all-to-all(f32[32,8,128]{2,1,0:T(8,128)S(1)} %get-tuple-element.122), channel_id=1, replica_groups=mesh['dp'=16,'rep'=2] {'dp','rep'}, dimensions={0} | all-to-all | bytes 262144 | tf_op jit(solution)/shard_map/all_to_all | solution.py:845
  67.0 3.6 %head.1 = (f32[512,1024]{1,0:T(8,128)S(1)}, f32[32,8,128]{2,1,0:T(8,128)S(1)}, f32[512,128]{1,0:T(8,128)S(1)}, f32[2,512,128]{2,1,0:T(8,128)S(1)}) custom-call(f32[32,8,128]{2,1,0:T(8,128)S(1)} %all_to_all.30.refs_0_, f32[512,1024]{1,0:T(8,128)S(1)} %get-tuple-element.123.refs_1_.refs_4_, ...), custom_call_target="tpu_custom_call" | custom-call | flops 1024 | bytes 1024 | tf_op jit(solution)/shard_map/head/pallas_call | solution.py:48
  70.6 10.0 %all_to_all.31.refs_1_ = f32[32,8,128]{2,1,0:T(8,128)S(1)} all-to-all(f32[32,8,128]{2,1,0:T(8,128)S(1)} %get-tuple-element.124), channel_id=1, replica_groups=mesh['dp'=16,'rep'=2] {'dp','rep'}, dimensions={0} | all-to-all | bytes 262144 | tf_op jit(solution)/shard_map/all_to_all | solution.py:845
  80.6 3.7 %turn.1 = (bf16[512,1024]{1,0:T(8,128)(2,1)S(1)}, f32[16,144,256]{2,1,0:T(8,128)S(1)}, bf16[16,144,256]{2,1,0:T(8,128)(2,1)S(1)}, f32[8,128]{1,0:T(8,128)S(1)}, bf16[4,2048,128]{2,1,0:T(8,128)(2,1)S(1)}) custom-call(s32[2]{0:T(128)S(1)} %pad_add_fusion.refs_0_, f32[32,8,128]{2,1,0:T(8,128)S(1)} %all_to_all.31.refs_1_, ...), custom_call_target="tpu_custom_call" | custom-call | flops 1024 | bytes 1024 | tf_op jit(solution)/shard_map/turn/pallas_call | solution.py:48
  84.3 0.3 collective-permute-start.10
  84.6 7.2 %back.2 = (bf16[16,2,32,128]{3,2,1,0:T(8,128)(2,1)S(1)}, f32[2,128,1024]{2,1,0:T(8,128)}) custom-call(s32[2]{0:T(128)S(1)} %pad_add_fusion.refs_0_, bf16[512,1024]{1,0:T(8,128)(2,1)S(1)} %get-tuple-element.129.refs_1_, bf16[4,128,1024]{2,1,0:T(8,128)(2,1)S(1)} %get-tuple-element.106.refs_0_.refs_2_.refs_4_, ...), custom_call_target="tpu_custom_call" | custom-call | flops 1024 | bytes 1024 | tf_op jit(solution)/shard_map/merge_sum/back/pallas_call | solution.py:48
  91.8 0.4 collective-permute-start.11
  92.1 0.8 merge_sum.2
  92.9 0.5 collective-permute-done.11.refs_8_
  93.4 0.4 collective-permute-start.12
  93.7 1.0 collective-permute-start.13
  94.7 2.1 %collective-permute-start.14 = (bf16[4,144,256]{2,1,0:T(8,128)(2,1)S(1)}, bf16[4,144,256]{2,1,0:T(8,128)(2,1)S(1)}, u32[]{:S(2)}, u32[]{:S(2)}) collective-permute-start(bf16[4,144,256]{2,1,0:T(8,128)(2,1)S(1)} %get-tuple-element.144), channel_id=1, source_target_pairs={{0,6},{1,25},{2,4},{3,27},{4,2},{5,29},{6,0},{7,31},{8,14},{9,17},... | collective-permute-start | bytes 884744 | tf_op jit(solution)/shard_map/merge_sum/ppermute | solution.py:837
  96.8 8.5 %back.3 = (bf16[16,2,32,128]{3,2,1,0:T(8,128)(2,1)}, f32[2,128,1024]{2,1,0:T(8,128)}) custom-call(s32[2]{0:T(128)S(1)} %pad_add_fusion.refs_0_, bf16[512,1024]{1,0:T(8,128)(2,1)S(1)} %get-tuple-element.129.refs_1_, bf16[4,128,1024]{2,1,0:T(8,128)(2,1)S(1)} %get-tuple-element.106.refs_0_.refs_2_.refs_4_, ...), custom_call_target="tpu_custom_call" | custom-call | flops 1024 | bytes 1024 | tf_op jit(solution)/shard_map/merge_sum/back/pallas_call | solution.py:48
  105.4 3.5 %all-to-all-start.4 = ((bf16[16,2,32,128]{3,2,1,0:T(8,128)(2,1)}), bf16[16,2,32,128]{3,2,1,0:T(8,128)(2,1)S(1)}, u32[]{:S(2)}, u32[]{:S(2)}) async-start(bf16[16,2,32,128]{3,2,1,0:T(8,128)(2,1)} %get-tuple-element.145), calls=%async_computation.4 | async-start | bytes 524288 | tf_op jit(solution)/shard_map/branch_sum/all_to_all | solution.py:1066
  108.9 0.7 merge_sum.3
  109.6 1.9 %collective-permute-start.15 = (bf16[144,256]{1,0:T(8,128)(2,1)S(1)}, bf16[144,256]{1,0:T(8,128)(2,1)S(1)}, u32[]{:S(2)}, u32[]{:S(2)}) collective-permute-start(bf16[144,256]{1,0:T(8,128)(2,1)S(1)} %get-tuple-element.152), channel_id=1, source_target_pairs={{0,8},{1,3},{2,10},{3,1},{4,12},{5,7},{6,14},{7,5},{8,0},{9,11},{1... | collective-permute-start | bytes 221192 | tf_op jit(solution)/shard_map/merge_sum/ppermute | solution.py:837
  111.5 2.4 %collective-permute-start.16 = (bf16[144,256]{1,0:T(8,128)(2,1)S(1)}, bf16[144,256]{1,0:T(8,128)(2,1)S(1)}, u32[]{:S(2)}, u32[]{:S(2)}) collective-permute-start(bf16[144,256]{1,0:T(8,128)(2,1)S(1)} %get-tuple-element.153), channel_id=1, source_target_pairs={{0,16},{1,5},{2,18},{3,7},{4,20},{5,1},{6,22},{7,3},{8,24},{9,13},... | collective-permute-start | bytes 221192 | tf_op jit(solution)/shard_map/merge_sum/ppermute | solution.py:837
  113.9 0.1 collective-permute-start.17
  114.1 1.0 collective-permute-done.15.refs_4_
  115.1 5.6 %collective-permute-done.16.refs_5_ = bf16[144,256]{1,0:T(8,128)(2,1)S(1)} collective-permute-done((bf16[144,256]{1,0:T(8,128)(2,1)S(1)}, bf16[144,256]{1,0:T(8,128)(2,1)S(1)}, u32[]{:S(2)}, u32[]{:S(2)}) %collective-permute-start.16) | collective-permute-done | bytes 73760 | tf_op jit(solution)/shard_map/merge_sum/ppermute | solution.py:837
  120.7 0.3 collective-permute-done.17.refs_6_
  121.0 3.5 %owner.1 = (f32[352,128]{1,0:T(8,128)S(1)}, f32[32,2,128]{2,1,0:T(2,128)}, bf16[4,128,512]{2,1,0:T(8,128)(2,1)S(1)}, f32[2,128,1024]{2,1,0:T(8,128)S(1)}, f32[2,...) custom-call(s32[2]{0:T(128)S(1)} %pad_add_fusion.refs_0_, ...), custom_call_target="tpu_custom_call" | custom-call | flops 1024 | bytes 1024 | tf_op jit(solution)/shard_map/owner/pallas_call | solution.py:48
  124.5 1.1 collective-permute-start.18
  125.6 10.3 %all_to_all.32.refs_1_ = f32[32,2,128]{2,1,0:T(2,128)S(1)} all-to-all(f32[32,2,128]{2,1,0:T(2,128)} %get-tuple-element.157), channel_id=1, replica_groups=mesh['dp'=16,'rep'=2] {'dp','rep'}, dimensions={0} | all-to-all | bytes 65536 | tf_op jit(solution)/shard_map/all_to_all | solution.py:845
  135.9 3.7 %final.1 = (f32[4,32,100]{2,1,0:T(8,128)}, f32[128,512]{1,0:T(8,128)}, f32[32,47]{1,0:T(8,128)}, f32[20,32]{1,0:T(8,128)}, f32[4,32,100]{2,1,0:T(8,128)}, /*inde...) custom-call(s32[2]{0:T(128)S(1)} %pad_add_fusion.refs_0_, ...), custom_call_target="tpu_custom_call" | custom-call | flops 1024 | bytes 1024 | tf_op jit(solution)/shard_map/final/pallas_call | solution.py:48
  (16 shorter events, 0.1 us)
Async XLA Ops:
  2.5 12.9 %collective-permute-start.2 = (bf16[320,128]{1,0:T(8,128)(2,1)S(1)}, bf16[320,128]{1,0:T(8,128)(2,1)S(1)}, u32[]{:S(2)}, u32[]{:S(2)}) collective-permute-start(bf16[320,128]{1,0:T(8,128)(2,1)S(1)} %get-tuple-element.108.refs_0_), channel_id=1, source_target_pairs={{0,24},{2,26},{4,28},{6,30},{8,16},{10,18},{12,20},{14,22},{16,8},... | collective-permute-start | bytes 245768 | tf_op jit(solution)/shard_map/ppermute | solution.py:828
  7.6 7.8 %collective-permute-start.1 = (bf16[320,128]{1,0:T(8,128)(2,1)S(1)}, bf16[320,128]{1,0:T(8,128)(2,1)S(1)}, u32[]{:S(2)}, u32[]{:S(2)}) collective-permute-start(bf16[320,128]{1,0:T(8,128)(2,1)S(1)} %get-tuple-element.108.refs_0_), channel_id=1, source_target_pairs={{0,16},{2,18},{4,20},{6,22},{8,24},{10,26},{12,28},{14,30},{16,0},... | collective-permute-start | bytes 245768 | tf_op jit(solution)/shard_map/ppermute | solution.py:828
  7.6 7.8 %collective-permute-start = (bf16[320,128]{1,0:T(8,128)(2,1)S(1)}, bf16[320,128]{1,0:T(8,128)(2,1)S(1)}, u32[]{:S(2)}, u32[]{:S(2)}) collective-permute-start(bf16[320,128]{1,0:T(8,128)(2,1)S(1)} %get-tuple-element.108.refs_0_), channel_id=1, source_target_pairs={{0,8},{2,10},{4,12},{6,14},{8,0},{10,2},{12,4},{14,6},{16,24},{18,... | collective-permute-start | bytes 245768 | tf_op jit(solution)/shard_map/ppermute | solution.py:828
  15.5 15.0 %all-to-all-start = ((f32[32,3,4,128]{3,2,1,0:T(4,128)}), f32[32,3,4,128]{3,2,1,0:T(4,128)S(1)}, u32[]{:S(2)}, u32[]{:S(2)}) async-start(f32[32,3,4,128]{3,2,1,0:T(4,128)} %bitcast.20), calls=%async_computation | async-start | bytes 393216 | tf_op jit(solution)/shard_map/gram_sum/all_to_all | solution.py:845
  21.5 13.4 %collective-permute-start.5 = (bf16[4,320,128]{2,1,0:T(8,128)(2,1)S(1)}, bf16[4,320,128]{2,1,0:T(8,128)(2,1)S(1)}, u32[]{:S(2)}, u32[]{:S(2)}) collective-permute-start(bf16[4,320,128]{2,1,0:T(8,128)(2,1)S(1)} %gram_sum.2.refs_2_), channel_id=1, source_target_pairs={{0,6},{2,4},{4,2},{6,0},{8,14},{10,12},{12,10},{14,8},{16,22},{18,... | collective-permute-start | bytes 983048 | tf_op jit(solution)/shard_map/ppermute | solution.py:828
  24.2 18.8 %collective-permute-start.4 = (bf16[4,320,128]{2,1,0:T(8,128)(2,1)S(1)}, bf16[4,320,128]{2,1,0:T(8,128)(2,1)S(1)}, u32[]{:S(2)}, u32[]{:S(2)}) collective-permute-start(bf16[4,320,128]{2,1,0:T(8,128)(2,1)S(1)} %gram_sum.2.refs_2_), channel_id=1, source_target_pairs={{0,4},{2,6},{4,0},{6,2},{8,12},{10,14},{12,8},{14,10},{16,20},{18,... | collective-permute-start | bytes 983048 | tf_op jit(solution)/shard_map/ppermute | solution.py:828
  24.8 18.2 %collective-permute-start.3 = (bf16[4,320,128]{2,1,0:T(8,128)(2,1)S(1)}, bf16[4,320,128]{2,1,0:T(8,128)(2,1)S(1)}, u32[]{:S(2)}, u32[]{:S(2)}) collective-permute-start(bf16[4,320,128]{2,1,0:T(8,128)(2,1)S(1)} %gram_sum.2.refs_2_), channel_id=1, source_target_pairs={{0,2},{2,0},{4,6},{6,4},{8,10},{10,8},{12,14},{14,12},{16,18},{18,... | collective-permute-start | bytes 983048 | tf_op jit(solution)/shard_map/ppermute | solution.py:828
  31.2 12.3 %all-to-all-start.1 = ((f32[32,3,4,128]{3,2,1,0:T(4,128)}), f32[32,3,4,128]{3,2,1,0:T(4,128)S(1)}, u32[]{:S(2)}, u32[]{:S(2)}) async-start(f32[32,3,4,128]{3,2,1,0:T(4,128)} %gram_sum.3), calls=%async_computation.1 | async-start | bytes 393216 | tf_op jit(solution)/shard_map/gram_sum/all_to_all | solution.py:845
  33.8 11.4 %collective-permute-start.6 = (bf16[4,320,128]{2,1,0:T(8,128)(2,1)S(1)}, bf16[4,320,128]{2,1,0:T(8,128)(2,1)S(1)}, u32[]{:S(2)}, u32[]{:S(2)}) collective-permute-start(bf16[4,320,128]{2,1,0:T(8,128)(2,1)S(1)} %gram_sum.2.refs_2_), channel_id=1, source_target_pairs={{0,1},{1,0},{2,3},{3,2},{4,5},{5,4},{6,7},{7,6},{8,9},{9,8},{10,11... | collective-permute-start | bytes 983048 | tf_op jit(solution)/shard_map/weights/ppermute | solution.py:841
  34.9 10.4 %collective-permute-start.9 = (bf16[4,320,128]{2,1,0:T(8,128)(2,1)S(1)}, bf16[4,320,128]{2,1,0:T(8,128)(2,1)S(1)}, u32[]{:S(2)}, u32[]{:S(2)}) collective-permute-start(bf16[4,320,128]{2,1,0:T(8,128)(2,1)S(1)} %collective-permute-done.5.refs_5_), channel_id=1, source_target_pairs={{0,1},{1,0},{2,3},{3,2},{4,5},{5,4},{6,7},{7,6},{8,9},{9,8},{10,11... | collective-permute-start | bytes 983048 | tf_op jit(solution)/shard_map/weights/ppermute | solution.py:841
  43.0 2.3 %collective-permute-start.8 = (bf16[4,320,128]{2,1,0:T(8,128)(2,1)S(1)}, bf16[4,320,128]{2,1,0:T(8,128)(2,1)S(1)}, u32[]{:S(2)}, u32[]{:S(2)}) collective-permute-start(bf16[4,320,128]{2,1,0:T(8,128)(2,1)S(1)} %collective-permute-done.4.refs_4_), channel_id=1, source_target_pairs={{0,1},{1,0},{2,3},{3,2},{4,5},{5,4},{6,7},{7,6},{8,9},{9,8},{10,11... | collective-permute-start | bytes 983048 | tf_op jit(solution)/shard_map/weights/ppermute | solution.py:841
  43.0 2.3 %collective-permute-start.7 = (bf16[4,320,128]{2,1,0:T(8,128)(2,1)S(1)}, bf16[4,320,128]{2,1,0:T(8,128)(2,1)}, u32[]{:S(2)}, u32[]{:S(2)}) collective-permute-start(bf16[4,320,128]{2,1,0:T(8,128)(2,1)S(1)} %collective-permute-done.3.refs_3_), channel_id=1, source_target_pairs={{0,1},{1,0},{2,3},{3,2},{4,5},{5,4},{6,7},{7,6},{8,9},{9,8},{10,11... | collective-permute-start | bytes 983048 | tf_op jit(solution)/shard_map/weights/ppermute | solution.py:841
  84.3 7.8 %collective-permute-start.10 = (bf16[16,144,256]{2,1,0:T(8,128)(2,1)S(1)}, bf16[16,144,256]{2,1,0:T(8,128)(2,1)S(1)}, u32[]{:S(2)}, u32[]{:S(2)}) collective-permute-start(bf16[16,144,256]{2,1,0:T(8,128)(2,1)S(1)} %get-tuple-element.134), channel_id=1, source_target_pairs={{0,1},{1,0},{2,3},{3,2},{4,5},{5,4},{6,7},{7,6},{8,9},{9,8},{10,11... | collective-permute-start | bytes 3538952 | tf_op jit(solution)/shard_map/ppermute | solution.py:841
  91.8 1.6 %collective-permute-start.11 = (bf16[16,2,32,128]{3,2,1,0:T(8,128)(2,1)S(1)}, bf16[16,2,32,128]{3,2,1,0:T(8,128)(2,1)S(1)}, u32[]{:S(2)}, u32[]{:S(2)}) collective-permute-start(bf16[16,2,32,128]{3,2,1,0:T(8,128)(2,1)S(1)} %get-tuple-element.139), channel_id=1, source_target_pairs={{0,1},{1,0},{2,3},{3,2},{4,5},{5,4},{6,7},{7,6},{8,9},{9,8},{10,11... | collective-permute-start | bytes 786440 | tf_op jit(solution)/shard_map/merge_sum/ppermute | solution.py:841
  93.4 12.0 %collective-permute-start.12 = (bf16[4,144,256]{2,1,0:T(8,128)(2,1)S(1)}, bf16[4,144,256]{2,1,0:T(8,128)(2,1)S(1)}, u32[]{:S(2)}, u32[]{:S(2)}) collective-permute-start(bf16[4,144,256]{2,1,0:T(8,128)(2,1)S(1)} %get-tuple-element.142), channel_id=1, source_target_pairs={{0,2},{1,9},{2,0},{3,11},{4,6},{5,13},{6,4},{7,15},{8,10},{9,1},{1... | collective-permute-start | bytes 884744 | tf_op jit(solution)/shard_map/merge_sum/ppermute | solution.py:837
  93.7 11.7 %collective-permute-start.13 = (bf16[4,144,256]{2,1,0:T(8,128)(2,1)S(1)}, bf16[4,144,256]{2,1,0:T(8,128)(2,1)S(1)}, u32[]{:S(2)}, u32[]{:S(2)}) collective-permute-start(bf16[4,144,256]{2,1,0:T(8,128)(2,1)S(1)} %get-tuple-element.143), channel_id=1, source_target_pairs={{0,4},{1,17},{2,6},{3,19},{4,0},{5,21},{6,2},{7,23},{8,12},{9,25},... | collective-permute-start | bytes 884744 | tf_op jit(solution)/shard_map/merge_sum/ppermute | solution.py:837
  94.7 10.7 %collective-permute-start.14 = (bf16[4,144,256]{2,1,0:T(8,128)(2,1)S(1)}, bf16[4,144,256]{2,1,0:T(8,128)(2,1)S(1)}, u32[]{:S(2)}, u32[]{:S(2)}) collective-permute-start(bf16[4,144,256]{2,1,0:T(8,128)(2,1)S(1)} %get-tuple-element.144), channel_id=1, source_target_pairs={{0,6},{1,25},{2,4},{3,27},{4,2},{5,29},{6,0},{7,31},{8,14},{9,17},... | collective-permute-start | bytes 884744 | tf_op jit(solution)/shard_map/merge_sum/ppermute | solution.py:837
  105.4 15.6 %all-to-all-start.4 = ((bf16[16,2,32,128]{3,2,1,0:T(8,128)(2,1)}), bf16[16,2,32,128]{3,2,1,0:T(8,128)(2,1)S(1)}, u32[]{:S(2)}, u32[]{:S(2)}) async-start(bf16[16,2,32,128]{3,2,1,0:T(8,128)(2,1)} %get-tuple-element.145), calls=%async_computation.4 | async-start | bytes 524288 | tf_op jit(solution)/shard_map/branch_sum/all_to_all | solution.py:1066
  109.6 5.5 %collective-permute-start.15 = (bf16[144,256]{1,0:T(8,128)(2,1)S(1)}, bf16[144,256]{1,0:T(8,128)(2,1)S(1)}, u32[]{:S(2)}, u32[]{:S(2)}) collective-permute-start(bf16[144,256]{1,0:T(8,128)(2,1)S(1)} %get-tuple-element.152), channel_id=1, source_target_pairs={{0,8},{1,3},{2,10},{3,1},{4,12},{5,7},{6,14},{7,5},{8,0},{9,11},{1... | collective-permute-start | bytes 221192 | tf_op jit(solution)/shard_map/merge_sum/ppermute | solution.py:837
  111.5 9.1 %collective-permute-start.16 = (bf16[144,256]{1,0:T(8,128)(2,1)S(1)}, bf16[144,256]{1,0:T(8,128)(2,1)S(1)}, u32[]{:S(2)}, u32[]{:S(2)}) collective-permute-start(bf16[144,256]{1,0:T(8,128)(2,1)S(1)} %get-tuple-element.153), channel_id=1, source_target_pairs={{0,16},{1,5},{2,18},{3,7},{4,20},{5,1},{6,22},{7,3},{8,24},{9,13},... | collective-permute-start | bytes 221192 | tf_op jit(solution)/shard_map/merge_sum/ppermute | solution.py:837
  113.9 7.0 %collective-permute-start.17 = (bf16[144,256]{1,0:T(8,128)(2,1)S(1)}, bf16[144,256]{1,0:T(8,128)(2,1)S(1)}, u32[]{:S(2)}, u32[]{:S(2)}) collective-permute-start(bf16[144,256]{1,0:T(8,128)(2,1)S(1)} %get-tuple-element.154), channel_id=1, source_target_pairs={{0,24},{1,7},{2,26},{3,5},{4,28},{5,3},{6,30},{7,1},{8,16},{9,15},... | collective-permute-start | bytes 221192 | tf_op jit(solution)/shard_map/merge_sum/ppermute | solution.py:837
  124.5 11.5 %collective-permute-start.18 = (f32[352,128]{1,0:T(8,128)S(1)}, f32[352,128]{1,0:T(8,128)S(1)}, u32[]{:S(2)}, u32[]{:S(2)}) collective-permute-start(f32[352,128]{1,0:T(8,128)S(1)} %get-tuple-element.158.refs_2_), channel_id=1, source_target_pairs={{0,1},{1,0},{2,3},{3,2},{4,5},{5,4},{6,7},{7,6},{8,9},{9,8},{10,11... | collective-permute-start | bytes 540680 | tf_op jit(solution)/shard_map/ppermute | solution.py:841

commit v9 on v7

--- a/solution.py
+++ b/solution.py
@@ -1048,8 +1048,8 @@
                 after=(sent_a,),
             )
             away, recv_b = lax.optimization_barrier((low[1:], recv_b))
-            moved = [turn_flip(v, t, dp, 1) for t, v in enumerate(away, 1)]
-            kept_b, kept_a = back(True, 0, 2, recv_b, after=(low[1],))
+            moved = [turn_flip(away[t - 1], t, dp, 1) for t in (3, 2, 1)]
+            kept_b, kept_a = back(True, 0, 2, recv_b)
             kept_b, moved = lax.optimization_barrier((kept_b, moved))
             high = call(
                 split_high_kernel,

time: 141 us -> 141 us (level)
  no operation moved by 1% of the time
where the time goes in v9:
time: 141 us; the launch traced here: 140 us
  Pallas kernels  53 us (38%)
  starting transfers between devices  32.3 us (23%)
  blocking collectives  32.2 us (23%)
  waiting for transfers between devices  21.5 us (15%)
    pallas_call x16, Pallas kernels, call(): pl.pallas_call(kernel, out_shape=tuple(outs), in_specs=in_specs, out_spec...  53 us
    all_to_all x3, blocking collectives, exchange(): return lax.all_to_all(value, BOTH, 0, 0, tiled=True)  32.2 us
    ppermute x6, starting transfers between devices, flip(): return lax.ppermute(value, 'dp', [(i, i ^ mask) for i in range(dp)])  9.31 us
    ppermute x6, waiting for transfers between devices, flip(): return lax.ppermute(value, 'dp', [(i, i ^ mask) for i in range(dp)])  8.75 us
    all_to_all x2, starting transfers between devices, exchange(): return lax.all_to_all(value, BOTH, 0, 0, tiled=True)  8.65 us
    ppermute x6, starting transfers between devices, turn_flip(): return lax.ppermute(value, BOTH, pairs)  7.94 us
    ppermute x6, waiting for transfers between devices, turn_flip(): return lax.ppermute(value, BOTH, pairs)  6.86 us
    all_to_all x2, waiting for transfers between devices, exchange(): return lax.all_to_all(value, BOTH, 0, 0, tiled=True)  5.39 us
  transfers between devices with their start and end apart: 22, of which 7 were waited for; matrix products, arithmetic and copies ran while one was open for 0% of the time, Pallas kernels for 19%

profile of v9, /device:TPU:0, one launch (start us, length us, event | category | flops | bytes accessed | tf_op | source)
XLA Modules:
  0.0 140.2 jit_solution(5695073856095079475)
XLA Ops:
  0.7 0.1 pad_add_fusion.refs_0_
  0.7 1.8 %prep.1 = (bf16[5,32,128]{2,1,0:T(8,128)(2,1)S(1)}, bf16[320,128]{1,0:T(8,128)(2,1)S(1)}) custom-call(s32[2]{0:T(128)S(1)} %pad_add_fusion.refs_0_, f32[4,32,100]{2,1,0:T(8,128)} %bitcast.18, f32[32,47]{1,0:T(8,128)} %refs_13_.1, f32[20,32]{1,0:T(8,128)} %refs_14_.1, f32[128,512]{1,0:T(8,128)} %refs_12_.1), custom_call_target="tpu_custom_call" | custom-call | flops 1024 | bytes 1024 | tf_op jit(solution)/shard_map/prep/pallas_call | solution.py:48
  2.5 5.1 %collective-permute-start.2 = (bf16[320,128]{1,0:T(8,128)(2,1)S(1)}, bf16[320,128]{1,0:T(8,128)(2,1)S(1)}, u32[]{:S(2)}, u32[]{:S(2)}) collective-permute-start(bf16[320,128]{1,0:T(8,128)(2,1)S(1)} %get-tuple-element.108.refs_0_), channel_id=1, source_target_pairs={{0,24},{2,26},{4,28},{6,30},{8,16},{10,18},{12,20},{14,22},{16,8},... | collective-permute-start | bytes 245768 | tf_op jit(solution)/shard_map/ppermute | solution.py:828
  7.6 0.0 collective-permute-start.1
  7.6 0.6 collective-permute-start
  8.3 7.2 %gather.1 = (bf16[4,128,1024]{2,1,0:T(8,128)(2,1)S(1)}, f32[96,4,128]{2,1,0:T(4,128)}, bf16[5,32,128]{2,1,0:T(8,128)(2,1)}) custom-call(s32[1,1024]{1,0:T(1,128)} %bitcast.24, f32[400,4096]{1,0:T(8,128)} %bitcast.17, bf16[5,32,128]{2,1,0:T(8,128)(2,1)S(1)} %get-tuple-element.105.refs_2_), custom_call_target="tpu_custom_call" | custom-call | flops 1024 | bytes 1024 | tf_op jit(solution)/shard_map/gather/pallas_call | solution.py:48
  15.4 0.0 collective-permute-done.2.refs_3_
  15.5 6.0 %all-to-all-start = ((f32[32,3,4,128]{3,2,1,0:T(4,128)}), f32[32,3,4,128]{3,2,1,0:T(4,128)S(1)}, u32[]{:S(2)}, u32[]{:S(2)}) async-start(f32[32,3,4,128]{3,2,1,0:T(4,128)} %bitcast.20), calls=%async_computation | async-start | bytes 393216 | tf_op jit(solution)/shard_map/gram_sum/all_to_all | solution.py:845
  21.5 2.7 %collective-permute-start.5 = (bf16[4,320,128]{2,1,0:T(8,128)(2,1)S(1)}, bf16[4,320,128]{2,1,0:T(8,128)(2,1)S(1)}, u32[]{:S(2)}, u32[]{:S(2)}) collective-permute-start(bf16[4,320,128]{2,1,0:T(8,128)(2,1)S(1)} %gram_sum.2.refs_2_), channel_id=1, source_target_pairs={{0,6},{2,4},{4,2},{6,0},{8,14},{10,12},{12,10},{14,8},{16,22},{18,... | collective-permute-start | bytes 983048 | tf_op jit(solution)/shard_map/ppermute | solution.py:828
  24.2 0.6 collective-permute-start.4
  24.8 0.3 collective-permute-start.3
  25.1 5.4 %all-to-all-done.refs_0_ = f32[32,3,4,128]{3,2,1,0:T(4,128)S(1)} async-done(((f32[32,3,4,128]{3,2,1,0:T(4,128)}), f32[32,3,4,128]{3,2,1,0:T(4,128)S(1)}, u32[]{:S(2)}, u32[]{:S(2)}) %all-to-all-start) | async-done | bytes 196640 | tf_op jit(solution)/shard_map/gram_sum/all_to_all | solution.py:845
  30.5 0.7 gram_sum.3
  31.2 2.7 %all-to-all-start.1 = ((f32[32,3,4,128]{3,2,1,0:T(4,128)}), f32[32,3,4,128]{3,2,1,0:T(4,128)S(1)}, u32[]{:S(2)}, u32[]{:S(2)}) async-start(f32[32,3,4,128]{3,2,1,0:T(4,128)} %gram_sum.3), calls=%async_computation.1 | async-start | bytes 393216 | tf_op jit(solution)/shard_map/gram_sum/all_to_all | solution.py:845
  33.8 0.4 collective-permute-start.6
  34.3 0.6 collective-permute-done.5.refs_5_
  34.9 0.0 collective-permute-start.9
  34.9 8.1 %collective-permute-done.4.refs_4_ = bf16[4,320,128]{2,1,0:T(8,128)(2,1)S(1)} collective-permute-done((bf16[4,320,128]{2,1,0:T(8,128)(2,1)S(1)}, bf16[4,320,128]{2,1,0:T(8,128)(2,1)S(1)}, u32[]{:S(2)}, u32[]{:S(2)}) %collective-permute-start.4) | collective-permute-done | bytes 327712 | tf_op jit(solution)/shard_map/ppermute | solution.py:828
  43.0 0.5 collective-permute-start.7
  43.5 1.8 %own_stats.1 = (f32[4,128,128]{2,1,0:T(8,128)S(1)}, f32[2,32,128]{2,1,0:T(8,128)S(1)}) custom-call(s32[2]{0:T(128)S(1)} %pad_add_fusion.refs_0_, f32[96,4,128]{2,1,0:T(4,128)S(1)} %bitcast.16, bf16[5,32,128]{2,1,0:T(8,128)(2,1)} %get-tuple-element.110.refs_2_), custom_call_target="tpu_custom_call" | custom-call | flops 1024 | bytes 1024 | tf_op jit(solution)/shard_map/own_stats/pallas_call | solution.py:48
  45.3 2.7 %weights.1 = (bf16[5,512,128]{2,1,0:T(8,128)(2,1)S(1)}, bf16[4,2048,128]{2,1,0:T(8,128)(2,1)}) custom-call(s32[2]{0:T(128)S(1)} %pad_add_fusion.refs_0_, f32[2,32,128]{2,1,0:T(8,128)S(1)} %get-tuple-element.112.refs_1_.refs_4_, bf16[4,320,128]{2,1,0:T(8,128)(2,1)S(1)} %gram_sum.2.refs_2_, bf16[4,320,128]{2,1,0:T(8,128)(2,1)S(1)} %collective-permute-done.3.refs_3_, ...), custom_call_target="tpu_custom_call" | custom-call | flops 1024 | bytes 1024 | tf_op jit(solution)/shard_map/weights/pallas_call | solution.py:48
  48.0 1.1 stats.1
  49.1 5.9 %forward.1 = (bf16[4,512,1024]{2,1,0:T(8,128)(2,1)S(1)}, f32[512,1024]{1,0:T(8,128)S(1)}, f32[32,8,128]{2,1,0:T(8,128)S(1)}, bf16[4,128,512]{2,1,0:T(8,128)(2,1)}, f32[2,32,128]{2,1,0:T(8,128)}) custom-call(bf16[4,128,1024]{2,1,0:T(8,128)(2,1)S(1)} %get-tuple-element.106.refs_0_.refs_2_.refs_4_, bf16[4,512,256]{2,1,0:T(8,128)(2,1)S(1)} %get-tuple-element.118.refs_1_.refs_3_, ...), custom_call_target="tpu_custom_call" | custom-call | flops 1024 | bytes 1024 | tf_op jit(solution)/shard_map/forward/pallas_call | solution.py:48
  54.9 12.1 %all_to_all.30.refs_0_ = f32[32,8,128]{2,1,0:T(8,128)S(1)} all-to-all(f32[32,8,128]{2,1,0:T(8,128)S(1)} %get-tuple-element.122), channel_id=1, replica_groups=mesh['dp'=16,'rep'=2] {'dp','rep'}, dimensions={0} | all-to-all | bytes 262144 | tf_op jit(solution)/shard_map/all_to_all | solution.py:845
  67.0 3.6 %head.1 = (f32[512,1024]{1,0:T(8,128)S(1)}, f32[32,8,128]{2,1,0:T(8,128)S(1)}, f32[512,128]{1,0:T(8,128)S(1)}, f32[2,512,128]{2,1,0:T(8,128)S(1)}) custom-call(f32[32,8,128]{2,1,0:T(8,128)S(1)} %all_to_all.30.refs_0_, f32[512,1024]{1,0:T(8,128)S(1)} %get-tuple-element.123.refs_1_.refs_4_, ...), custom_call_target="tpu_custom_call" | custom-call | flops 1024 | bytes 1024 | tf_op jit(solution)/shard_map/head/pallas_call | solution.py:48
  70.6 10.0 %all_to_all.31.refs_1_ = f32[32,8,128]{2,1,0:T(8,128)S(1)} all-to-all(f32[32,8,128]{2,1,0:T(8,128)S(1)} %get-tuple-element.124), channel_id=1, replica_groups=mesh['dp'=16,'rep'=2] {'dp','rep'}, dimensions={0} | all-to-all | bytes 262144 | tf_op jit(solution)/shard_map/all_to_all | solution.py:845
  80.6 3.6 %turn.1 = (bf16[512,1024]{1,0:T(8,128)(2,1)S(1)}, f32[16,144,256]{2,1,0:T(8,128)S(1)}, bf16[16,144,256]{2,1,0:T(8,128)(2,1)S(1)}, f32[8,128]{1,0:T(8,128)S(1)}, bf16[4,2048,128]{2,1,0:T(8,128)(2,1)S(1)}) custom-call(s32[2]{0:T(128)S(1)} %pad_add_fusion.refs_0_, f32[32,8,128]{2,1,0:T(8,128)S(1)} %all_to_all.31.refs_1_, ...), custom_call_target="tpu_custom_call" | custom-call | flops 1024 | bytes 1024 | tf_op jit(solution)/shard_map/turn/pallas_call | solution.py:48
  84.3 0.3 collective-permute-start.10
  84.5 7.5 %back.2 = (bf16[16,2,32,128]{3,2,1,0:T(8,128)(2,1)S(1)}, f32[2,128,1024]{2,1,0:T(8,128)}) custom-call(s32[2]{0:T(128)S(1)} %pad_add_fusion.refs_0_, bf16[512,1024]{1,0:T(8,128)(2,1)S(1)} %get-tuple-element.129.refs_1_, bf16[4,128,1024]{2,1,0:T(8,128)(2,1)S(1)} %get-tuple-element.106.refs_0_.refs_2_.refs_4_, ...), custom_call_target="tpu_custom_call" | custom-call | flops 1024 | bytes 1024 | tf_op jit(solution)/shard_map/merge_sum/back/pallas_call | solution.py:48
  92.0 0.4 collective-permute-start.11
  92.4 0.8 merge_sum.2
  93.2 0.5 collective-permute-done.11.refs_8_
  93.6 0.8 collective-permute-start.12
  94.4 1.0 collective-permute-start.13
  95.4 1.7 %collective-permute-start.14 = (bf16[4,144,256]{2,1,0:T(8,128)(2,1)S(1)}, bf16[4,144,256]{2,1,0:T(8,128)(2,1)S(1)}, u32[]{:S(2)}, u32[]{:S(2)}) collective-permute-start(bf16[4,144,256]{2,1,0:T(8,128)(2,1)S(1)} %get-tuple-element.144), channel_id=1, source_target_pairs={{0,2},{1,9},{2,0},{3,11},{4,6},{5,13},{6,4},{7,15},{8,10},{9,1},{1... | collective-permute-start | bytes 884744 | tf_op jit(solution)/shard_map/merge_sum/ppermute | solution.py:837
  97.1 8.6 %back.3 = (bf16[16,2,32,128]{3,2,1,0:T(8,128)(2,1)}, f32[2,128,1024]{2,1,0:T(8,128)}) custom-call(s32[2]{0:T(128)S(1)} %pad_add_fusion.refs_0_, bf16[512,1024]{1,0:T(8,128)(2,1)S(1)} %get-tuple-element.129.refs_1_, bf16[4,128,1024]{2,1,0:T(8,128)(2,1)S(1)} %get-tuple-element.106.refs_0_.refs_2_.refs_4_, ...), custom_call_target="tpu_custom_call" | custom-call | flops 1024 | bytes 1024 | tf_op jit(solution)/shard_map/merge_sum/back/pallas_call | solution.py:48
  105.8 3.5 %all-to-all-start.4 = ((bf16[16,2,32,128]{3,2,1,0:T(8,128)(2,1)}), bf16[16,2,32,128]{3,2,1,0:T(8,128)(2,1)S(1)}, u32[]{:S(2)}, u32[]{:S(2)}) async-start(bf16[16,2,32,128]{3,2,1,0:T(8,128)(2,1)} %get-tuple-element.145), calls=%async_computation.4 | async-start | bytes 524288 | tf_op jit(solution)/shard_map/branch_sum/all_to_all | solution.py:1066
  109.3 0.7 merge_sum.3
  110.0 1.9 %collective-permute-start.15 = (bf16[144,256]{1,0:T(8,128)(2,1)S(1)}, bf16[144,256]{1,0:T(8,128)(2,1)S(1)}, u32[]{:S(2)}, u32[]{:S(2)}) collective-permute-start(bf16[144,256]{1,0:T(8,128)(2,1)S(1)} %get-tuple-element.152), channel_id=1, source_target_pairs={{0,8},{1,3},{2,10},{3,1},{4,12},{5,7},{6,14},{7,5},{8,0},{9,11},{1... | collective-permute-start | bytes 221192 | tf_op jit(solution)/shard_map/merge_sum/ppermute | solution.py:837
  111.9 2.4 %collective-permute-start.16 = (bf16[144,256]{1,0:T(8,128)(2,1)S(1)}, bf16[144,256]{1,0:T(8,128)(2,1)S(1)}, u32[]{:S(2)}, u32[]{:S(2)}) collective-permute-start(bf16[144,256]{1,0:T(8,128)(2,1)S(1)} %get-tuple-element.153), channel_id=1, source_target_pairs={{0,16},{1,5},{2,18},{3,7},{4,20},{5,1},{6,22},{7,3},{8,24},{9,13},... | collective-permute-start | bytes 221192 | tf_op jit(solution)/shard_map/merge_sum/ppermute | solution.py:837
  114.3 0.1 collective-permute-start.17
  114.5 1.2 collective-permute-done.15.refs_4_
  115.6 5.5 %collective-permute-done.16.refs_5_ = bf16[144,256]{1,0:T(8,128)(2,1)S(1)} collective-permute-done((bf16[144,256]{1,0:T(8,128)(2,1)S(1)}, bf16[144,256]{1,0:T(8,128)(2,1)S(1)}, u32[]{:S(2)}, u32[]{:S(2)}) %collective-permute-start.16) | collective-permute-done | bytes 73760 | tf_op jit(solution)/shard_map/merge_sum/ppermute | solution.py:837
  121.2 0.1 collective-permute-done.17.refs_6_
  121.3 3.5 %owner.1 = (f32[352,128]{1,0:T(8,128)S(1)}, f32[32,2,128]{2,1,0:T(2,128)}, bf16[4,128,512]{2,1,0:T(8,128)(2,1)S(1)}, f32[2,128,1024]{2,1,0:T(8,128)S(1)}, f32[2,...) custom-call(s32[2]{0:T(128)S(1)} %pad_add_fusion.refs_0_, ...), custom_call_target="tpu_custom_call" | custom-call | flops 1024 | bytes 1024 | tf_op jit(solution)/shard_map/owner/pallas_call | solution.py:48
  124.8 1.3 collective-permute-start.18
  126.1 10.2 %all_to_all.32.refs_1_ = f32[32,2,128]{2,1,0:T(2,128)S(1)} all-to-all(f32[32,2,128]{2,1,0:T(2,128)} %get-tuple-element.157), channel_id=1, replica_groups=mesh['dp'=16,'rep'=2] {'dp','rep'}, dimensions={0} | all-to-all | bytes 65536 | tf_op jit(solution)/shard_map/all_to_all | solution.py:845
  136.3 3.7 %final.1 = (f32[4,32,100]{2,1,0:T(8,128)}, f32[128,512]{1,0:T(8,128)}, f32[32,47]{1,0:T(8,128)}, f32[20,32]{1,0:T(8,128)}, f32[4,32,100]{2,1,0:T(8,128)}, /*inde...) custom-call(s32[2]{0:T(128)S(1)} %pad_add_fusion.refs_0_, ...), custom_call_target="tpu_custom_call" | custom-call | flops 1024 | bytes 1024 | tf_op jit(solution)/shard_map/final/pallas_call | solution.py:48
  (16 shorter events, 0.1 us)
Async XLA Ops:
  2.5 12.9 %collective-permute-start.2 = (bf16[320,128]{1,0:T(8,128)(2,1)S(1)}, bf16[320,128]{1,0:T(8,128)(2,1)S(1)}, u32[]{:S(2)}, u32[]{:S(2)}) collective-permute-start(bf16[320,128]{1,0:T(8,128)(2,1)S(1)} %get-tuple-element.108.refs_0_), channel_id=1, source_target_pairs={{0,24},{2,26},{4,28},{6,30},{8,16},{10,18},{12,20},{14,22},{16,8},... | collective-permute-start | bytes 245768 | tf_op jit(solution)/shard_map/ppermute | solution.py:828
  7.6 7.8 %collective-permute-start.1 = (bf16[320,128]{1,0:T(8,128)(2,1)S(1)}, bf16[320,128]{1,0:T(8,128)(2,1)S(1)}, u32[]{:S(2)}, u32[]{:S(2)}) collective-permute-start(bf16[320,128]{1,0:T(8,128)(2,1)S(1)} %get-tuple-element.108.refs_0_), channel_id=1, source_target_pairs={{0,16},{2,18},{4,20},{6,22},{8,24},{10,26},{12,28},{14,30},{16,0},... | collective-permute-start | bytes 245768 | tf_op jit(solution)/shard_map/ppermute | solution.py:828
  7.6 7.8 %collective-permute-start = (bf16[320,128]{1,0:T(8,128)(2,1)S(1)}, bf16[320,128]{1,0:T(8,128)(2,1)S(1)}, u32[]{:S(2)}, u32[]{:S(2)}) collective-permute-start(bf16[320,128]{1,0:T(8,128)(2,1)S(1)} %get-tuple-element.108.refs_0_), channel_id=1, source_target_pairs={{0,8},{2,10},{4,12},{6,14},{8,0},{10,2},{12,4},{14,6},{16,24},{18,... | collective-permute-start | bytes 245768 | tf_op jit(solution)/shard_map/ppermute | solution.py:828
  15.5 15.0 %all-to-all-start = ((f32[32,3,4,128]{3,2,1,0:T(4,128)}), f32[32,3,4,128]{3,2,1,0:T(4,128)S(1)}, u32[]{:S(2)}, u32[]{:S(2)}) async-start(f32[32,3,4,128]{3,2,1,0:T(4,128)} %bitcast.20), calls=%async_computation | async-start | bytes 393216 | tf_op jit(solution)/shard_map/gram_sum/all_to_all | solution.py:845
  21.5 13.4 %collective-permute-start.5 = (bf16[4,320,128]{2,1,0:T(8,128)(2,1)S(1)}, bf16[4,320,128]{2,1,0:T(8,128)(2,1)S(1)}, u32[]{:S(2)}, u32[]{:S(2)}) collective-permute-start(bf16[4,320,128]{2,1,0:T(8,128)(2,1)S(1)} %gram_sum.2.refs_2_), channel_id=1, source_target_pairs={{0,6},{2,4},{4,2},{6,0},{8,14},{10,12},{12,10},{14,8},{16,22},{18,... | collective-permute-start | bytes 983048 | tf_op jit(solution)/shard_map/ppermute | solution.py:828
  24.2 18.8 %collective-permute-start.4 = (bf16[4,320,128]{2,1,0:T(8,128)(2,1)S(1)}, bf16[4,320,128]{2,1,0:T(8,128)(2,1)S(1)}, u32[]{:S(2)}, u32[]{:S(2)}) collective-permute-start(bf16[4,320,128]{2,1,0:T(8,128)(2,1)S(1)} %gram_sum.2.refs_2_), channel_id=1, source_target_pairs={{0,4},{2,6},{4,0},{6,2},{8,12},{10,14},{12,8},{14,10},{16,20},{18,... | collective-permute-start | bytes 983048 | tf_op jit(solution)/shard_map/ppermute | solution.py:828
  24.8 18.2 %collective-permute-start.3 = (bf16[4,320,128]{2,1,0:T(8,128)(2,1)S(1)}, bf16[4,320,128]{2,1,0:T(8,128)(2,1)S(1)}, u32[]{:S(2)}, u32[]{:S(2)}) collective-permute-start(bf16[4,320,128]{2,1,0:T(8,128)(2,1)S(1)} %gram_sum.2.refs_2_), channel_id=1, source_target_pairs={{0,2},{2,0},{4,6},{6,4},{8,10},{10,8},{12,14},{14,12},{16,18},{18,... | collective-permute-start | bytes 983048 | tf_op jit(solution)/shard_map/ppermute | solution.py:828
  31.2 12.3 %all-to-all-start.1 = ((f32[32,3,4,128]{3,2,1,0:T(4,128)}), f32[32,3,4,128]{3,2,1,0:T(4,128)S(1)}, u32[]{:S(2)}, u32[]{:S(2)}) async-start(f32[32,3,4,128]{3,2,1,0:T(4,128)} %gram_sum.3), calls=%async_computation.1 | async-start | bytes 393216 | tf_op jit(solution)/shard_map/gram_sum/all_to_all | solution.py:845
  33.8 11.4 %collective-permute-start.6 = (bf16[4,320,128]{2,1,0:T(8,128)(2,1)S(1)}, bf16[4,320,128]{2,1,0:T(8,128)(2,1)S(1)}, u32[]{:S(2)}, u32[]{:S(2)}) collective-permute-start(bf16[4,320,128]{2,1,0:T(8,128)(2,1)S(1)} %gram_sum.2.refs_2_), channel_id=1, source_target_pairs={{0,1},{1,0},{2,3},{3,2},{4,5},{5,4},{6,7},{7,6},{8,9},{9,8},{10,11... | collective-permute-start | bytes 983048 | tf_op jit(solution)/shard_map/weights/ppermute | solution.py:841
  34.9 10.4 %collective-permute-start.9 = (bf16[4,320,128]{2,1,0:T(8,128)(2,1)S(1)}, bf16[4,320,128]{2,1,0:T(8,128)(2,1)S(1)}, u32[]{:S(2)}, u32[]{:S(2)}) collective-permute-start(bf16[4,320,128]{2,1,0:T(8,128)(2,1)S(1)} %collective-permute-done.5.refs_5_), channel_id=1, source_target_pairs={{0,1},{1,0},{2,3},{3,2},{4,5},{5,4},{6,7},{7,6},{8,9},{9,8},{10,11... | collective-permute-start | bytes 983048 | tf_op jit(solution)/shard_map/weights/ppermute | solution.py:841
  43.0 2.3 %collective-permute-start.8 = (bf16[4,320,128]{2,1,0:T(8,128)(2,1)S(1)}, bf16[4,320,128]{2,1,0:T(8,128)(2,1)S(1)}, u32[]{:S(2)}, u32[]{:S(2)}) collective-permute-start(bf16[4,320,128]{2,1,0:T(8,128)(2,1)S(1)} %collective-permute-done.4.refs_4_), channel_id=1, source_target_pairs={{0,1},{1,0},{2,3},{3,2},{4,5},{5,4},{6,7},{7,6},{8,9},{9,8},{10,11... | collective-permute-start | bytes 983048 | tf_op jit(solution)/shard_map/weights/ppermute | solution.py:841
  43.0 2.3 %collective-permute-start.7 = (bf16[4,320,128]{2,1,0:T(8,128)(2,1)S(1)}, bf16[4,320,128]{2,1,0:T(8,128)(2,1)}, u32[]{:S(2)}, u32[]{:S(2)}) collective-permute-start(bf16[4,320,128]{2,1,0:T(8,128)(2,1)S(1)} %collective-permute-done.3.refs_3_), channel_id=1, source_target_pairs={{0,1},{1,0},{2,3},{3,2},{4,5},{5,4},{6,7},{7,6},{8,9},{9,8},{10,11... | collective-permute-start | bytes 983048 | tf_op jit(solution)/shard_map/weights/ppermute | solution.py:841
  84.3 8.1 %collective-permute-start.10 = (bf16[16,144,256]{2,1,0:T(8,128)(2,1)S(1)}, bf16[16,144,256]{2,1,0:T(8,128)(2,1)S(1)}, u32[]{:S(2)}, u32[]{:S(2)}) collective-permute-start(bf16[16,144,256]{2,1,0:T(8,128)(2,1)S(1)} %get-tuple-element.134), channel_id=1, source_target_pairs={{0,1},{1,0},{2,3},{3,2},{4,5},{5,4},{6,7},{7,6},{8,9},{9,8},{10,11... | collective-permute-start | bytes 3538952 | tf_op jit(solution)/shard_map/ppermute | solution.py:841
  92.0 1.6 %collective-permute-start.11 = (bf16[16,2,32,128]{3,2,1,0:T(8,128)(2,1)S(1)}, bf16[16,2,32,128]{3,2,1,0:T(8,128)(2,1)S(1)}, u32[]{:S(2)}, u32[]{:S(2)}) collective-permute-start(bf16[16,2,32,128]{3,2,1,0:T(8,128)(2,1)S(1)} %get-tuple-element.139), channel_id=1, source_target_pairs={{0,1},{1,0},{2,3},{3,2},{4,5},{5,4},{6,7},{7,6},{8,9},{9,8},{10,11... | collective-permute-start | bytes 786440 | tf_op jit(solution)/shard_map/merge_sum/ppermute | solution.py:841
  93.6 12.1 %collective-permute-start.12 = (bf16[4,144,256]{2,1,0:T(8,128)(2,1)S(1)}, bf16[4,144,256]{2,1,0:T(8,128)(2,1)S(1)}, u32[]{:S(2)}, u32[]{:S(2)}) collective-permute-start(bf16[4,144,256]{2,1,0:T(8,128)(2,1)S(1)} %get-tuple-element.142), channel_id=1, source_target_pairs={{0,6},{1,25},{2,4},{3,27},{4,2},{5,29},{6,0},{7,31},{8,14},{9,17},... | collective-permute-start | bytes 884744 | tf_op jit(solution)/shard_map/merge_sum/ppermute | solution.py:837
  94.4 11.3 %collective-permute-start.13 = (bf16[4,144,256]{2,1,0:T(8,128)(2,1)S(1)}, bf16[4,144,256]{2,1,0:T(8,128)(2,1)S(1)}, u32[]{:S(2)}, u32[]{:S(2)}) collective-permute-start(bf16[4,144,256]{2,1,0:T(8,128)(2,1)S(1)} %get-tuple-element.143), channel_id=1, source_target_pairs={{0,4},{1,17},{2,6},{3,19},{4,0},{5,21},{6,2},{7,23},{8,12},{9,25},... | collective-permute-start | bytes 884744 | tf_op jit(solution)/shard_map/merge_sum/ppermute | solution.py:837
  95.4 10.3 %collective-permute-start.14 = (bf16[4,144,256]{2,1,0:T(8,128)(2,1)S(1)}, bf16[4,144,256]{2,1,0:T(8,128)(2,1)S(1)}, u32[]{:S(2)}, u32[]{:S(2)}) collective-permute-start(bf16[4,144,256]{2,1,0:T(8,128)(2,1)S(1)} %get-tuple-element.144), channel_id=1, source_target_pairs={{0,2},{1,9},{2,0},{3,11},{4,6},{5,13},{6,4},{7,15},{8,10},{9,1},{1... | collective-permute-start | bytes 884744 | tf_op jit(solution)/shard_map/merge_sum/ppermute | solution.py:837
  105.8 15.6 %all-to-all-start.4 = ((bf16[16,2,32,128]{3,2,1,0:T(8,128)(2,1)}), bf16[16,2,32,128]{3,2,1,0:T(8,128)(2,1)S(1)}, u32[]{:S(2)}, u32[]{:S(2)}) async-start(bf16[16,2,32,128]{3,2,1,0:T(8,128)(2,1)} %get-tuple-element.145), calls=%async_computation.4 | async-start | bytes 524288 | tf_op jit(solution)/shard_map/branch_sum/all_to_all | solution.py:1066
  110.0 5.6 %collective-permute-start.15 = (bf16[144,256]{1,0:T(8,128)(2,1)S(1)}, bf16[144,256]{1,0:T(8,128)(2,1)S(1)}, u32[]{:S(2)}, u32[]{:S(2)}) collective-permute-start(bf16[144,256]{1,0:T(8,128)(2,1)S(1)} %get-tuple-element.152), channel_id=1, source_target_pairs={{0,8},{1,3},{2,10},{3,1},{4,12},{5,7},{6,14},{7,5},{8,0},{9,11},{1... | collective-permute-start | bytes 221192 | tf_op jit(solution)/shard_map/merge_sum/ppermute | solution.py:837
  111.9 9.3 %collective-permute-start.16 = (bf16[144,256]{1,0:T(8,128)(2,1)S(1)}, bf16[144,256]{1,0:T(8,128)(2,1)S(1)}, u32[]{:S(2)}, u32[]{:S(2)}) collective-permute-start(bf16[144,256]{1,0:T(8,128)(2,1)S(1)} %get-tuple-element.153), channel_id=1, source_target_pairs={{0,16},{1,5},{2,18},{3,7},{4,20},{5,1},{6,22},{7,3},{8,24},{9,13},... | collective-permute-start | bytes 221192 | tf_op jit(solution)/shard_map/merge_sum/ppermute | solution.py:837
  114.3 7.0 %collective-permute-start.17 = (bf16[144,256]{1,0:T(8,128)(2,1)S(1)}, bf16[144,256]{1,0:T(8,128)(2,1)S(1)}, u32[]{:S(2)}, u32[]{:S(2)}) collective-permute-start(bf16[144,256]{1,0:T(8,128)(2,1)S(1)} %get-tuple-element.154), channel_id=1, source_target_pairs={{0,24},{1,7},{2,26},{3,5},{4,28},{5,3},{6,30},{7,1},{8,16},{9,15},... | collective-permute-start | bytes 221192 | tf_op jit(solution)/shard_map/merge_sum/ppermute | solution.py:837
  124.8 11.5 %collective-permute-start.18 = (f32[352,128]{1,0:T(8,128)S(1)}, f32[352,128]{1,0:T(8,128)S(1)}, u32[]{:S(2)}, u32[]{:S(2)}) collective-permute-start(f32[352,128]{1,0:T(8,128)S(1)} %get-tuple-element.158.refs_2_), channel_id=1, source_target_pairs={{0,1},{1,0},{2,3},{3,2},{4,5},{5,4},{6,7},{7,6},{8,9},{9,8},{10,11... | collective-permute-start | bytes 540680 | tf_op jit(solution)/shard_map/ppermute | solution.py:841
